TPU v7x, 32 devices: a whole 2x2x4 slice. The times are simulated.
32 devices in a mesh: gx: 16 (over z, y, core), gy: 2 (over x).
Axes of the slice: x: 2, y: 2, z: 4, core: 2. Of those that a mesh axis runs over, the one named last changes fastest.
Arguments:
- target: float32 [256, 128, 256], P('gx', None, 'gy'), may hold values from -6 to 6
- plane_xy: float32 [32, 256, 256], P(None, 'gx', 'gy'), may hold values from 0.4 to 1.6
- plane_xz: float32 [32, 256, 128], P(None, 'gx', 'gy'), may hold values from 0.4 to 1.6
- plane_yz: float32 [32, 128, 256], P(None, 'gx', 'gy'), may hold values from 0.4 to 1.6
- first_xy: float32 [32, 256, 256], P(None, 'gx', 'gy'), may hold values from -6 to 6
- first_xz: float32 [32, 256, 128], P(None, 'gx', 'gy'), may hold values from -6 to 6
- first_yz: float32 [32, 128, 256], P(None, 'gx', 'gy'), may hold values from -6 to 6
- second_xy: float32 [32, 256, 256], P(None, 'gx', 'gy'), may hold values from 0.5 to 8
- second_xz: float32 [32, 256, 128], P(None, 'gx', 'gy'), may hold values from 0.5 to 8
- second_yz: float32 [32, 128, 256], P(None, 'gx', 'gy'), may hold values from 0.5 to 8
- w_hidden: bfloat16 [32, 32], replicated, may hold values from -1 to 1
- b_hidden: float32 [32], replicated, may hold values from -3 to 3
- w_output: bfloat16 [32], replicated, may hold values from -1 to 1
- b_output: float32 [1], replicated, may hold values from -3 to 3
Outputs:
- updated_xy: float32 [32, 256, 256], P(None, 'gx', 'gy')
- updated_xz: float32 [32, 256, 128], P(None, 'gx', 'gy')
- updated_yz: float32 [32, 128, 256], P(None, 'gx', 'gy')
- mean_xy: float32 [32, 256, 256], P(None, 'gx', 'gy')
- mean_xz: float32 [32, 256, 128], P(None, 'gx', 'gy')
- mean_yz: float32 [32, 128, 256], P(None, 'gx', 'gy')
- square_xy: float32 [32, 256, 256], P(None, 'gx', 'gy')
- square_xz: float32 [32, 256, 128], P(None, 'gx', 'gy')
- square_yz: float32 [32, 128, 256], P(None, 'gx', 'gy')
All inputs are finite; a program needn't handle non-finite values.
Results may differ from a plain program's by a relative error of at most 0.00053.
Values sent between devices are 32-bit elements; how exact they have to be, the bound alone decides.
No kernel may reach another device: no remote copies, remote signals or barrier semaphores. Data moves between devices by JAX's collectives and lax.ppermute only.
A program may use at most 64 MiB of HBM per device.

v0:
```python
import jax
import jax.numpy as jnp
from jax import lax
from jax.sharding import PartitionSpec as P

STEPS = 2
START = 20


SMOOTHING = 0.5
BETA_ONE = 0.9
BETA_TWO = 0.99
LEARN_RATE = 0.01
EPSILON = 1e-08


def padded_2(x, sides, width):
    for axis, dim in sides:
        peers, length = (lax.axis_size(axis), x.shape[dim])
        up = [(i, (i + 1) % peers) for i in range(peers - 1)]
        down = [(j, i) for i, j in up]
        last = lax.slice_in_dim(x, length - width, length, axis=dim)
        first = lax.slice_in_dim(x, 0, width, axis=dim)
        before = lax.ppermute(last, axis, up)
        after = lax.ppermute(first, axis, down)
        x = jnp.concatenate([before, x, after], axis=dim)
    return x


def smooth(plane):
    padded = padded_2(plane, (("gx", 1), ("gy", 2)), 1)
    down = padded[:, 1:, 1:-1] - padded[:, :-1, 1:-1]
    across = padded[:, 1:-1, 1:] - padded[:, 1:-1, :-1]
    row_count = down.shape[1]
    col_count = across.shape[2]
    row_places = jnp.arange(row_count)
    col_places = jnp.arange(col_count)
    lowest_x = lax.axis_index("gx") == 0
    highest_x = lax.axis_index("gx") == lax.axis_size("gx") - 1
    lowest_y = lax.axis_index("gy") == 0
    highest_y = lax.axis_index("gy") == lax.axis_size("gy") - 1
    row_keeps = jnp.where(
        (row_places == 0) & lowest_x | (row_places == row_count - 1) & highest_x, 0.0, 1.0
    )
    col_keeps = jnp.where(
        (col_places == 0) & lowest_y | (col_places == col_count - 1) & highest_y, 0.0, 1.0
    )
    down = down * row_keeps[None, :, None]
    across = across * col_keeps[None, None, :]
    return (
        2.0 * SMOOTHING * (down[:, :-1, :] - down[:, 1:, :] + across[:, :, :-1] - across[:, :, 1:])
    )


def data_grads(target, plane_xy, whole_xz, whole_yz, w_hidden, b_hidden, w_output, b_output):
    weights_out = w_output.astype(jnp.float32)

    def one_row(running, inputs):
        target_row, row_xy, row_xz = inputs
        cross = row_xz[:, :, None] * whole_yz
        features = (row_xy[:, None, :] * cross).astype(jnp.bfloat16)
        preact = (
            jnp.einsum("ch,czy->hzy", w_hidden, features, preferred_element_type=jnp.float32)
            + b_hidden[:, None, None]
        )
        sigma = jax.nn.sigmoid(preact)
        hidden = (preact * sigma).astype(jnp.bfloat16)
        output = (
            jnp.einsum("h,hzy->zy", w_output, hidden, preferred_element_type=jnp.float32)
            + b_output[0]
        )
        residual = output - target_row
        back_hidden = (
            weights_out[:, None, None] * residual[None] * (sigma * (1.0 + preact * (1.0 - sigma)))
        ).astype(jnp.bfloat16)
        back_feature = jnp.einsum(
            "ch,hzy->czy", w_hidden, back_hidden, preferred_element_type=jnp.float32
        )
        grad_row_xy = jnp.sum(back_feature * cross, axis=1)
        with_xy = back_feature * row_xy[:, None, :]
        grad_row_xz = jnp.sum(with_xy * whole_yz, axis=2)
        running = running + with_xy * row_xz[:, :, None]
        return (running, (grad_row_xy, grad_row_xz))

    start = jnp.zeros(whole_yz.shape, jnp.float32)
    grad_yz, (rows_xy, rows_xz) = lax.scan(
        one_row, start, (target, jnp.moveaxis(plane_xy, 1, 0), jnp.moveaxis(whole_xz, 1, 0))
    )
    return (jnp.moveaxis(rows_xy, 0, 1), jnp.moveaxis(rows_xz, 0, 1), grad_yz)


def adam(plane, first, second, grads, count):
    first = BETA_ONE * first + (1.0 - BETA_ONE) * grads
    second = BETA_TWO * second + (1.0 - BETA_TWO) * grads * grads
    corr_one = 1.0 - BETA_ONE**count
    corr_two = 1.0 - BETA_TWO**count
    plane = plane - LEARN_RATE * (first / corr_one) / (jnp.sqrt(second / corr_two) + EPSILON)
    return (plane, first, second)


def per_device(
    target,
    plane_xy,
    plane_xz,
    plane_yz,
    first_xy,
    first_xz,
    first_yz,
    second_xy,
    second_xz,
    second_yz,
    w_hidden,
    b_hidden,
    w_output,
    b_output,
):
    for iteration in range(STEPS):
        whole_xz = lax.all_gather(plane_xz, "gy", axis=2, tiled=True)
        whole_yz = lax.all_gather(plane_yz, "gx", axis=1, tiled=True)
        grad_xy, term_xz, term_yz = data_grads(
            target, plane_xy, whole_xz, whole_yz, w_hidden, b_hidden, w_output, b_output
        )
        grad_xy = grad_xy + smooth(plane_xy)
        grad_xz = lax.psum_scatter(term_xz, "gy", scatter_dimension=2, tiled=True) + smooth(
            plane_xz
        )
        grad_yz = lax.psum_scatter(term_yz, "gx", scatter_dimension=1, tiled=True) + smooth(
            plane_yz
        )
        count = START + iteration + 1
        plane_xy, first_xy, second_xy = adam(plane_xy, first_xy, second_xy, grad_xy, count)
        plane_xz, first_xz, second_xz = adam(plane_xz, first_xz, second_xz, grad_xz, count)
        plane_yz, first_yz, second_yz = adam(plane_yz, first_yz, second_yz, grad_yz, count)
    return (
        plane_xy,
        plane_xz,
        plane_yz,
        first_xy,
        first_xz,
        first_yz,
        second_xy,
        second_xz,
        second_yz,
    )


def solution(mesh):
    return jax.shard_map(
        per_device,
        mesh=mesh,
        in_specs=(
            P("gx", None, "gy"),
            P(None, "gx", "gy"),
            P(None, "gx", "gy"),
            P(None, "gx", "gy"),
            P(None, "gx", "gy"),
            P(None, "gx", "gy"),
            P(None, "gx", "gy"),
            P(None, "gx", "gy"),
            P(None, "gx", "gy"),
            P(None, "gx", "gy"),
            P(),
            P(),
            P(),
            P(),
        ),
        out_specs=(
            P(None, "gx", "gy"),
            P(None, "gx", "gy"),
            P(None, "gx", "gy"),
            P(None, "gx", "gy"),
            P(None, "gx", "gy"),
            P(None, "gx", "gy"),
            P(None, "gx", "gy"),
            P(None, "gx", "gy"),
            P(None, "gx", "gy"),
        ),
        check_vma=False,
    )
```

profile of v0, /device:TPU:0, one launch (start us, length us, event | category | flops | bytes accessed | tf_op | source)
XLA Modules:
  0.0 718.8 jit_solution(16919359880765177254)
XLA Ops:
  13.0 15.6 %all_gather.12 = f32[32,16,128]{0,2,1:T(8,128)} all-gather(f32[32,16,64]{0,2,1:T(8,128)S(1)} %copy.40), channel_id=1, replica_groups=mesh['gx'=16,'gy'=2] {'gy'}, dimensions={2}, use_global_device_ids=true | all-gather | bytes 393216 | tf_op jit(solution)/shard_map/all_gather | solution.py:118
  28.6 26.4 %all-gather.3.cloned.1.call-done = f32[32,128,128]{2,0,1:T(8,128)} async-done(((f32[32,8,128]{2,0,1:T(8,128)}), f32[32,128,128]{2,0,1:T(8,128)}) %all-gather.3.cloned.1.call-update) | async-done | bytes 2097168 | tf_op jit(solution)/shard_map/all_gather | solution.py:119
  55.1 220.1 %while.30 = (s32[]{:T(128)}, f32[32,128,128]{2,0,1:T(8,128)}, f32[16,32,128]{2,0,1:T(8,128)S(1)}, f32[16,32,128]{1,2,0:T(8,128)S(1)}, f32[32]{0:T(128)}, /*index...) while((s32[]{:T(128)}, f32[32,128,128]{2,0,1:T(8,128)}, ...), condition=%wide.region_3.4_spmd.clone, body=%wide.region_0.3_spmd.clone.sunk | while | flops 83386368 | bytes 32117412 | solution.py:86
  62.1 5.3 multiply_reduce_fusion.4
  75.2 6.0 multiply_reduce_fusion.4
  89.0 6.0 multiply_reduce_fusion.4
  102.8 6.0 multiply_reduce_fusion.4
  116.6 6.0 multiply_reduce_fusion.4
  130.4 6.0 multiply_reduce_fusion.4
  144.2 6.0 multiply_reduce_fusion.4
  158.0 6.0 multiply_reduce_fusion.4
  171.8 6.0 multiply_reduce_fusion.4
  185.6 6.0 multiply_reduce_fusion.4
  199.4 6.0 multiply_reduce_fusion.4
  213.2 6.0 multiply_reduce_fusion.4
  227.0 6.0 multiply_reduce_fusion.4
  240.8 6.0 multiply_reduce_fusion.4
  254.6 6.0 multiply_reduce_fusion.4
  268.4 6.0 multiply_reduce_fusion.4
  288.0 6.0 collective-permute-start.11
  301.3 38.9 %reduce-scatter.9.cloned.1.call-done = f32[32,8,128]{2,1,0:T(8,128)} async-done(((f32[32,128,128]{2,1,0:T(8,128)}), f32[32,8,128]{2,1,0:T(8,128)}) %reduce-scatter.9.cloned.1.call-update) | async-done | bytes 131088 | tf_op jit(solution)/shard_map/reduce_scatter | solution.py:127
  353.3 4.6 collective-permute-start.7
  358.1 7.1 collective-permute-done.6
  368.9 4.8 collective-permute-start.3
  373.8 7.6 %collective-permute-done.2 = f32[32,18,1]{2,1,0:T(8,128)S(1)} collective-permute-done((f32[32,18,1]{2,1,0:T(8,128)S(1)}, f32[32,18,1]{2,1,0:T(8,128)S(1)}, u32[]{:S(2)}, u32[]{:S(2)}) %collective-permute-start.2) | collective-permute-done | bytes 2336 | tf_op jit(solution)/shard_map/ppermute | solution.py:25
  388.7 15.0 %all_gather.14 = f32[32,16,128]{0,1,2:T(8,128)} all-gather(f32[32,16,64]{0,1,2:T(8,128)S(1)} %copy.45), channel_id=1, replica_groups=mesh['gx'=16,'gy'=2] {'gy'}, dimensions={2}, use_global_device_ids=true | all-gather | bytes 393216 | tf_op jit(solution)/shard_map/all_gather | solution.py:118
  408.4 219.2 %while.31 = (s32[]{:T(128)}, f32[32,128,128]{2,0,1:T(8,128)}, f32[16,32,128]{2,0,1:T(8,128)}, f32[16,32,128]{1,2,0:T(8,128)}, f32[32]{0:T(128)}, /*index=5*/f32[...) while((s32[]{:T(128)}, f32[32,128,128]{2,0,1:T(8,128)}, ...), condition=%wide.region_9.10_spmd.clone, body=%wide.region_6.9_spmd.clone.sunk | while | flops 83386368 | bytes 23680136 | solution.py:86
  413.9 5.3 multiply_reduce_fusion.5
  427.0 6.0 multiply_reduce_fusion.5
  440.7 6.0 multiply_reduce_fusion.5
  454.5 6.0 multiply_reduce_fusion.5
  468.2 6.0 multiply_reduce_fusion.5
  481.9 6.0 multiply_reduce_fusion.5
  495.7 6.0 multiply_reduce_fusion.5
  509.4 6.0 multiply_reduce_fusion.5
  523.2 6.0 multiply_reduce_fusion.5
  536.9 6.0 multiply_reduce_fusion.5
  550.7 6.0 multiply_reduce_fusion.5
  564.4 6.0 multiply_reduce_fusion.5
  578.2 6.0 multiply_reduce_fusion.5
  591.9 6.0 multiply_reduce_fusion.5
  605.7 6.0 multiply_reduce_fusion.5
  619.4 6.0 multiply_reduce_fusion.5
  639.5 6.0 collective-permute-start.15
  656.7 4.6 collective-permute-start.19
  671.7 4.6 collective-permute-start.23
  677.1 4.4 collective-permute-done.22
  688.0 22.1 %reduce-scatter.11.cloned.1.call-done = f32[32,8,128]{2,1,0:T(8,128)} async-done(((f32[32,128,128]{2,1,0:T(8,128)}), f32[32,8,128]{2,1,0:T(8,128)}) %reduce-scatter.11.cloned.1.call-update) | async-done | bytes 131088 | tf_op jit(solution)/shard_map/reduce_scatter | solution.py:127
  (500 shorter events, 344.6 us)
Async XLA Ops:
  7.2 47.8 %all-gather.3.cloned.1.call-start = ((), (), s32[]{:S(2)}) async-start(), calls=%async_computation.4 | async-start | bytes 2228224 | tf_op jit(solution)/shard_map/all_gather | solution.py:119
  8.8 331.4 %reduce-scatter.9.cloned.1.call-start = ((), (), s32[]{:S(2)}) async-start(), calls=%async_computation.5 | async-start | bytes 2228224 | tf_op jit(solution)/shard_map/reduce_scatter | solution.py:127
  279.5 104.4 %reduce-scatter.13.cloned.1.call-start = ((), (), s32[]{:S(2)}) async-start(), calls=%async_computation.8 | async-start | bytes 393216
  280.4 5.4 collective-permute-start.8
  281.7 4.1 collective-permute-start.9
  286.8 10.9 %collective-permute-start.10 = (f32[32,10,1]{2,1,0:T(8,128)}, f32[32,10,1]{2,1,0:T(8,128)}, u32[]{:S(2)}, u32[]{:S(2)}) collective-permute-start(f32[32,10,1]{2,1,0:T(8,128)} %get-tuple-element.361), channel_id=1, source_target_pairs={{1,0},{3,2},{5,4},{7,6},{9,8},{11,10},{13,12},{15,14},{17,16},{19,... | collective-permute-start | bytes 3848 | tf_op jit(solution)/shard_map/ppermute | solution.py:25
  288.0 12.0 %collective-permute-start.11 = (f32[32,10,1]{2,1,0:T(8,128)}, f32[32,10,1]{2,1,0:T(8,128)}, u32[]{:S(2)}, u32[]{:S(2)}) collective-permute-start(f32[32,10,1]{2,1,0:T(8,128)} %get-tuple-element.362), channel_id=1, source_target_pairs={{0,1},{2,3},{4,5},{6,7},{8,9},{10,11},{12,13},{14,15},{16,17},{18,... | collective-permute-start | bytes 3848 | tf_op jit(solution)/shard_map/ppermute | solution.py:24
  294.7 45.5 %copy-start.20 = (f32[32,8,128]{2,1,0:T(8,128)S(1)}, f32[32,8,128]{2,1,0:T(8,128)}, u32[]{:S(2)}) copy-start(f32[32,8,128]{2,1,0:T(8,128)} %param.24) | copy-start | bytes 393220
  294.7 45.5 %copy-start.22 = (f32[32,8,128]{2,1,0:T(8,128)S(1)}, f32[32,8,128]{2,1,0:T(8,128)}, u32[]{:S(2)}) copy-start(f32[32,8,128]{2,1,0:T(8,128)} %param.27) | copy-start | bytes 393220
  297.0 45.0 %copy-start.4 = (f32[32,16,128]{2,1,0:T(8,128)S(1)}, f32[32,16,128]{2,1,0:T(8,128)}, u32[]{:S(2)}) copy-start(f32[32,16,128]{2,1,0:T(8,128)} %param.19) | copy-start | bytes 786436
  297.0 49.4 %copy-start.3 = (f32[32,16,64]{2,1,0:T(8,128)S(1)}, f32[32,16,64]{2,1,0:T(8,128)}, u32[]{:S(2)}) copy-start(f32[32,16,64]{2,1,0:T(8,128)} %param.20) | copy-start | bytes 393220
  297.0 106.7 %all-gather.5.cloned.1.call-start = ((), (), s32[]{:S(2)}) async-start(), calls=%async_computation.6 | async-start | bytes 2228224 | tf_op jit(solution)/shard_map/all_gather | solution.py:119
  342.0 342.9 %reduce-scatter.15.cloned.1.call-start = ((), (), s32[]{:S(2)}) async-start(), calls=%async_computation.9 | async-start | bytes 393216
  342.1 25.1 %collective-permute-start = (f32[32,1,128]{2,1,0:T(1,128)S(1)}, f32[32,1,128]{2,1,0:T(1,128)S(1)}, u32[]{:S(2)}, u32[]{:S(2)}) collective-permute-start(f32[32,1,128]{2,1,0:T(1,128)S(1)} %get-tuple-element.368), channel_id=1, source_target_pairs={{2,0},{4,2},{6,4},{8,6},{10,8},{12,10},{14,12},{16,14},{18,16},{20... | collective-permute-start | bytes 49160 | tf_op jit(solution)/shard_map/ppermute | solution.py:25
  343.4 23.8 %collective-permute-start.1 = (f32[32,1,128]{2,1,0:T(1,128)S(1)}, f32[32,1,128]{2,1,0:T(1,128)S(1)}, u32[]{:S(2)}, u32[]{:S(2)}) collective-permute-start(f32[32,1,128]{2,1,0:T(1,128)S(1)} %get-tuple-element.367), channel_id=1, source_target_pairs={{0,2},{2,4},{4,6},{6,8},{8,10},{10,12},{12,14},{14,16},{16,18},{18... | collective-permute-start | bytes 49160 | tf_op jit(solution)/shard_map/ppermute | solution.py:24
  346.5 4.6 collective-permute-start.4
  347.8 4.0 collective-permute-start.5
  351.0 22.7 %copy-start.29 = (f32[17]{0:T(128)}, f32[17]{0:T(128)S(1)}, u32[]{:S(2)}) copy-start(f32[17]{0:T(128)S(1)} %or_select_fusion.3) | copy-start | bytes 208
  351.0 16.1 %copy-start.31 = (f32[65]{0:T(128)}, f32[65]{0:T(128)S(1)}, u32[]{:S(2)}) copy-start(f32[65]{0:T(128)S(1)} %or_select_fusion.1) | copy-start | bytes 784
  352.0 13.1 %collective-permute-start.6 = (f32[32,18,1]{2,1,0:T(8,128)S(1)}, f32[32,18,1]{2,1,0:T(8,128)S(1)}, u32[]{:S(2)}, u32[]{:S(2)}) collective-permute-start(f32[32,18,1]{2,1,0:T(8,128)S(1)} %get-tuple-element.351), channel_id=1, source_target_pairs={{1,0},{3,2},{5,4},{7,6},{9,8},{11,10},{13,12},{15,14},{17,16},{19,... | collective-permute-start | bytes 6920 | tf_op jit(solution)/shard_map/ppermute | solution.py:25
  353.3 13.5 %collective-permute-start.7 = (f32[32,18,1]{2,1,0:T(8,128)S(1)}, f32[32,18,1]{2,1,0:T(8,128)S(1)}, u32[]{:S(2)}, u32[]{:S(2)}) collective-permute-start(f32[32,18,1]{2,1,0:T(8,128)S(1)} %get-tuple-element.352), channel_id=1, source_target_pairs={{0,1},{2,3},{4,5},{6,7},{8,9},{10,11},{12,13},{14,15},{16,17},{18,... | collective-permute-start | bytes 6920 | tf_op jit(solution)/shard_map/ppermute | solution.py:24
  358.0 24.5 %copy-start.27 = (f32[129]{0:T(256)S(1)}, f32[129]{0:T(256)}, u32[]{:S(2)}) copy-start(f32[129]{0:T(256)} %or_select_fusion.2) | copy-start | bytes 1552
  367.2 15.6 %copy-start.8 = (f32[32,16,128]{2,1,0:T(8,128)S(1)}, f32[32,16,128]{2,1,0:T(8,128)}, u32[]{:S(2)}) copy-start(f32[32,16,128]{2,1,0:T(8,128)} %param.22) | copy-start | bytes 786436
  367.2 15.6 %copy-start.9 = (f32[32,16,128]{2,1,0:T(8,128)S(1)}, f32[32,16,128]{2,1,0:T(8,128)}, u32[]{:S(2)}) copy-start(f32[32,16,128]{2,1,0:T(8,128)} %param.25) | copy-start | bytes 786436
  367.4 13.9 %collective-permute-start.2 = (f32[32,18,1]{2,1,0:T(8,128)S(1)}, f32[32,18,1]{2,1,0:T(8,128)S(1)}, u32[]{:S(2)}, u32[]{:S(2)}) collective-permute-start(f32[32,18,1]{2,1,0:T(8,128)S(1)} %get-tuple-element.355), channel_id=1, source_target_pairs={{1,0},{3,2},{5,4},{7,6},{9,8},{11,10},{13,12},{15,14},{17,16},{19,... | collective-permute-start | bytes 6920 | tf_op jit(solution)/shard_map/ppermute | solution.py:25
  368.9 13.7 %collective-permute-start.3 = (f32[32,18,1]{2,1,0:T(8,128)S(1)}, f32[32,18,1]{2,1,0:T(8,128)S(1)}, u32[]{:S(2)}, u32[]{:S(2)}) collective-permute-start(f32[32,18,1]{2,1,0:T(8,128)S(1)} %get-tuple-element.356), channel_id=1, source_target_pairs={{0,1},{2,3},{4,5},{6,7},{8,9},{10,11},{12,13},{14,15},{16,17},{18,... | collective-permute-start | bytes 6920 | tf_op jit(solution)/shard_map/ppermute | solution.py:24
  631.8 78.4 %reduce-scatter.11.cloned.1.call-start = ((), (), s32[]{:S(2)}) async-start(), calls=%async_computation.7 | async-start | bytes 2228224 | tf_op jit(solution)/shard_map/reduce_scatter | solution.py:127
  631.8 4.5 collective-permute-start.12
  633.3 3.9 collective-permute-start.13
  638.2 15.4 %collective-permute-start.14 = (f32[32,18,1]{2,1,0:T(8,128)}, f32[32,18,1]{2,1,0:T(8,128)}, u32[]{:S(2)}, u32[]{:S(2)}) collective-permute-start(f32[32,18,1]{2,1,0:T(8,128)} %get-tuple-element.353), channel_id=1, source_target_pairs={{1,0},{3,2},{5,4},{7,6},{9,8},{11,10},{13,12},{15,14},{17,16},{19,... | collective-permute-start | bytes 6920 | tf_op jit(solution)/shard_map/ppermute | solution.py:25
  639.5 14.3 %collective-permute-start.15 = (f32[32,18,1]{2,1,0:T(8,128)}, f32[32,18,1]{2,1,0:T(8,128)}, u32[]{:S(2)}, u32[]{:S(2)}) collective-permute-start(f32[32,18,1]{2,1,0:T(8,128)} %get-tuple-element.354), channel_id=1, source_target_pairs={{0,1},{2,3},{4,5},{6,7},{8,9},{10,11},{12,13},{14,15},{16,17},{18,... | collective-permute-start | bytes 6920 | tf_op jit(solution)/shard_map/ppermute | solution.py:24
  648.9 6.3 collective-permute-start.16
  650.2 19.8 %copy-start.32 = (f32[65]{0:T(128)S(1)}, f32[65]{0:T(128)}, u32[]{:S(2)}) copy-start(f32[65]{0:T(128)} %copy-done.31) | copy-start | bytes 784
  650.2 5.0 collective-permute-start.17
  655.4 20.9 %copy-start.34 = (f32[9]{0:T(128)S(1)}, f32[9]{0:T(128)}, u32[]{:S(2)}) copy-start(f32[9]{0:T(128)} %or_select_fusion) | copy-start | bytes 112
  655.4 12.8 %collective-permute-start.18 = (f32[32,18,1]{2,1,0:T(8,128)S(1)}, f32[32,18,1]{2,1,0:T(8,128)S(1)}, u32[]{:S(2)}, u32[]{:S(2)}) collective-permute-start(f32[32,18,1]{2,1,0:T(8,128)S(1)} %get-tuple-element.349), channel_id=1, source_target_pairs={{1,0},{3,2},{5,4},{7,6},{9,8},{11,10},{13,12},{15,14},{17,16},{19,... | collective-permute-start | bytes 6920 | tf_op jit(solution)/shard_map/ppermute | solution.py:25
  656.7 13.2 %collective-permute-start.19 = (f32[32,18,1]{2,1,0:T(8,128)S(1)}, f32[32,18,1]{2,1,0:T(8,128)S(1)}, u32[]{:S(2)}, u32[]{:S(2)}) collective-permute-start(f32[32,18,1]{2,1,0:T(8,128)S(1)} %get-tuple-element.350), channel_id=1, source_target_pairs={{0,1},{2,3},{4,5},{6,7},{8,9},{10,11},{12,13},{14,15},{16,17},{18,... | collective-permute-start | bytes 6920 | tf_op jit(solution)/shard_map/ppermute | solution.py:24
  661.5 8.7 %collective-permute-start.20 = (f32[32,1,128]{2,1,0:T(1,128)S(1)}, f32[32,1,128]{2,1,0:T(1,128)S(1)}, u32[]{:S(2)}, u32[]{:S(2)}) collective-permute-start(f32[32,1,128]{2,1,0:T(1,128)S(1)} %get-tuple-element.370), channel_id=1, source_target_pairs={{2,0},{4,2},{6,4},{8,6},{10,8},{12,10},{14,12},{16,14},{18,16},{20... | collective-permute-start | bytes 49160 | tf_op jit(solution)/shard_map/ppermute | solution.py:25
  662.8 20.8 %copy-start.14 = (f32[32,16,128]{2,1,0:T(8,128)S(1)}, f32[32,16,128]{2,1,0:T(8,128)}, u32[]{:S(2)}) copy-start(f32[32,16,128]{2,1,0:T(8,128)} %get-tuple-element.346) | copy-start | bytes 786436
  662.8 20.8 %copy-start.15 = (f32[16,32,128]{2,0,1:T(8,128)S(1)}, f32[16,32,128]{2,0,1:T(8,128)}, u32[]{:S(2)}) copy-start(f32[16,32,128]{2,0,1:T(8,128)} %get-tuple-element.150) | copy-start | bytes 786436
  662.8 7.4 %collective-permute-start.21 = (f32[32,1,128]{2,1,0:T(1,128)S(1)}, f32[32,1,128]{2,1,0:T(1,128)S(1)}, u32[]{:S(2)}, u32[]{:S(2)}) collective-permute-start(f32[32,1,128]{2,1,0:T(1,128)S(1)} %get-tuple-element.369), channel_id=1, source_target_pairs={{0,2},{2,4},{4,6},{6,8},{8,10},{10,12},{12,14},{14,16},{16,18},{18... | collective-permute-start | bytes 49160 | tf_op jit(solution)/shard_map/ppermute | solution.py:24
  670.4 11.1 %collective-permute-start.22 = (f32[32,10,1]{2,1,0:T(8,128)S(1)}, f32[32,10,1]{2,1,0:T(8,128)S(1)}, u32[]{:S(2)}, u32[]{:S(2)}) collective-permute-start(f32[32,10,1]{2,1,0:T(8,128)S(1)} %get-tuple-element.357), channel_id=1, source_target_pairs={{1,0},{3,2},{5,4},{7,6},{9,8},{11,10},{13,12},{15,14},{17,16},{19,... | collective-permute-start | bytes 3848 | tf_op jit(solution)/shard_map/ppermute | solution.py:25
  671.7 11.0 %collective-permute-start.23 = (f32[32,10,1]{2,1,0:T(8,128)S(1)}, f32[32,10,1]{2,1,0:T(8,128)S(1)}, u32[]{:S(2)}, u32[]{:S(2)}) collective-permute-start(f32[32,10,1]{2,1,0:T(8,128)S(1)} %get-tuple-element.358), channel_id=1, source_target_pairs={{0,1},{2,3},{4,5},{6,7},{8,9},{10,11},{12,13},{14,15},{16,17},{18,... | collective-permute-start | bytes 3848 | tf_op jit(solution)/shard_map/ppermute | solution.py:24
  686.2 24.0 %copy-start.18 = (f32[32,8,129]{2,1,0:T(8,128)S(1)}, f32[32,8,129]{2,1,0:T(8,128)}, u32[]{:S(2)}) copy-start(f32[32,8,129]{2,1,0:T(8,128)} %fusion.55) | copy-start | bytes 396292
  686.2 24.0 %copy-start.21 = (f32[32,8,128]{2,1,0:T(8,128)S(1)}, f32[32,8,128]{2,1,0:T(8,128)}, u32[]{:S(2)}) copy-start(f32[32,8,128]{2,1,0:T(8,128)} %param.24) | copy-start | bytes 393220
  686.8 23.4 %copy-start.19 = (f32[32,9,128]{2,1,0:T(8,128)S(1)}, f32[32,9,128]{2,1,0:T(8,128)}, u32[]{:S(2)}) copy-start(f32[32,9,128]{2,1,0:T(8,128)} %fusion.67) | copy-start | bytes 442372
  686.8 23.4 %copy-start.23 = (f32[32,8,128]{2,1,0:T(8,128)S(1)}, f32[32,8,128]{2,1,0:T(8,128)}, u32[]{:S(2)}) copy-start(f32[32,8,128]{2,1,0:T(8,128)} %param.27) | copy-start | bytes 393220
  686.8 23.4 %copy-start.24 = (f32[32,8,128]{2,1,0:T(8,128)S(1)}, f32[32,8,128]{2,1,0:T(8,128)}, u32[]{:S(2)}) copy-start(f32[32,8,128]{2,1,0:T(8,128)} %get-tuple-element.342) | copy-start | bytes 393220
  (62 other events, 178.3 us)
Sparse Core Ops, SparseCore 0:
  10.7 44.2 all-gather.2
  279.6 60.5 reduce-scatter.8
  343.0 10.6 reduce-scatter.12
  356.3 41.0 all-gather.4
  631.9 9.8 reduce-scatter.14
  648.2 61.8 reduce-scatter.10
where the time goes:
time: 727 us; the launch traced here: 719 us
  matrix products  299 us (41%)
  local copies, waits for them, and re-layouts  123 us (17%)
  waiting for transfers between devices  118 us (16%)
  starting transfers between devices  66.4 us (9%)
  other arithmetic  65.1 us (9%)
  blocking collectives  30.7 us (4%)
  between operations  14.9 us (2%)
    dot_general x32, matrix products, one_row(): jnp.einsum('ch,hzy->czy', w_hidden, back_hidden, preferred_element_type=j...  190 us
    reduce_scatter x2, waiting for transfers between devices, per_device(): lax.psum_scatter(term_yz, 'gx', scatter_dimension=1, tiled=True)  61 us
    dot_general x32, matrix products, one_row(): jnp.einsum('ch,czy->hzy', w_hidden, features, preferred_element_type=jnp....  58.7 us
    ppermute x12, starting transfers between devices, padded_2(): before = lax.ppermute(last, axis, up)  50.4 us
    dot_general x32, matrix products, one_row(): jnp.einsum('h,hzy->zy', w_output, hidden, preferred_element_type=jnp.floa...  49.7 us
    dynamic_update_slice x64, local copies, waits for them, and re-layouts, data_grads(): lax.scan(one_row, start, (target, jnp.moveaxis(plane_xy, 1, 0), jnp.movea...  48.3 us
    sub x32, other arithmetic, one_row(): residual = output - target_row  48 us
    all_gather x2, blocking collectives, per_device(): whole_xz = lax.all_gather(plane_xz, 'gy', axis=2, tiled=True)  30.7 us
  transfers between devices with their start and end apart: 30, of which 16 were waited for; matrix products, arithmetic and copies ran while one was open for 4% of the time, Pallas kernels for 0%

commit v1 on v0

v1 whole, which is shorter than its diff:
```python
import functools
import jax
import jax.numpy as jnp
from jax import lax
from jax.experimental import pallas as pl
from jax.experimental.pallas import tpu as pltpu
from jax.sharding import PartitionSpec as P

STEPS = 2
START = 20


SMOOTHING = 0.5
BETA_ONE = 0.9
BETA_TWO = 0.99
LEARN_RATE = 0.01
EPSILON = 1e-08

LANES = 128
BLOCK = 256
ROWS = 16
BOTH = ("gx", "gy")
f32 = jnp.float32
bf16 = jnp.bfloat16


def ring_order(chips):
    return list(range(0, chips, 2)) + list(range(chips - 1, 0, -2))


def send(x, move):
    n, peers = lax.axis_size("gx"), lax.axis_size("gy")
    pairs = []
    for g in range(n):
        for y in range(peers):
            to = move(g // 2, g % 2, y)
            if to is not None:
                pairs.append((g * peers + y, (to[0] * 2 + to[1]) * peers + to[2]))
    return lax.ppermute(x, BOTH, pairs)


def to_core(x):
    return send(x, lambda k, c, y: (k, 1 - c, y))


def to_ring(x, step):
    chips = lax.axis_size("gx") // 2
    order = ring_order(chips)
    at = {k: i for i, k in enumerate(order)}
    return send(x, lambda k, c, y: (order[(at[k] + step) % chips], c, y))


def to_gy(x, step):
    peers = lax.axis_size("gy")
    return send(x, lambda k, c, y: (k, c, (y + step) % peers))


def grads_kernel(
    slot_yz, slot_xz, w_in, w_out, w_back, bias, scale, target, xy, xza, xzb, yza, yzb, gxy, gxz, gyz
):
    p = pl.program_id(0)
    x_count, y_count, _ = xy.shape
    z_count = target.shape[2] // 2
    block_yz = jnp.concatenate([yza[0], yzb[0]], axis=1)

    @pl.when(p == 0)
    def _():
        gxy[...] = jnp.zeros_like(gxy)

    gyz[...] = jnp.zeros_like(gyz)
    row = lax.broadcasted_iota(jnp.int32, (2 * z_count, BLOCK), 0) % z_count
    col = lax.broadcasted_iota(jnp.int32, (2 * z_count, BLOCK), 1) // 32
    pick = jnp.where(row == p * 8 + col, -1.0, 0.0).astype(bf16)
    w_res = jnp.concatenate([w_out[...], pick], axis=0)

    def some_rows(i, carry):
        xs = [i * ROWS + j for j in range(ROWS)]
        xzs = [
            jnp.concatenate([xza[0, pl.ds(x, 1), :], xzb[0, pl.ds(x, 1), :]], axis=1) for x in xs
        ]
        xys = [jnp.concatenate([xy[x], xy[x]], axis=1) for x in xs]
        features = jnp.concatenate(
            [(a * block_yz * r).astype(bf16) for a, r in zip(xys, xzs)], axis=0
        )
        half = jnp.dot(features, w_in[...], preferred_element_type=f32) + bias[...]
        t = jnp.tanh(half)
        up = 1.0 + t
        hidden = half * up
        slope = (up + hidden * (1.0 - t)) * scale[...]
        wanted = jnp.concatenate([target[x] for x in xs], axis=0)
        residual = jnp.dot(
            jnp.concatenate([hidden.astype(bf16), wanted], axis=1),
            w_res,
            preferred_element_type=f32,
        )
        back_hidden = (residual * slope).astype(bf16)
        back = jnp.dot(back_hidden, w_back[...], preferred_element_type=f32)
        total = None
        for j, x in enumerate(xs):
            b = back[j * y_count : (j + 1) * y_count]
            e = b * xzs[j]
            k = e * block_yz
            gxy[x] += k[:, :LANES] + k[:, LANES:]
            part = e * xys[j]
            total = part if total is None else total + part
            line = jnp.sum(b * (xys[j] * block_yz), axis=0, keepdims=True)
            gxz[0, pl.ds(x, 1), :] = line[:, :LANES]
            gxz[1, pl.ds(x, 1), :] = line[:, LANES:]
        gyz[0] += total[:, :LANES]
        gyz[1] += total[:, LANES:]
        return carry

    lax.fori_loop(0, x_count // ROWS, some_rows, 0)


def block_grads(slot_yz, slot_xz, weights, target, xy, xz, yz):
    tiles = yz.shape[0]
    x_count, y_count, _ = xy.shape

    def whole(a):
        return pl.BlockSpec(a.shape, lambda p, *_: (0,) * a.ndim)

    def tile_of(which, half, rows):
        return pl.BlockSpec(
            (1, rows, LANES), lambda p, sy, sx: ((sy, sx)[which][2 * p + half], 0, 0)
        )

    flops = 3 * 2 * x_count * y_count * tiles * LANES * BLOCK
    return pl.pallas_call(
        grads_kernel,
        grid_spec=pltpu.PrefetchScalarGridSpec(
            num_scalar_prefetch=2,
            grid=(tiles // 2,),
            in_specs=[whole(w) for w in weights]
            + [
                whole(target),
                whole(xy),
                tile_of(1, 0, x_count),
                tile_of(1, 1, x_count),
                tile_of(0, 0, y_count),
                tile_of(0, 1, y_count),
            ],
            out_specs=[
                whole(xy),
                pl.BlockSpec((2, x_count, LANES), lambda p, *_: (p, 0, 0)),
                pl.BlockSpec((2, y_count, LANES), lambda p, *_: (p, 0, 0)),
            ],
        ),
        out_shape=[
            jax.ShapeDtypeStruct(xy.shape, f32),
            jax.ShapeDtypeStruct((tiles, x_count, LANES), f32),
            jax.ShapeDtypeStruct((tiles, y_count, LANES), f32),
        ],
        compiler_params=pltpu.CompilerParams(vmem_limit_bytes=58 * 2**20),
        cost_estimate=pl.CostEstimate(flops=flops, bytes_accessed=16 * 2**20, transcendentals=0),
    )(slot_yz, slot_xz, *weights, target, xy, xz, xz, yz, yz)


def lanes_xy(plane):
    return jnp.tile(plane.transpose(1, 2, 0), (1, 1, LANES // plane.shape[0]))


def lanes_xz(plane):
    c, x, z = plane.shape
    per = LANES // c
    return plane.reshape(c, x, z // per, per).transpose(2, 1, 3, 0).reshape(z // per, x, LANES)


def plane_xz_of(tiles, c):
    z, x, _ = tiles.shape
    per = LANES // c
    return tiles.reshape(z, x, per, c).transpose(3, 1, 0, 2).reshape(c, x, z * per)


def lanes_yz(plane):
    c, z, y = plane.shape
    per = LANES // c
    return plane.reshape(c, z // per, per, y).transpose(1, 3, 2, 0).reshape(z // per, y, LANES)


def plane_yz_of(tiles, c):
    z, y, _ = tiles.shape
    per = LANES // c
    return tiles.reshape(z, y, per, c).transpose(3, 0, 2, 1).reshape(c, z * per, y)


def gather_ring(own):
    steps = lax.axis_size("gx") // 4
    middle = own.shape[1] // 2
    slots = [own]
    left, right = own, own
    for d in range(1, steps):
        left, right = to_ring(left, 1), to_ring(right, -1)
        slots += [left, right]
    first, second = to_ring(left[:, :middle], 1), to_ring(right[:, middle:], -1)
    slots.append(jnp.concatenate([first, second], axis=1))
    return jnp.concatenate(slots, axis=0)


def ring_tables(chips):
    order = ring_order(chips)
    at = {k: i for i, k in enumerate(order)}
    slots, owners = [], []
    for k in range(chips):
        row = []
        for other in range(chips):
            o = (at[other] - at[k]) % chips
            row.append(2 * o if o < chips // 2 else 2 * (chips - o) - 1)
        slots.append(row)
        owners.append([order[(at[k] + o) % chips] for o in range(chips)])
    return jnp.array(slots, jnp.int32), jnp.array(owners, jnp.int32)


def scatter_ring(tiles, owners, per):
    chips = lax.axis_size("gx") // 2
    middle = tiles.shape[1] // 2

    def chunk(o):
        return lax.dynamic_slice_in_dim(tiles, owners[o % chips] * per, per, axis=0)

    far = chunk(chips // 2)
    ahead, behind = to_ring(far[:, :middle], 1), to_ring(far[:, middle:], -1)
    for d in range(chips // 2 - 1, 0, -1):
        a, b = chunk(d), chunk(-d)
        if d == chips // 2 - 1:
            a = jnp.concatenate([a[:, :middle] + ahead, a[:, middle:]], axis=1)
            b = jnp.concatenate([b[:, :middle], b[:, middle:] + behind], axis=1)
        else:
            a, b = a + ahead, b + behind
        ahead, behind = to_ring(a, 1), to_ring(b, -1)
    return chunk(0) + ahead + behind


def borders(planes):
    n, peers = lax.axis_size("gx"), lax.axis_size("gy")
    up = [(i, i + 1) for i in range(n - 1)]
    last = jnp.concatenate([p[:, -1, :] for p in planes], axis=1)
    first = jnp.concatenate([p[:, 0, :] for p in planes], axis=1)
    above = lax.ppermute(last, "gx", up)
    below = lax.ppermute(first, "gx", [(j, i) for i, j in up])
    last = jnp.concatenate([p[:, :, -1] for p in planes], axis=1)
    first = jnp.concatenate([p[:, :, 0] for p in planes], axis=1)
    if peers == 2:
        left = right = lax.ppermute(
            jnp.where(lax.axis_index("gy") == 0, last, first), "gy", [(0, 1), (1, 0)]
        )
    else:
        up = [(i, i + 1) for i in range(peers - 1)]
        left = lax.ppermute(last, "gy", up)
        right = lax.ppermute(first, "gy", [(j, i) for i, j in up])
    out = []
    row, col = 0, 0
    for p in planes:
        a, b = p.shape[1:]
        out.append(
            (
                above[:, None, col : col + b],
                below[:, None, col : col + b],
                left[:, row : row + a, None],
                right[:, row : row + a, None],
            )
        )
        row, col = row + a, col + b
    return out


def smooth(plane, around):
    above, below, left, right = around
    rows = jnp.concatenate([above, plane, below], axis=1)
    cols = jnp.concatenate([left, plane, right], axis=2)
    down = rows[:, 1:, :] - rows[:, :-1, :]
    across = cols[:, :, 1:] - cols[:, :, :-1]
    row_count = down.shape[1]
    col_count = across.shape[2]
    row_places = jnp.arange(row_count)
    col_places = jnp.arange(col_count)
    lowest_x = lax.axis_index("gx") == 0
    highest_x = lax.axis_index("gx") == lax.axis_size("gx") - 1
    lowest_y = lax.axis_index("gy") == 0
    highest_y = lax.axis_index("gy") == lax.axis_size("gy") - 1
    row_keeps = jnp.where(
        (row_places == 0) & lowest_x | (row_places == row_count - 1) & highest_x, 0.0, 1.0
    )
    col_keeps = jnp.where(
        (col_places == 0) & lowest_y | (col_places == col_count - 1) & highest_y, 0.0, 1.0
    )
    down = down * row_keeps[None, :, None]
    across = across * col_keeps[None, None, :]
    return (
        2.0 * SMOOTHING * (down[:, :-1, :] - down[:, 1:, :] + across[:, :, :-1] - across[:, :, 1:])
    )


def adam(plane, first, second, grads, count):
    first = BETA_ONE * first + (1.0 - BETA_ONE) * grads
    second = BETA_TWO * second + (1.0 - BETA_TWO) * grads * grads
    corr_one = 1.0 - BETA_ONE**count
    corr_two = 1.0 - BETA_TWO**count
    plane = plane - LEARN_RATE * (first / corr_one) / (jnp.sqrt(second / corr_two) + EPSILON)
    return (plane, first, second)


def split_cores(x, axis, zl):
    c = lax.axis_index("gx") % 2
    shape = x.shape[:axis] + (x.shape[axis] // (2 * zl), 2, zl) + x.shape[axis + 1 :]
    half = x.shape[:axis] + (x.shape[axis] // 2,) + x.shape[axis + 1 :]
    x = x.reshape(shape)
    mine = lax.dynamic_index_in_dim(x, c, axis + 1, keepdims=False)
    other = lax.dynamic_index_in_dim(x, 1 - c, axis + 1, keepdims=False)
    return mine.reshape(half), other.reshape(half)


def make_weights(w_hidden, b_hidden, w_output):
    h = w_hidden.shape[1]
    times = BLOCK // h
    eye = jnp.eye(times, dtype=f32)
    wide = w_hidden.astype(f32)
    out = w_output.astype(f32)
    return (
        jnp.kron(eye, 0.5 * wide).astype(bf16),
        jnp.kron(eye, jnp.broadcast_to(out[:, None], (h, h))).astype(bf16),
        jnp.kron(eye, wide.T).astype(bf16),
        jnp.tile(0.5 * b_hidden, times)[None],
        jnp.tile(0.5 * out, times)[None],
    )


def per_device(
    target,
    plane_xy,
    plane_xz,
    plane_yz,
    first_xy,
    first_xz,
    first_yz,
    second_xy,
    second_xz,
    second_yz,
    w_hidden,
    b_hidden,
    w_output,
    b_output,
):
    n, peers = lax.axis_size("gx"), lax.axis_size("gy")
    chips = n // 2
    gx, gy = lax.axis_index("gx"), lax.axis_index("gy")
    channels, x_count, y_count = plane_xy.shape
    zl, zs = plane_yz.shape[1], plane_xz.shape[2]
    z_per = LANES // channels
    per = zl // z_per
    tiles = chips * per
    tiles_gy = tiles // peers

    slot_table, owner_table = ring_tables(chips)
    slots = lax.dynamic_index_in_dim(slot_table, gx // 2, 0, keepdims=False)
    owners = lax.dynamic_index_in_dim(owner_table, gx // 2, 0, keepdims=False)
    tile = jnp.arange(tiles, dtype=jnp.int32)
    slot_yz = jnp.repeat(slots, per) * per + tile % per
    slot_xz = (gy - tile // tiles_gy) % peers * tiles_gy + tile % tiles_gy

    weights = make_weights(w_hidden, b_hidden, w_output)
    mine, other = split_cores(target - b_output[0], 1, zl)
    wanted = jnp.concatenate([mine, to_core(other)], axis=0).transpose(0, 2, 1)
    high = lax.reduce_precision(wanted, 8, 7)
    wanted = jnp.concatenate([high.astype(bf16), (wanted - high).astype(bf16)], axis=2)

    for iteration in range(STEPS):
        yz = gather_ring(lanes_yz(plane_yz))
        xy = jnp.concatenate([lanes_xy(plane_xy), lanes_xy(to_core(plane_xy))], axis=0)
        mine, other = split_cores(plane_xz, 2, zl)
        own = lanes_xz(jnp.concatenate([mine, to_core(other)], axis=1))
        xz = jnp.concatenate([own] + [to_gy(own, s) for s in range(1, peers)], axis=0)
        around = borders((plane_xy, plane_xz, plane_yz))

        part_xy, part_xz, part_yz = block_grads(slot_yz, slot_xz, weights, wanted, xy, xz, yz)

        part_xy = part_xy.reshape(2 * x_count, y_count, z_per, channels).sum(2).transpose(2, 0, 1)
        grad_xy = part_xy[:, :x_count] + to_core(part_xy[:, x_count:])

        def piece(s):
            return lax.dynamic_slice_in_dim(part_xz, (gy + s) % peers * tiles_gy, tiles_gy, axis=0)

        total = piece(0)
        for s in range(1, peers):
            total = total + to_gy(piece(s), s)
        total = plane_xz_of(total, channels)
        mine, other = total[:, :x_count], to_core(total[:, x_count:])
        even = jnp.where(gx % 2 == 0, mine, other)
        odd = jnp.where(gx % 2 == 0, other, mine)
        shape = (channels, x_count, zs // (2 * zl), zl)
        grad_xz = jnp.stack([even.reshape(shape), odd.reshape(shape)], axis=3).reshape(plane_xz.shape)

        grad_yz = plane_yz_of(scatter_ring(part_yz, owners, per), channels)

        grad_xy = grad_xy + smooth(plane_xy, around[0])
        grad_xz = grad_xz + smooth(plane_xz, around[1])
        grad_yz = grad_yz + smooth(plane_yz, around[2])
        count = START + iteration + 1
        plane_xy, first_xy, second_xy = adam(plane_xy, first_xy, second_xy, grad_xy, count)
        plane_xz, first_xz, second_xz = adam(plane_xz, first_xz, second_xz, grad_xz, count)
        plane_yz, first_yz, second_yz = adam(plane_yz, first_yz, second_yz, grad_yz, count)
    return (
        plane_xy,
        plane_xz,
        plane_yz,
        first_xy,
        first_xz,
        first_yz,
        second_xy,
        second_xz,
        second_yz,
    )


def solution(mesh):
    return jax.shard_map(
        per_device,
        mesh=mesh,
        in_specs=(
            P("gx", None, "gy"),
            P(None, "gx", "gy"),
            P(None, "gx", "gy"),
            P(None, "gx", "gy"),
            P(None, "gx", "gy"),
            P(None, "gx", "gy"),
            P(None, "gx", "gy"),
            P(None, "gx", "gy"),
            P(None, "gx", "gy"),
            P(None, "gx", "gy"),
            P(),
            P(),
            P(),
            P(),
        ),
        out_specs=(
            P(None, "gx", "gy"),
            P(None, "gx", "gy"),
            P(None, "gx", "gy"),
            P(None, "gx", "gy"),
            P(None, "gx", "gy"),
            P(None, "gx", "gy"),
            P(None, "gx", "gy"),
            P(None, "gx", "gy"),
            P(None, "gx", "gy"),
        ),
        check_vma=False,
    )
```

time: 727 us -> 274 us (0.38)
  matrix products: 299 us -> 0 us
  waiting for transfers between devices: 118 us -> 24.2 us
  Pallas kernels: 0 us -> 70.2 us
  local copies, waits for them, and re-layouts: 123 us -> 61.3 us
  blocking collectives: 30.7 us -> 0 us
  starting transfers between devices: 66.4 us -> 54.7 us
  other arithmetic: 65.1 us -> 54.3 us
  between operations: 14.9 us -> 7.51 us
    dot_general x96 -> x0, matrix products: 299 us -> none  [the longest x32 190 us: one_row(): jnp.einsum('ch,hzy->czy', w_hidden, back_hidden, preferred_element_type=j...]
    pallas_call x0 -> x2, Pallas kernels: none -> 70.2 us  [block_grads(): pl.pallas_call(grads_kernel, grid_spec=pltpu.PrefetchScalarGridSpec(num_s...]
    reduce_scatter x2 -> x0, waiting for transfers between devices: 61 us -> none  [per_device(): lax.psum_scatter(term_yz, 'gx', scatter_dimension=1, tiled=True)]
    dynamic_update_slice x64 -> x0, local copies, waits for them, and re-layouts: 48.3 us -> none  [data_grads(): lax.scan(one_row, start, (target, jnp.moveaxis(plane_xy, 1, 0), jnp.movea...]
    sub x32 -> x1, other arithmetic: 48 us -> 1.36 us  [per_device(): mine, other = split_cores(target - b_output[0], 1, zl)]
    all_gather x2 -> x0, blocking collectives: 30.7 us -> none  [per_device(): whole_xz = lax.all_gather(plane_xz, 'gy', axis=2, tiled=True)]
    all_gather x2 -> x0, waiting for transfers between devices: 26.4 us -> none  [per_device(): whole_yz = lax.all_gather(plane_yz, 'gx', axis=1, tiled=True)]
    mul x32 -> x9, local copies, waits for them, and re-layouts: 25.1 us -> 3.41 us  [the longest x4 2.21 us: make_weights(): jnp.kron(eye, 0.5 * wide).astype(bf16)]
  transfers between devices with their start and end apart: 30 -> 51, of which waited for: 16 -> 15; matrix products, arithmetic and copies ran while one was open for 4% -> 36% of each run, Pallas kernels for 0% -> 0%
where the time goes in v1:
time: 274 us; the launch traced here: 272 us
  Pallas kernels  70.2 us (26%)
  local copies, waits for them, and re-layouts  61.3 us (22%)
  starting transfers between devices  54.7 us (20%)
  other arithmetic  54.3 us (20%)
  waiting for transfers between devices  24.2 us (9%)
  between operations  7.51 us (3%)
    pallas_call x2, Pallas kernels, block_grads(): pl.pallas_call(grads_kernel, grid_spec=pltpu.PrefetchScalarGridSpec(num_s...  70.2 us
    ppermute x45, starting transfers between devices, send(): return lax.ppermute(x, BOTH, pairs)  45.6 us
    ppermute x45, waiting for transfers between devices, send(): return lax.ppermute(x, BOTH, pairs)  20.1 us
    unnamed x141, local copies, waits for them, and re-layouts  19.9 us
    add x6, other arithmetic, scatter_ring(): a, b = (a + ahead, b + behind)  7.91 us
    sub x6, other arithmetic, adam(): plane - LEARN_RATE * (first / corr_one) / (jnp.sqrt(second / corr_two) +...  6.09 us
    concatenate x2, other arithmetic, per_device(): jnp.concatenate([lanes_xy(plane_xy), lanes_xy(to_core(plane_xy))], axis=0)  5.87 us
  transfers between devices with their start and end apart: 51, of which 15 were waited for; matrix products, arithmetic and copies ran while one was open for 36% of the time, Pallas kernels for 0%

profile of v1, /device:TPU:0, one launch (start us, length us, event | category | flops | bytes accessed | tf_op | source)
XLA Modules:
  0.0 272.2 jit_solution(7798650413255829817)
XLA Ops:
  2.3 3.1 %collective-permute-start.4 = (f32[2,128,128]{2,1,0:T(8,128)}, f32[2,128,128]{2,1,0:T(8,128)}, u32[]{:S(2)}, u32[]{:S(2)}) collective-permute-start(f32[2,128,128]{2,1,0:T(8,128)} %copy.1511), channel_id=1, source_target_pairs={{0,8},{1,9},{2,10},{3,11},{4,0},{5,1},{6,2},{7,3},{8,16},{9,17},{1... | collective-permute-start | bytes 393224 | tf_op jit(solution)/shard_map/ppermute | solution.py:39
  6.1 1.4 broadcast_subtract_fusion
  10.9 1.9 collective-permute-start.15
  13.0 1.6 constant_dynamic-update-slice_fusion.6
  26.5 1.4 pad_maximum_fusion.12
  28.6 1.8 multiply_convert_fusion
  39.2 1.8 collective-permute-start.14
  46.3 3.2 %collective-permute-done.13 = f32[32,320]{1,0:T(8,128)S(1)} collective-permute-done((f32[32,320]{1,0:T(8,128)S(1)}, f32[32,320]{1,0:T(8,128)S(1)}, u32[]{:S(2)}, u32[]{:S(2)}) %collective-permute-start.13) | collective-permute-done | bytes 40992 | tf_op jit(solution)/shard_map/ppermute | solution.py:240
  49.5 2.8 %collective-permute-start.2 = (f32[32,16,32]{0,2,1:T(8,128)S(1)}, f32[32,16,32]{0,2,1:T(8,128)S(1)}, u32[]{:S(2)}, u32[]{:S(2)}) collective-permute-start(f32[32,16,32]{0,2,1:T(8,128)S(1)} %copy-done.31), channel_id=1, source_target_pairs={{0,2},{1,3},{2,0},{3,1},{4,6},{5,7},{6,4},{7,5},{8,10},{9,11},{10,... | collective-permute-start | bytes 196616 | tf_op jit(solution)/shard_map/ppermute | solution.py:39
  56.3 1.6 collective-permute-start.6
  57.8 1.6 constant_dynamic-update-slice_fusion.5
  60.3 1.6 constant_dynamic-update-slice_fusion.4
  63.8 1.3 copy.1503
  66.3 3.1 %pad_maximum_fusion.xy = f32[32,128,128]{2,1,0:T(8,128)} fusion(f32[16,128,128]{2,1,0:T(8,128)} %copy.1503, f32[16,128,128]{2,1,0:T(8,128)} %copy.1502), kind=kLoop, calls=%fused_computation.4 | loop fusion | flops 524288 | bytes 4194304 | tf_op jit(solution)/shard_map/concatenate | solution.py:369
  72.8 1.6 collective-permute-done.9
  76.5 2.1 collective-permute-done.11
  79.3 1.4 copy.1499
  81.2 1.6 pad_maximum_fusion.2.target
  82.8 35.1 %shard_map.223 = (f32[32,128,128]{2,1,0:T(8,128)}, f32[16,32,128]{2,1,0:T(8,128)}, f32[16,128,128]{2,1,0:T(8,128)}) custom-call(s32[16]{0:T(128)} %fusion.30.slot_yz, s32[16]{0:T(128)} %fusion.29.slot_xz, bf16[256,256]{1,0:T(8,128)(2,1)} %get-tuple-element.211.w_in, bf16[256,256]{1,0:T(8,128)(2,1)} %get-tuple-element.210.w_out, ...), custom_call_target="tpu_custom_call" | custom-call | flops 12884901888 | bytes 16777216 | tf_op jit(solution)/shard_map/pallas_call | solution.py:129
  117.9 1.5 constant_dynamic-slice_fusion.3
  119.4 1.6 collective-permute-start.21
  121.5 1.6 constant_dynamic-slice_fusion.11
  123.0 1.5 collective-permute-start.17
  124.5 1.9 copy.1512
  137.9 1.6 dynamic-slice_add_fusion.7
  143.5 2.1 divide_subtract_fusion.3
  146.2 1.8 dynamic-slice_add_fusion.8
  151.7 1.6 pad_maximum_fusion.6.xza.xzb
  153.5 1.6 dynamic-slice_add_fusion.6
  156.4 1.3 copy.1538
  157.8 2.8 %pad_maximum_fusion.1.xy = f32[32,128,128]{2,1,0:T(8,128)} fusion(f32[16,128,128]{2,1,0:T(8,128)} %copy.1538, f32[16,128,128]{2,1,0:T(8,128)S(1)} %copy.1537), kind=kLoop, calls=%fused_computation.5 | loop fusion | flops 524288 | bytes 4194304 | tf_op jit(solution)/shard_map/concatenate | solution.py:369
  163.0 1.6 collective-permute-start.29
  166.5 1.6 collective-permute-start.40
  174.7 4.3 %collective-permute-start.31 = (f32[2,128,128]{2,1,0:T(8,128)S(1)}, f32[2,128,128]{2,1,0:T(8,128)S(1)}, u32[]{:S(2)}, u32[]{:S(2)}) collective-permute-start(f32[2,128,128]{2,1,0:T(8,128)S(1)} %collective-permute-done.29), channel_id=1, source_target_pairs={{0,8},{1,9},{2,10},{3,11},{4,0},{5,1},{6,2},{7,3},{8,16},{9,17},{1... | collective-permute-start | bytes 393224 | tf_op jit(solution)/shard_map/ppermute | solution.py:39
  179.1 2.9 %collective-permute-done.31 = f32[2,128,128]{2,1,0:T(8,128)S(1)} collective-permute-done((f32[2,128,128]{2,1,0:T(8,128)S(1)}, f32[2,128,128]{2,1,0:T(8,128)S(1)}, u32[]{:S(2)}, u32[]{:S(2)}) %collective-permute-start.31) | collective-permute-done | bytes 131104 | tf_op jit(solution)/shard_map/ppermute | solution.py:39
  182.0 2.5 collective-permute-start.33
  185.2 3.2 %collective-permute-done.33 = f32[2,128,128]{2,1,0:T(8,128)S(1)} collective-permute-done((f32[2,128,128]{2,1,0:T(8,128)S(1)}, f32[2,128,128]{2,1,0:T(8,128)S(1)}, u32[]{:S(2)}, u32[]{:S(2)}) %collective-permute-start.33) | collective-permute-done | bytes 131104 | tf_op jit(solution)/shard_map/ppermute | solution.py:39
  190.5 2.1 collective-permute-done.35
  194.8 35.1 %shard_map.224 = (f32[32,128,128]{2,1,0:T(8,128)}, f32[16,32,128]{2,1,0:T(8,128)}, f32[16,128,128]{2,1,0:T(8,128)}) custom-call(s32[16]{0:T(128)} %fusion.30.slot_yz, s32[16]{0:T(128)} %fusion.29.slot_xz, bf16[256,256]{1,0:T(8,128)(2,1)} %get-tuple-element.211.w_in, bf16[256,256]{1,0:T(8,128)(2,1)} %get-tuple-element.210.w_out, ...), custom_call_target="tpu_custom_call" | custom-call | flops 12884901888 | bytes 16777216 | tf_op jit(solution)/shard_map/pallas_call | solution.py:129
  229.9 1.5 constant_dynamic-slice_fusion.1
  231.4 1.6 collective-permute-start.43
  233.5 1.6 constant_dynamic-slice_fusion.6
  235.6 1.9 copy.1570
  246.3 3.2 %collective-permute-done.44 = f32[2,128,128]{2,1,0:T(8,128)S(1)} collective-permute-done((f32[2,128,128]{2,1,0:T(8,128)S(1)}, f32[2,128,128]{2,1,0:T(8,128)S(1)}, u32[]{:S(2)}, u32[]{:S(2)}) %collective-permute-start.44) | collective-permute-done | bytes 131104 | tf_op jit(solution)/shard_map/ppermute | solution.py:39
  254.1 1.4 collective-permute-done.45
  256.7 1.8 collective-permute-start.49
  262.7 1.8 collective-permute-start.50
  264.6 1.5 divide_subtract_fusion.1
  (370 shorter events, 104.5 us)
Async XLA Ops:
  2.3 53.9 %collective-permute-start.4 = (f32[2,128,128]{2,1,0:T(8,128)}, f32[2,128,128]{2,1,0:T(8,128)}, u32[]{:S(2)}, u32[]{:S(2)}) collective-permute-start(f32[2,128,128]{2,1,0:T(8,128)} %copy.1511), channel_id=1, source_target_pairs={{0,8},{1,9},{2,10},{3,11},{4,0},{5,1},{6,2},{7,3},{8,16},{9,17},{1... | collective-permute-start | bytes 393224 | tf_op jit(solution)/shard_map/ppermute | solution.py:39
  5.4 54.1 %collective-permute-start.5 = (f32[2,128,128]{2,1,0:T(8,128)}, f32[2,128,128]{2,1,0:T(8,128)}, u32[]{:S(2)}, u32[]{:S(2)}) collective-permute-start(f32[2,128,128]{2,1,0:T(8,128)} %copy.1511), channel_id=1, source_target_pairs={{0,4},{1,5},{2,6},{3,7},{4,12},{5,13},{6,14},{7,15},{8,0},{9,1},{1... | collective-permute-start | bytes 393224 | tf_op jit(solution)/shard_map/ppermute | solution.py:39
  8.3 70.9 %collective-permute-start = (f32[16,64,128]{2,1,0:T(8,128)}, f32[16,64,128]{2,1,0:T(8,128)}, u32[]{:S(2)}, u32[]{:S(2)}) collective-permute-start(f32[16,64,128]{2,1,0:T(8,128)} %get-tuple-element.200), channel_id=1, source_target_pairs={{0,2},{1,3},{2,0},{3,1},{4,6},{5,7},{6,4},{7,5},{8,10},{9,11},{10,... | collective-permute-start | bytes 1572872 | tf_op jit(solution)/shard_map/ppermute | solution.py:39
  8.3 54.3 %collective-permute-start.1 = (f32[32,16,128]{2,1,0:T(8,128)S(1)}, f32[32,16,128]{2,1,0:T(8,128)}, u32[]{:S(2)}, u32[]{:S(2)}) collective-permute-start(f32[32,16,128]{2,1,0:T(8,128)S(1)} %copy-done.1), channel_id=1, source_target_pairs={{0,2},{1,3},{2,0},{3,1},{4,6},{5,7},{6,4},{7,5},{8,10},{9,11},{10,... | collective-permute-start | bytes 786440 | tf_op jit(solution)/shard_map/ppermute | solution.py:39
  10.9 28.4 %collective-permute-start.15 = (f32[32,40]{0,1:T(8,128)}, f32[32,40]{0,1:T(8,128)}, u32[]{:S(2)}, u32[]{:S(2)}) collective-permute-start(f32[32,40]{0,1:T(8,128)} %maximum_select_fusion), channel_id=1, source_target_pairs={{0,1},{1,0},{2,3},{3,2},{4,5},{5,4},{6,7},{7,6},{8,9},{9,8},{10,11... | collective-permute-start | bytes 15368 | tf_op jit(solution)/shard_map/ppermute | solution.py:244
  39.2 5.7 %collective-permute-start.14 = (f32[32,320]{1,0:T(8,128)}, f32[32,320]{1,0:T(8,128)S(1)}, u32[]{:S(2)}, u32[]{:S(2)}) collective-permute-start(f32[32,320]{1,0:T(8,128)} %pad_maximum_fusion.12), channel_id=1, source_target_pairs={{0,2},{2,4},{4,6},{6,8},{8,10},{10,12},{12,14},{14,16},{16,18},{18... | collective-permute-start | bytes 122888 | tf_op jit(solution)/shard_map/ppermute | solution.py:239
  45.0 4.5 %collective-permute-start.13 = (f32[32,320]{1,0:T(8,128)S(1)}, f32[32,320]{1,0:T(8,128)S(1)}, u32[]{:S(2)}, u32[]{:S(2)}) collective-permute-start(f32[32,320]{1,0:T(8,128)S(1)} %copy-done.39), channel_id=1, source_target_pairs={{2,0},{4,2},{6,4},{8,6},{10,8},{12,10},{14,12},{16,14},{18,16},{20... | collective-permute-start | bytes 122888 | tf_op jit(solution)/shard_map/ppermute | solution.py:240
  49.5 5.3 %collective-permute-start.2 = (f32[32,16,32]{0,2,1:T(8,128)S(1)}, f32[32,16,32]{0,2,1:T(8,128)S(1)}, u32[]{:S(2)}, u32[]{:S(2)}) collective-permute-start(f32[32,16,32]{0,2,1:T(8,128)S(1)} %copy-done.31), channel_id=1, source_target_pairs={{0,2},{1,3},{2,0},{3,1},{4,6},{5,7},{6,4},{7,5},{8,10},{9,11},{10,... | collective-permute-start | bytes 196616 | tf_op jit(solution)/shard_map/ppermute | solution.py:39
  55.7 6.2 %collective-permute-start.3 = (f32[8,32,128]{2,1,0:T(8,128)S(1)}, f32[8,32,128]{2,1,0:T(8,128)S(1)}, u32[]{:S(2)}, u32[]{:S(2)}) collective-permute-start(f32[8,32,128]{2,1,0:T(8,128)S(1)} %reshape.231), channel_id=1, source_target_pairs={{0,1},{1,0},{2,3},{3,2},{4,5},{5,4},{6,7},{7,6},{8,9},{9,8},{10,11... | collective-permute-start | bytes 393224 | tf_op jit(solution)/shard_map/ppermute | solution.py:39
  56.3 8.8 %collective-permute-start.6 = (f32[2,128,128]{2,1,0:T(8,128)}, f32[2,128,128]{2,1,0:T(8,128)S(1)}, u32[]{:S(2)}, u32[]{:S(2)}) collective-permute-start(f32[2,128,128]{2,1,0:T(8,128)} %collective-permute-done.4), channel_id=1, source_target_pairs={{0,8},{1,9},{2,10},{3,11},{4,0},{5,1},{6,2},{7,3},{8,16},{9,17},{1... | collective-permute-start | bytes 393224 | tf_op jit(solution)/shard_map/ppermute | solution.py:39
  59.4 9.9 %collective-permute-start.7 = (f32[2,128,128]{2,1,0:T(8,128)}, f32[2,128,128]{2,1,0:T(8,128)S(1)}, u32[]{:S(2)}, u32[]{:S(2)}) collective-permute-start(f32[2,128,128]{2,1,0:T(8,128)} %collective-permute-done.5), channel_id=1, source_target_pairs={{0,4},{1,5},{2,6},{3,7},{4,12},{5,13},{6,14},{7,15},{8,0},{9,1},{1... | collective-permute-start | bytes 393224 | tf_op jit(solution)/shard_map/ppermute | solution.py:39
  65.1 6.4 %collective-permute-start.8 = (f32[2,128,128]{2,1,0:T(8,128)S(1)}, f32[2,128,128]{2,1,0:T(8,128)S(1)}, u32[]{:S(2)}, u32[]{:S(2)}) collective-permute-start(f32[2,128,128]{2,1,0:T(8,128)S(1)} %collective-permute-done.6), channel_id=1, source_target_pairs={{0,8},{1,9},{2,10},{3,11},{4,0},{5,1},{6,2},{7,3},{8,16},{9,17},{1... | collective-permute-start | bytes 393224 | tf_op jit(solution)/shard_map/ppermute | solution.py:39
  69.4 5.0 %collective-permute-start.9 = (f32[2,128,128]{2,1,0:T(8,128)S(1)}, f32[2,128,128]{2,1,0:T(8,128)S(1)}, u32[]{:S(2)}, u32[]{:S(2)}) collective-permute-start(f32[2,128,128]{2,1,0:T(8,128)S(1)} %collective-permute-done.7), channel_id=1, source_target_pairs={{0,4},{1,5},{2,6},{3,7},{4,12},{5,13},{6,14},{7,15},{8,0},{9,1},{1... | collective-permute-start | bytes 393224 | tf_op jit(solution)/shard_map/ppermute | solution.py:39
  71.5 5.0 %collective-permute-start.10 = (f32[2,64,128]{2,1,0:T(8,128)S(1)}, f32[2,64,128]{2,1,0:T(8,128)S(1)}, u32[]{:S(2)}, u32[]{:S(2)}) collective-permute-start(f32[2,64,128]{2,1,0:T(8,128)S(1)} %slice.462), channel_id=1, source_target_pairs={{0,8},{1,9},{2,10},{3,11},{4,0},{5,1},{6,2},{7,3},{8,16},{9,17},{1... | collective-permute-start | bytes 196616 | tf_op jit(solution)/shard_map/ppermute | solution.py:39
  74.3 4.3 %collective-permute-start.11 = (f32[2,64,128]{2,1,0:T(8,128)S(1)}, f32[2,64,128]{2,1,0:T(8,128)S(1)}, u32[]{:S(2)}, u32[]{:S(2)}) collective-permute-start(f32[2,64,128]{2,1,0:T(8,128)S(1)} %slice.463), channel_id=1, source_target_pairs={{0,4},{1,5},{2,6},{3,7},{4,12},{5,13},{6,14},{7,15},{8,0},{9,1},{1... | collective-permute-start | bytes 196616 | tf_op jit(solution)/shard_map/ppermute | solution.py:39
  119.4 7.6 %collective-permute-start.21 = (f32[2,64,128]{2,1,0:T(8,128)}, f32[2,64,128]{2,1,0:T(8,128)S(1)}, u32[]{:S(2)}, u32[]{:S(2)}) collective-permute-start(f32[2,64,128]{2,1,0:T(8,128)} %get-tuple-element.197), channel_id=1, source_target_pairs={{0,8},{1,9},{2,10},{3,11},{4,0},{5,1},{6,2},{7,3},{8,16},{9,17},{1... | collective-permute-start | bytes 196616 | tf_op jit(solution)/shard_map/ppermute | solution.py:39
  121.0 6.6 %collective-permute-start.25 = (f32[2,64,128]{2,1,0:T(8,128)S(1)}, f32[2,64,128]{2,1,0:T(8,128)}, u32[]{:S(2)}, u32[]{:S(2)}) collective-permute-start(f32[2,64,128]{2,1,0:T(8,128)S(1)} %get-tuple-element.198), channel_id=1, source_target_pairs={{0,4},{1,5},{2,6},{3,7},{4,12},{5,13},{6,14},{7,15},{8,0},{9,1},{1... | collective-permute-start | bytes 196616 | tf_op jit(solution)/shard_map/ppermute | solution.py:39
  123.0 7.2 %collective-permute-start.17 = (f32[8,32,128]{2,1,0:T(8,128)}, f32[8,32,128]{2,1,0:T(8,128)}, u32[]{:S(2)}, u32[]{:S(2)}) collective-permute-start(f32[8,32,128]{2,1,0:T(8,128)} %constant_dynamic-slice_fusion.11), channel_id=1, source_target_pairs={{0,1},{1,0},{2,3},{3,2},{4,5},{5,4},{6,7},{7,6},{8,9},{9,8},{10,11... | collective-permute-start | bytes 393224 | tf_op jit(solution)/shard_map/ppermute | solution.py:39
  126.9 16.5 %collective-permute-start.12 = (f32[32,16,128]{2,1,0:T(8,128)S(1)}, f32[32,16,128]{2,1,0:T(8,128)}, u32[]{:S(2)}, u32[]{:S(2)}) collective-permute-start(f32[32,16,128]{2,1,0:T(8,128)S(1)} %copy.1513), channel_id=1, source_target_pairs={{0,2},{1,3},{2,0},{3,1},{4,6},{5,7},{6,4},{7,5},{8,10},{9,11},{10,... | collective-permute-start | bytes 786440 | tf_op jit(solution)/shard_map/ppermute | solution.py:39
  129.3 16.9 %collective-permute-start.26 = (f32[2,128,128]{2,1,0:T(8,128)}, f32[2,128,128]{2,1,0:T(8,128)}, u32[]{:S(2)}, u32[]{:S(2)}) collective-permute-start(f32[2,128,128]{2,1,0:T(8,128)} %pad_maximum_fusion.8), channel_id=1, source_target_pairs={{0,4},{1,5},{2,6},{3,7},{4,12},{5,13},{6,14},{7,15},{8,0},{9,1},{1... | collective-permute-start | bytes 393224 | tf_op jit(solution)/shard_map/ppermute | solution.py:39
  131.9 6.0 %collective-permute-start.22 = (f32[2,128,128]{2,1,0:T(8,128)S(1)}, f32[2,128,128]{2,1,0:T(8,128)S(1)}, u32[]{:S(2)}, u32[]{:S(2)}) collective-permute-start(f32[2,128,128]{2,1,0:T(8,128)S(1)} %pad_maximum_fusion.7), channel_id=1, source_target_pairs={{0,8},{1,9},{2,10},{3,11},{4,0},{5,1},{6,2},{7,3},{8,16},{9,17},{1... | collective-permute-start | bytes 393224 | tf_op jit(solution)/shard_map/ppermute | solution.py:39
  139.5 6.7 %collective-permute-start.23 = (f32[2,128,128]{2,1,0:T(8,128)}, f32[2,128,128]{2,1,0:T(8,128)}, u32[]{:S(2)}, u32[]{:S(2)}) collective-permute-start(f32[2,128,128]{2,1,0:T(8,128)} %dynamic-slice_add_fusion.7), channel_id=1, source_target_pairs={{0,8},{1,9},{2,10},{3,11},{4,0},{5,1},{6,2},{7,3},{8,16},{9,17},{1... | collective-permute-start | bytes 393224 | tf_op jit(solution)/shard_map/ppermute | solution.py:39
  142.9 8.9 %collective-permute-start.20 = (f32[8,32,128]{2,1,0:T(8,128)S(1)}, f32[8,32,128]{2,1,0:T(8,128)}, u32[]{:S(2)}, u32[]{:S(2)}) collective-permute-start(f32[8,32,128]{2,1,0:T(8,128)S(1)} %reshape.240), channel_id=1, source_target_pairs={{0,1},{1,0},{2,3},{3,2},{4,5},{5,4},{6,7},{7,6},{8,9},{9,8},{10,11... | collective-permute-start | bytes 393224 | tf_op jit(solution)/shard_map/ppermute | solution.py:39
  148.0 5.5 %collective-permute-start.27 = (f32[2,128,128]{2,1,0:T(8,128)}, f32[2,128,128]{2,1,0:T(8,128)S(1)}, u32[]{:S(2)}, u32[]{:S(2)}) collective-permute-start(f32[2,128,128]{2,1,0:T(8,128)} %get-tuple-element.192), channel_id=1, source_target_pairs={{0,4},{1,5},{2,6},{3,7},{4,12},{5,13},{6,14},{7,15},{8,0},{9,1},{1... | collective-permute-start | bytes 393224 | tf_op jit(solution)/shard_map/ppermute | solution.py:39
  150.2 6.0 %collective-permute-start.16 = (f32[32,16,128]{2,1,0:T(8,128)S(1)}, f32[32,16,128]{2,1,0:T(8,128)S(1)}, u32[]{:S(2)}, u32[]{:S(2)}) collective-permute-start(f32[32,16,128]{2,1,0:T(8,128)S(1)} %copy.1535), channel_id=1, source_target_pairs={{0,2},{1,3},{2,0},{3,1},{4,6},{5,7},{6,4},{7,5},{8,10},{9,11},{10,... | collective-permute-start | bytes 786440 | tf_op jit(solution)/shard_map/ppermute | solution.py:39
  150.8 9.9 %collective-permute-start.24 = (f32[2,128,128]{2,1,0:T(8,128)}, f32[2,128,128]{2,1,0:T(8,128)S(1)}, u32[]{:S(2)}, u32[]{:S(2)}) collective-permute-start(f32[2,128,128]{2,1,0:T(8,128)} %get-tuple-element.191), channel_id=1, source_target_pairs={{0,8},{1,9},{2,10},{3,11},{4,0},{5,1},{6,2},{7,3},{8,16},{9,17},{1... | collective-permute-start | bytes 393224 | tf_op jit(solution)/shard_map/ppermute | solution.py:39
  155.1 5.7 %collective-permute-start.28 = (f32[2,128,128]{2,1,0:T(8,128)}, f32[2,128,128]{2,1,0:T(8,128)S(1)}, u32[]{:S(2)}, u32[]{:S(2)}) collective-permute-start(f32[2,128,128]{2,1,0:T(8,128)} %dynamic-slice_add_fusion.6), channel_id=1, source_target_pairs={{0,4},{1,5},{2,6},{3,7},{4,12},{5,13},{6,14},{7,15},{8,0},{9,1},{1... | collective-permute-start | bytes 393224 | tf_op jit(solution)/shard_map/ppermute | solution.py:39
  163.0 11.8 %collective-permute-start.29 = (f32[2,128,128]{2,1,0:T(8,128)S(1)}, f32[2,128,128]{2,1,0:T(8,128)S(1)}, u32[]{:S(2)}, u32[]{:S(2)}) collective-permute-start(f32[2,128,128]{2,1,0:T(8,128)S(1)} %copy.1569), channel_id=1, source_target_pairs={{0,8},{1,9},{2,10},{3,11},{4,0},{5,1},{6,2},{7,3},{8,16},{9,17},{1... | collective-permute-start | bytes 393224 | tf_op jit(solution)/shard_map/ppermute | solution.py:39
  164.6 14.4 %collective-permute-start.30 = (f32[2,128,128]{2,1,0:T(8,128)S(1)}, f32[2,128,128]{2,1,0:T(8,128)S(1)}, u32[]{:S(2)}, u32[]{:S(2)}) collective-permute-start(f32[2,128,128]{2,1,0:T(8,128)S(1)} %copy.1569), channel_id=1, source_target_pairs={{0,4},{1,5},{2,6},{3,7},{4,12},{5,13},{6,14},{7,15},{8,0},{9,1},{1... | collective-permute-start | bytes 393224 | tf_op jit(solution)/shard_map/ppermute | solution.py:39
  165.1 7.8 %collective-permute-start.39 = (f32[32,320]{1,0:T(8,128)S(1)}, f32[32,320]{1,0:T(8,128)S(1)}, u32[]{:S(2)}, u32[]{:S(2)}) collective-permute-start(f32[32,320]{1,0:T(8,128)S(1)} %pad_maximum_fusion.14), channel_id=1, source_target_pairs={{0,2},{2,4},{4,6},{6,8},{8,10},{10,12},{12,14},{14,16},{16,18},{18... | collective-permute-start | bytes 122888 | tf_op jit(solution)/shard_map/ppermute | solution.py:239
  168.1 4.8 %collective-permute-start.38 = (f32[32,320]{1,0:T(8,128)S(1)}, f32[32,320]{1,0:T(8,128)S(1)}, u32[]{:S(2)}, u32[]{:S(2)}) collective-permute-start(f32[32,320]{1,0:T(8,128)S(1)} %pad_maximum_fusion.13), channel_id=1, source_target_pairs={{2,0},{4,2},{6,4},{8,6},{10,8},{12,10},{14,12},{16,14},{18,16},{20... | collective-permute-start | bytes 122888 | tf_op jit(solution)/shard_map/ppermute | solution.py:240
  174.7 7.2 %collective-permute-start.31 = (f32[2,128,128]{2,1,0:T(8,128)S(1)}, f32[2,128,128]{2,1,0:T(8,128)S(1)}, u32[]{:S(2)}, u32[]{:S(2)}) collective-permute-start(f32[2,128,128]{2,1,0:T(8,128)S(1)} %collective-permute-done.29), channel_id=1, source_target_pairs={{0,8},{1,9},{2,10},{3,11},{4,0},{5,1},{6,2},{7,3},{8,16},{9,17},{1... | collective-permute-start | bytes 393224 | tf_op jit(solution)/shard_map/ppermute | solution.py:39
  179.0 5.4 %collective-permute-start.32 = (f32[2,128,128]{2,1,0:T(8,128)S(1)}, f32[2,128,128]{2,1,0:T(8,128)S(1)}, u32[]{:S(2)}, u32[]{:S(2)}) collective-permute-start(f32[2,128,128]{2,1,0:T(8,128)S(1)} %collective-permute-done.30), channel_id=1, source_target_pairs={{0,4},{1,5},{2,6},{3,7},{4,12},{5,13},{6,14},{7,15},{8,0},{9,1},{1... | collective-permute-start | bytes 393224 | tf_op jit(solution)/shard_map/ppermute | solution.py:39
  182.0 6.4 %collective-permute-start.33 = (f32[2,128,128]{2,1,0:T(8,128)S(1)}, f32[2,128,128]{2,1,0:T(8,128)S(1)}, u32[]{:S(2)}, u32[]{:S(2)}) collective-permute-start(f32[2,128,128]{2,1,0:T(8,128)S(1)} %collective-permute-done.31), channel_id=1, source_target_pairs={{0,8},{1,9},{2,10},{3,11},{4,0},{5,1},{6,2},{7,3},{8,16},{9,17},{1... | collective-permute-start | bytes 393224 | tf_op jit(solution)/shard_map/ppermute | solution.py:39
  184.4 5.0 %collective-permute-start.34 = (f32[2,128,128]{2,1,0:T(8,128)S(1)}, f32[2,128,128]{2,1,0:T(8,128)S(1)}, u32[]{:S(2)}, u32[]{:S(2)}) collective-permute-start(f32[2,128,128]{2,1,0:T(8,128)S(1)} %collective-permute-done.32), channel_id=1, source_target_pairs={{0,4},{1,5},{2,6},{3,7},{4,12},{5,13},{6,14},{7,15},{8,0},{9,1},{1... | collective-permute-start | bytes 393224 | tf_op jit(solution)/shard_map/ppermute | solution.py:39
  188.4 4.3 %collective-permute-start.35 = (f32[2,64,128]{2,1,0:T(8,128)S(1)}, f32[2,64,128]{2,1,0:T(8,128)S(1)}, u32[]{:S(2)}, u32[]{:S(2)}) collective-permute-start(f32[2,64,128]{2,1,0:T(8,128)S(1)} %slice.495), channel_id=1, source_target_pairs={{0,8},{1,9},{2,10},{3,11},{4,0},{5,1},{6,2},{7,3},{8,16},{9,17},{1... | collective-permute-start | bytes 196616 | tf_op jit(solution)/shard_map/ppermute | solution.py:39
  189.4 4.3 %collective-permute-start.36 = (f32[2,64,128]{2,1,0:T(8,128)S(1)}, f32[2,64,128]{2,1,0:T(8,128)S(1)}, u32[]{:S(2)}, u32[]{:S(2)}) collective-permute-start(f32[2,64,128]{2,1,0:T(8,128)S(1)} %slice.496), channel_id=1, source_target_pairs={{0,4},{1,5},{2,6},{3,7},{4,12},{5,13},{6,14},{7,15},{8,0},{9,1},{1... | collective-permute-start | bytes 196616 | tf_op jit(solution)/shard_map/ppermute | solution.py:39
  231.4 9.0 %collective-permute-start.43 = (f32[2,64,128]{2,1,0:T(8,128)}, f32[2,64,128]{2,1,0:T(8,128)S(1)}, u32[]{:S(2)}, u32[]{:S(2)}) collective-permute-start(f32[2,64,128]{2,1,0:T(8,128)} %get-tuple-element.185), channel_id=1, source_target_pairs={{0,8},{1,9},{2,10},{3,11},{4,0},{5,1},{6,2},{7,3},{8,16},{9,17},{1... | collective-permute-start | bytes 196616 | tf_op jit(solution)/shard_map/ppermute | solution.py:39
  233.0 8.1 %collective-permute-start.47 = (f32[2,64,128]{2,1,0:T(8,128)S(1)}, f32[2,64,128]{2,1,0:T(8,128)}, u32[]{:S(2)}, u32[]{:S(2)}) collective-permute-start(f32[2,64,128]{2,1,0:T(8,128)S(1)} %get-tuple-element.186), channel_id=1, source_target_pairs={{0,4},{1,5},{2,6},{3,7},{4,12},{5,13},{6,14},{7,15},{8,0},{9,1},{1... | collective-permute-start | bytes 196616 | tf_op jit(solution)/shard_map/ppermute | solution.py:39
  235.0 9.9 %collective-permute-start.41 = (f32[8,32,128]{2,1,0:T(8,128)}, f32[8,32,128]{2,1,0:T(8,128)}, u32[]{:S(2)}, u32[]{:S(2)}) collective-permute-start(f32[8,32,128]{2,1,0:T(8,128)} %constant_dynamic-slice_fusion.6), channel_id=1, source_target_pairs={{0,1},{1,0},{2,3},{3,2},{4,5},{5,4},{6,7},{7,6},{8,9},{9,8},{10,11... | collective-permute-start | bytes 393224 | tf_op jit(solution)/shard_map/ppermute | solution.py:39
  240.5 24.1 %collective-permute-start.37 = (f32[32,16,128]{2,1,0:T(8,128)}, f32[32,16,128]{2,1,0:T(8,128)}, u32[]{:S(2)}, u32[]{:S(2)}) collective-permute-start(f32[32,16,128]{2,1,0:T(8,128)} %copy.1571), channel_id=1, source_target_pairs={{0,2},{1,3},{2,0},{3,1},{4,6},{5,7},{6,4},{7,5},{8,10},{9,11},{10,... | collective-permute-start | bytes 786440 | tf_op jit(solution)/shard_map/ppermute | solution.py:39
  242.8 11.3 %collective-permute-start.48 = (f32[2,128,128]{2,1,0:T(8,128)}, f32[2,128,128]{2,1,0:T(8,128)}, u32[]{:S(2)}, u32[]{:S(2)}) collective-permute-start(f32[2,128,128]{2,1,0:T(8,128)} %pad_maximum_fusion.10), channel_id=1, source_target_pairs={{0,4},{1,5},{2,6},{3,7},{4,12},{5,13},{6,14},{7,15},{8,0},{9,1},{1... | collective-permute-start | bytes 393224 | tf_op jit(solution)/shard_map/ppermute | solution.py:39
  243.8 5.7 %collective-permute-start.44 = (f32[2,128,128]{2,1,0:T(8,128)S(1)}, f32[2,128,128]{2,1,0:T(8,128)S(1)}, u32[]{:S(2)}, u32[]{:S(2)}) collective-permute-start(f32[2,128,128]{2,1,0:T(8,128)S(1)} %pad_maximum_fusion.9), channel_id=1, source_target_pairs={{0,8},{1,9},{2,10},{3,11},{4,0},{5,1},{6,2},{7,3},{8,16},{9,17},{1... | collective-permute-start | bytes 393224 | tf_op jit(solution)/shard_map/ppermute | solution.py:39
  246.2 5.3 %collective-permute-start.42 = (f32[32,16,32]{1,0,2:T(8,128)S(1)}, f32[32,16,32]{1,0,2:T(8,128)S(1)}, u32[]{:S(2)}, u32[]{:S(2)}) collective-permute-start(f32[32,16,32]{1,0,2:T(8,128)S(1)} %slice.519), channel_id=1, source_target_pairs={{0,2},{1,3},{2,0},{3,1},{4,6},{5,7},{6,4},{7,5},{8,10},{9,11},{10,... | collective-permute-start | bytes 196616 | tf_op jit(solution)/shard_map/ppermute | solution.py:39
  250.4 5.1 %collective-permute-start.45 = (f32[2,128,128]{2,1,0:T(8,128)S(1)}, f32[2,128,128]{2,1,0:T(8,128)}, u32[]{:S(2)}, u32[]{:S(2)}) collective-permute-start(f32[2,128,128]{2,1,0:T(8,128)S(1)} %dynamic-slice_add_fusion.2), channel_id=1, source_target_pairs={{0,8},{1,9},{2,10},{3,11},{4,0},{5,1},{6,2},{7,3},{8,16},{9,17},{1... | collective-permute-start | bytes 393224 | tf_op jit(solution)/shard_map/ppermute | solution.py:39
  256.7 5.1 %collective-permute-start.49 = (f32[2,128,128]{2,1,0:T(8,128)S(1)}, f32[2,128,128]{2,1,0:T(8,128)S(1)}, u32[]{:S(2)}, u32[]{:S(2)}) collective-permute-start(f32[2,128,128]{2,1,0:T(8,128)S(1)} %get-tuple-element.180), channel_id=1, source_target_pairs={{0,4},{1,5},{2,6},{3,7},{4,12},{5,13},{6,14},{7,15},{8,0},{9,1},{1... | collective-permute-start | bytes 393224 | tf_op jit(solution)/shard_map/ppermute | solution.py:39
  261.5 7.2 %collective-permute-start.46 = (f32[2,128,128]{2,1,0:T(8,128)S(1)}, f32[2,128,128]{2,1,0:T(8,128)S(1)}, u32[]{:S(2)}, u32[]{:S(2)}) collective-permute-start(f32[2,128,128]{2,1,0:T(8,128)S(1)} %get-tuple-element.179), channel_id=1, source_target_pairs={{0,8},{1,9},{2,10},{3,11},{4,0},{5,1},{6,2},{7,3},{8,16},{9,17},{1... | collective-permute-start | bytes 393224 | tf_op jit(solution)/shard_map/ppermute | solution.py:39
  262.7 6.0 %collective-permute-start.50 = (f32[2,128,128]{2,1,0:T(8,128)S(1)}, f32[2,128,128]{2,1,0:T(8,128)S(1)}, u32[]{:S(2)}, u32[]{:S(2)}) collective-permute-start(f32[2,128,128]{2,1,0:T(8,128)S(1)} %dynamic-slice_add_fusion.1), channel_id=1, source_target_pairs={{0,4},{1,5},{2,6},{3,7},{4,12},{5,13},{6,14},{7,15},{8,0},{9,1},{1... | collective-permute-start | bytes 393224 | tf_op jit(solution)/shard_map/ppermute | solution.py:39
  (57 other events, 304.6 us)

commit v2 on v1

v2 whole, which is shorter than its diff:
```python
import functools
import jax
import jax.numpy as jnp
from jax import lax
from jax.experimental import pallas as pl
from jax.experimental.pallas import tpu as pltpu
from jax.sharding import PartitionSpec as P

STEPS = 2
START = 20


SMOOTHING = 0.5
BETA_ONE = 0.9
BETA_TWO = 0.99
LEARN_RATE = 0.01
EPSILON = 1e-08

LANES = 128
ROWS = 16
BOTH = ("gx", "gy")
f32 = jnp.float32
bf16 = jnp.bfloat16


def ring_order(chips):
    return list(range(0, chips, 2)) + list(range(chips - 1, 0, -2))


def send(x, move):
    n, peers = lax.axis_size("gx"), lax.axis_size("gy")
    pairs = []
    for g in range(n):
        for y in range(peers):
            to = move(g // 2, g % 2, y)
            if to is not None:
                pairs.append((g * peers + y, (to[0] * 2 + to[1]) * peers + to[2]))
    return lax.ppermute(x, BOTH, pairs)


def to_core(x):
    return send(x, lambda k, c, y: (k, 1 - c, y))


def to_ring(x, step):
    chips = lax.axis_size("gx") // 2
    order = ring_order(chips)
    at = {k: i for i, k in enumerate(order)}
    return send(x, lambda k, c, y: (order[(at[k] + step) % chips], c, y))


def to_gy(x, step):
    peers = lax.axis_size("gy")
    return send(x, lambda k, c, y: (k, c, (y + step) % peers))


def offsets(chips):
    out = [0]
    for d in range(1, chips // 2):
        out += [-d, d]
    return out + [chips // 2]


def chip_in_slot(gx, slot, chips):
    k = gx // 2
    at = jnp.where(k % 2 == 0, k // 2, chips - 1 - k // 2)
    i = (at + offsets(chips)[slot] + chips) % chips
    return jnp.where(i < chips // 2, 2 * i, 2 * chips - 1 - 2 * i)


def vmem(count):
    return [pl.BlockSpec(memory_space=pltpu.VMEM)] * count


SCALARS = pl.BlockSpec(memory_space=pltpu.SMEM)


def cost(flops, size):
    return pl.CostEstimate(flops=flops, bytes_accessed=size, transcendentals=0)


def diagonal(small, times):
    size = small.shape[0] * times
    wide = jnp.concatenate([small.astype(f32)] * times, axis=1)
    full = jnp.concatenate([wide] * times, axis=0)
    row = lax.broadcasted_iota(jnp.int32, (size, size), 0) // small.shape[0]
    col = lax.broadcasted_iota(jnp.int32, (size, size), 1) // small.shape[0]
    return jnp.where(row == col, full, 0.0)


def fixed_kernel(
    chips, zl, info, b_output, target_a, target_b, w, w_t, w_o, b, o, wanted, w_in, w_out, w_back, bias, scale
):
    gx = info[0]
    x_count = target_a.shape[0]
    starts = [
        pl.multiple_of((2 * chip_in_slot(gx, s, chips) + gx % 2) * zl, zl) for s in range(chips)
    ]
    for side, ref in enumerate((target_a, target_b)):

        def one(x, carry):
            rows = jnp.concatenate([ref[x, pl.ds(z, zl), :] for z in starts], axis=0)
            rows = rows - b_output[0]
            high = rows.astype(bf16).astype(f32)
            both = jnp.concatenate([high, rows - high], axis=0)
            wanted[side * x_count + x] = both.T.astype(bf16)
            return carry

        lax.fori_loop(0, x_count, one, 0)
    times = w_in.shape[0] // w.shape[0]
    w_in[...] = diagonal(0.5 * w[...].astype(f32), times).astype(bf16)
    w_out[...] = diagonal(w_o[...], times).astype(bf16)
    w_back[...] = diagonal(w_t[...], times).astype(bf16)
    bias[...] = jnp.concatenate([0.5 * b[...]] * times, axis=1)
    scale[...] = jnp.concatenate([0.5 * o[...]] * times, axis=1)


def fixed_parts(info, target, target_b, zl, w_hidden, b_hidden, w_output, b_output):
    chips = lax.axis_size("gx") // 2
    x_count, z_count, y_count = target.shape
    hidden = w_hidden.shape[1]
    width = zl * hidden
    square = jax.ShapeDtypeStruct((width, width), bf16)
    line = jax.ShapeDtypeStruct((1, width), f32)
    return pl.pallas_call(
        functools.partial(fixed_kernel, chips, zl),
        in_specs=[SCALARS, SCALARS] + vmem(7),
        out_specs=vmem(6),
        out_shape=[
            jax.ShapeDtypeStruct((2 * x_count, y_count, z_count), bf16),
            square,
            square,
            square,
            line,
            line,
        ],
        cost_estimate=cost(0, 4 * 2**20),
    )(
        info,
        b_output,
        target,
        target_b,
        w_hidden,
        w_hidden.T,
        jnp.broadcast_to(w_output[:, None], (hidden, hidden)),
        b_hidden[None],
        w_output.astype(f32)[None],
    )


def lanes_kernel(plane, out):
    c, zl, _ = plane.shape
    per = LANES // c
    for t in range(zl // per):
        rows = jnp.concatenate([plane[:, t * per + j, :] for j in range(per)], axis=0)
        out[:, t * LANES : (t + 1) * LANES] = rows.T


def lanes_yz(plane):
    c, zl, y = plane.shape
    return pl.pallas_call(
        lanes_kernel,
        in_specs=vmem(1),
        out_specs=vmem(1)[0],
        out_shape=jax.ShapeDtypeStruct((y, zl * c), f32),
        cost_estimate=cost(0, 2**18),
    )(plane)


def natural_kernel(a, b, d, out):
    c, zl, _ = out.shape
    per = LANES // c
    for t in range(zl // per):
        at = slice(t * LANES, (t + 1) * LANES)
        rows = (a[:, at] + b[:, at] + d[:, at]).T
        for j in range(per):
            out[:, t * per + j, :] = rows[j * c : (j + 1) * c]


def natural_yz(a, b, d, shape):
    return pl.pallas_call(
        natural_kernel,
        in_specs=vmem(3),
        out_specs=vmem(1)[0],
        out_shape=jax.ShapeDtypeStruct(shape, f32),
        cost_estimate=cost(0, 2**19),
    )(a, b, d)


def z_places(gx, gy, slot, chips, peers, zl, zs):
    z = (2 * chip_in_slot(gx, slot, chips) + gx % 2) * zl
    return (gy - z // zs + peers) % peers * zs + z % zs


def spread_kernel(chips, peers, zl, info, xy_a, xy_b, *refs):
    xzs, (xy, xz, held) = refs[: 2 * peers], refs[2 * peers :]
    c, x_count, _ = xy_a.shape
    zs = xzs[0].shape[2]
    for side, ref in enumerate((xy_a, xy_b)):
        for x in range(x_count):
            xy[side * x_count + x] = jnp.concatenate([ref[:, x, :]] * (LANES // c), axis=0).T
    for s in range(peers):
        for side in range(2):
            for x in range(x_count):
                held[s * zs : (s + 1) * zs, side * x_count + x, :] = xzs[2 * s + side][:, x, :].T
    for p in range(chips):
        at = z_places(info[0], info[1], p, chips, peers, zl, zs)
        xz[p] = jnp.concatenate([held[at + j] for j in range(zl)], axis=1)


def spread(info, xy_a, xy_b, xzs, zl):
    peers, chips = lax.axis_size("gy"), lax.axis_size("gx") // 2
    c, x_count, y_count = xy_a.shape
    return pl.pallas_call(
        functools.partial(spread_kernel, chips, peers, zl),
        in_specs=[SCALARS] + vmem(2 + len(xzs)),
        out_specs=vmem(2),
        out_shape=[
            jax.ShapeDtypeStruct((2 * x_count, y_count, LANES), f32),
            jax.ShapeDtypeStruct((chips, 2 * x_count, zl * c), f32),
        ],
        scratch_shapes=[pltpu.VMEM((peers * xzs[0].shape[2], 2 * x_count, c), f32)],
        cost_estimate=cost(0, 4 * 2**20),
    )(info, xy_a, xy_b, *xzs)


def collect_kernel(chips, peers, zl, info, part_xy, part_xz, xy_a, xy_b, *refs):
    outs, held = refs[: 2 * peers], refs[2 * peers]
    c, x_count, _ = xy_a.shape
    zs = outs[0].shape[2]
    for side, ref in enumerate((xy_a, xy_b)):
        for x in range(x_count):
            rows = part_xy[side * x_count + x].T
            ref[:, x, :] = sum(rows[j * c : (j + 1) * c] for j in range(LANES // c))
    held[...] = jnp.zeros_like(held)
    for p in range(chips):
        at = z_places(info[0], info[1], p, chips, peers, zl, zs)
        rows = part_xz[p]
        for j in range(zl):
            held[at + j] = rows[:, j * c : (j + 1) * c]
    for s in range(peers):
        for side in range(2):
            for x in range(x_count):
                outs[2 * s + side][:, x, :] = held[s * zs : (s + 1) * zs, side * x_count + x, :].T


def collect(info, part_xy, part_xz, shape_xy, shape_xz, zl):
    peers, chips = lax.axis_size("gy"), lax.axis_size("gx") // 2
    c, x_count, _ = shape_xy
    outs = pl.pallas_call(
        functools.partial(collect_kernel, chips, peers, zl),
        in_specs=[SCALARS] + vmem(2),
        out_specs=vmem(2 + 2 * peers),
        out_shape=[jax.ShapeDtypeStruct(shape_xy, f32)] * 2
        + [jax.ShapeDtypeStruct(shape_xz, f32)] * (2 * peers),
        scratch_shapes=[pltpu.VMEM((peers * shape_xz[2], 2 * x_count, c), f32)],
        cost_estimate=cost(0, 4 * 2**20),
    )(info, part_xy, part_xz)
    return outs[0], outs[1], outs[2:]


def grads_kernel(count, w_in, w_out, w_back, bias, scale, wanted, xy, xz, *refs):
    yzs, (gxy, gxz), gyzs, (block_yz, total_yz) = (
        refs[:count],
        refs[count : count + 2],
        refs[count + 2 : 2 * count + 2],
        refs[2 * count + 2 :],
    )
    p = pl.program_id(0)
    x_count, y_count, _ = xy.shape
    width = w_in.shape[0]
    z_count = wanted.shape[2] // 2
    zl = z_count // count
    times = width // LANES

    @pl.when(p == 0)
    def _():
        gxy[...] = jnp.zeros_like(gxy)

    for j in range(count):

        @pl.when(p == j)
        def _():
            block_yz[...] = yzs[j][...]

    total_yz[...] = jnp.zeros_like(total_yz)
    row = lax.broadcasted_iota(jnp.int32, (2 * z_count, width), 0) % z_count
    col = lax.broadcasted_iota(jnp.int32, (2 * z_count, width), 1) // (width // zl)
    pick = jnp.where(row == p * zl + col, -1.0, 0.0).astype(bf16)
    w_res = jnp.concatenate([w_out[...], pick], axis=0)

    def some_rows(i, carry):
        xs = [i * ROWS + j for j in range(ROWS)]
        yz = block_yz[...]
        xzs = [xz[0, pl.ds(x, 1), :] for x in xs]
        xys = [jnp.concatenate([xy[x]] * times, axis=1) for x in xs]
        features = jnp.concatenate([(a * yz * r).astype(bf16) for a, r in zip(xys, xzs)], axis=0)
        half = jnp.dot(features, w_in[...], preferred_element_type=f32) + bias[...]
        t = jnp.tanh(half)
        up = 1.0 + t
        hidden = half * up
        slope = (up + hidden * (1.0 - t)) * scale[...]
        residual = jnp.dot(
            jnp.concatenate(
                [hidden.astype(bf16), jnp.concatenate([wanted[x] for x in xs], axis=0)], axis=1
            ),
            w_res,
            preferred_element_type=f32,
        )
        back_hidden = (residual * slope).astype(bf16)
        back = jnp.dot(back_hidden, w_back[...], preferred_element_type=f32)
        total = None
        for j, x in enumerate(xs):
            b = back[j * y_count : (j + 1) * y_count]
            e = b * xzs[j]
            k = e * yz
            gxy[x] += sum(k[:, h * LANES : (h + 1) * LANES] for h in range(times))
            part = e * xys[j]
            total = part if total is None else total + part
            gxz[0, pl.ds(x, 1), :] = jnp.sum(b * (xys[j] * yz), axis=0, keepdims=True)
        total_yz[...] += total
        return carry

    lax.fori_loop(0, x_count // ROWS, some_rows, 0)
    for j in range(count):

        @pl.when(p == j)
        def _():
            gyzs[j][...] = total_yz[...]


def block_grads(weights, wanted, xy, xz, yzs):
    count = len(yzs)
    x_count, y_count, _ = xy.shape
    width = yzs[0].shape[1]

    def whole(a):
        return pl.BlockSpec(a.shape, lambda p: (0,) * a.ndim)

    slot = pl.BlockSpec((1, x_count, width), lambda p: (p, 0, 0))
    outs = pl.pallas_call(
        functools.partial(grads_kernel, count),
        grid=(count,),
        in_specs=[whole(w) for w in weights] + [whole(wanted), whole(xy), slot] + [whole(a) for a in yzs],
        out_specs=[whole(xy), slot] + [whole(a) for a in yzs],
        out_shape=[jax.ShapeDtypeStruct(a.shape, f32) for a in (xy, xz, *yzs)],
        scratch_shapes=[pltpu.VMEM((y_count, width), f32)] * 2,
        compiler_params=pltpu.CompilerParams(vmem_limit_bytes=58 * 2**20),
        cost_estimate=cost(6 * x_count * y_count * count * width * width, 8 * 2**20),
    )(*weights, wanted, xy, xz, *yzs)
    return outs[0], outs[1], outs[2:]


def gather_ring(own):
    steps = lax.axis_size("gx") // 4
    middle = own.shape[0] // 2
    slots = [own]
    left, right = own, own
    for d in range(1, steps):
        left, right = to_ring(left, 1), to_ring(right, -1)
        slots += [left, right]
    first, second = to_ring(left[:middle], 1), to_ring(right[middle:], -1)
    slots.append(jnp.concatenate([first, second], axis=0))
    return slots


def scatter_ring(parts):
    chips = len(parts)
    slot = {o: s for s, o in enumerate(offsets(chips))}
    middle = parts[0].shape[0] // 2
    far = parts[slot[chips // 2]]
    ahead, behind = to_ring(far[:middle], 1), to_ring(far[middle:], -1)
    for d in range(chips // 2 - 1, 0, -1):
        if d == chips // 2 - 1:
            ahead = jnp.pad(ahead, ((0, middle), (0, 0)))
            behind = jnp.pad(behind, ((middle, 0), (0, 0)))
        ahead = to_ring(parts[slot[d]] + ahead, 1)
        behind = to_ring(parts[slot[-d]] + behind, -1)
    return parts[0], ahead, behind


def borders(planes):
    n, peers = lax.axis_size("gx"), lax.axis_size("gy")
    up = [(i, i + 1) for i in range(n - 1)]
    last = jnp.concatenate([p[:, -1, :] for p in planes], axis=1)
    first = jnp.concatenate([p[:, 0, :] for p in planes], axis=1)
    above = lax.ppermute(last, "gx", up)
    below = lax.ppermute(first, "gx", [(j, i) for i, j in up])
    last = jnp.concatenate([p[:, :, -1] for p in planes], axis=1)
    first = jnp.concatenate([p[:, :, 0] for p in planes], axis=1)
    if peers == 2:
        left = right = lax.ppermute(
            jnp.where(lax.axis_index("gy") == 0, last, first), "gy", [(0, 1), (1, 0)]
        )
    else:
        up = [(i, i + 1) for i in range(peers - 1)]
        left = lax.ppermute(last, "gy", up)
        right = lax.ppermute(first, "gy", [(j, i) for i, j in up])
    out = []
    row, col = 0, 0
    for p in planes:
        a, b = p.shape[1:]
        out.append(
            (
                above[:, None, col : col + b],
                below[:, None, col : col + b],
                left[:, row : row + a, None],
                right[:, row : row + a, None],
            )
        )
        row, col = row + a, col + b
    return out


def smooth(plane, around):
    above, below, left, right = around
    rows = jnp.concatenate([above, plane, below], axis=1)
    cols = jnp.concatenate([left, plane, right], axis=2)
    down = rows[:, 1:, :] - rows[:, :-1, :]
    across = cols[:, :, 1:] - cols[:, :, :-1]
    row_count = down.shape[1]
    col_count = across.shape[2]
    row_places = jnp.arange(row_count)
    col_places = jnp.arange(col_count)
    lowest_x = lax.axis_index("gx") == 0
    highest_x = lax.axis_index("gx") == lax.axis_size("gx") - 1
    lowest_y = lax.axis_index("gy") == 0
    highest_y = lax.axis_index("gy") == lax.axis_size("gy") - 1
    row_keeps = jnp.where(
        (row_places == 0) & lowest_x | (row_places == row_count - 1) & highest_x, 0.0, 1.0
    )
    col_keeps = jnp.where(
        (col_places == 0) & lowest_y | (col_places == col_count - 1) & highest_y, 0.0, 1.0
    )
    down = down * row_keeps[None, :, None]
    across = across * col_keeps[None, None, :]
    return (
        2.0 * SMOOTHING * (down[:, :-1, :] - down[:, 1:, :] + across[:, :, :-1] - across[:, :, 1:])
    )


def adam(plane, first, second, grads, count):
    first = BETA_ONE * first + (1.0 - BETA_ONE) * grads
    second = BETA_TWO * second + (1.0 - BETA_TWO) * grads * grads
    corr_one = 1.0 - BETA_ONE**count
    corr_two = 1.0 - BETA_TWO**count
    plane = plane - LEARN_RATE * (first / corr_one) / (jnp.sqrt(second / corr_two) + EPSILON)
    return (plane, first, second)


def per_device(
    target,
    plane_xy,
    plane_xz,
    plane_yz,
    first_xy,
    first_xz,
    first_yz,
    second_xy,
    second_xz,
    second_yz,
    w_hidden,
    b_hidden,
    w_output,
    b_output,
):
    peers = lax.axis_size("gy")
    info = jnp.stack([lax.axis_index("gx"), lax.axis_index("gy")]).astype(jnp.int32)
    zl = plane_yz.shape[1]
    lanes = lanes_yz(plane_yz)
    target_b = to_core(target)
    fixed = None

    for iteration in range(STEPS):
        yzs = gather_ring(lanes)
        xy_b, xz_b = to_core(plane_xy), to_core(plane_xz)
        xzs = [plane_xz, xz_b]
        for s in range(1, peers):
            xzs += [to_gy(plane_xz, s), to_gy(xz_b, s)]
        around = borders((plane_xy, plane_xz, plane_yz))
        if fixed is None:
            fixed = fixed_parts(info, target, target_b, zl, w_hidden, b_hidden, w_output, b_output)
        wanted, weights = fixed[0], fixed[1:]
        xy, xz = spread(info, plane_xy, xy_b, xzs, zl)

        part_xy, part_xz, part_yz = block_grads(weights, wanted, xy, xz, yzs)
        grad_xy, far_xy, parts_xz = collect(
            info, part_xy, part_xz, plane_xy.shape, plane_xz.shape, zl
        )
        grad_xy = grad_xy + to_core(far_xy)
        grad_xz, far_xz = parts_xz[:2]
        for s in range(1, peers):
            grad_xz = grad_xz + to_gy(parts_xz[2 * s], -s)
            far_xz = far_xz + to_gy(parts_xz[2 * s + 1], -s)
        grad_xz = grad_xz + to_core(far_xz)
        grad_yz = natural_yz(*scatter_ring(part_yz), plane_yz.shape)

        grad_xy = grad_xy + smooth(plane_xy, around[0])
        grad_xz = grad_xz + smooth(plane_xz, around[1])
        grad_yz = grad_yz + smooth(plane_yz, around[2])
        count = START + iteration + 1
        plane_yz, first_yz, second_yz = adam(plane_yz, first_yz, second_yz, grad_yz, count)
        if iteration + 1 < STEPS:
            lanes = lanes_yz(plane_yz)
        plane_xy, first_xy, second_xy = adam(plane_xy, first_xy, second_xy, grad_xy, count)
        plane_xz, first_xz, second_xz = adam(plane_xz, first_xz, second_xz, grad_xz, count)
    return (
        plane_xy,
        plane_xz,
        plane_yz,
        first_xy,
        first_xz,
        first_yz,
        second_xy,
        second_xz,
        second_yz,
    )


def solution(mesh):
    return jax.shard_map(
        per_device,
        mesh=mesh,
        in_specs=(
            P("gx", None, "gy"),
            P(None, "gx", "gy"),
            P(None, "gx", "gy"),
            P(None, "gx", "gy"),
            P(None, "gx", "gy"),
            P(None, "gx", "gy"),
            P(None, "gx", "gy"),
            P(None, "gx", "gy"),
            P(None, "gx", "gy"),
            P(None, "gx", "gy"),
            P(),
            P(),
            P(),
            P(),
        ),
        out_specs=(
            P(None, "gx", "gy"),
            P(None, "gx", "gy"),
            P(None, "gx", "gy"),
            P(None, "gx", "gy"),
            P(None, "gx", "gy"),
            P(None, "gx", "gy"),
            P(None, "gx", "gy"),
            P(None, "gx", "gy"),
            P(None, "gx", "gy"),
        ),
        check_vma=False,
    )
```

time: 274 us -> 255 us (0.931)
  Pallas kernels: 70.2 us -> 105 us
  other arithmetic: 54.3 us -> 21.2 us
  local copies, waits for them, and re-layouts: 61.3 us -> 37.5 us
  between operations: 7.51 us -> 2.27 us
  starting transfers between devices: 54.7 us -> 59.5 us
  waiting for transfers between devices: 24.2 us -> 28.9 us
    pallas_call x2 -> x11, Pallas kernels: 70.2 us -> 105 us  [the longest x2 72 us: block_grads(): pl.pallas_call(functools.partial(grads_kernel, count), grid=(count,), in_...]
    add x14, other arithmetic: 14.8 us -> 3.17 us  [the longest x2 1.17 us: per_device(): far_xz = far_xz + to_gy(parts_xz[2 * s + 1], -s)]
    concatenate x11 -> x2, other arithmetic: 11.8 us -> 2.17 us  [gather_ring(): slots.append(jnp.concatenate([first, second], axis=0))]
    unnamed x141 -> x143, local copies, waits for them, and re-layouts: 19.9 us -> 11.5 us
    another operation x14 -> x0, local copies, waits for them, and re-layouts: 6.07 us -> none  [the longest x8 4.76 us: lanes_xy(): return jnp.tile(plane.transpose(1, 2, 0), (1, 1, LANES // plane.shape[0]))]
    dynamic_slice x7 -> x0, local copies, waits for them, and re-layouts: 5.62 us -> none  [the longest x2 3.13 us: piece(): lax.dynamic_slice_in_dim(part_xz, (gy + s) % peers * tiles_gy, tiles_gy,...]
    ppermute x3 -> x4, local copies, waits for them, and re-layouts: 1.69 us -> 6.32 us  [send(): return lax.ppermute(x, BOTH, pairs)]
    ppermute x45 -> x49, starting transfers between devices: 45.6 us -> 50.1 us  [send(): return lax.ppermute(x, BOTH, pairs)]
  transfers between devices with their start and end apart: 51 -> 55, of which waited for: 15 -> 20; matrix products, arithmetic and copies ran while one was open for 36% -> 19% of each run, Pallas kernels for 0% -> 10%
where the time goes in v2:
time: 255 us; the launch traced here: 254 us
  Pallas kernels  105 us (41%)
  starting transfers between devices  59.5 us (23%)
  local copies, waits for them, and re-layouts  37.5 us (15%)
  waiting for transfers between devices  28.9 us (11%)
  other arithmetic  21.2 us (8%)
    pallas_call x2, Pallas kernels, block_grads(): pl.pallas_call(functools.partial(grads_kernel, count), grid=(count,), in_...  72 us
    ppermute x49, starting transfers between devices, send(): return lax.ppermute(x, BOTH, pairs)  50.1 us
    ppermute x49, waiting for transfers between devices, send(): return lax.ppermute(x, BOTH, pairs)  22.4 us
    unnamed x143, local copies, waits for them, and re-layouts  11.5 us
    pallas_call x2, Pallas kernels, spread(): pl.pallas_call(functools.partial(spread_kernel, chips, peers, zl), in_spe...  10.3 us
    pallas_call x2, Pallas kernels, collect(): pl.pallas_call(functools.partial(collect_kernel, chips, peers, zl), in_sp...  9.06 us
    ppermute x4, local copies, waits for them, and re-layouts, send(): return lax.ppermute(x, BOTH, pairs)  6.32 us
    sub x6, other arithmetic, adam(): plane - LEARN_RATE * (first / corr_one) / (jnp.sqrt(second / corr_two) +...  6.25 us
  transfers between devices with their start and end apart: 55, of which 20 were waited for; matrix products, arithmetic and copies ran while one was open for 19% of the time, Pallas kernels for 10%

profile of v2, /device:TPU:0, one launch (start us, length us, event | category | flops | bytes accessed | tf_op | source)
XLA Modules:
  0.0 253.8 jit_solution(8790864272144425952)
XLA Ops:
  1.7 1.7 shard_map.207.refs_0_
  3.4 2.6 %collective-permute-start.5 = (f32[128,256]{1,0:T(8,128)}, f32[128,256]{1,0:T(8,128)}, u32[]{:S(2)}, u32[]{:S(2)}) collective-permute-start(f32[128,256]{1,0:T(8,128)} %shard_map.207.refs_0_), channel_id=1, source_target_pairs={{0,8},{1,9},{2,10},{3,11},{4,0},{5,1},{6,2},{7,3},{8,16},{9,17},{1... | collective-permute-start | bytes 393224 | tf_op jit(solution)/shard_map/ppermute | solution.py:38
  9.6 1.6 collective-permute-start.16
  16.2 1.4 copy.795
  18.3 2.4 collective-permute-start.15
  26.9 2.2 collective-permute-start.6
  29.2 2.1 collective-permute-start.7
  31.2 3.7 %collective-permute-done.6.refs_2_ = f32[128,256]{1,0:T(8,128)S(1)} collective-permute-done((f32[128,256]{1,0:T(8,128)}, f32[128,256]{1,0:T(8,128)S(1)}, u32[]{:S(2)}, u32[]{:S(2)}) %collective-permute-start.6) | collective-permute-done | bytes 131104 | tf_op jit(solution)/shard_map/ppermute | solution.py:38
  35.4 2.0 collective-permute-start.9
  37.4 2.7 %collective-permute-done.8.refs_4_ = f32[128,256]{1,0:T(8,128)S(1)} collective-permute-done((f32[128,256]{1,0:T(8,128)S(1)}, f32[128,256]{1,0:T(8,128)S(1)}, u32[]{:S(2)}, u32[]{:S(2)}) %collective-permute-start.8) | collective-permute-done | bytes 131104 | tf_op jit(solution)/shard_map/ppermute | solution.py:38
  41.2 1.9 collective-permute-start.4
  43.8 1.4 collective-permute-done.10.refs_6_
  47.8 1.4 fusion.44
  51.6 5.1 %shard_map.206 = (f32[32,128,128]{2,1,0:T(8,128)}, f32[8,32,256]{2,1,0:T(8,128)}) custom-call(s32[2]{0:T(128)} %pad_add_fusion.4.info, f32[32,16,128]{2,1,0:T(8,128)} %xy_a.1, f32[32,16,128]{2,1,0:T(8,128)} %copy-done.25, f32[32,16,64]{2,1,0:T(8,128)} %refs_0_.1, f32[32,16,64]{2,1,0:T(8,128)} %copy-done.24, f32[32,16,64]{2,1,0:T(8,128)} %copy-done.26, ...), custom_call_target="tpu_custom_call" | custom-call | bytes 4194304 | tf_op jit(solution)/shard_map/pallas_call | solution.py:214
  56.7 1.5 pad_maximum_fusion.refs_7_
  59.6 6.1 %shard_map.205 = (bf16[32,128,128]{2,1,0:T(8,128)(2,1)}, bf16[256,256]{1,0:T(8,128)(2,1)}, bf16[256,256]{1,0:T(8,128)(2,1)}, bf16[256,256]{1,0:T(8,128)(2,1)}, f32[1,256]{1,0:T(1,128)}, /*index=5*/f32[1,256]{1,0:T(1,128)}) custom-call(s32[2]{0:T(128)} %pad_add_fusion.4.info, f32[1]{0:T(128)S(6)} %copy.926.b_output, f32[16,128,128]{2,1,0:T(8,128)} %target_a.1, ...), custom_call_target="tpu_custom_call" | custom-call | bytes 4194304 | tf_op jit(solution)/shard_map/pallas_call | solution.py:125
  65.7 36.0 %shard_map.208 = (f32[32,128,128]{2,1,0:T(8,128)}, f32[8,32,256]{2,1,0:T(8,128)}, f32[128,256]{1,0:T(8,128)}, f32[128,256]{1,0:T(8,128)}, f32[128,256]{1,0:T(8,1...) custom-call(bf16[256,256]{1,0:T(8,128)(2,1)} %get-tuple-element.51.w, ...), custom_call_target="tpu_custom_call" | custom-call | flops 12884901888 | bytes 8388608 | tf_op jit(solution)/shard_map/pallas_call | solution.py:341
  103.6 4.5 %shard_map.209 = (f32[32,16,128]{2,1,0:T(8,128)}, f32[32,16,128]{2,1,0:T(8,128)}, f32[32,16,64]{2,1,0:T(8,128)}, f32[32,16,64]{2,1,0:T(8,128)}, f32[32,16,64]{2,1,0:T(8,128)}, /*index=5*/f32[32,16,64]{2,1,0:T(8,128)}) custom-call(s32[2]{0:T(128)} %pad_add_fusion.4.info, f32[32,128,128]{2,1,0:T(8,128)} %get-tuple-element.59.part_xy, ...), custom_call_target="tpu_custom_call" | custom-call | bytes 4194304 | tf_op jit(solution)/shard_map/pallas_call | solution.py:250
  109.3 1.6 collective-permute-start.19
  114.8 2.0 collective-permute-done.24
  116.8 1.4 collective-permute-start.25
  120.5 1.6 collective-permute-start.30
  124.3 1.6 collective-permute-start.22
  131.9 1.8 copy.834.refs_1_
  135.3 1.8 shard_map.211
  137.2 1.7 divide_subtract_fusion.5
  139.5 1.7 shard_map.212.refs_0_
  143.5 1.6 collective-permute-start.43
  145.3 2.1 collective-permute-done.43
  152.1 3.2 %collective-permute-done.41 = f32[32,320]{1,0:T(8,128)S(1)} collective-permute-done((f32[32,320]{1,0:T(8,128)S(1)}, f32[32,320]{1,0:T(8,128)S(1)}, u32[]{:S(2)}, u32[]{:S(2)}) %collective-permute-start.41) | collective-permute-done | bytes 40992 | tf_op jit(solution)/shard_map/ppermute | solution.py:388
  155.4 3.2 %collective-permute-start.34 = (f32[128,256]{1,0:T(8,128)S(1)}, f32[128,256]{1,0:T(8,128)S(1)}, u32[]{:S(2)}, u32[]{:S(2)}) collective-permute-start(f32[128,256]{1,0:T(8,128)S(1)} %collective-permute-done.32.refs_1_), channel_id=1, source_target_pairs={{0,8},{1,9},{2,10},{3,11},{4,0},{5,1},{6,2},{7,3},{8,16},{9,17},{1... | collective-permute-start | bytes 393224 | tf_op jit(solution)/shard_map/ppermute | solution.py:38
  158.7 3.5 %collective-permute-done.34.refs_3_ = f32[128,256]{1,0:T(8,128)S(1)} collective-permute-done((f32[128,256]{1,0:T(8,128)S(1)}, f32[128,256]{1,0:T(8,128)S(1)}, u32[]{:S(2)}, u32[]{:S(2)}) %collective-permute-start.34) | collective-permute-done | bytes 131104 | tf_op jit(solution)/shard_map/ppermute | solution.py:38
  162.2 2.5 collective-permute-start.36
  165.3 3.0 %collective-permute-done.36.refs_5_ = f32[128,256]{1,0:T(8,128)S(1)} collective-permute-done((f32[128,256]{1,0:T(8,128)S(1)}, f32[128,256]{1,0:T(8,128)S(1)}, u32[]{:S(2)}, u32[]{:S(2)}) %collective-permute-start.36) | collective-permute-done | bytes 131104 | tf_op jit(solution)/shard_map/ppermute | solution.py:38
  168.3 2.3 collective-permute-start.38
  171.5 1.8 copy.836.refs_3_
  173.3 1.8 copy.832.xy_b
  175.1 5.1 %shard_map.210 = (f32[32,128,128]{2,1,0:T(8,128)}, f32[8,32,256]{2,1,0:T(8,128)}) custom-call(s32[2]{0:T(128)} %pad_add_fusion.4.info, f32[32,16,128]{2,1,0:T(8,128)} %copy.831.xy_a, f32[32,16,128]{2,1,0:T(8,128)} %copy.832.xy_b, f32[32,16,64]{2,1,0:T(8,128)} %copy.833.refs_0_, f32[32,16,64]{2,1,0:T(8,128)} %copy.834.refs_1_, f32[32,16,64]{2,1,0:T(8,128)} %copy.835.refs_2_, ...), custom_call_target="tpu_custom_call" | custom-call | bytes 4194304 | tf_op jit(solution)/shard_map/pallas_call | solution.py:214
  180.9 36.0 %shard_map.213 = (f32[32,128,128]{2,1,0:T(8,128)}, f32[8,32,256]{2,1,0:T(8,128)}, f32[128,256]{1,0:T(8,128)}, f32[128,256]{1,0:T(8,128)}, f32[128,256]{1,0:T(8,1...) custom-call(bf16[256,256]{1,0:T(8,128)(2,1)} %get-tuple-element.51.w, ...), custom_call_target="tpu_custom_call" | custom-call | flops 12884901888 | bytes 8388608 | tf_op jit(solution)/shard_map/pallas_call | solution.py:341
  216.9 1.5 fusion.36
  219.2 1.6 collective-permute-start.47
  220.8 4.5 %shard_map.214 = (f32[32,16,128]{2,1,0:T(8,128)}, f32[32,16,128]{2,1,0:T(8,128)}, f32[32,16,64]{2,1,0:T(8,128)}, f32[32,16,64]{2,1,0:T(8,128)}, f32[32,16,64]{2,1,0:T(8,128)}, /*index=5*/f32[32,16,64]{2,1,0:T(8,128)}) custom-call(s32[2]{0:T(128)} %pad_add_fusion.4.info, f32[32,128,128]{2,1,0:T(8,128)} %get-tuple-element.77.part_xy, ...), custom_call_target="tpu_custom_call" | custom-call | bytes 4194304 | tf_op jit(solution)/shard_map/pallas_call | solution.py:250
  233.5 1.4 collective-permute-start.48
  236.0 1.8 collective-permute-done.52
  239.2 1.4 collective-permute-start.49
  244.5 1.4 collective-permute-start.50
  250.2 1.8 shard_map.215
  252.0 1.8 divide_subtract_fusion.4
  (313 shorter events, 72.5 us)
Async XLA Ops:
  0.7 57.6 %collective-permute-start = (f32[16,128,128]{2,1,0:T(8,128)}, f32[16,128,128]{2,1,0:T(8,128)S(1)}, u32[]{:S(2)}, u32[]{:S(2)}) collective-permute-start(f32[16,128,128]{2,1,0:T(8,128)} %target_a.1), channel_id=1, source_target_pairs={{0,2},{1,3},{2,0},{3,1},{4,6},{5,7},{6,4},{7,5},{8,10},{9,11},{10,... | collective-permute-start | bytes 3145736 | tf_op jit(solution)/shard_map/ppermute | solution.py:38
  1.2 33.8 %collective-permute-start.2 = (f32[32,16,64]{2,1,0:T(8,128)}, f32[32,16,64]{2,1,0:T(8,128)S(1)}, u32[]{:S(2)}, u32[]{:S(2)}) collective-permute-start(f32[32,16,64]{2,1,0:T(8,128)} %refs_0_.1), channel_id=1, source_target_pairs={{0,2},{1,3},{2,0},{3,1},{4,6},{5,7},{6,4},{7,5},{8,10},{9,11},{10,... | collective-permute-start | bytes 393224 | tf_op jit(solution)/shard_map/ppermute | solution.py:38
  1.3 49.6 %collective-permute-start.1 = (f32[32,16,128]{2,1,0:T(8,128)}, f32[32,16,128]{2,1,0:T(8,128)S(1)}, u32[]{:S(2)}, u32[]{:S(2)}) collective-permute-start(f32[32,16,128]{2,1,0:T(8,128)} %xy_a.1), channel_id=1, source_target_pairs={{0,2},{1,3},{2,0},{3,1},{4,6},{5,7},{6,4},{7,5},{8,10},{9,11},{10,... | collective-permute-start | bytes 786440 | tf_op jit(solution)/shard_map/ppermute | solution.py:38
  3.4 25.7 %collective-permute-start.5 = (f32[128,256]{1,0:T(8,128)}, f32[128,256]{1,0:T(8,128)}, u32[]{:S(2)}, u32[]{:S(2)}) collective-permute-start(f32[128,256]{1,0:T(8,128)} %shard_map.207.refs_0_), channel_id=1, source_target_pairs={{0,8},{1,9},{2,10},{3,11},{4,0},{5,1},{6,2},{7,3},{8,16},{9,17},{1... | collective-permute-start | bytes 393224 | tf_op jit(solution)/shard_map/ppermute | solution.py:38
  9.6 8.7 %collective-permute-start.16 = (f32[32,40]{0,1:T(8,128)S(1)}, f32[32,40]{0,1:T(8,128)S(1)}, u32[]{:S(2)}, u32[]{:S(2)}) collective-permute-start(f32[32,40]{0,1:T(8,128)S(1)} %maximum_select_fusion), channel_id=1, source_target_pairs={{0,1},{1,0},{2,3},{3,2},{4,5},{5,4},{6,7},{7,6},{8,9},{9,8},{10,11... | collective-permute-start | bytes 15368 | tf_op jit(solution)/shard_map/ppermute | solution.py:392
  18.3 5.5 %collective-permute-start.15 = (f32[32,320]{1,0:T(8,128)}, f32[32,320]{1,0:T(8,128)}, u32[]{:S(2)}, u32[]{:S(2)}) collective-permute-start(f32[32,320]{1,0:T(8,128)} %pad_maximum_fusion.3), channel_id=1, source_target_pairs={{0,2},{2,4},{4,6},{6,8},{8,10},{10,12},{12,14},{14,16},{16,18},{18... | collective-permute-start | bytes 122888 | tf_op jit(solution)/shard_map/ppermute | solution.py:387
  26.9 8.0 %collective-permute-start.6 = (f32[128,256]{1,0:T(8,128)}, f32[128,256]{1,0:T(8,128)S(1)}, u32[]{:S(2)}, u32[]{:S(2)}) collective-permute-start(f32[128,256]{1,0:T(8,128)} %shard_map.207.refs_0_), channel_id=1, source_target_pairs={{0,4},{1,5},{2,6},{3,7},{4,12},{5,13},{6,14},{7,15},{8,0},{9,1},{1... | collective-permute-start | bytes 393224 | tf_op jit(solution)/shard_map/ppermute | solution.py:38
  29.2 6.2 %collective-permute-start.7 = (f32[128,256]{1,0:T(8,128)}, f32[128,256]{1,0:T(8,128)S(1)}, u32[]{:S(2)}, u32[]{:S(2)}) collective-permute-start(f32[128,256]{1,0:T(8,128)} %collective-permute-done.5.refs_1_), channel_id=1, source_target_pairs={{0,8},{1,9},{2,10},{3,11},{4,0},{5,1},{6,2},{7,3},{8,16},{9,17},{1... | collective-permute-start | bytes 393224 | tf_op jit(solution)/shard_map/ppermute | solution.py:38
  34.9 5.3 %collective-permute-start.8 = (f32[128,256]{1,0:T(8,128)S(1)}, f32[128,256]{1,0:T(8,128)S(1)}, u32[]{:S(2)}, u32[]{:S(2)}) collective-permute-start(f32[128,256]{1,0:T(8,128)S(1)} %collective-permute-done.6.refs_2_), channel_id=1, source_target_pairs={{0,4},{1,5},{2,6},{3,7},{4,12},{5,13},{6,14},{7,15},{8,0},{9,1},{1... | collective-permute-start | bytes 393224 | tf_op jit(solution)/shard_map/ppermute | solution.py:38
  35.0 12.0 %collective-permute-start.3 = (f32[32,16,64]{2,1,0:T(8,128)S(1)}, f32[32,16,64]{2,1,0:T(8,128)S(1)}, u32[]{:S(2)}, u32[]{:S(2)}) collective-permute-start(f32[32,16,64]{2,1,0:T(8,128)S(1)} %copy-done.2), channel_id=1, source_target_pairs={{0,1},{1,0},{2,3},{3,2},{4,5},{5,4},{6,7},{7,6},{8,9},{9,8},{10,11... | collective-permute-start | bytes 393224 | tf_op jit(solution)/shard_map/ppermute | solution.py:38
  35.4 5.8 %collective-permute-start.9 = (f32[128,256]{1,0:T(8,128)S(1)}, f32[128,256]{1,0:T(8,128)S(1)}, u32[]{:S(2)}, u32[]{:S(2)}) collective-permute-start(f32[128,256]{1,0:T(8,128)S(1)} %collective-permute-done.7.refs_3_), channel_id=1, source_target_pairs={{0,8},{1,9},{2,10},{3,11},{4,0},{5,1},{6,2},{7,3},{8,16},{9,17},{1... | collective-permute-start | bytes 393224 | tf_op jit(solution)/shard_map/ppermute | solution.py:38
  41.2 8.9 %collective-permute-start.4 = (f32[32,16,64]{2,1,0:T(8,128)S(1)}, f32[32,16,64]{2,1,0:T(8,128)S(1)}, u32[]{:S(2)}, u32[]{:S(2)}) collective-permute-start(f32[32,16,64]{2,1,0:T(8,128)S(1)} %collective-permute-done.2.refs_1_), channel_id=1, source_target_pairs={{0,1},{1,0},{2,3},{3,2},{4,5},{5,4},{6,7},{7,6},{8,9},{9,8},{10,11... | collective-permute-start | bytes 393224 | tf_op jit(solution)/shard_map/ppermute | solution.py:38
  45.1 11.6 %collective-permute-start.11 = (f32[64,256]{1,0:T(8,128)}, f32[64,256]{1,0:T(8,128)}, u32[]{:S(2)}, u32[]{:S(2)}) collective-permute-start(f32[64,256]{1,0:T(8,128)} %slice.350), channel_id=1, source_target_pairs={{0,8},{1,9},{2,10},{3,11},{4,0},{5,1},{6,2},{7,3},{8,16},{9,17},{1... | collective-permute-start | bytes 196616 | tf_op jit(solution)/shard_map/ppermute | solution.py:38
  47.0 9.7 %collective-permute-start.12 = (f32[64,256]{1,0:T(8,128)}, f32[64,256]{1,0:T(8,128)S(1)}, u32[]{:S(2)}, u32[]{:S(2)}) collective-permute-start(f32[64,256]{1,0:T(8,128)} %slice.351), channel_id=1, source_target_pairs={{0,4},{1,5},{2,6},{3,7},{4,12},{5,13},{6,14},{7,15},{8,0},{9,1},{1... | collective-permute-start | bytes 196616 | tf_op jit(solution)/shard_map/ppermute | solution.py:38
  102.7 11.1 %collective-permute-start.28 = (f32[64,256]{1,0:T(8,128)S(1)}, f32[64,256]{1,0:T(8,128)S(1)}, u32[]{:S(2)}, u32[]{:S(2)}) collective-permute-start(f32[64,256]{1,0:T(8,128)S(1)} %get-tuple-element.238), channel_id=1, source_target_pairs={{0,4},{1,5},{2,6},{3,7},{4,12},{5,13},{6,14},{7,15},{8,0},{9,1},{1... | collective-permute-start | bytes 196616 | tf_op jit(solution)/shard_map/ppermute | solution.py:38
  109.3 9.2 %collective-permute-start.19 = (f32[32,16,64]{2,0,1:T(8,128)S(1)}, f32[32,16,64]{2,0,1:T(8,128)S(1)}, u32[]{:S(2)}, u32[]{:S(2)}) collective-permute-start(f32[32,16,64]{2,0,1:T(8,128)S(1)} %copy.821), channel_id=1, source_target_pairs={{0,1},{1,0},{2,3},{3,2},{4,5},{5,4},{6,7},{7,6},{8,9},{9,8},{10,11... | collective-permute-start | bytes 393224 | tf_op jit(solution)/shard_map/ppermute | solution.py:38
  111.9 11.5 %collective-permute-start.18 = (f32[32,16,64]{2,0,1:T(8,128)S(1)}, f32[32,16,64]{2,0,1:T(8,128)S(1)}, u32[]{:S(2)}, u32[]{:S(2)}) collective-permute-start(f32[32,16,64]{2,0,1:T(8,128)S(1)} %copy.819), channel_id=1, source_target_pairs={{0,1},{1,0},{2,3},{3,2},{4,5},{5,4},{6,7},{7,6},{8,9},{9,8},{10,11... | collective-permute-start | bytes 393224 | tf_op jit(solution)/shard_map/ppermute | solution.py:38
  113.8 6.6 %collective-permute-start.29 = (f32[128,256]{1,0:T(8,128)S(1)}, f32[128,256]{1,0:T(8,128)S(1)}, u32[]{:S(2)}, u32[]{:S(2)}) collective-permute-start(f32[128,256]{1,0:T(8,128)S(1)} %pad_add_fusion.2), channel_id=1, source_target_pairs={{0,4},{1,5},{2,6},{3,7},{4,12},{5,13},{6,14},{7,15},{8,0},{9,1},{1... | collective-permute-start | bytes 393224 | tf_op jit(solution)/shard_map/ppermute | solution.py:38
  116.8 5.3 %collective-permute-start.25 = (f32[128,256]{1,0:T(8,128)S(1)}, f32[128,256]{1,0:T(8,128)S(1)}, u32[]{:S(2)}, u32[]{:S(2)}) collective-permute-start(f32[128,256]{1,0:T(8,128)S(1)} %pad_add_fusion.3), channel_id=1, source_target_pairs={{0,8},{1,9},{2,10},{3,11},{4,0},{5,1},{6,2},{7,3},{8,16},{9,17},{1... | collective-permute-start | bytes 393224 | tf_op jit(solution)/shard_map/ppermute | solution.py:38
  119.9 6.9 %collective-permute-start.13 = (f32[32,16,128]{2,0,1:T(8,128)S(1)}, f32[32,16,128]{2,0,1:T(8,128)S(1)}, u32[]{:S(2)}, u32[]{:S(2)}) collective-permute-start(f32[32,16,128]{2,0,1:T(8,128)S(1)} %copy.796), channel_id=1, source_target_pairs={{0,2},{1,3},{2,0},{3,1},{4,6},{5,7},{6,4},{7,5},{8,10},{9,11},{10,... | collective-permute-start | bytes 786440 | tf_op jit(solution)/shard_map/ppermute | solution.py:38
  120.5 7.5 %collective-permute-start.30 = (f32[128,256]{1,0:T(8,128)S(1)}, f32[128,256]{1,0:T(8,128)S(1)}, u32[]{:S(2)}, u32[]{:S(2)}) collective-permute-start(f32[128,256]{1,0:T(8,128)S(1)} %add.176), channel_id=1, source_target_pairs={{0,4},{1,5},{2,6},{3,7},{4,12},{5,13},{6,14},{7,15},{8,0},{9,1},{1... | collective-permute-start | bytes 393224 | tf_op jit(solution)/shard_map/ppermute | solution.py:38
  122.1 7.2 %collective-permute-start.26 = (f32[128,256]{1,0:T(8,128)S(1)}, f32[128,256]{1,0:T(8,128)S(1)}, u32[]{:S(2)}, u32[]{:S(2)}) collective-permute-start(f32[128,256]{1,0:T(8,128)S(1)} %add.173), channel_id=1, source_target_pairs={{0,8},{1,9},{2,10},{3,11},{4,0},{5,1},{6,2},{7,3},{8,16},{9,17},{1... | collective-permute-start | bytes 393224 | tf_op jit(solution)/shard_map/ppermute | solution.py:38
  124.2 7.1 %collective-permute-start.21 = (f32[32,16,64]{2,0,1:T(8,128)S(1)}, f32[32,16,64]{2,0,1:T(8,128)}, u32[]{:S(2)}, u32[]{:S(2)}) collective-permute-start(f32[32,16,64]{2,0,1:T(8,128)S(1)} %get-tuple-element.214), channel_id=1, source_target_pairs={{0,2},{1,3},{2,0},{3,1},{4,6},{5,7},{6,4},{7,5},{8,10},{9,11},{10,... | collective-permute-start | bytes 393224 | tf_op jit(solution)/shard_map/ppermute | solution.py:38
  124.3 9.4 %collective-permute-start.22 = (f32[32,16,64]{2,0,1:T(8,128)S(1)}, f32[32,16,64]{2,0,1:T(8,128)S(1)}, u32[]{:S(2)}, u32[]{:S(2)}) collective-permute-start(f32[32,16,64]{2,0,1:T(8,128)S(1)} %get-tuple-element.214), channel_id=1, source_target_pairs={{0,1},{1,0},{2,3},{3,2},{4,5},{5,4},{6,7},{7,6},{8,9},{9,8},{10,11... | collective-permute-start | bytes 393224 | tf_op jit(solution)/shard_map/ppermute | solution.py:38
  128.0 6.6 %collective-permute-start.31 = (f32[128,256]{1,0:T(8,128)S(1)}, f32[128,256]{1,0:T(8,128)S(1)}, u32[]{:S(2)}, u32[]{:S(2)}) collective-permute-start(f32[128,256]{1,0:T(8,128)S(1)} %add.177), channel_id=1, source_target_pairs={{0,4},{1,5},{2,6},{3,7},{4,12},{5,13},{6,14},{7,15},{8,0},{9,1},{1... | collective-permute-start | bytes 393224 | tf_op jit(solution)/shard_map/ppermute | solution.py:38
  129.4 5.3 %collective-permute-start.27 = (f32[128,256]{1,0:T(8,128)S(1)}, f32[128,256]{1,0:T(8,128)S(1)}, u32[]{:S(2)}, u32[]{:S(2)}) collective-permute-start(f32[128,256]{1,0:T(8,128)S(1)} %add.174), channel_id=1, source_target_pairs={{0,8},{1,9},{2,10},{3,11},{4,0},{5,1},{6,2},{7,3},{8,16},{9,17},{1... | collective-permute-start | bytes 393224 | tf_op jit(solution)/shard_map/ppermute | solution.py:38
  130.2 43.1 %collective-permute-start.17 = (f32[32,16,128]{2,0,1:T(8,128)S(1)}, f32[32,16,128]{2,0,1:T(8,128)}, u32[]{:S(2)}, u32[]{:S(2)}) collective-permute-start(f32[32,16,128]{2,0,1:T(8,128)S(1)} %get-tuple-element.218), channel_id=1, source_target_pairs={{0,2},{1,3},{2,0},{3,1},{4,6},{5,7},{6,4},{7,5},{8,10},{9,11},{10,... | collective-permute-start | bytes 786440 | tf_op jit(solution)/shard_map/ppermute | solution.py:38
  131.4 40.1 %collective-permute-start.23 = (f32[32,16,64]{2,0,1:T(8,128)}, f32[32,16,64]{2,0,1:T(8,128)}, u32[]{:S(2)}, u32[]{:S(2)}) collective-permute-start(f32[32,16,64]{2,0,1:T(8,128)} %collective-permute-done.21), channel_id=1, source_target_pairs={{0,1},{1,0},{2,3},{3,2},{4,5},{5,4},{6,7},{7,6},{8,9},{9,8},{10,11... | collective-permute-start | bytes 393224 | tf_op jit(solution)/shard_map/ppermute | solution.py:38
  141.2 14.2 %collective-permute-start.32 = (f32[128,256]{1,0:T(8,128)}, f32[128,256]{1,0:T(8,128)S(1)}, u32[]{:S(2)}, u32[]{:S(2)}) collective-permute-start(f32[128,256]{1,0:T(8,128)} %shard_map.212.refs_0_), channel_id=1, source_target_pairs={{0,8},{1,9},{2,10},{3,11},{4,0},{5,1},{6,2},{7,3},{8,16},{9,17},{1... | collective-permute-start | bytes 393224 | tf_op jit(solution)/shard_map/ppermute | solution.py:38
  142.0 16.6 %collective-permute-start.33 = (f32[128,256]{1,0:T(8,128)}, f32[128,256]{1,0:T(8,128)}, u32[]{:S(2)}, u32[]{:S(2)}) collective-permute-start(f32[128,256]{1,0:T(8,128)} %shard_map.212.refs_0_), channel_id=1, source_target_pairs={{0,4},{1,5},{2,6},{3,7},{4,12},{5,13},{6,14},{7,15},{8,0},{9,1},{1... | collective-permute-start | bytes 393224 | tf_op jit(solution)/shard_map/ppermute | solution.py:38
  155.4 6.8 %collective-permute-start.34 = (f32[128,256]{1,0:T(8,128)S(1)}, f32[128,256]{1,0:T(8,128)S(1)}, u32[]{:S(2)}, u32[]{:S(2)}) collective-permute-start(f32[128,256]{1,0:T(8,128)S(1)} %collective-permute-done.32.refs_1_), channel_id=1, source_target_pairs={{0,8},{1,9},{2,10},{3,11},{4,0},{5,1},{6,2},{7,3},{8,16},{9,17},{1... | collective-permute-start | bytes 393224 | tf_op jit(solution)/shard_map/ppermute | solution.py:38
  158.6 6.6 %collective-permute-start.35 = (f32[128,256]{1,0:T(8,128)}, f32[128,256]{1,0:T(8,128)S(1)}, u32[]{:S(2)}, u32[]{:S(2)}) collective-permute-start(f32[128,256]{1,0:T(8,128)} %collective-permute-done.33.refs_2_), channel_id=1, source_target_pairs={{0,4},{1,5},{2,6},{3,7},{4,12},{5,13},{6,14},{7,15},{8,0},{9,1},{1... | collective-permute-start | bytes 393224 | tf_op jit(solution)/shard_map/ppermute | solution.py:38
  162.2 6.0 %collective-permute-start.36 = (f32[128,256]{1,0:T(8,128)S(1)}, f32[128,256]{1,0:T(8,128)S(1)}, u32[]{:S(2)}, u32[]{:S(2)}) collective-permute-start(f32[128,256]{1,0:T(8,128)S(1)} %collective-permute-done.34.refs_3_), channel_id=1, source_target_pairs={{0,8},{1,9},{2,10},{3,11},{4,0},{5,1},{6,2},{7,3},{8,16},{9,17},{1... | collective-permute-start | bytes 393224 | tf_op jit(solution)/shard_map/ppermute | solution.py:38
  165.2 5.5 %collective-permute-start.37 = (f32[128,256]{1,0:T(8,128)S(1)}, f32[128,256]{1,0:T(8,128)S(1)}, u32[]{:S(2)}, u32[]{:S(2)}) collective-permute-start(f32[128,256]{1,0:T(8,128)S(1)} %collective-permute-done.35.refs_4_), channel_id=1, source_target_pairs={{0,4},{1,5},{2,6},{3,7},{4,12},{5,13},{6,14},{7,15},{8,0},{9,1},{1... | collective-permute-start | bytes 393224 | tf_op jit(solution)/shard_map/ppermute | solution.py:38
  168.3 11.9 %collective-permute-start.38 = (f32[64,256]{1,0:T(8,128)S(1)}, f32[64,256]{1,0:T(8,128)S(1)}, u32[]{:S(2)}, u32[]{:S(2)}) collective-permute-start(f32[64,256]{1,0:T(8,128)S(1)} %slice.377), channel_id=1, source_target_pairs={{0,8},{1,9},{2,10},{3,11},{4,0},{5,1},{6,2},{7,3},{8,16},{9,17},{1... | collective-permute-start | bytes 196616 | tf_op jit(solution)/shard_map/ppermute | solution.py:38
  170.7 9.5 %collective-permute-start.39 = (f32[64,256]{1,0:T(8,128)S(1)}, f32[64,256]{1,0:T(8,128)S(1)}, u32[]{:S(2)}, u32[]{:S(2)}) collective-permute-start(f32[64,256]{1,0:T(8,128)S(1)} %slice.378), channel_id=1, source_target_pairs={{0,4},{1,5},{2,6},{3,7},{4,12},{5,13},{6,14},{7,15},{8,0},{9,1},{1... | collective-permute-start | bytes 196616 | tf_op jit(solution)/shard_map/ppermute | solution.py:38
  218.4 12.5 %collective-permute-start.51 = (f32[64,256]{1,0:T(8,128)}, f32[64,256]{1,0:T(8,128)S(1)}, u32[]{:S(2)}, u32[]{:S(2)}) collective-permute-start(f32[64,256]{1,0:T(8,128)} %get-tuple-element.232), channel_id=1, source_target_pairs={{0,4},{1,5},{2,6},{3,7},{4,12},{5,13},{6,14},{7,15},{8,0},{9,1},{1... | collective-permute-start | bytes 196616 | tf_op jit(solution)/shard_map/ppermute | solution.py:38
  219.2 13.3 %collective-permute-start.47 = (f32[64,256]{1,0:T(8,128)}, f32[64,256]{1,0:T(8,128)}, u32[]{:S(2)}, u32[]{:S(2)}) collective-permute-start(f32[64,256]{1,0:T(8,128)} %get-tuple-element.233), channel_id=1, source_target_pairs={{0,8},{1,9},{2,10},{3,11},{4,0},{5,1},{6,2},{7,3},{8,16},{9,17},{1... | collective-permute-start | bytes 196616 | tf_op jit(solution)/shard_map/ppermute | solution.py:38
  226.6 9.2 %collective-permute-start.45 = (f32[32,16,64]{2,0,1:T(8,128)S(1)}, f32[32,16,64]{2,0,1:T(8,128)S(1)}, u32[]{:S(2)}, u32[]{:S(2)}) collective-permute-start(f32[32,16,64]{2,0,1:T(8,128)S(1)} %copy.849), channel_id=1, source_target_pairs={{0,1},{1,0},{2,3},{3,2},{4,5},{5,4},{6,7},{7,6},{8,9},{9,8},{10,11... | collective-permute-start | bytes 393224 | tf_op jit(solution)/shard_map/ppermute | solution.py:38
  228.6 17.3 %collective-permute-start.44 = (f32[32,16,64]{2,0,1:T(8,128)S(1)}, f32[32,16,64]{2,0,1:T(8,128)S(1)}, u32[]{:S(2)}, u32[]{:S(2)}) collective-permute-start(f32[32,16,64]{2,0,1:T(8,128)S(1)} %copy.847), channel_id=1, source_target_pairs={{0,1},{1,0},{2,3},{3,2},{4,5},{5,4},{6,7},{7,6},{8,9},{9,8},{10,11... | collective-permute-start | bytes 393224 | tf_op jit(solution)/shard_map/ppermute | solution.py:38
  230.8 9.8 %collective-permute-start.40 = (f32[32,16,128]{2,0,1:T(8,128)S(1)}, f32[32,16,128]{2,0,1:T(8,128)S(1)}, u32[]{:S(2)}, u32[]{:S(2)}) collective-permute-start(f32[32,16,128]{2,0,1:T(8,128)S(1)} %copy.839), channel_id=1, source_target_pairs={{0,2},{1,3},{2,0},{3,1},{4,6},{5,7},{6,4},{7,5},{8,10},{9,11},{10,... | collective-permute-start | bytes 786440 | tf_op jit(solution)/shard_map/ppermute | solution.py:38
  231.8 5.9 %collective-permute-start.52 = (f32[128,256]{1,0:T(8,128)S(1)}, f32[128,256]{1,0:T(8,128)S(1)}, u32[]{:S(2)}, u32[]{:S(2)}) collective-permute-start(f32[128,256]{1,0:T(8,128)S(1)} %pad_add_fusion), channel_id=1, source_target_pairs={{0,4},{1,5},{2,6},{3,7},{4,12},{5,13},{6,14},{7,15},{8,0},{9,1},{1... | collective-permute-start | bytes 393224 | tf_op jit(solution)/shard_map/ppermute | solution.py:38
  233.5 5.7 %collective-permute-start.48 = (f32[128,256]{1,0:T(8,128)S(1)}, f32[128,256]{1,0:T(8,128)S(1)}, u32[]{:S(2)}, u32[]{:S(2)}) collective-permute-start(f32[128,256]{1,0:T(8,128)S(1)} %pad_add_fusion.1), channel_id=1, source_target_pairs={{0,8},{1,9},{2,10},{3,11},{4,0},{5,1},{6,2},{7,3},{8,16},{9,17},{1... | collective-permute-start | bytes 393224 | tf_op jit(solution)/shard_map/ppermute | solution.py:38
  235.9 10.0 %collective-permute-start.46 = (f32[32,16,64]{2,0,1:T(8,128)S(1)}, f32[32,16,64]{2,0,1:T(8,128)S(1)}, u32[]{:S(2)}, u32[]{:S(2)}) collective-permute-start(f32[32,16,64]{2,0,1:T(8,128)S(1)} %copy_add_fusion), channel_id=1, source_target_pairs={{0,2},{1,3},{2,0},{3,1},{4,6},{5,7},{6,4},{7,5},{8,10},{9,11},{10,... | collective-permute-start | bytes 393224 | tf_op jit(solution)/shard_map/ppermute | solution.py:38
  237.8 6.0 %collective-permute-start.53 = (f32[128,256]{1,0:T(8,128)S(1)}, f32[128,256]{1,0:T(8,128)S(1)}, u32[]{:S(2)}, u32[]{:S(2)}) collective-permute-start(f32[128,256]{1,0:T(8,128)S(1)} %add.201), channel_id=1, source_target_pairs={{0,4},{1,5},{2,6},{3,7},{4,12},{5,13},{6,14},{7,15},{8,0},{9,1},{1... | collective-permute-start | bytes 393224 | tf_op jit(solution)/shard_map/ppermute | solution.py:38
  239.2 5.3 %collective-permute-start.49 = (f32[128,256]{1,0:T(8,128)S(1)}, f32[128,256]{1,0:T(8,128)S(1)}, u32[]{:S(2)}, u32[]{:S(2)}) collective-permute-start(f32[128,256]{1,0:T(8,128)S(1)} %add.198), channel_id=1, source_target_pairs={{0,8},{1,9},{2,10},{3,11},{4,0},{5,1},{6,2},{7,3},{8,16},{9,17},{1... | collective-permute-start | bytes 393224 | tf_op jit(solution)/shard_map/ppermute | solution.py:38
  243.8 5.3 %collective-permute-start.54 = (f32[128,256]{1,0:T(8,128)S(1)}, f32[128,256]{1,0:T(8,128)S(1)}, u32[]{:S(2)}, u32[]{:S(2)}) collective-permute-start(f32[128,256]{1,0:T(8,128)S(1)} %add.202), channel_id=1, source_target_pairs={{0,4},{1,5},{2,6},{3,7},{4,12},{5,13},{6,14},{7,15},{8,0},{9,1},{1... | collective-permute-start | bytes 393224 | tf_op jit(solution)/shard_map/ppermute | solution.py:38
  244.5 5.0 %collective-permute-start.50 = (f32[128,256]{1,0:T(8,128)S(1)}, f32[128,256]{1,0:T(8,128)S(1)}, u32[]{:S(2)}, u32[]{:S(2)}) collective-permute-start(f32[128,256]{1,0:T(8,128)S(1)} %add.199), channel_id=1, source_target_pairs={{0,8},{1,9},{2,10},{3,11},{4,0},{5,1},{6,2},{7,3},{8,16},{9,17},{1... | collective-permute-start | bytes 393224 | tf_op jit(solution)/shard_map/ppermute | solution.py:38
  (71 other events, 669.3 us)

commit v3 on v2

v3 whole, which is shorter than its diff:
```python
import functools
import jax
import jax.numpy as jnp
from jax import lax
from jax.experimental import pallas as pl
from jax.experimental.pallas import tpu as pltpu
from jax.sharding import PartitionSpec as P


STEPS = 2
START = 20


SMOOTHING = 0.5
BETA_ONE = 0.9
BETA_TWO = 0.99
LEARN_RATE = 0.01
EPSILON = 1e-08

LANES = 128
CHANNELS = 32
BOTH = ("gx", "gy")
f32 = jnp.float32
bf16 = jnp.bfloat16


def ring_order(chips):
    return list(range(0, chips, 2)) + list(range(chips - 1, 0, -2))


def send(x, move):
    n, peers = lax.axis_size("gx"), lax.axis_size("gy")
    pairs = []
    for g in range(n):
        for y in range(peers):
            to = move(g // 2, g % 2, y)
            if to is not None:
                pairs.append((g * peers + y, (to[0] * 2 + to[1]) * peers + to[2]))
    return lax.ppermute(x, BOTH, pairs)


def to_core(x):
    return send(x, lambda k, c, y: (k, 1 - c, y))


def to_ring(x, step):
    chips = lax.axis_size("gx") // 2
    order = ring_order(chips)
    at = {k: i for i, k in enumerate(order)}
    return send(x, lambda k, c, y: (order[(at[k] + step) % chips], c, y))


def to_gy(x, step):
    peers = lax.axis_size("gy")
    return send(x, lambda k, c, y: (k, c, (y + step) % peers))


def offsets(chips):
    out = [0]
    for d in range(1, chips // 2):
        out += [-d, d]
    return out + [chips // 2]


def chip_in_slot(gx, slot, chips):
    k = gx // 2
    at = jnp.where(k % 2 == 0, k // 2, chips - 1 - k // 2)
    i = (at + offsets(chips)[slot] + chips) % chips
    return jnp.where(i < chips // 2, 2 * i, 2 * chips - 1 - 2 * i)


def vmem(count):
    return [pl.BlockSpec(memory_space=pltpu.VMEM)] * count


SCALARS = pl.BlockSpec(memory_space=pltpu.SMEM)
SMALL = pltpu.CompilerParams(vmem_limit_bytes=20 * 2**20)


def cost(flops, size):
    return pl.CostEstimate(flops=flops, bytes_accessed=size, transcendentals=0)


def diagonal(small, times):
    size = small.shape[0] * times
    wide = jnp.concatenate([small.astype(f32)] * times, axis=1)
    full = jnp.concatenate([wide] * times, axis=0)
    row = lax.broadcasted_iota(jnp.int32, (size, size), 0) // small.shape[0]
    col = lax.broadcasted_iota(jnp.int32, (size, size), 1) // small.shape[0]
    return jnp.where(row == col, full, 0.0)


def fixed_kernel(
    chips, zl, info, b_output, target_a, target_b, w, w_t, w_o, b, o, wanted, w_in, w_out, w_back, bias, scale
):
    gx = info[0]
    x_count = target_a.shape[0]
    starts = [
        pl.multiple_of((2 * chip_in_slot(gx, s, chips) + gx % 2) * zl, zl) for s in range(chips)
    ]
    for side, ref in enumerate((target_a, target_b)):

        def one(x, carry):
            rows = jnp.concatenate([ref[x, pl.ds(z, zl), :] for z in starts], axis=0)
            rows = rows - b_output[0]
            high = rows.astype(bf16).astype(f32)
            both = jnp.concatenate([high, rows - high], axis=0)
            wanted[side * x_count + x] = both.T.astype(bf16)
            return carry

        lax.fori_loop(0, x_count, one, 0)
    times = w_in.shape[0] // w.shape[0]
    w_in[...] = diagonal(0.5 * w[...].astype(f32), times).astype(bf16)
    w_out[...] = diagonal(w_o[...], times).astype(bf16)
    w_back[...] = diagonal(w_t[...], times).astype(bf16)
    bias[...] = jnp.concatenate([0.5 * b[...]] * times, axis=1)
    scale[...] = jnp.concatenate([0.5 * o[...]] * times, axis=1)


def fixed_parts(info, target, target_b, zl, w_hidden, b_hidden, w_output, b_output):
    chips = lax.axis_size("gx") // 2
    x_count, z_count, y_count = target.shape
    hidden = w_hidden.shape[1]
    width = zl * hidden
    square = jax.ShapeDtypeStruct((width, width), bf16)
    line = jax.ShapeDtypeStruct((1, width), f32)
    return pl.pallas_call(
        functools.partial(fixed_kernel, chips, zl),
        in_specs=[SCALARS, SCALARS] + vmem(7),
        out_specs=vmem(6),
        out_shape=[
            jax.ShapeDtypeStruct((2 * x_count, y_count, z_count), bf16),
            square,
            square,
            square,
            line,
            line,
        ],
        compiler_params=SMALL,
        cost_estimate=cost(0, 4 * 2**20),
    )(
        info,
        b_output,
        target,
        target_b,
        w_hidden,
        w_hidden.T,
        jnp.broadcast_to(w_output[:, None], (hidden, hidden)),
        b_hidden[None],
        w_output.astype(f32)[None],
    )


def lanes_kernel(plane, out):
    c, zl, _ = plane.shape
    per = LANES // c
    for t in range(zl // per):
        rows = jnp.concatenate([plane[:, t * per + j, :] for j in range(per)], axis=0)
        out[:, t * LANES : (t + 1) * LANES] = rows.T


def lanes_yz(plane):
    c, zl, y = plane.shape
    return pl.pallas_call(
        lanes_kernel,
        in_specs=vmem(1),
        out_specs=vmem(1)[0],
        out_shape=jax.ShapeDtypeStruct((y, zl * c), f32),
        compiler_params=SMALL,
        cost_estimate=cost(0, 2**18),
    )(plane)


def z_places(gx, gy, slot, chips, peers, zl, zs):
    z = (2 * chip_in_slot(gx, slot, chips) + gx % 2) * zl
    return (gy - z // zs + peers) % peers * zs + z % zs


def spread_kernel(chips, peers, zl, info, xy_a, xy_b, *refs):
    xzs, (xy, xz, held) = refs[: 2 * peers], refs[2 * peers :]
    c, x_count, _ = xy_a.shape
    zs = xzs[0].shape[2]
    for side, ref in enumerate((xy_a, xy_b)):
        for x in range(x_count):
            xy[side * x_count + x] = jnp.concatenate([ref[:, x, :]] * (LANES // c), axis=0).T
    for s in range(peers):
        for side in range(2):
            for x in range(x_count):
                held[s * zs : (s + 1) * zs, side * x_count + x, :] = xzs[2 * s + side][:, x, :].T
    for p in range(chips):
        at = z_places(info[0], info[1], p, chips, peers, zl, zs)
        xz[p] = jnp.concatenate([held[at + j] for j in range(zl)], axis=1)


def spread(info, xy_a, xy_b, xzs, zl):
    peers, chips = lax.axis_size("gy"), lax.axis_size("gx") // 2
    c, x_count, y_count = xy_a.shape
    return pl.pallas_call(
        functools.partial(spread_kernel, chips, peers, zl),
        in_specs=[SCALARS] + vmem(2 + len(xzs)),
        out_specs=vmem(2),
        out_shape=[
            jax.ShapeDtypeStruct((2 * x_count, y_count, LANES), f32),
            jax.ShapeDtypeStruct((chips, 2 * x_count, zl * c), f32),
        ],
        scratch_shapes=[pltpu.VMEM((peers * xzs[0].shape[2], 2 * x_count, c), f32)],
        compiler_params=SMALL,
        cost_estimate=cost(0, 4 * 2**20),
    )(info, xy_a, xy_b, *xzs)


def collect_kernel(chips, peers, zl, info, part_xy, xy_a, xy_b, *refs):
    parts, outs, held = refs[:chips], refs[chips : chips + 2 + 2 * peers], refs[chips + 2 + 2 * peers]
    c, x_count, _ = xy_a.shape
    outs_xz = outs[2:]
    zs = outs_xz[0].shape[2]
    for side, ref in enumerate((xy_a, xy_b)):
        for x in range(x_count):
            rows = part_xy[side * x_count + x].T
            total = sum(rows[j * c : (j + 1) * c] for j in range(LANES // c))
            outs[side][:, x, :] = total / ref[:, x, :]
    held[...] = jnp.zeros_like(held)
    for p in range(chips):
        at = z_places(info[0], info[1], p, chips, peers, zl, zs)
        rows = parts[p][...]
        for j in range(zl):
            held[at + j] = rows[:, j * c : (j + 1) * c]
    for s in range(peers):
        for side in range(2):
            for x in range(x_count):
                outs_xz[2 * s + side][:, x, :] = held[s * zs : (s + 1) * zs, side * x_count + x, :].T


def collect(info, part_xy, xy_a, xy_b, parts_xz, shape_xz, zl):
    peers, chips = lax.axis_size("gy"), lax.axis_size("gx") // 2
    c, x_count, _ = xy_a.shape
    outs = pl.pallas_call(
        functools.partial(collect_kernel, chips, peers, zl),
        in_specs=[SCALARS] + vmem(3 + chips),
        out_specs=vmem(2 + 2 * peers),
        out_shape=[jax.ShapeDtypeStruct(xy_a.shape, f32)] * 2
        + [jax.ShapeDtypeStruct(shape_xz, f32)] * (2 * peers),
        scratch_shapes=[pltpu.VMEM((peers * shape_xz[2], 2 * x_count, c), f32)],
        compiler_params=SMALL,
        cost_estimate=cost(0, 8 * 2**20),
    )(info, part_xy, xy_a, xy_b, *parts_xz)
    return outs[0], outs[1], outs[2:]


def grads_kernel(slots, first, w_in, w_out, w_back, bias, scale, wanted, xy, *refs):
    count = len(slots)
    refs = list(refs)
    take = lambda k: [refs.pop(0) for _ in range(k)]
    xzs, yzs = take(count), take(count)
    before = None if first else take(1)[0]
    gxy = take(1)[0]
    gxzs, gyzs, picks = take(count), take(count), take(count)
    step = pl.program_id(0)
    x_count, y_count, _ = xy.shape
    width = w_in.shape[0]
    z_count = wanted.shape[2] // 2
    zl = width // CHANNELS
    times = width // LANES

    @pl.when(step == 0)
    def _():
        row = lax.broadcasted_iota(jnp.int32, (2 * z_count, width), 0) % z_count
        col = lax.broadcasted_iota(jnp.int32, (2 * z_count, width), 1) // CHANNELS
        for s, pick, gyz in zip(slots, picks, gyzs):
            pick[:width] = w_out[...]
            pick[width:] = jnp.where(row == s * zl + col, -1.0, 0.0).astype(bf16)
            gyz[...] = jnp.zeros_like(gyz)

    for j in range(count):
        yz = yzs[j][...]
        lines = [xzs[j][0, x : x + 1, :] for x in range(x_count)]
        pairs = [jnp.concatenate([xy[x]] * times, axis=1) * yz for x in range(x_count)]
        features = jnp.concatenate([(g * r).astype(bf16) for g, r in zip(pairs, lines)], axis=0)
        half = jnp.dot(features, w_in[...], preferred_element_type=f32) + bias[...]
        t = jnp.tanh(half)
        up = 1.0 + t
        hidden = half * up
        slope = (up + hidden * (1.0 - t)) * scale[...]
        residual = jnp.dot(
            jnp.concatenate(
                [
                    hidden.astype(bf16),
                    jnp.concatenate([wanted[x] for x in range(x_count)], axis=0),
                ],
                axis=1,
            ),
            picks[j][...],
            preferred_element_type=f32,
        )
        back_hidden = (residual * slope).astype(bf16)
        back = jnp.dot(back_hidden, w_back[...], preferred_element_type=f32)
        total = None
        for x in range(x_count):
            b = back[x * y_count : (x + 1) * y_count] * pairs[x]
            gxzs[j][x : x + 1, :] = jnp.sum(b, axis=0, keepdims=True)
            e = b * lines[x]
            folded = sum(e[:, h * LANES : (h + 1) * LANES] for h in range(times))
            if j > 0:
                gxy[x] += folded
            elif first:
                gxy[x] = folded
            else:
                gxy[x] = before[x] + folded
            total = e if total is None else total + e
        gyzs[j][...] += total

    @pl.when(step == 1)
    def _():
        for gyz, ref in zip(gyzs, yzs):
            gyz[...] = gyz[...] / ref[...]


def block_grads(slots, weights, wanted, xy, xz, yzs, before):
    count = len(slots)
    rows, y_count, _ = xy.shape
    rows = rows // 2
    width = yzs[0].shape[1]

    def whole(a):
        return pl.BlockSpec(a.shape, lambda i: (0,) * a.ndim)

    side = pl.BlockSpec((rows, y_count, LANES), lambda i: (i, 0, 0))
    line = pl.BlockSpec((rows, width), lambda i: (i, 0))
    outs = pl.pallas_call(
        functools.partial(grads_kernel, slots, before is None),
        grid=(2,),
        in_specs=[whole(w) for w in weights]
        + [side, side]
        + [pl.BlockSpec((1, rows, width), lambda i, s=s: (s, i, 0)) for s in slots]
        + [whole(a) for a in yzs]
        + ([] if before is None else [side]),
        out_specs=[side] + [line] * count + [whole(a) for a in yzs],
        out_shape=[jax.ShapeDtypeStruct(xy.shape, f32)]
        + [jax.ShapeDtypeStruct((2 * rows, width), f32)] * count
        + [jax.ShapeDtypeStruct(a.shape, f32) for a in yzs],
        scratch_shapes=[pltpu.VMEM((width + wanted.shape[2], width), bf16)] * count,
        compiler_params=pltpu.CompilerParams(vmem_limit_bytes=44 * 2**20),
        cost_estimate=cost(12 * rows * y_count * count * width * width, count * 10 * 2**20),
    )(*weights, wanted, xy, *([xz] * count), *yzs, *([] if before is None else [before]))
    return outs[0], outs[1 : 1 + count], outs[1 + count :]


def near_sides(p, above, below, left, right):
    rows, cols = p.shape[1:]
    row = lax.broadcasted_iota(jnp.int32, p.shape, 1)
    col = lax.broadcasted_iota(jnp.int32, p.shape, 2)
    up = jnp.where(row == 0, above, pltpu.roll(p, 1, 1))
    down = jnp.where(row == rows - 1, below, pltpu.roll(p, rows - 1, 1))
    wide = p if cols % LANES == 0 else jnp.concatenate([p] * (LANES // cols), axis=2)
    back = pltpu.roll(wide, 1, 2)[:, :, :cols]
    ahead = pltpu.roll(wide, wide.shape[2] - 1, 2)[:, :, :cols]
    return up, down, jnp.where(col == 0, left, back), jnp.where(col == cols - 1, right, ahead)


def update(info, ends, count, plane, first, second, grad, borders, at_row, at_col, outs):
    above, below, left, right = borders
    p = plane[...]
    rows, cols = p.shape[1:]
    above = jnp.where(info[0] == 0, p[:, :1, :], above[:, :, at_row : at_row + cols])
    below = jnp.where(info[0] == ends[0], p[:, rows - 1 :, :], below[:, :, at_row : at_row + cols])
    left = jnp.where(info[1] == 0, p[:, :, :1], left[:, at_col : at_col + rows][:, :, None])
    right = jnp.where(info[1] == ends[1], p[:, :, cols - 1 :], right[:, at_col : at_col + rows][:, :, None])
    up, down, back, ahead = near_sides(p, above, below, left, right)
    grad = grad + 2.0 * SMOOTHING * ((p - up) + (p - down) + (p - back) + (p - ahead))
    m = BETA_ONE * first[...] + (1.0 - BETA_ONE) * grad
    v = BETA_TWO * second[...] + (1.0 - BETA_TWO) * grad * grad
    corr_one = 1.0 - BETA_ONE**count
    corr_two = 1.0 - BETA_TWO**count
    outs[1][...] = m
    outs[2][...] = v
    outs[0][...] = p - LEARN_RATE * (m / corr_one) / (jnp.sqrt(v / corr_two) + EPSILON)


def update_two_kernel(ends, count, info, above, below, left, right, *refs):
    borders = (above, below, left, right)
    xy, xz, outs = refs[:5], refs[5:10], refs[10:]
    width_y = xy[0].shape[2]
    rows = xy[0].shape[1]
    update(info, ends, count, *xy[:3], xy[3][...] + xy[4][...], borders, 0, 0, outs[:3])
    update(info, ends, count, *xz[:3], xz[3][...] + xz[4][...], borders, 2 * width_y, rows, outs[3:])


def update_two(info, count, borders, xy, xz):
    ends = (lax.axis_size("gx") - 1, lax.axis_size("gy") - 1)
    shapes = [jax.ShapeDtypeStruct(a.shape, f32) for a in (*xy[:3], *xz[:3])]
    outs = pl.pallas_call(
        functools.partial(update_two_kernel, ends, count),
        in_specs=[SCALARS] + vmem(14),
        out_specs=vmem(6),
        out_shape=shapes,
        compiler_params=SMALL,
        cost_estimate=cost(0, 4 * 2**20),
    )(info, *borders, *xy, *xz)
    return outs[:3], outs[3:]


def update_yz_kernel(ends, count, info, above, below, left, right, plane, first, second, a, b, d, *refs):
    outs, lanes, held = refs[:3], refs[3], refs[4]
    c, zl, width = plane.shape
    per = LANES // c
    for t in range(zl // per):
        at = slice(t * LANES, (t + 1) * LANES)
        rows = (a[:, at] + b[:, at] + d[:, at]).T
        for j in range(per):
            held[:, t * per + j, :] = rows[j * c : (j + 1) * c]
    borders = (above, below, left, right)
    at_col = left.shape[1] - zl
    update(info, ends, count, plane, first, second, held[...], borders, width, at_col, outs)
    lanes_kernel(outs[0], lanes)


def update_yz(info, count, borders, state, parts):
    ends = (lax.axis_size("gx") - 1, lax.axis_size("gy") - 1)
    outs = pl.pallas_call(
        functools.partial(update_yz_kernel, ends, count),
        in_specs=[SCALARS] + vmem(10),
        out_specs=vmem(4),
        out_shape=[jax.ShapeDtypeStruct(a.shape, f32) for a in (*state, parts[0])],
        scratch_shapes=[pltpu.VMEM(state[0].shape, f32)],
        compiler_params=SMALL,
        cost_estimate=cost(0, 2 * 2**20),
    )(info, *borders, *state, *parts)
    return outs[:3], outs[3]


def borders(planes):
    n, peers = lax.axis_size("gx"), lax.axis_size("gy")
    xy, xz, yz = planes
    up = [(i, i + 1) for i in range(n - 1)]
    last = jnp.concatenate([p[:, -1:, :] for p in (xy, yz, xz)], axis=2)
    first = jnp.concatenate([p[:, :1, :] for p in (xy, yz, xz)], axis=2)
    above = lax.ppermute(last, "gx", up)
    below = lax.ppermute(first, "gx", [(j, i) for i, j in up])
    last = jnp.concatenate([p[:, :, -1] for p in (xy, xz, yz)], axis=1)
    first = jnp.concatenate([p[:, :, 0] for p in (xy, xz, yz)], axis=1)
    if peers == 2:
        left = right = lax.ppermute(
            jnp.where(lax.axis_index("gy") == 0, last, first), "gy", [(0, 1), (1, 0)]
        )
    else:
        up = [(i, i + 1) for i in range(peers - 1)]
        left = lax.ppermute(last, "gy", up)
        right = lax.ppermute(first, "gy", [(j, i) for i, j in up])
    return above, below, left, right


def per_device(
    target,
    plane_xy,
    plane_xz,
    plane_yz,
    first_xy,
    first_xz,
    first_yz,
    second_xy,
    second_xz,
    second_yz,
    w_hidden,
    b_hidden,
    w_output,
    b_output,
):
    peers = lax.axis_size("gy")
    info = jnp.stack([lax.axis_index("gx"), lax.axis_index("gy")]).astype(jnp.int32)
    zl = plane_yz.shape[1]
    lanes = lanes_yz(plane_yz)
    target_b = to_core(target)
    fixed = None

    chips = lax.axis_size("gx") // 2
    half = chips // 2
    slot = {o: i for i, o in enumerate(offsets(chips))}
    middle = lanes.shape[0] // 2

    for iteration in range(STEPS):
        back, ahead = {0: lanes}, {0: lanes}
        for d in range(1, half):
            back[d], ahead[d] = to_ring(back[d - 1], 1), to_ring(ahead[d - 1], -1)
        parts = to_ring(back[half - 1][:middle], 1), to_ring(ahead[half - 1][middle:], -1)
        far = jnp.concatenate(parts, axis=0)
        yzs = {0: lanes, half: far}
        for d in range(1, half):
            yzs[-d], yzs[d] = back[d], ahead[d]
        xy_b, xz_b = to_core(plane_xy), to_core(plane_xz)
        xzs = [plane_xz, xz_b]
        for s in range(1, peers):
            xzs += [to_gy(plane_xz, s), to_gy(xz_b, s)]
        if fixed is None:
            fixed = fixed_parts(
                info, target, target_b, zl, w_hidden, b_hidden, w_output, b_output
            )
        wanted, weights = fixed[0], fixed[1:]
        xy, xz = spread(info, plane_xy, xy_b, xzs, zl)

        order = [(0,), (-1,), (1,), (half,)] + [(-d, d) for d in range(half - 1, 1, -1)]
        part_xy, parts_xz, parts_yz = None, {}, {}
        send_ahead, send_back = None, None
        for group in order:
            part_xy, lines, blocks = block_grads(
                [slot[o] for o in group], weights, wanted, xy, xz, [yzs[o] for o in group], part_xy
            )
            for o, line, block in zip(group, lines, blocks):
                parts_xz[slot[o]], parts_yz[o] = line, block
            if group == (0,):
                gated = lax.optimization_barrier((plane_xy, plane_xz, plane_yz, lines[0]))[:3]
                around = borders(gated)
        block = parts_yz[half]
        send_ahead, send_back = to_ring(block[:middle], 1), to_ring(block[middle:], -1)
        for d in range(half - 1, 0, -1):
            if d == half - 1:
                send_ahead = jnp.pad(send_ahead, ((0, middle), (0, 0)))
                send_back = jnp.pad(send_back, ((middle, 0), (0, 0)))
            send_ahead, send_back = parts_yz[d] + send_ahead, parts_yz[-d] + send_back
            send_ahead, send_back = to_ring(send_ahead, 1), to_ring(send_back, -1)

        grad_xy, far_xy, pieces = collect(
            info, part_xy, plane_xy, xy_b, [parts_xz[i] for i in range(chips)], plane_xz.shape, zl
        )
        grad_xz, far_xz = pieces[:2]
        for s in range(1, peers):
            grad_xz = grad_xz + to_gy(pieces[2 * s], -s)
            far_xz = far_xz + to_gy(pieces[2 * s + 1], -s)
        count = START + iteration + 1
        (plane_xy, first_xy, second_xy), (plane_xz, first_xz, second_xz) = update_two(
            info,
            count,
            around,
            (plane_xy, first_xy, second_xy, grad_xy, to_core(far_xy)),
            (plane_xz, first_xz, second_xz, grad_xz, to_core(far_xz)),
        )
        (plane_yz, first_yz, second_yz), lanes = update_yz(
            info, count, around, (plane_yz, first_yz, second_yz), (parts_yz[0], send_ahead, send_back)
        )
    return (
        plane_xy,
        plane_xz,
        plane_yz,
        first_xy,
        first_xz,
        first_yz,
        second_xy,
        second_xz,
        second_yz,
    )


def solution(mesh):
    return jax.shard_map(
        per_device,
        mesh=mesh,
        in_specs=(
            P("gx", None, "gy"),
            P(None, "gx", "gy"),
            P(None, "gx", "gy"),
            P(None, "gx", "gy"),
            P(None, "gx", "gy"),
            P(None, "gx", "gy"),
            P(None, "gx", "gy"),
            P(None, "gx", "gy"),
            P(None, "gx", "gy"),
            P(None, "gx", "gy"),
            P(),
            P(),
            P(),
            P(),
        ),
        out_specs=(
            P(None, "gx", "gy"),
            P(None, "gx", "gy"),
            P(None, "gx", "gy"),
            P(None, "gx", "gy"),
            P(None, "gx", "gy"),
            P(None, "gx", "gy"),
            P(None, "gx", "gy"),
            P(None, "gx", "gy"),
            P(None, "gx", "gy"),
        ),
        check_vma=False,
    )
```

time: 255 us -> 238 us (0.933)
  the two profiles are of different devices: /device:TPU:0 before, /device:TPU:24 now
where the time goes in v3:
time: 238 us; the launch traced here: 234 us
  Pallas kernels  83.6 us (35%)
  starting transfers between devices  52.3 us (22%)
  local copies, waits for them, and re-layouts  49.1 us (21%)
  waiting for transfers between devices  43 us (18%)
  between operations  2.89 us (1%)
  other arithmetic  2.67 us (1%)
    pallas_call x12, Pallas kernels, block_grads(): pl.pallas_call(functools.partial(grads_kernel, slots, before is None), gr...  58.4 us
    ppermute x49, starting transfers between devices, send(): return lax.ppermute(x, BOTH, pairs)  42 us
    ppermute x49, waiting for transfers between devices, send(): return lax.ppermute(x, BOTH, pairs)  30.2 us
    optimization_barrier x6, local copies, waits for them, and re-layouts, per_device(): lax.optimization_barrier((plane_xy, plane_xz, plane_yz, lines[0]))[:3]  20.6 us
    unnamed x163, local copies, waits for them, and re-layouts  17.7 us
    slice x5, local copies, waits for them, and re-layouts, borders(): first = jnp.concatenate([p[:, :1, :] for p in (xy, yz, xz)], axis=2)  6.95 us
    ppermute x2, waiting for transfers between devices, borders(): lax.ppermute(jnp.where(lax.axis_index('gy') == 0, last, first), 'gy', [(0...  6.43 us
    ppermute x2, waiting for transfers between devices, borders(): above = lax.ppermute(last, 'gx', up)  6.36 us
  transfers between devices with their start and end apart: 55, of which 18 were waited for; matrix products, arithmetic and copies ran while one was open for 10% of the time, Pallas kernels for 18%

profile of v3, /device:TPU:24, one launch (start us, length us, event | category | flops | bytes accessed | tf_op | source)
XLA Modules:
  0.0 233.5 jit_solution(10719482317241964424)
XLA Ops:
  4.5 3.2 %collective-permute-done.8.refs_1_ = f32[128,256]{1,0:T(8,128)S(1)} collective-permute-done((f32[128,256]{1,0:T(8,128)S(1)}, f32[128,256]{1,0:T(8,128)S(1)}, u32[]{:S(2)}, u32[]{:S(2)}) %collective-permute-start.8) | collective-permute-done | bytes 131104 | tf_op jit(solution)/shard_map/ppermute | solution.py:39
  10.5 2.3 collective-permute-done.9.refs_2_
  24.9 2.6 %collective-permute-done.4.refs_3_ = f32[32,16,64]{2,1,0:T(8,128)S(1)} collective-permute-done((f32[32,16,64]{2,1,0:T(8,128)S(1)}, f32[32,16,64]{2,1,0:T(8,128)S(1)}, u32[]{:S(2)}, u32[]{:S(2)}) %collective-permute-start.4) | collective-permute-done | bytes 131104 | tf_op jit(solution)/shard_map/ppermute | solution.py:39
  29.4 3.0 %shard_map.206 = (f32[32,128,128]{2,1,0:T(8,128)S(1)}, f32[8,32,256]{2,1,0:T(8,128)S(1)}) custom-call(s32[2]{0:T(128)S(1)} %pad_add_fusion.4.info, f32[32,16,128]{2,1,0:T(8,128)S(1)} %copy-done, f32[32,16,128]{2,1,0:T(8,128)S(1)} %collective-permute-done.1.xy_b, f32[32,16,64]{2,1,0:T(8,128)S(1)} %copy-done.4, ...), custom_call_target="tpu_custom_call" | custom-call | bytes 4194304 | tf_op jit(solution)/shard_map/pallas_call | solution.py:198
  33.3 4.9 %shard_map.205 = (bf16[32,128,128]{2,1,0:T(8,128)(2,1)S(1)}, bf16[256,256]{1,0:T(8,128)(2,1)S(1)}, bf16[256,256]{1,0:T(8,128)(2,1)S(1)}, bf16[256,256]{1,0:T(8,1...) custom-call(s32[2]{0:T(128)S(1)} %pad_add_fusion.4.info, f32[1]{0:T(128)S(6)} %copy.36.b_output, ...), custom_call_target="tpu_custom_call" | custom-call | bytes 4194304 | tf_op jit(solution)/shard_map/pallas_call | solution.py:127
  38.2 3.4 %shard_map.208 = (f32[32,128,128]{2,1,0:T(8,128)S(1)}, f32[32,256]{1,0:T(8,128)S(1)}, f32[128,256]{1,0:T(8,128)S(1)}) custom-call(bf16[256,256]{1,0:T(8,128)(2,1)S(1)} %get-tuple-element.100.w_in, bf16[256,256]{1,0:T(8,128)(2,1)S(1)} %get-tuple-element.101.w_out, bf16[256,256]{1,0:T(8,128)(2,1)S(1)} %get-tuple-element.102.w_back, ...), custom_call_target="tpu_custom_call" | custom-call | flops 1610612736 | bytes 10485760 | tf_op jit(solution)/shard_map/pallas_call | solution.py:329
  44.3 3.8 %copy.24 = f32[32,16,128]{1,0,2:T(8,128)} copy(f32[32,16,128]{2,1,0:T(8,128)} %refs_0_.3) | data formatting | bytes 524288 | tf_op jit(solution)/shard_map/optimization_barrier | solution.py:510
  48.1 3.8 %copy.26 = f32[32,8,128]{1,0,2:T(8,128)} copy(f32[32,8,128]{2,1,0:T(8,128)} %plane.3) | data formatting | bytes 262144 | tf_op jit(solution)/shard_map/optimization_barrier | solution.py:510
  51.9 1.8 fusion.2
  53.7 2.7 %copy.25 = f32[32,16,64]{1,0,2:T(8,128)} copy(f32[32,16,64]{2,1,0:T(8,128)} %refs_5_.1) | data formatting | bytes 262144 | tf_op jit(solution)/shard_map/optimization_barrier | solution.py:510
  60.8 3.5 %shard_map.209 = (f32[32,128,128]{2,1,0:T(8,128)S(1)}, f32[32,256]{1,0:T(8,128)S(1)}, f32[128,256]{1,0:T(8,128)S(1)}) custom-call(bf16[256,256]{1,0:T(8,128)(2,1)S(1)} %get-tuple-element.100.w_in, bf16[256,256]{1,0:T(8,128)(2,1)S(1)} %get-tuple-element.101.w_out, bf16[256,256]{1,0:T(8,128)(2,1)S(1)} %get-tuple-element.102.w_back, ...), custom_call_target="tpu_custom_call" | custom-call | flops 1610612736 | bytes 10485760 | tf_op jit(solution)/shard_map/pallas_call | solution.py:329
  64.4 3.6 %shard_map.210 = (f32[32,128,128]{2,1,0:T(8,128)S(1)}, f32[32,256]{1,0:T(8,128)S(1)}, f32[128,256]{1,0:T(8,128)S(1)}) custom-call(bf16[256,256]{1,0:T(8,128)(2,1)S(1)} %get-tuple-element.100.w_in, bf16[256,256]{1,0:T(8,128)(2,1)S(1)} %get-tuple-element.101.w_out, bf16[256,256]{1,0:T(8,128)(2,1)S(1)} %get-tuple-element.102.w_back, ...), custom_call_target="tpu_custom_call" | custom-call | flops 1610612736 | bytes 10485760 | tf_op jit(solution)/shard_map/pallas_call | solution.py:329
  68.0 3.5 %shard_map.211 = (f32[32,128,128]{2,1,0:T(8,128)S(1)}, f32[32,256]{1,0:T(8,128)S(1)}, f32[128,256]{1,0:T(8,128)S(1)}) custom-call(bf16[256,256]{1,0:T(8,128)(2,1)S(1)} %get-tuple-element.100.w_in, bf16[256,256]{1,0:T(8,128)(2,1)S(1)} %get-tuple-element.101.w_out, bf16[256,256]{1,0:T(8,128)(2,1)S(1)} %get-tuple-element.102.w_back, ...), custom_call_target="tpu_custom_call" | custom-call | flops 1610612736 | bytes 10485760 | tf_op jit(solution)/shard_map/pallas_call | solution.py:329
  71.6 7.2 %shard_map.212 = (f32[32,128,128]{2,1,0:T(8,128)S(1)}, f32[32,256]{1,0:T(8,128)S(1)}, f32[32,256]{1,0:T(8,128)S(1)}, f32[128,256]{1,0:T(8,128)S(1)}, f32[128,256]{1,0:T(8,128)S(1)}) custom-call(bf16[256,256]{1,0:T(8,128)(2,1)S(1)} %get-tuple-element.100.w_in, bf16[256,256]{1,0:T(8,128)(2,1)S(1)} %get-tuple-element.101.w_out, ...), custom_call_target="tpu_custom_call" | custom-call | flops 3221225472 | bytes 20971520 | tf_op jit(solution)/shard_map/pallas_call | solution.py:329
  78.9 6.8 %shard_map.213 = (f32[32,128,128]{2,1,0:T(8,128)S(1)}, f32[32,256]{1,0:T(8,128)S(1)}, f32[32,256]{1,0:T(8,128)S(1)}, f32[128,256]{1,0:T(8,128)S(1)}, f32[128,256]{1,0:T(8,128)S(1)}) custom-call(bf16[256,256]{1,0:T(8,128)(2,1)S(1)} %get-tuple-element.100.w_in, bf16[256,256]{1,0:T(8,128)(2,1)S(1)} %get-tuple-element.101.w_out, ...), custom_call_target="tpu_custom_call" | custom-call | flops 3221225472 | bytes 20971520 | tf_op jit(solution)/shard_map/pallas_call | solution.py:329
  85.8 3.0 %shard_map.214 = (f32[32,16,128]{2,1,0:T(8,128)S(1)}, f32[32,16,128]{2,1,0:T(8,128)S(1)}, f32[32,16,64]{2,1,0:T(8,128)S(1)}, f32[32,16,64]{2,1,0:T(8,128)S(1)}, ...) custom-call(s32[2]{0:T(128)S(1)} %pad_add_fusion.4.info, f32[32,128,128]{2,1,0:T(8,128)S(1)} %get-tuple-element.117.part_xy, ...), custom_call_target="tpu_custom_call" | custom-call | bytes 8388608 | tf_op jit(solution)/shard_map/pallas_call | solution.py:237
  94.7 3.7 %collective-permute-done.24 = f32[64,256]{1,0:T(8,128)S(1)} collective-permute-done((f32[64,256]{1,0:T(8,128)S(1)}, f32[64,256]{1,0:T(8,128)S(1)}, u32[]{:S(2)}, u32[]{:S(2)}) %collective-permute-start.24) | collective-permute-done | bytes 65568 | tf_op jit(solution)/shard_map/ppermute | solution.py:39
  98.9 3.8 %collective-permute-done.20 = f32[64,256]{1,0:T(8,128)S(1)} collective-permute-done((f32[64,256]{1,0:T(8,128)S(1)}, f32[64,256]{1,0:T(8,128)S(1)}, u32[]{:S(2)}, u32[]{:S(2)}) %collective-permute-start.20) | collective-permute-done | bytes 65568 | tf_op jit(solution)/shard_map/ppermute | solution.py:39
  105.0 2.3 collective-permute-start.6
  107.6 1.9 collective-permute-start.5
  110.3 1.7 collective-permute-start.22
  112.0 2.0 collective-permute-done.5.above
  114.1 1.9 shard_map.215
  122.4 1.8 shard_map.216
  126.2 1.8 collective-permute-done.30.refs_2_
  127.9 4.2 %collective-permute-done.31.refs_3_ = f32[32,16,64]{2,1,0:T(8,128)S(1)} collective-permute-done((f32[32,16,64]{2,1,0:T(8,128)S(1)}, f32[32,16,64]{2,1,0:T(8,128)S(1)}, u32[]{:S(2)}, u32[]{:S(2)}) %collective-permute-start.31) | collective-permute-done | bytes 131104 | tf_op jit(solution)/shard_map/ppermute | solution.py:39
  132.2 3.0 %shard_map.217 = (f32[32,128,128]{2,1,0:T(8,128)S(1)}, f32[8,32,256]{2,1,0:T(8,128)S(1)}) custom-call(s32[2]{0:T(128)S(1)} %pad_add_fusion.4.info, f32[32,16,128]{2,1,0:T(8,128)S(1)} %get-tuple-element.146.xy_a.refs_0_, f32[32,16,128]{2,1,0:T(8,128)S(1)} %collective-permute-done.28.xy_b, f32[32,16,64]{2,1,0:T(8,128)S(1)} %get-tuple-element.148.refs_0_.refs_5_, ...), custom_call_target="tpu_custom_call" | custom-call | bytes 4194304 | tf_op jit(solution)/shard_map/pallas_call | solution.py:198
  135.3 4.4 %shard_map.218 = (f32[32,128,128]{2,1,0:T(8,128)S(1)}, f32[32,256]{1,0:T(8,128)S(1)}, f32[128,256]{1,0:T(8,128)S(1)}) custom-call(bf16[256,256]{1,0:T(8,128)(2,1)S(1)} %get-tuple-element.100.w_in, bf16[256,256]{1,0:T(8,128)(2,1)S(1)} %get-tuple-element.101.w_out, bf16[256,256]{1,0:T(8,128)(2,1)S(1)} %get-tuple-element.102.w_back, ...), custom_call_target="tpu_custom_call" | custom-call | flops 1610612736 | bytes 10485760 | tf_op jit(solution)/shard_map/pallas_call | solution.py:329
  142.3 3.8 %copy.30 = f32[32,16,128]{1,0,2:T(8,128)} copy(f32[32,16,128]{2,1,0:T(8,128)} %copy-done.2) | data formatting | bytes 524288 | tf_op jit(solution)/shard_map/optimization_barrier | solution.py:510
  147.7 2.7 %copy.31 = f32[32,16,64]{1,0,2:T(8,128)} copy(f32[32,16,64]{2,1,0:T(8,128)} %copy-done.6) | data formatting | bytes 262144 | tf_op jit(solution)/shard_map/optimization_barrier | solution.py:510
  152.0 3.8 %copy.32 = f32[32,8,128]{1,0,2:T(8,128)} copy(f32[32,8,128]{2,1,0:T(8,128)} %copy-done.25) | data formatting | bytes 262144 | tf_op jit(solution)/shard_map/optimization_barrier | solution.py:510
  160.3 2.4 %collective-permute-done.36.refs_2_ = f32[128,256]{1,0:T(8,128)S(1)} collective-permute-done((f32[128,256]{1,0:T(8,128)}, f32[128,256]{1,0:T(8,128)S(1)}, u32[]{:S(2)}, u32[]{:S(2)}) %collective-permute-start.36) | collective-permute-done | bytes 131104 | tf_op jit(solution)/shard_map/ppermute | solution.py:39
  167.3 4.4 %shard_map.219 = (f32[32,128,128]{2,1,0:T(8,128)S(1)}, f32[32,256]{1,0:T(8,128)S(1)}, f32[128,256]{1,0:T(8,128)S(1)}) custom-call(bf16[256,256]{1,0:T(8,128)(2,1)S(1)} %get-tuple-element.100.w_in, bf16[256,256]{1,0:T(8,128)(2,1)S(1)} %get-tuple-element.101.w_out, bf16[256,256]{1,0:T(8,128)(2,1)S(1)} %get-tuple-element.102.w_back, ...), custom_call_target="tpu_custom_call" | custom-call | flops 1610612736 | bytes 10485760 | tf_op jit(solution)/shard_map/pallas_call | solution.py:329
  173.9 4.5 %shard_map.220 = (f32[32,128,128]{2,1,0:T(8,128)S(1)}, f32[32,256]{1,0:T(8,128)S(1)}, f32[128,256]{1,0:T(8,128)S(1)}) custom-call(bf16[256,256]{1,0:T(8,128)(2,1)S(1)} %get-tuple-element.100.w_in, bf16[256,256]{1,0:T(8,128)(2,1)S(1)} %get-tuple-element.101.w_out, bf16[256,256]{1,0:T(8,128)(2,1)S(1)} %get-tuple-element.102.w_back, ...), custom_call_target="tpu_custom_call" | custom-call | flops 1610612736 | bytes 10485760 | tf_op jit(solution)/shard_map/pallas_call | solution.py:329
  178.4 3.5 %shard_map.221 = (f32[32,128,128]{2,1,0:T(8,128)S(1)}, f32[32,256]{1,0:T(8,128)S(1)}, f32[128,256]{1,0:T(8,128)S(1)}) custom-call(bf16[256,256]{1,0:T(8,128)(2,1)S(1)} %get-tuple-element.100.w_in, bf16[256,256]{1,0:T(8,128)(2,1)S(1)} %get-tuple-element.101.w_out, bf16[256,256]{1,0:T(8,128)(2,1)S(1)} %get-tuple-element.102.w_back, ...), custom_call_target="tpu_custom_call" | custom-call | flops 1610612736 | bytes 10485760 | tf_op jit(solution)/shard_map/pallas_call | solution.py:329
  182.3 1.9 collective-permute-start.47
  184.2 6.8 %shard_map.222 = (f32[32,128,128]{2,1,0:T(8,128)S(1)}, f32[32,256]{1,0:T(8,128)S(1)}, f32[32,256]{1,0:T(8,128)S(1)}, f32[128,256]{1,0:T(8,128)S(1)}, f32[128,256]{1,0:T(8,128)S(1)}) custom-call(bf16[256,256]{1,0:T(8,128)(2,1)S(1)} %get-tuple-element.100.w_in, bf16[256,256]{1,0:T(8,128)(2,1)S(1)} %get-tuple-element.101.w_out, ...), custom_call_target="tpu_custom_call" | custom-call | flops 3221225472 | bytes 20971520 | tf_op jit(solution)/shard_map/pallas_call | solution.py:329
  191.1 6.8 %shard_map.223 = (f32[32,128,128]{2,1,0:T(8,128)S(1)}, f32[32,256]{1,0:T(8,128)S(1)}, f32[32,256]{1,0:T(8,128)S(1)}, f32[128,256]{1,0:T(8,128)S(1)}, f32[128,256]{1,0:T(8,128)S(1)}) custom-call(bf16[256,256]{1,0:T(8,128)(2,1)S(1)} %get-tuple-element.100.w_in, bf16[256,256]{1,0:T(8,128)(2,1)S(1)} %get-tuple-element.101.w_out, ...), custom_call_target="tpu_custom_call" | custom-call | flops 3221225472 | bytes 20971520 | tf_op jit(solution)/shard_map/pallas_call | solution.py:329
  197.9 3.0 %shard_map.224 = (f32[32,16,128]{2,1,0:T(8,128)S(1)}, f32[32,16,128]{2,1,0:T(8,128)S(1)}, f32[32,16,64]{2,1,0:T(8,128)S(1)}, f32[32,16,64]{2,1,0:T(8,128)S(1)}, ...) custom-call(s32[2]{0:T(128)S(1)} %pad_add_fusion.4.info, f32[32,128,128]{2,1,0:T(8,128)S(1)} %get-tuple-element.156.part_xy, ...), custom_call_target="tpu_custom_call" | custom-call | bytes 8388608 | tf_op jit(solution)/shard_map/pallas_call | solution.py:237
  202.0 1.7 collective-permute-start.48
  204.5 2.5 %collective-permute-done.52 = f32[128,256]{1,0:T(8,128)S(1)} collective-permute-done((f32[128,256]{1,0:T(8,128)S(1)}, f32[128,256]{1,0:T(8,128)S(1)}, u32[]{:S(2)}, u32[]{:S(2)}) %collective-permute-start.52) | collective-permute-done | bytes 131104 | tf_op jit(solution)/shard_map/ppermute | solution.py:39
  207.4 1.7 collective-permute-start.49
  209.2 1.9 collective-permute-start.33
  213.8 6.4 %collective-permute-done.34.left.right = f32[32,40]{1,0:T(8,128)S(1)} collective-permute-done((f32[32,40]{1,0:T(8,128)S(1)}, f32[32,40]{1,0:T(8,128)S(1)}, u32[]{:S(2)}, u32[]{:S(2)}) %collective-permute-start.34) | collective-permute-done | bytes 5152 | tf_op jit(solution)/shard_map/ppermute | solution.py:442
  222.3 1.9 collective-permute-start.32
  224.3 4.3 %collective-permute-done.32.above = f32[32,1,320]{2,1,0:T(1,128)S(1)} collective-permute-done((f32[32,1,320]{2,1,0:T(1,128)S(1)}, f32[32,1,320]{2,1,0:T(1,128)S(1)}, u32[]{:S(2)}, u32[]{:S(2)}) %collective-permute-start.32) | collective-permute-done | bytes 40992 | tf_op jit(solution)/shard_map/ppermute | solution.py:437
  228.7 2.7 %shard_map.225 = (f32[32,16,128]{2,1,0:T(8,128)}, f32[32,16,128]{2,1,0:T(8,128)}, f32[32,16,128]{2,1,0:T(8,128)}, f32[32,16,64]{2,1,0:T(8,128)}, f32[32,16,64]{2,1,0:T(8,128)}, /*index=5*/f32[32,16,64]{2,1,0:T(8,128)}) custom-call(s32[2]{0:T(128)S(1)} %pad_add_fusion.4.info, f32[32,1,320]{2,1,0:T(1,128)S(1)} %collective-permute-done.32.above, ...), custom_call_target="tpu_custom_call" | custom-call | bytes 4194304 | tf_op jit(solution)/shard_map/pallas_call | solution.py:391
  231.5 1.8 shard_map.226
  (296 shorter events, 70.4 us)
Async XLA Ops:
  0.6 32.5 %collective-permute-start = (f32[16,128,128]{2,1,0:T(8,128)}, f32[16,128,128]{2,1,0:T(8,128)}, u32[]{:S(2)}, u32[]{:S(2)}) collective-permute-start(f32[16,128,128]{2,1,0:T(8,128)} %target_a.1), channel_id=1, source_target_pairs={{0,2},{1,3},{2,0},{3,1},{4,6},{5,7},{6,4},{7,5},{8,10},{9,11},{10,... | collective-permute-start | bytes 3145736 | tf_op jit(solution)/shard_map/ppermute | solution.py:39
  1.8 5.9 %collective-permute-start.8 = (f32[128,256]{1,0:T(8,128)S(1)}, f32[128,256]{1,0:T(8,128)S(1)}, u32[]{:S(2)}, u32[]{:S(2)}) collective-permute-start(f32[128,256]{1,0:T(8,128)S(1)} %shard_map.207.refs_1_), channel_id=1, source_target_pairs={{0,8},{1,9},{2,10},{3,11},{4,0},{5,1},{6,2},{7,3},{8,16},{9,17},{1... | collective-permute-start | bytes 393224 | tf_op jit(solution)/shard_map/ppermute | solution.py:39
  3.3 6.6 %collective-permute-start.10 = (f32[128,256]{1,0:T(8,128)S(1)}, f32[128,256]{1,0:T(8,128)S(1)}, u32[]{:S(2)}, u32[]{:S(2)}) collective-permute-start(f32[128,256]{1,0:T(8,128)S(1)} %shard_map.207.refs_1_), channel_id=1, source_target_pairs={{0,4},{1,5},{2,6},{3,7},{4,12},{5,13},{6,14},{7,15},{8,0},{9,1},{1... | collective-permute-start | bytes 393224 | tf_op jit(solution)/shard_map/ppermute | solution.py:39
  9.9 6.5 %collective-permute-start.2 = (f32[32,16,64]{2,1,0:T(8,128)}, f32[32,16,64]{2,1,0:T(8,128)S(1)}, u32[]{:S(2)}, u32[]{:S(2)}) collective-permute-start(f32[32,16,64]{2,1,0:T(8,128)} %refs_5_.1), channel_id=1, source_target_pairs={{0,2},{1,3},{2,0},{3,1},{4,6},{5,7},{6,4},{7,5},{8,10},{9,11},{10,... | collective-permute-start | bytes 393224 | tf_op jit(solution)/shard_map/ppermute | solution.py:39
  9.9 6.5 %collective-permute-start.11 = (f32[128,256]{1,0:T(8,128)S(1)}, f32[128,256]{1,0:T(8,128)S(1)}, u32[]{:S(2)}, u32[]{:S(2)}) collective-permute-start(f32[128,256]{1,0:T(8,128)S(1)} %collective-permute-done.10.refs_1_), channel_id=1, source_target_pairs={{0,4},{1,5},{2,6},{3,7},{4,12},{5,13},{6,14},{7,15},{8,0},{9,1},{1... | collective-permute-start | bytes 393224 | tf_op jit(solution)/shard_map/ppermute | solution.py:39
  14.9 9.3 %collective-permute-start.3 = (f32[32,16,64]{2,1,0:T(8,128)}, f32[32,16,64]{2,1,0:T(8,128)S(1)}, u32[]{:S(2)}, u32[]{:S(2)}) collective-permute-start(f32[32,16,64]{2,1,0:T(8,128)} %refs_5_.1), channel_id=1, source_target_pairs={{0,1},{1,0},{2,3},{3,2},{4,5},{5,4},{6,7},{7,6},{8,9},{9,8},{10,11... | collective-permute-start | bytes 393224 | tf_op jit(solution)/shard_map/ppermute | solution.py:39
  16.4 11.1 %collective-permute-start.1 = (f32[32,16,128]{2,1,0:T(8,128)}, f32[32,16,128]{2,1,0:T(8,128)S(1)}, u32[]{:S(2)}, u32[]{:S(2)}) collective-permute-start(f32[32,16,128]{2,1,0:T(8,128)} %refs_0_.3), channel_id=1, source_target_pairs={{0,2},{1,3},{2,0},{3,1},{4,6},{5,7},{6,4},{7,5},{8,10},{9,11},{10,... | collective-permute-start | bytes 786440 | tf_op jit(solution)/shard_map/ppermute | solution.py:39
  16.4 11.0 %collective-permute-start.4 = (f32[32,16,64]{2,1,0:T(8,128)S(1)}, f32[32,16,64]{2,1,0:T(8,128)S(1)}, u32[]{:S(2)}, u32[]{:S(2)}) collective-permute-start(f32[32,16,64]{2,1,0:T(8,128)S(1)} %collective-permute-done.2.refs_1_), channel_id=1, source_target_pairs={{0,1},{1,0},{2,3},{3,2},{4,5},{5,4},{6,7},{7,6},{8,9},{9,8},{10,11... | collective-permute-start | bytes 393224 | tf_op jit(solution)/shard_map/ppermute | solution.py:39
  22.7 9.7 %collective-permute-start.14 = (f32[64,256]{1,0:T(8,128)S(1)}, f32[64,256]{1,0:T(8,128)S(1)}, u32[]{:S(2)}, u32[]{:S(2)}) collective-permute-start(f32[64,256]{1,0:T(8,128)S(1)} %slice.134), channel_id=1, source_target_pairs={{0,8},{1,9},{2,10},{3,11},{4,0},{5,1},{6,2},{7,3},{8,16},{9,17},{1... | collective-permute-start | bytes 196616 | tf_op jit(solution)/shard_map/ppermute | solution.py:39
  24.2 8.2 %collective-permute-start.15 = (f32[64,256]{1,0:T(8,128)S(1)}, f32[64,256]{1,0:T(8,128)S(1)}, u32[]{:S(2)}, u32[]{:S(2)}) collective-permute-start(f32[64,256]{1,0:T(8,128)S(1)} %slice.135), channel_id=1, source_target_pairs={{0,4},{1,5},{2,6},{3,7},{4,12},{5,13},{6,14},{7,15},{8,0},{9,1},{1... | collective-permute-start | bytes 196616 | tf_op jit(solution)/shard_map/ppermute | solution.py:39
  88.8 14.4 %collective-permute-start.18 = (f32[32,16,64]{2,1,0:T(8,128)S(1)}, f32[32,16,64]{2,1,0:T(8,128)S(1)}, u32[]{:S(2)}, u32[]{:S(2)}) collective-permute-start(f32[32,16,64]{2,1,0:T(8,128)S(1)} %get-tuple-element.130), channel_id=1, source_target_pairs={{0,1},{1,0},{2,3},{3,2},{4,5},{5,4},{6,7},{7,6},{8,9},{9,8},{10,11... | collective-permute-start | bytes 393224 | tf_op jit(solution)/shard_map/ppermute | solution.py:39
  90.4 14.6 %collective-permute-start.17 = (f32[32,16,64]{2,1,0:T(8,128)S(1)}, f32[32,16,64]{2,1,0:T(8,128)S(1)}, u32[]{:S(2)}, u32[]{:S(2)}) collective-permute-start(f32[32,16,64]{2,1,0:T(8,128)S(1)} %get-tuple-element.128), channel_id=1, source_target_pairs={{0,1},{1,0},{2,3},{3,2},{4,5},{5,4},{6,7},{7,6},{8,9},{9,8},{10,11... | collective-permute-start | bytes 393224 | tf_op jit(solution)/shard_map/ppermute | solution.py:39
  90.9 23.1 %collective-permute-start.16 = (f32[32,16,128]{2,1,0:T(8,128)S(1)}, f32[32,16,128]{2,1,0:T(8,128)S(1)}, u32[]{:S(2)}, u32[]{:S(2)}) collective-permute-start(f32[32,16,128]{2,1,0:T(8,128)S(1)} %get-tuple-element.126), channel_id=1, source_target_pairs={{0,2},{1,3},{2,0},{3,1},{4,6},{5,7},{6,4},{7,5},{8,10},{9,11},{10,... | collective-permute-start | bytes 786440 | tf_op jit(solution)/shard_map/ppermute | solution.py:39
  92.5 12.3 %collective-permute-start.7 = (f32[32,40]{1,0:T(8,128)S(1)}, f32[32,40]{1,0:T(8,128)S(1)}, u32[]{:S(2)}, u32[]{:S(2)}) collective-permute-start(f32[32,40]{1,0:T(8,128)S(1)} %maximum_select_fusion), channel_id=1, source_target_pairs={{0,1},{1,0},{2,3},{3,2},{4,5},{5,4},{6,7},{7,6},{8,9},{9,8},{10,11... | collective-permute-start | bytes 15368 | tf_op jit(solution)/shard_map/ppermute | solution.py:442
  103.2 6.5 %collective-permute-start.21 = (f32[128,256]{1,0:T(8,128)S(1)}, f32[128,256]{1,0:T(8,128)S(1)}, u32[]{:S(2)}, u32[]{:S(2)}) collective-permute-start(f32[128,256]{1,0:T(8,128)S(1)} %pad_add_fusion.3), channel_id=1, source_target_pairs={{0,8},{1,9},{2,10},{3,11},{4,0},{5,1},{6,2},{7,3},{8,16},{9,17},{1... | collective-permute-start | bytes 393224 | tf_op jit(solution)/shard_map/ppermute | solution.py:39
  104.8 9.2 %collective-permute-start.19 = (f32[32,16,64]{2,1,0:T(8,128)S(1)}, f32[32,16,64]{2,1,0:T(8,128)S(1)}, u32[]{:S(2)}, u32[]{:S(2)}) collective-permute-start(f32[32,16,64]{2,1,0:T(8,128)S(1)} %add.57), channel_id=1, source_target_pairs={{0,2},{1,3},{2,0},{3,1},{4,6},{5,7},{6,4},{7,5},{8,10},{9,11},{10,... | collective-permute-start | bytes 393224 | tf_op jit(solution)/shard_map/ppermute | solution.py:39
  105.0 5.3 %collective-permute-start.6 = (f32[32,1,320]{2,1,0:T(1,128)S(1)}, f32[32,1,320]{2,1,0:T(1,128)S(1)}, u32[]{:S(2)}, u32[]{:S(2)}) collective-permute-start(f32[32,1,320]{2,1,0:T(1,128)S(1)} %pad_maximum_fusion.3), channel_id=1, source_target_pairs={{2,0},{4,2},{6,4},{8,6},{10,8},{12,10},{14,12},{16,14},{18,16},{20... | collective-permute-start | bytes 122888 | tf_op jit(solution)/shard_map/ppermute | solution.py:438
  107.6 6.4 %collective-permute-start.5 = (f32[32,1,320]{2,1,0:T(1,128)S(1)}, f32[32,1,320]{2,1,0:T(1,128)S(1)}, u32[]{:S(2)}, u32[]{:S(2)}) collective-permute-start(f32[32,1,320]{2,1,0:T(1,128)S(1)} %pad_maximum_fusion.2), channel_id=1, source_target_pairs={{0,2},{2,4},{4,6},{6,8},{8,10},{10,12},{12,14},{14,16},{16,18},{18... | collective-permute-start | bytes 122888 | tf_op jit(solution)/shard_map/ppermute | solution.py:437
  109.7 6.9 %collective-permute-start.26 = (f32[128,256]{1,0:T(8,128)S(1)}, f32[128,256]{1,0:T(8,128)S(1)}, u32[]{:S(2)}, u32[]{:S(2)}) collective-permute-start(f32[128,256]{1,0:T(8,128)S(1)} %add.62), channel_id=1, source_target_pairs={{0,4},{1,5},{2,6},{3,7},{4,12},{5,13},{6,14},{7,15},{8,0},{9,1},{1... | collective-permute-start | bytes 393224 | tf_op jit(solution)/shard_map/ppermute | solution.py:39
  110.3 6.8 %collective-permute-start.22 = (f32[128,256]{1,0:T(8,128)S(1)}, f32[128,256]{1,0:T(8,128)S(1)}, u32[]{:S(2)}, u32[]{:S(2)}) collective-permute-start(f32[128,256]{1,0:T(8,128)S(1)} %add.59), channel_id=1, source_target_pairs={{0,8},{1,9},{2,10},{3,11},{4,0},{5,1},{6,2},{7,3},{8,16},{9,17},{1... | collective-permute-start | bytes 393224 | tf_op jit(solution)/shard_map/ppermute | solution.py:39
  116.1 16.1 %collective-permute-start.28 = (f32[32,16,128]{2,1,0:T(8,128)S(1)}, f32[32,16,128]{2,1,0:T(8,128)S(1)}, u32[]{:S(2)}, u32[]{:S(2)}) collective-permute-start(f32[32,16,128]{2,1,0:T(8,128)S(1)} %get-tuple-element.146.xy_a.refs_0_), channel_id=1, source_target_pairs={{0,2},{1,3},{2,0},{3,1},{4,6},{5,7},{6,4},{7,5},{8,10},{9,11},{10,... | collective-permute-start | bytes 786440 | tf_op jit(solution)/shard_map/ppermute | solution.py:39
  116.6 5.6 %collective-permute-start.27 = (f32[128,256]{1,0:T(8,128)S(1)}, f32[128,256]{1,0:T(8,128)S(1)}, u32[]{:S(2)}, u32[]{:S(2)}) collective-permute-start(f32[128,256]{1,0:T(8,128)S(1)} %add.63), channel_id=1, source_target_pairs={{0,4},{1,5},{2,6},{3,7},{4,12},{5,13},{6,14},{7,15},{8,0},{9,1},{1... | collective-permute-start | bytes 393224 | tf_op jit(solution)/shard_map/ppermute | solution.py:39
  117.1 5.3 %collective-permute-start.23 = (f32[128,256]{1,0:T(8,128)S(1)}, f32[128,256]{1,0:T(8,128)S(1)}, u32[]{:S(2)}, u32[]{:S(2)}) collective-permute-start(f32[128,256]{1,0:T(8,128)S(1)} %add.60), channel_id=1, source_target_pairs={{0,8},{1,9},{2,10},{3,11},{4,0},{5,1},{6,2},{7,3},{8,16},{9,17},{1... | collective-permute-start | bytes 393224 | tf_op jit(solution)/shard_map/ppermute | solution.py:39
  118.8 9.2 %collective-permute-start.30 = (f32[32,16,64]{2,1,0:T(8,128)S(1)}, f32[32,16,64]{2,1,0:T(8,128)S(1)}, u32[]{:S(2)}, u32[]{:S(2)}) collective-permute-start(f32[32,16,64]{2,1,0:T(8,128)S(1)} %get-tuple-element.148.refs_0_.refs_5_), channel_id=1, source_target_pairs={{0,1},{1,0},{2,3},{3,2},{4,5},{5,4},{6,7},{7,6},{8,9},{9,8},{10,11... | collective-permute-start | bytes 393224 | tf_op jit(solution)/shard_map/ppermute | solution.py:39
  119.3 12.9 %collective-permute-start.31 = (f32[32,16,64]{2,1,0:T(8,128)S(1)}, f32[32,16,64]{2,1,0:T(8,128)S(1)}, u32[]{:S(2)}, u32[]{:S(2)}) collective-permute-start(f32[32,16,64]{2,1,0:T(8,128)S(1)} %collective-permute-done.29.refs_1_), channel_id=1, source_target_pairs={{0,1},{1,0},{2,3},{3,2},{4,5},{5,4},{6,7},{7,6},{8,9},{9,8},{10,11... | collective-permute-start | bytes 393224 | tf_op jit(solution)/shard_map/ppermute | solution.py:39
  124.2 33.4 %collective-permute-start.35 = (f32[128,256]{1,0:T(8,128)}, f32[128,256]{1,0:T(8,128)}, u32[]{:S(2)}, u32[]{:S(2)}) collective-permute-start(f32[128,256]{1,0:T(8,128)} %get-tuple-element.144.refs_1_), channel_id=1, source_target_pairs={{0,8},{1,9},{2,10},{3,11},{4,0},{5,1},{6,2},{7,3},{8,16},{9,17},{1... | collective-permute-start | bytes 393224 | tf_op jit(solution)/shard_map/ppermute | solution.py:39
  125.8 32.2 %collective-permute-start.37 = (f32[128,256]{1,0:T(8,128)}, f32[128,256]{1,0:T(8,128)}, u32[]{:S(2)}, u32[]{:S(2)}) collective-permute-start(f32[128,256]{1,0:T(8,128)} %get-tuple-element.144.refs_1_), channel_id=1, source_target_pairs={{0,4},{1,5},{2,6},{3,7},{4,12},{5,13},{6,14},{7,15},{8,0},{9,1},{1... | collective-permute-start | bytes 393224 | tf_op jit(solution)/shard_map/ppermute | solution.py:39
  157.6 5.2 %collective-permute-start.36 = (f32[128,256]{1,0:T(8,128)}, f32[128,256]{1,0:T(8,128)S(1)}, u32[]{:S(2)}, u32[]{:S(2)}) collective-permute-start(f32[128,256]{1,0:T(8,128)} %collective-permute-done.35.refs_1_), channel_id=1, source_target_pairs={{0,8},{1,9},{2,10},{3,11},{4,0},{5,1},{6,2},{7,3},{8,16},{9,17},{1... | collective-permute-start | bytes 393224 | tf_op jit(solution)/shard_map/ppermute | solution.py:39
  158.1 5.3 %collective-permute-start.38 = (f32[128,256]{1,0:T(8,128)}, f32[128,256]{1,0:T(8,128)S(1)}, u32[]{:S(2)}, u32[]{:S(2)}) collective-permute-start(f32[128,256]{1,0:T(8,128)} %collective-permute-done.37.refs_1_), channel_id=1, source_target_pairs={{0,4},{1,5},{2,6},{3,7},{4,12},{5,13},{6,14},{7,15},{8,0},{9,1},{1... | collective-permute-start | bytes 393224 | tf_op jit(solution)/shard_map/ppermute | solution.py:39
  162.7 9.0 %collective-permute-start.39 = (f32[128,256]{1,0:T(8,128)S(1)}, f32[128,256]{1,0:T(8,128)S(1)}, u32[]{:S(2)}, u32[]{:S(2)}) collective-permute-start(f32[128,256]{1,0:T(8,128)S(1)} %collective-permute-done.36.refs_2_), channel_id=1, source_target_pairs={{0,8},{1,9},{2,10},{3,11},{4,0},{5,1},{6,2},{7,3},{8,16},{9,17},{1... | collective-permute-start | bytes 393224 | tf_op jit(solution)/shard_map/ppermute | solution.py:39
  163.3 9.0 %collective-permute-start.40 = (f32[128,256]{1,0:T(8,128)S(1)}, f32[128,256]{1,0:T(8,128)S(1)}, u32[]{:S(2)}, u32[]{:S(2)}) collective-permute-start(f32[128,256]{1,0:T(8,128)S(1)} %collective-permute-done.38.refs_3_), channel_id=1, source_target_pairs={{0,4},{1,5},{2,6},{3,7},{4,12},{5,13},{6,14},{7,15},{8,0},{9,1},{1... | collective-permute-start | bytes 393224 | tf_op jit(solution)/shard_map/ppermute | solution.py:39
  171.7 6.6 %collective-permute-start.41 = (f32[64,256]{1,0:T(8,128)S(1)}, f32[64,256]{1,0:T(8,128)S(1)}, u32[]{:S(2)}, u32[]{:S(2)}) collective-permute-start(f32[64,256]{1,0:T(8,128)S(1)} %slice.142), channel_id=1, source_target_pairs={{0,8},{1,9},{2,10},{3,11},{4,0},{5,1},{6,2},{7,3},{8,16},{9,17},{1... | collective-permute-start | bytes 196616 | tf_op jit(solution)/shard_map/ppermute | solution.py:39
  172.4 6.0 %collective-permute-start.42 = (f32[64,256]{1,0:T(8,128)S(1)}, f32[64,256]{1,0:T(8,128)S(1)}, u32[]{:S(2)}, u32[]{:S(2)}) collective-permute-start(f32[64,256]{1,0:T(8,128)S(1)} %slice.143), channel_id=1, source_target_pairs={{0,4},{1,5},{2,6},{3,7},{4,12},{5,13},{6,14},{7,15},{8,0},{9,1},{1... | collective-permute-start | bytes 196616 | tf_op jit(solution)/shard_map/ppermute | solution.py:39
  181.9 19.6 %collective-permute-start.51 = (f32[64,256]{1,0:T(8,128)S(1)}, f32[64,256]{1,0:T(8,128)S(1)}, u32[]{:S(2)}, u32[]{:S(2)}) collective-permute-start(f32[64,256]{1,0:T(8,128)S(1)} %get-tuple-element.211), channel_id=1, source_target_pairs={{0,4},{1,5},{2,6},{3,7},{4,12},{5,13},{6,14},{7,15},{8,0},{9,1},{1... | collective-permute-start | bytes 196616 | tf_op jit(solution)/shard_map/ppermute | solution.py:39
  182.3 19.7 %collective-permute-start.47 = (f32[64,256]{1,0:T(8,128)S(1)}, f32[64,256]{1,0:T(8,128)S(1)}, u32[]{:S(2)}, u32[]{:S(2)}) collective-permute-start(f32[64,256]{1,0:T(8,128)S(1)} %get-tuple-element.212), channel_id=1, source_target_pairs={{0,8},{1,9},{2,10},{3,11},{4,0},{5,1},{6,2},{7,3},{8,16},{9,17},{1... | collective-permute-start | bytes 196616 | tf_op jit(solution)/shard_map/ppermute | solution.py:39
  200.9 11.7 %collective-permute-start.45 = (f32[32,16,64]{2,1,0:T(8,128)S(1)}, f32[32,16,64]{2,1,0:T(8,128)S(1)}, u32[]{:S(2)}, u32[]{:S(2)}) collective-permute-start(f32[32,16,64]{2,1,0:T(8,128)S(1)} %get-tuple-element.171), channel_id=1, source_target_pairs={{0,1},{1,0},{2,3},{3,2},{4,5},{5,4},{6,7},{7,6},{8,9},{9,8},{10,11... | collective-permute-start | bytes 393224 | tf_op jit(solution)/shard_map/ppermute | solution.py:39
  201.6 5.4 %collective-permute-start.52 = (f32[128,256]{1,0:T(8,128)S(1)}, f32[128,256]{1,0:T(8,128)S(1)}, u32[]{:S(2)}, u32[]{:S(2)}) collective-permute-start(f32[128,256]{1,0:T(8,128)S(1)} %pad_add_fusion), channel_id=1, source_target_pairs={{0,4},{1,5},{2,6},{3,7},{4,12},{5,13},{6,14},{7,15},{8,0},{9,1},{1... | collective-permute-start | bytes 393224 | tf_op jit(solution)/shard_map/ppermute | solution.py:39
  202.0 5.4 %collective-permute-start.48 = (f32[128,256]{1,0:T(8,128)S(1)}, f32[128,256]{1,0:T(8,128)S(1)}, u32[]{:S(2)}, u32[]{:S(2)}) collective-permute-start(f32[128,256]{1,0:T(8,128)S(1)} %pad_add_fusion.1), channel_id=1, source_target_pairs={{0,8},{1,9},{2,10},{3,11},{4,0},{5,1},{6,2},{7,3},{8,16},{9,17},{1... | collective-permute-start | bytes 393224 | tf_op jit(solution)/shard_map/ppermute | solution.py:39
  207.0 6.0 %collective-permute-start.53 = (f32[128,256]{1,0:T(8,128)S(1)}, f32[128,256]{1,0:T(8,128)S(1)}, u32[]{:S(2)}, u32[]{:S(2)}) collective-permute-start(f32[128,256]{1,0:T(8,128)S(1)} %add.70), channel_id=1, source_target_pairs={{0,4},{1,5},{2,6},{3,7},{4,12},{5,13},{6,14},{7,15},{8,0},{9,1},{1... | collective-permute-start | bytes 393224 | tf_op jit(solution)/shard_map/ppermute | solution.py:39
  207.4 6.3 %collective-permute-start.49 = (f32[128,256]{1,0:T(8,128)S(1)}, f32[128,256]{1,0:T(8,128)S(1)}, u32[]{:S(2)}, u32[]{:S(2)}) collective-permute-start(f32[128,256]{1,0:T(8,128)S(1)} %add.67), channel_id=1, source_target_pairs={{0,8},{1,9},{2,10},{3,11},{4,0},{5,1},{6,2},{7,3},{8,16},{9,17},{1... | collective-permute-start | bytes 393224 | tf_op jit(solution)/shard_map/ppermute | solution.py:39
  209.2 11.4 %collective-permute-start.33 = (f32[32,1,320]{2,1,0:T(1,128)S(1)}, f32[32,1,320]{2,1,0:T(1,128)S(1)}, u32[]{:S(2)}, u32[]{:S(2)}) collective-permute-start(f32[32,1,320]{2,1,0:T(1,128)S(1)} %pad_maximum_fusion.5), channel_id=1, source_target_pairs={{2,0},{4,2},{6,4},{8,6},{10,8},{12,10},{14,12},{16,14},{18,16},{20... | collective-permute-start | bytes 122888 | tf_op jit(solution)/shard_map/ppermute | solution.py:438
  211.1 11.2 %collective-permute-start.44 = (f32[32,16,64]{2,1,0:T(8,128)S(1)}, f32[32,16,64]{2,1,0:T(8,128)S(1)}, u32[]{:S(2)}, u32[]{:S(2)}) collective-permute-start(f32[32,16,64]{2,1,0:T(8,128)S(1)} %get-tuple-element.169), channel_id=1, source_target_pairs={{0,1},{1,0},{2,3},{3,2},{4,5},{5,4},{6,7},{7,6},{8,9},{9,8},{10,11... | collective-permute-start | bytes 393224 | tf_op jit(solution)/shard_map/ppermute | solution.py:39
  212.7 16.0 %collective-permute-start.43 = (f32[32,16,128]{2,1,0:T(8,128)S(1)}, f32[32,16,128]{2,1,0:T(8,128)S(1)}, u32[]{:S(2)}, u32[]{:S(2)}) collective-permute-start(f32[32,16,128]{2,1,0:T(8,128)S(1)} %get-tuple-element.165), channel_id=1, source_target_pairs={{0,2},{1,3},{2,0},{3,1},{4,6},{5,7},{6,4},{7,5},{8,10},{9,11},{10,... | collective-permute-start | bytes 786440 | tf_op jit(solution)/shard_map/ppermute | solution.py:39
  213.0 7.3 %collective-permute-start.34 = (f32[32,40]{1,0:T(8,128)S(1)}, f32[32,40]{1,0:T(8,128)S(1)}, u32[]{:S(2)}, u32[]{:S(2)}) collective-permute-start(f32[32,40]{1,0:T(8,128)S(1)} %maximum_select_fusion.1), channel_id=1, source_target_pairs={{0,1},{1,0},{2,3},{3,2},{4,5},{5,4},{6,7},{7,6},{8,9},{9,8},{10,11... | collective-permute-start | bytes 15368 | tf_op jit(solution)/shard_map/ppermute | solution.py:442
  213.7 14.9 %collective-permute-start.46 = (f32[32,16,64]{2,1,0:T(8,128)S(1)}, f32[32,16,64]{2,1,0:T(8,128)S(1)}, u32[]{:S(2)}, u32[]{:S(2)}) collective-permute-start(f32[32,16,64]{2,1,0:T(8,128)S(1)} %add.65), channel_id=1, source_target_pairs={{0,2},{1,3},{2,0},{3,1},{4,6},{5,7},{6,4},{7,5},{8,10},{9,11},{10,... | collective-permute-start | bytes 393224 | tf_op jit(solution)/shard_map/ppermute | solution.py:39
  220.2 11.2 %collective-permute-start.54 = (f32[128,256]{1,0:T(8,128)S(1)}, f32[128,256]{1,0:T(8,128)S(1)}, u32[]{:S(2)}, u32[]{:S(2)}) collective-permute-start(f32[128,256]{1,0:T(8,128)S(1)} %add.71), channel_id=1, source_target_pairs={{0,4},{1,5},{2,6},{3,7},{4,12},{5,13},{6,14},{7,15},{8,0},{9,1},{1... | collective-permute-start | bytes 393224 | tf_op jit(solution)/shard_map/ppermute | solution.py:39
  220.6 10.8 %collective-permute-start.50 = (f32[128,256]{1,0:T(8,128)S(1)}, f32[128,256]{1,0:T(8,128)S(1)}, u32[]{:S(2)}, u32[]{:S(2)}) collective-permute-start(f32[128,256]{1,0:T(8,128)S(1)} %add.68), channel_id=1, source_target_pairs={{0,8},{1,9},{2,10},{3,11},{4,0},{5,1},{6,2},{7,3},{8,16},{9,17},{1... | collective-permute-start | bytes 393224 | tf_op jit(solution)/shard_map/ppermute | solution.py:39
  222.3 6.3 %collective-permute-start.32 = (f32[32,1,320]{2,1,0:T(1,128)S(1)}, f32[32,1,320]{2,1,0:T(1,128)S(1)}, u32[]{:S(2)}, u32[]{:S(2)}) collective-permute-start(f32[32,1,320]{2,1,0:T(1,128)S(1)} %pad_maximum_fusion.4), channel_id=1, source_target_pairs={{0,2},{2,4},{4,6},{6,8},{8,10},{10,12},{12,14},{14,16},{16,18},{18... | collective-permute-start | bytes 122888 | tf_op jit(solution)/shard_map/ppermute | solution.py:437
  (88 other events, 977.6 us)

commit v4 on v3

--- a/solution.py
+++ b/solution.py
@@ -19,6 +19,8 @@
 
 LANES = 128
 CHANNELS = 32
+UNROLL = 4
+GRADS_VMEM = 16 * 2**20
 BOTH = ("gx", "gy")
 f32 = jnp.float32
 bf16 = jnp.bfloat16
@@ -177,19 +179,25 @@
 
 
 def spread_kernel(chips, peers, zl, info, xy_a, xy_b, *refs):
-    xzs, (xy, xz, held) = refs[: 2 * peers], refs[2 * peers :]
+    xzs, xy, xz, held = refs[: 2 * peers], refs[2 * peers], refs[2 * peers + 1 : -1], refs[-1]
     c, x_count, _ = xy_a.shape
     zs = xzs[0].shape[2]
-    for side, ref in enumerate((xy_a, xy_b)):
-        for x in range(x_count):
-            xy[side * x_count + x] = jnp.concatenate([ref[:, x, :]] * (LANES // c), axis=0).T
-    for s in range(peers):
-        for side in range(2):
-            for x in range(x_count):
-                held[s * zs : (s + 1) * zs, side * x_count + x, :] = xzs[2 * s + side][:, x, :].T
+
+    def some(i, carry):
+        for x in range(UNROLL):
+            x += i * UNROLL
+            for side, ref in enumerate((xy_a, xy_b)):
+                xy[side * x_count + x] = jnp.concatenate([ref[:, x, :]] * (LANES // c), axis=0).T
+            for s in range(peers):
+                for side in range(2):
+                    held[s * zs : (s + 1) * zs, side * x_count + x, :] = xzs[2 * s + side][:, x, :].T
+        return carry
+
+    lax.fori_loop(0, x_count // UNROLL, some, 0)
+
     for p in range(chips):
         at = z_places(info[0], info[1], p, chips, peers, zl, zs)
-        xz[p] = jnp.concatenate([held[at + j] for j in range(zl)], axis=1)
+        xz[p][...] = jnp.concatenate([held[at + j] for j in range(zl)], axis=1)
 
 
 def spread(info, xy_a, xy_b, xzs, zl):
@@ -198,11 +206,9 @@
     return pl.pallas_call(
         functools.partial(spread_kernel, chips, peers, zl),
         in_specs=[SCALARS] + vmem(2 + len(xzs)),
-        out_specs=vmem(2),
-        out_shape=[
-            jax.ShapeDtypeStruct((2 * x_count, y_count, LANES), f32),
-            jax.ShapeDtypeStruct((chips, 2 * x_count, zl * c), f32),
-        ],
+        out_specs=vmem(1 + chips),
+        out_shape=[jax.ShapeDtypeStruct((2 * x_count, y_count, LANES), f32)]
+        + [jax.ShapeDtypeStruct((2 * x_count, zl * c), f32)] * chips,
         scratch_shapes=[pltpu.VMEM((peers * xzs[0].shape[2], 2 * x_count, c), f32)],
         compiler_params=SMALL,
         cost_estimate=cost(0, 4 * 2**20),
@@ -214,21 +220,28 @@
     c, x_count, _ = xy_a.shape
     outs_xz = outs[2:]
     zs = outs_xz[0].shape[2]
-    for side, ref in enumerate((xy_a, xy_b)):
-        for x in range(x_count):
-            rows = part_xy[side * x_count + x].T
-            total = sum(rows[j * c : (j + 1) * c] for j in range(LANES // c))
-            outs[side][:, x, :] = total / ref[:, x, :]
     held[...] = jnp.zeros_like(held)
     for p in range(chips):
         at = z_places(info[0], info[1], p, chips, peers, zl, zs)
         rows = parts[p][...]
         for j in range(zl):
             held[at + j] = rows[:, j * c : (j + 1) * c]
-    for s in range(peers):
-        for side in range(2):
-            for x in range(x_count):
-                outs_xz[2 * s + side][:, x, :] = held[s * zs : (s + 1) * zs, side * x_count + x, :].T
+
+    def some(i, carry):
+        for x in range(UNROLL):
+            x += i * UNROLL
+            for side, ref in enumerate((xy_a, xy_b)):
+                rows = part_xy[side * x_count + x].T
+                total = sum(rows[j * c : (j + 1) * c] for j in range(LANES // c))
+                outs[side][:, x, :] = total / ref[:, x, :]
+            for s in range(peers):
+                for side in range(2):
+                    outs_xz[2 * s + side][:, x, :] = held[
+                        s * zs : (s + 1) * zs, side * x_count + x, :
+                    ].T
+        return carry
+
+    lax.fori_loop(0, x_count // UNROLL, some, 0)
 
 
 def collect(info, part_xy, xy_a, xy_b, parts_xz, shape_xz, zl):
@@ -247,14 +260,14 @@
     return outs[0], outs[1], outs[2:]
 
 
-def grads_kernel(slots, first, w_in, w_out, w_back, bias, scale, wanted, xy, *refs):
-    count = len(slots)
+def grads_kernel(count, first, slot, w_in, w_out, w_back, bias, scale, wanted, xy, *refs):
     refs = list(refs)
     take = lambda k: [refs.pop(0) for _ in range(k)]
     xzs, yzs = take(count), take(count)
     before = None if first else take(1)[0]
     gxy = take(1)[0]
-    gxzs, gyzs, picks = take(count), take(count), take(count)
+    gxzs, gyzs = take(count), take(count)
+    pick, xz, yzb, gxz, gyz = refs
     step = pl.program_id(0)
     x_count, y_count, _ = xy.shape
     width = w_in.shape[0]
@@ -266,14 +279,22 @@
     def _():
         row = lax.broadcasted_iota(jnp.int32, (2 * z_count, width), 0) % z_count
         col = lax.broadcasted_iota(jnp.int32, (2 * z_count, width), 1) // CHANNELS
-        for s, pick, gyz in zip(slots, picks, gyzs):
-            pick[:width] = w_out[...]
-            pick[width:] = jnp.where(row == s * zl + col, -1.0, 0.0).astype(bf16)
-            gyz[...] = jnp.zeros_like(gyz)
+        for j in range(count):
+            pick[j, :width] = w_out[...]
+            pick[j, width:] = jnp.where(row == (slot[0] + j) * zl + col, -1.0, 0.0).astype(bf16)
+            yzb[j] = yzs[j][...]
+        gyz[...] = jnp.zeros_like(gyz)
 
     for j in range(count):
-        yz = yzs[j][...]
-        lines = [xzs[j][0, x : x + 1, :] for x in range(x_count)]
+        xz[j] = xzs[j][...]
+    if first:
+        gxy[...] = jnp.zeros_like(gxy)
+    else:
+        gxy[...] = before[...]
+
+    def one_block(j, carry):
+        yz = yzb[j]
+        lines = [xz[j, x : x + 1, :] for x in range(x_count)]
         pairs = [jnp.concatenate([xy[x]] * times, axis=1) * yz for x in range(x_count)]
         features = jnp.concatenate([(g * r).astype(bf16) for g, r in zip(pairs, lines)], axis=0)
         half = jnp.dot(features, w_in[...], preferred_element_type=f32) + bias[...]
@@ -289,7 +310,7 @@
                 ],
                 axis=1,
             ),
-            picks[j][...],
+            pick[j],
             preferred_element_type=f32,
         )
         back_hidden = (residual * slope).astype(bf16)
@@ -297,25 +318,24 @@
         total = None
         for x in range(x_count):
             b = back[x * y_count : (x + 1) * y_count] * pairs[x]
-            gxzs[j][x : x + 1, :] = jnp.sum(b, axis=0, keepdims=True)
+            gxz[j, x : x + 1, :] = jnp.sum(b, axis=0, keepdims=True)
             e = b * lines[x]
-            folded = sum(e[:, h * LANES : (h + 1) * LANES] for h in range(times))
-            if j > 0:
-                gxy[x] += folded
-            elif first:
-                gxy[x] = folded
-            else:
-                gxy[x] = before[x] + folded
+            gxy[x] += sum(e[:, h * LANES : (h + 1) * LANES] for h in range(times))
             total = e if total is None else total + e
-        gyzs[j][...] += total
+        gyz[j] += total
+        return carry
+
+    lax.fori_loop(0, count, one_block, 0)
+    for j in range(count):
+        gxzs[j][...] = gxz[j]
 
     @pl.when(step == 1)
     def _():
-        for gyz, ref in zip(gyzs, yzs):
-            gyz[...] = gyz[...] / ref[...]
-
-
-def block_grads(slots, weights, wanted, xy, xz, yzs, before):
+        for j in range(count):
+            gyzs[j][...] = gyz[j] / yzb[j]
+
+
+def block_grads(slots, weights, wanted, xy, xzs, yzs, before):
     count = len(slots)
     rows, y_count, _ = xy.shape
     rows = rows // 2
@@ -327,21 +347,36 @@
     side = pl.BlockSpec((rows, y_count, LANES), lambda i: (i, 0, 0))
     line = pl.BlockSpec((rows, width), lambda i: (i, 0))
     outs = pl.pallas_call(
-        functools.partial(grads_kernel, slots, before is None),
+        functools.partial(grads_kernel, count, before is None),
         grid=(2,),
-        in_specs=[whole(w) for w in weights]
+        in_specs=[SCALARS]
+        + [whole(w) for w in weights]
         + [side, side]
-        + [pl.BlockSpec((1, rows, width), lambda i, s=s: (s, i, 0)) for s in slots]
+        + [line] * count
         + [whole(a) for a in yzs]
         + ([] if before is None else [side]),
         out_specs=[side] + [line] * count + [whole(a) for a in yzs],
         out_shape=[jax.ShapeDtypeStruct(xy.shape, f32)]
         + [jax.ShapeDtypeStruct((2 * rows, width), f32)] * count
         + [jax.ShapeDtypeStruct(a.shape, f32) for a in yzs],
-        scratch_shapes=[pltpu.VMEM((width + wanted.shape[2], width), bf16)] * count,
-        compiler_params=pltpu.CompilerParams(vmem_limit_bytes=44 * 2**20),
+        scratch_shapes=[
+            pltpu.VMEM((count, width + wanted.shape[2], width), bf16),
+            pltpu.VMEM((count, rows, width), f32),
+            pltpu.VMEM((count, y_count, width), f32),
+            pltpu.VMEM((count, rows, width), f32),
+            pltpu.VMEM((count, y_count, width), f32),
+        ],
+        compiler_params=pltpu.CompilerParams(vmem_limit_bytes=GRADS_VMEM),
         cost_estimate=cost(12 * rows * y_count * count * width * width, count * 10 * 2**20),
-    )(*weights, wanted, xy, *([xz] * count), *yzs, *([] if before is None else [before]))
+    )(
+        jnp.array(slots[:1], jnp.int32),
+        *weights,
+        wanted,
+        xy,
+        *[xzs[s] for s in slots],
+        *yzs,
+        *([] if before is None else [before]),
+    )
     return outs[0], outs[1 : 1 + count], outs[1 + count :]
 
 
@@ -357,14 +392,20 @@
     return up, down, jnp.where(col == 0, left, back), jnp.where(col == cols - 1, right, ahead)
 
 
+def upright(ref, at, shape):
+    c, rows, cols = shape
+    line = ref[:, at : at + c * rows]
+    return jnp.broadcast_to(line, (cols, c * rows)).T.reshape(shape)
+
+
 def update(info, ends, count, plane, first, second, grad, borders, at_row, at_col, outs):
     above, below, left, right = borders
     p = plane[...]
     rows, cols = p.shape[1:]
     above = jnp.where(info[0] == 0, p[:, :1, :], above[:, :, at_row : at_row + cols])
     below = jnp.where(info[0] == ends[0], p[:, rows - 1 :, :], below[:, :, at_row : at_row + cols])
-    left = jnp.where(info[1] == 0, p[:, :, :1], left[:, at_col : at_col + rows][:, :, None])
-    right = jnp.where(info[1] == ends[1], p[:, :, cols - 1 :], right[:, at_col : at_col + rows][:, :, None])
+    left = jnp.where(info[1] == 0, p, upright(left, at_col, p.shape))
+    right = jnp.where(info[1] == ends[1], p, upright(right, at_col, p.shape))
     up, down, back, ahead = near_sides(p, above, below, left, right)
     grad = grad + 2.0 * SMOOTHING * ((p - up) + (p - down) + (p - back) + (p - ahead))
     m = BETA_ONE * first[...] + (1.0 - BETA_ONE) * grad
@@ -378,11 +419,11 @@
 
 def update_two_kernel(ends, count, info, above, below, left, right, *refs):
     borders = (above, below, left, right)
-    xy, xz, outs = refs[:5], refs[5:10], refs[10:]
+    xy, xz, outs = refs[:5], refs[5:11], refs[11:]
     width_y = xy[0].shape[2]
     rows = xy[0].shape[1]
     update(info, ends, count, *xy[:3], xy[3][...] + xy[4][...], borders, 0, 0, outs[:3])
-    update(info, ends, count, *xz[:3], xz[3][...] + xz[4][...], borders, 2 * width_y, rows, outs[3:])
+    update(info, ends, count, *xz[:3], xz[3][...] + xz[4][...] + xz[5][...], borders, 2 * width_y, xy[0].shape[0] * rows, outs[3:])
 
 
 def update_two(info, count, borders, xy, xz):
@@ -390,7 +431,7 @@
     shapes = [jax.ShapeDtypeStruct(a.shape, f32) for a in (*xy[:3], *xz[:3])]
     outs = pl.pallas_call(
         functools.partial(update_two_kernel, ends, count),
-        in_specs=[SCALARS] + vmem(14),
+        in_specs=[SCALARS] + vmem(15),
         out_specs=vmem(6),
         out_shape=shapes,
         compiler_params=SMALL,
@@ -409,7 +450,7 @@
         for j in range(per):
             held[:, t * per + j, :] = rows[j * c : (j + 1) * c]
     borders = (above, below, left, right)
-    at_col = left.shape[1] - zl
+    at_col = left.shape[1] - c * zl
     update(info, ends, count, plane, first, second, held[...], borders, width, at_col, outs)
     lanes_kernel(outs[0], lanes)
 
@@ -428,24 +469,48 @@
     return outs[:3], outs[3]
 
 
-def borders(planes):
+def edges_kernel(peers, info, xy, xz, yz, gate, *outs):
+    width = xy.shape[2]
+    for ref, at in ((xy, 0), (yz, width), (xz, 2 * width)):
+        rows, cols = ref.shape[1:]
+        outs[0][:, :, at : at + cols] = ref[:, rows - 1 :, :]
+        outs[1][:, :, at : at + cols] = ref[:, :1, :]
+    at = 0
+    for ref in (xy, xz, yz):
+        c, rows, cols = ref.shape
+        flat = ref[...].reshape(c * rows, cols).T
+        last, first = flat[cols - 1 :], flat[:1]
+        here = slice(at, at + c * rows)
+        if peers == 2:
+            outs[2][:, here] = jnp.where(info[1] == 0, last, first)
+        else:
+            outs[2][:, here] = last
+            outs[3][:, here] = first
+        at += c * rows
+
+
+def borders(info, planes, gate):
     n, peers = lax.axis_size("gx"), lax.axis_size("gy")
-    xy, xz, yz = planes
+    c = planes[0].shape[0]
+    row = jax.ShapeDtypeStruct((c, 1, sum(p.shape[2] for p in planes)), f32)
+    col = jax.ShapeDtypeStruct((1, sum(c * p.shape[1] for p in planes)), f32)
+    outs = pl.pallas_call(
+        functools.partial(edges_kernel, peers),
+        in_specs=[SCALARS] + vmem(3) + [pl.BlockSpec(memory_space=pl.ANY)],
+        out_specs=vmem(3 if peers == 2 else 4),
+        out_shape=[row, row] + [col] * (1 if peers == 2 else 2),
+        compiler_params=SMALL,
+        cost_estimate=cost(0, 2**20),
+    )(info, *planes, gate)
     up = [(i, i + 1) for i in range(n - 1)]
-    last = jnp.concatenate([p[:, -1:, :] for p in (xy, yz, xz)], axis=2)
-    first = jnp.concatenate([p[:, :1, :] for p in (xy, yz, xz)], axis=2)
-    above = lax.ppermute(last, "gx", up)
-    below = lax.ppermute(first, "gx", [(j, i) for i, j in up])
-    last = jnp.concatenate([p[:, :, -1] for p in (xy, xz, yz)], axis=1)
-    first = jnp.concatenate([p[:, :, 0] for p in (xy, xz, yz)], axis=1)
+    above = lax.ppermute(outs[0], "gx", up)
+    below = lax.ppermute(outs[1], "gx", [(j, i) for i, j in up])
     if peers == 2:
-        left = right = lax.ppermute(
-            jnp.where(lax.axis_index("gy") == 0, last, first), "gy", [(0, 1), (1, 0)]
-        )
+        left = right = lax.ppermute(outs[2], "gy", [(0, 1), (1, 0)])
     else:
         up = [(i, i + 1) for i in range(peers - 1)]
-        left = lax.ppermute(last, "gy", up)
-        right = lax.ppermute(first, "gy", [(j, i) for i, j in up])
+        left = lax.ppermute(outs[2], "gy", up)
+        right = lax.ppermute(outs[3], "gy", [(j, i) for i, j in up])
     return above, below, left, right
 
 
@@ -489,13 +554,12 @@
         xy_b, xz_b = to_core(plane_xy), to_core(plane_xz)
         xzs = [plane_xz, xz_b]
         for s in range(1, peers):
-            xzs += [to_gy(plane_xz, s), to_gy(xz_b, s)]
+            xz_y = to_gy(plane_xz, s)
+            xzs += [xz_y, to_core(xz_y)]
         if fixed is None:
-            fixed = fixed_parts(
-                info, target, target_b, zl, w_hidden, b_hidden, w_output, b_output
-            )
+            fixed = fixed_parts(info, target, target_b, zl, w_hidden, b_hidden, w_output, b_output)
         wanted, weights = fixed[0], fixed[1:]
-        xy, xz = spread(info, plane_xy, xy_b, xzs, zl)
+        xy, *xz = spread(info, plane_xy, xy_b, xzs, zl)
 
         order = [(0,), (-1,), (1,), (half,)] + [(-d, d) for d in range(half - 1, 1, -1)]
         part_xy, parts_xz, parts_yz = None, {}, {}
@@ -507,8 +571,7 @@
             for o, line, block in zip(group, lines, blocks):
                 parts_xz[slot[o]], parts_yz[o] = line, block
             if group == (0,):
-                gated = lax.optimization_barrier((plane_xy, plane_xz, plane_yz, lines[0]))[:3]
-                around = borders(gated)
+                around = borders(info, (plane_xy, plane_xz, plane_yz), lines[0])
         block = parts_yz[half]
         send_ahead, send_back = to_ring(block[:middle], 1), to_ring(block[middle:], -1)
         for d in range(half - 1, 0, -1):
@@ -521,17 +584,18 @@
         grad_xy, far_xy, pieces = collect(
             info, part_xy, plane_xy, xy_b, [parts_xz[i] for i in range(chips)], plane_xz.shape, zl
         )
-        grad_xz, far_xz = pieces[:2]
-        for s in range(1, peers):
-            grad_xz = grad_xz + to_gy(pieces[2 * s], -s)
-            far_xz = far_xz + to_gy(pieces[2 * s + 1], -s)
+        sides = [pieces[2 * s] + to_core(pieces[2 * s + 1]) for s in range(1, peers)]
+        grads_xz = [to_gy(side, -s) for s, side in enumerate(sides, 1)]
+        near_xz, far_xz = pieces[0], to_core(pieces[1])
+        for extra in grads_xz[1:]:
+            near_xz = near_xz + extra
         count = START + iteration + 1
         (plane_xy, first_xy, second_xy), (plane_xz, first_xz, second_xz) = update_two(
             info,
             count,
             around,
             (plane_xy, first_xy, second_xy, grad_xy, to_core(far_xy)),
-            (plane_xz, first_xz, second_xz, grad_xz, to_core(far_xz)),
+            (plane_xz, first_xz, second_xz, near_xz, far_xz, grads_xz[0]),
         )
         (plane_yz, first_yz, second_yz), lanes = update_yz(
             info, count, around, (plane_yz, first_yz, second_yz), (parts_yz[0], send_ahead, send_back)

time: 238 us -> 177 us (0.74)
  the two profiles are of different devices: /device:TPU:24 before, /device:TPU:0 now
where the time goes in v4:
time: 177 us
  Pallas kernels  83.1 us (47%)
  starting transfers between devices  59.7 us (34%)
  waiting for transfers between devices  27.3 us (15%)
  local copies, waits for them, and re-layouts  3.77 us (2%)
  between operations  1.93 us (1%)
    pallas_call x12, Pallas kernels, block_grads(): pl.pallas_call(functools.partial(grads_kernel, count, before is None), gr...  57.7 us
    ppermute x49, starting transfers between devices, send(): return lax.ppermute(x, BOTH, pairs)  51.5 us
    ppermute x49, waiting for transfers between devices, send(): return lax.ppermute(x, BOTH, pairs)  23 us
    pallas_call x2, Pallas kernels, collect(): pl.pallas_call(functools.partial(collect_kernel, chips, peers, zl), in_sp...  6.41 us
    pallas_call x2, Pallas kernels, spread(): pl.pallas_call(functools.partial(spread_kernel, chips, peers, zl), in_spe...  6.13 us
    pallas_call x2, Pallas kernels, update_two(): pl.pallas_call(functools.partial(update_two_kernel, ends, count), in_spec...  4.39 us
    ppermute x2, waiting for transfers between devices, borders(): left = right = lax.ppermute(outs[2], 'gy', [(0, 1), (1, 0)])  4.26 us
    pallas_call x1, Pallas kernels, fixed_parts(): pl.pallas_call(functools.partial(fixed_kernel, chips, zl), in_specs=[SCAL...  4.07 us
  transfers between devices with their start and end apart: 55, of which 12 were waited for; matrix products, arithmetic and copies ran while one was open for 1% of the time, Pallas kernels for 34%

profile of v4, /device:TPU:0, one launch (start us, length us, event | category | flops | bytes accessed | tf_op | source)
XLA Modules:
  0.0 176.8 jit_solution(17427040722666380827)
XLA Ops:
  2.3 2.6 %collective-permute-start.10 = (f32[128,256]{1,0:T(8,128)S(1)}, f32[128,256]{1,0:T(8,128)S(1)}, u32[]{:S(2)}, u32[]{:S(2)}) collective-permute-start(f32[128,256]{1,0:T(8,128)S(1)} %shard_map.315.refs_1_), channel_id=1, source_target_pairs={{0,4},{1,5},{2,6},{3,7},{4,12},{5,13},{6,14},{7,15},{8,0},{9,1},{1... | collective-permute-start | bytes 393224 | tf_op jit(solution)/shard_map/ppermute | solution.py:41
  4.9 4.1 %collective-permute-done.10.refs_1_ = f32[128,256]{1,0:T(8,128)S(1)} collective-permute-done((f32[128,256]{1,0:T(8,128)S(1)}, f32[128,256]{1,0:T(8,128)S(1)}, u32[]{:S(2)}, u32[]{:S(2)}) %collective-permute-start.10) | collective-permute-done | bytes 131104 | tf_op jit(solution)/shard_map/ppermute | solution.py:41
  9.0 1.7 collective-permute-start.11
  10.7 1.5 collective-permute-start.3
  12.7 1.6 collective-permute-done.11.refs_3_
  15.8 2.7 %collective-permute-done.3.refs_2_ = f32[32,16,64]{2,1,0:T(8,128)S(1)} collective-permute-done((f32[32,16,64]{2,1,0:T(8,128)}, f32[32,16,64]{2,1,0:T(8,128)S(1)}, u32[]{:S(2)}, u32[]{:S(2)}) %collective-permute-start.3) | collective-permute-done | bytes 131104 | tf_op jit(solution)/shard_map/ppermute | solution.py:41
  19.3 1.5 collective-permute-start.12
  22.9 1.6 collective-permute-done.12.refs_2_
  24.5 1.6 collective-permute-start.15
  28.5 3.0 %shard_map.314 = (f32[32,128,128]{2,1,0:T(8,128)S(1)}, f32[32,256]{1,0:T(8,128)S(1)}, f32[32,256]{1,0:T(8,128)S(1)}, f32[32,256]{1,0:T(8,128)S(1)}, f32[32,256]{...) custom-call(s32[2]{0:T(128)S(1)} %pad_add_fusion.4.info, ...), custom_call_target="tpu_custom_call" | custom-call | bytes 4194304 | tf_op jit(solution)/shard_map/pallas_call | solution.py:206
  31.7 4.1 %shard_map.313 = (bf16[32,128,128]{2,1,0:T(8,128)(2,1)S(1)}, bf16[256,256]{1,0:T(8,128)(2,1)S(1)}, bf16[256,256]{1,0:T(8,128)(2,1)S(1)}, bf16[256,256]{1,0:T(8,1...) custom-call(s32[2]{0:T(128)S(1)} %pad_add_fusion.4.info, f32[1]{0:T(128)S(6)} %copy.36.b_output, ...), custom_call_target="tpu_custom_call" | custom-call | bytes 4194304 | tf_op jit(solution)/shard_map/pallas_call | solution.py:129
  35.8 3.5 %shard_map.316 = (f32[32,128,128]{2,1,0:T(8,128)S(1)}, f32[32,256]{1,0:T(8,128)S(1)}, f32[128,256]{1,0:T(8,128)S(1)}) custom-call(s32[1]{0:T(128)} %constant.23.clone.slot, bf16[256,256]{1,0:T(8,128)(2,1)S(1)} %get-tuple-element.114.w_in, bf16[256,256]{1,0:T(8,128)(2,1)S(1)} %get-tuple-element.115.w_out, bf16[256,256]{1,0:T(8,128)(2,1)S(1)} %get-tuple-element.116.w_back, ...), custom_call_target="tpu_custom_call" | custom-call | flops 1610612736 | bytes 10485760 | tf_op jit(solution)/shard_map/pallas_call | solution.py:349
  39.3 3.6 %shard_map.318 = (f32[32,128,128]{2,1,0:T(8,128)S(1)}, f32[32,256]{1,0:T(8,128)S(1)}, f32[128,256]{1,0:T(8,128)S(1)}) custom-call(s32[1]{0:T(128)} %constant.24.clone.slot, bf16[256,256]{1,0:T(8,128)(2,1)S(1)} %get-tuple-element.114.w_in, bf16[256,256]{1,0:T(8,128)(2,1)S(1)} %get-tuple-element.115.w_out, bf16[256,256]{1,0:T(8,128)(2,1)S(1)} %get-tuple-element.116.w_back, ...), custom_call_target="tpu_custom_call" | custom-call | flops 1610612736 | bytes 10485760 | tf_op jit(solution)/shard_map/pallas_call | solution.py:349
  42.9 3.6 %shard_map.319 = (f32[32,128,128]{2,1,0:T(8,128)S(1)}, f32[32,256]{1,0:T(8,128)S(1)}, f32[128,256]{1,0:T(8,128)S(1)}) custom-call(s32[1]{0:T(128)} %constant.25.clone.slot, bf16[256,256]{1,0:T(8,128)(2,1)S(1)} %get-tuple-element.114.w_in, bf16[256,256]{1,0:T(8,128)(2,1)S(1)} %get-tuple-element.115.w_out, bf16[256,256]{1,0:T(8,128)(2,1)S(1)} %get-tuple-element.116.w_back, ...), custom_call_target="tpu_custom_call" | custom-call | flops 1610612736 | bytes 10485760 | tf_op jit(solution)/shard_map/pallas_call | solution.py:349
  46.6 3.6 %shard_map.320 = (f32[32,128,128]{2,1,0:T(8,128)S(1)}, f32[32,256]{1,0:T(8,128)S(1)}, f32[128,256]{1,0:T(8,128)S(1)}) custom-call(s32[1]{0:T(128)} %constant.26.clone.slot, bf16[256,256]{1,0:T(8,128)(2,1)S(1)} %get-tuple-element.114.w_in, bf16[256,256]{1,0:T(8,128)(2,1)S(1)} %get-tuple-element.115.w_out, bf16[256,256]{1,0:T(8,128)(2,1)S(1)} %get-tuple-element.116.w_back, ...), custom_call_target="tpu_custom_call" | custom-call | flops 1610612736 | bytes 10485760 | tf_op jit(solution)/shard_map/pallas_call | solution.py:349
  50.2 1.6 collective-permute-start.24
  52.3 7.1 %shard_map.321 = (f32[32,128,128]{2,1,0:T(8,128)S(1)}, f32[32,256]{1,0:T(8,128)S(1)}, f32[32,256]{1,0:T(8,128)S(1)}, f32[128,256]{1,0:T(8,128)S(1)}, f32[128,256]{1,0:T(8,128)S(1)}) custom-call(s32[1]{0:T(128)} %constant.27.clone.slot, bf16[256,256]{1,0:T(8,128)(2,1)S(1)} %get-tuple-element.114.w_in, bf16[256,256]{1,0:T(8,128)(2,1)S(1)} %get-tuple-element.115.w_out, ...), custom_call_target="tpu_custom_call" | custom-call | flops 3221225472 | bytes 20971520 | tf_op jit(solution)/shard_map/pallas_call | solution.py:349
  59.4 7.3 %shard_map.322 = (f32[32,128,128]{2,1,0:T(8,128)S(1)}, f32[32,256]{1,0:T(8,128)S(1)}, f32[32,256]{1,0:T(8,128)S(1)}, f32[128,256]{1,0:T(8,128)S(1)}, f32[128,256]{1,0:T(8,128)S(1)}) custom-call(s32[1]{0:T(128)} %constant.28.clone.slot, bf16[256,256]{1,0:T(8,128)(2,1)S(1)} %get-tuple-element.114.w_in, bf16[256,256]{1,0:T(8,128)(2,1)S(1)} %get-tuple-element.115.w_out, ...), custom_call_target="tpu_custom_call" | custom-call | flops 3221225472 | bytes 20971520 | tf_op jit(solution)/shard_map/pallas_call | solution.py:349
  66.8 3.2 %shard_map.323 = (f32[32,16,128]{2,1,0:T(8,128)S(1)}, f32[32,16,128]{2,1,0:T(8,128)S(1)}, f32[32,16,64]{2,1,0:T(8,128)S(1)}, f32[32,16,64]{2,1,0:T(8,128)S(1)}, ...) custom-call(s32[2]{0:T(128)S(1)} %pad_add_fusion.4.info, f32[32,128,128]{2,1,0:T(8,128)S(1)} %get-tuple-element.138.part_xy, ...), custom_call_target="tpu_custom_call" | custom-call | bytes 8388608 | tf_op jit(solution)/shard_map/pallas_call | solution.py:250
  73.6 1.6 collective-permute-start.7
  75.1 2.1 %collective-permute-done.7.left.right = f32[1,1280]{1,0:T(1,128)S(1)} collective-permute-done((f32[1,1280]{1,0:T(1,128)S(1)}, f32[1,1280]{1,0:T(1,128)S(1)}, u32[]{:S(2)}, u32[]{:S(2)}) %collective-permute-start.7) | collective-permute-done | bytes 5152 | tf_op jit(solution)/shard_map/ppermute | solution.py:509
  79.9 3.0 %collective-permute-start.17 = (f32[32,16,64]{2,1,0:T(8,128)S(1)}, f32[32,16,64]{2,1,0:T(8,128)S(1)}, u32[]{:S(2)}, u32[]{:S(2)}) collective-permute-start(f32[32,16,64]{2,1,0:T(8,128)S(1)} %get-tuple-element.149), channel_id=1, source_target_pairs={{0,2},{1,3},{2,0},{3,1},{4,6},{5,7},{6,4},{7,5},{8,10},{9,11},{10,... | collective-permute-start | bytes 393224 | tf_op jit(solution)/shard_map/ppermute | solution.py:41
  82.9 1.5 collective-permute-start.19
  84.5 2.4 %collective-permute-start.22 = (f32[128,256]{1,0:T(8,128)S(1)}, f32[128,256]{1,0:T(8,128)S(1)}, u32[]{:S(2)}, u32[]{:S(2)}) collective-permute-start(f32[128,256]{1,0:T(8,128)S(1)} %add.52), channel_id=1, source_target_pairs={{0,8},{1,9},{2,10},{3,11},{4,0},{5,1},{6,2},{7,3},{8,16},{9,17},{1... | collective-permute-start | bytes 393224 | tf_op jit(solution)/shard_map/ppermute | solution.py:41
  86.9 4.3 %collective-permute-done.19.refs_10_ = f32[32,16,64]{2,1,0:T(8,128)S(1)} collective-permute-done((f32[32,16,64]{2,1,0:T(8,128)S(1)}, f32[32,16,64]{2,1,0:T(8,128)S(1)}, u32[]{:S(2)}, u32[]{:S(2)}) %collective-permute-start.19) | collective-permute-done | bytes 131104 | tf_op jit(solution)/shard_map/ppermute | solution.py:41
  91.3 1.8 shard_map.324
  93.0 1.6 collective-permute-start.30
  94.6 2.7 %collective-permute-start.23 = (f32[128,256]{1,0:T(8,128)S(1)}, f32[128,256]{1,0:T(8,128)S(1)}, u32[]{:S(2)}, u32[]{:S(2)}) collective-permute-start(f32[128,256]{1,0:T(8,128)S(1)} %add.53), channel_id=1, source_target_pairs={{0,8},{1,9},{2,10},{3,11},{4,0},{5,1},{6,2},{7,3},{8,16},{9,17},{1... | collective-permute-start | bytes 393224 | tf_op jit(solution)/shard_map/ppermute | solution.py:41
  98.0 2.6 %collective-permute-done.30.refs_2_ = f32[32,16,64]{2,1,0:T(8,128)S(1)} collective-permute-done((f32[32,16,64]{2,1,0:T(8,128)S(1)}, f32[32,16,64]{2,1,0:T(8,128)S(1)}, u32[]{:S(2)}, u32[]{:S(2)}) %collective-permute-start.30) | collective-permute-done | bytes 131104 | tf_op jit(solution)/shard_map/ppermute | solution.py:41
  100.5 1.8 %collective-permute-done.27.d = f32[128,256]{1,0:T(8,128)S(1)} collective-permute-done((f32[128,256]{1,0:T(8,128)S(1)}, f32[128,256]{1,0:T(8,128)S(1)}, u32[]{:S(2)}, u32[]{:S(2)}) %collective-permute-start.27) | collective-permute-done | bytes 131104 | tf_op jit(solution)/shard_map/ppermute | solution.py:41
  105.5 3.1 %shard_map.326 = (f32[32,128,128]{2,1,0:T(8,128)S(1)}, f32[32,256]{1,0:T(8,128)S(1)}, f32[32,256]{1,0:T(8,128)S(1)}, f32[32,256]{1,0:T(8,128)S(1)}, f32[32,256]{...) custom-call(s32[2]{0:T(128)S(1)} %pad_add_fusion.4.info, ...), custom_call_target="tpu_custom_call" | custom-call | bytes 4194304 | tf_op jit(solution)/shard_map/pallas_call | solution.py:206
  110.8 3.5 %shard_map.327 = (f32[32,128,128]{2,1,0:T(8,128)S(1)}, f32[32,256]{1,0:T(8,128)S(1)}, f32[128,256]{1,0:T(8,128)S(1)}) custom-call(s32[1]{0:T(128)} %constant.23.clone.slot, bf16[256,256]{1,0:T(8,128)(2,1)S(1)} %get-tuple-element.114.w_in, bf16[256,256]{1,0:T(8,128)(2,1)S(1)} %get-tuple-element.115.w_out, bf16[256,256]{1,0:T(8,128)(2,1)S(1)} %get-tuple-element.116.w_back, ...), custom_call_target="tpu_custom_call" | custom-call | flops 1610612736 | bytes 10485760 | tf_op jit(solution)/shard_map/pallas_call | solution.py:349
  116.4 3.6 %shard_map.329 = (f32[32,128,128]{2,1,0:T(8,128)S(1)}, f32[32,256]{1,0:T(8,128)S(1)}, f32[128,256]{1,0:T(8,128)S(1)}) custom-call(s32[1]{0:T(128)} %constant.24.clone.slot, bf16[256,256]{1,0:T(8,128)(2,1)S(1)} %get-tuple-element.114.w_in, bf16[256,256]{1,0:T(8,128)(2,1)S(1)} %get-tuple-element.115.w_out, bf16[256,256]{1,0:T(8,128)(2,1)S(1)} %get-tuple-element.116.w_back, ...), custom_call_target="tpu_custom_call" | custom-call | flops 1610612736 | bytes 10485760 | tf_op jit(solution)/shard_map/pallas_call | solution.py:349
  122.2 3.6 %shard_map.330 = (f32[32,128,128]{2,1,0:T(8,128)S(1)}, f32[32,256]{1,0:T(8,128)S(1)}, f32[128,256]{1,0:T(8,128)S(1)}) custom-call(s32[1]{0:T(128)} %constant.25.clone.slot, bf16[256,256]{1,0:T(8,128)(2,1)S(1)} %get-tuple-element.114.w_in, bf16[256,256]{1,0:T(8,128)(2,1)S(1)} %get-tuple-element.115.w_out, bf16[256,256]{1,0:T(8,128)(2,1)S(1)} %get-tuple-element.116.w_back, ...), custom_call_target="tpu_custom_call" | custom-call | flops 1610612736 | bytes 10485760 | tf_op jit(solution)/shard_map/pallas_call | solution.py:349
  125.8 3.6 %shard_map.331 = (f32[32,128,128]{2,1,0:T(8,128)S(1)}, f32[32,256]{1,0:T(8,128)S(1)}, f32[128,256]{1,0:T(8,128)S(1)}) custom-call(s32[1]{0:T(128)} %constant.26.clone.slot, bf16[256,256]{1,0:T(8,128)(2,1)S(1)} %get-tuple-element.114.w_in, bf16[256,256]{1,0:T(8,128)(2,1)S(1)} %get-tuple-element.115.w_out, bf16[256,256]{1,0:T(8,128)(2,1)S(1)} %get-tuple-element.116.w_back, ...), custom_call_target="tpu_custom_call" | custom-call | flops 1610612736 | bytes 10485760 | tf_op jit(solution)/shard_map/pallas_call | solution.py:349
  131.6 7.3 %shard_map.332 = (f32[32,128,128]{2,1,0:T(8,128)S(1)}, f32[32,256]{1,0:T(8,128)S(1)}, f32[32,256]{1,0:T(8,128)S(1)}, f32[128,256]{1,0:T(8,128)S(1)}, f32[128,256]{1,0:T(8,128)S(1)}) custom-call(s32[1]{0:T(128)} %constant.27.clone.slot, bf16[256,256]{1,0:T(8,128)(2,1)S(1)} %get-tuple-element.114.w_in, bf16[256,256]{1,0:T(8,128)(2,1)S(1)} %get-tuple-element.115.w_out, ...), custom_call_target="tpu_custom_call" | custom-call | flops 3221225472 | bytes 20971520 | tf_op jit(solution)/shard_map/pallas_call | solution.py:349
  138.9 1.8 %collective-permute-start.48 = (f32[128,256]{1,0:T(8,128)S(1)}, f32[128,256]{1,0:T(8,128)S(1)}, u32[]{:S(2)}, u32[]{:S(2)}) collective-permute-start(f32[128,256]{1,0:T(8,128)S(1)} %pad_add_fusion.1), channel_id=1, source_target_pairs={{0,8},{1,9},{2,10},{3,11},{4,0},{5,1},{6,2},{7,3},{8,16},{9,17},{1... | collective-permute-start | bytes 393224 | tf_op jit(solution)/shard_map/ppermute | solution.py:41
  141.0 7.3 %shard_map.333 = (f32[32,128,128]{2,1,0:T(8,128)S(1)}, f32[32,256]{1,0:T(8,128)S(1)}, f32[32,256]{1,0:T(8,128)S(1)}, f32[128,256]{1,0:T(8,128)S(1)}, f32[128,256]{1,0:T(8,128)S(1)}) custom-call(s32[1]{0:T(128)} %constant.28.clone.slot, bf16[256,256]{1,0:T(8,128)(2,1)S(1)} %get-tuple-element.114.w_in, bf16[256,256]{1,0:T(8,128)(2,1)S(1)} %get-tuple-element.115.w_out, ...), custom_call_target="tpu_custom_call" | custom-call | flops 3221225472 | bytes 20971520 | tf_op jit(solution)/shard_map/pallas_call | solution.py:349
  148.3 3.2 %shard_map.334 = (f32[32,16,128]{2,1,0:T(8,128)S(1)}, f32[32,16,128]{2,1,0:T(8,128)S(1)}, f32[32,16,64]{2,1,0:T(8,128)S(1)}, f32[32,16,64]{2,1,0:T(8,128)S(1)}, ...) custom-call(s32[2]{0:T(128)S(1)} %pad_add_fusion.4.info, f32[32,128,128]{2,1,0:T(8,128)S(1)} %get-tuple-element.184.part_xy, ...), custom_call_target="tpu_custom_call" | custom-call | bytes 8388608 | tf_op jit(solution)/shard_map/pallas_call | solution.py:250
  152.1 1.8 %collective-permute-start.49 = (f32[128,256]{1,0:T(8,128)S(1)}, f32[128,256]{1,0:T(8,128)S(1)}, u32[]{:S(2)}, u32[]{:S(2)}) collective-permute-start(f32[128,256]{1,0:T(8,128)S(1)} %add.59), channel_id=1, source_target_pairs={{0,8},{1,9},{2,10},{3,11},{4,0},{5,1},{6,2},{7,3},{8,16},{9,17},{1... | collective-permute-start | bytes 393224 | tf_op jit(solution)/shard_map/ppermute | solution.py:41
  155.1 1.6 collective-permute-start.34
  156.6 2.1 %collective-permute-done.34.left.right = f32[1,1280]{1,0:T(1,128)S(1)} collective-permute-done((f32[1,1280]{1,0:T(1,128)S(1)}, f32[1,1280]{1,0:T(1,128)S(1)}, u32[]{:S(2)}, u32[]{:S(2)}) %collective-permute-start.34) | collective-permute-done | bytes 5152 | tf_op jit(solution)/shard_map/ppermute | solution.py:509
  161.4 2.7 %collective-permute-start.44 = (f32[32,16,64]{2,1,0:T(8,128)S(1)}, f32[32,16,64]{2,1,0:T(8,128)S(1)}, u32[]{:S(2)}, u32[]{:S(2)}) collective-permute-start(f32[32,16,64]{2,1,0:T(8,128)S(1)} %get-tuple-element.197), channel_id=1, source_target_pairs={{0,2},{1,3},{2,0},{3,1},{4,6},{5,7},{6,4},{7,5},{8,10},{9,11},{10,... | collective-permute-start | bytes 393224 | tf_op jit(solution)/shard_map/ppermute | solution.py:41
  164.1 1.5 collective-permute-start.46
  165.7 3.1 %collective-permute-start.50 = (f32[128,256]{1,0:T(8,128)S(1)}, f32[128,256]{1,0:T(8,128)S(1)}, u32[]{:S(2)}, u32[]{:S(2)}) collective-permute-start(f32[128,256]{1,0:T(8,128)S(1)} %add.60), channel_id=1, source_target_pairs={{0,8},{1,9},{2,10},{3,11},{4,0},{5,1},{6,2},{7,3},{8,16},{9,17},{1... | collective-permute-start | bytes 393224 | tf_op jit(solution)/shard_map/ppermute | solution.py:41
  168.8 3.7 %collective-permute-done.46.refs_10_ = f32[32,16,64]{2,1,0:T(8,128)S(1)} collective-permute-done((f32[32,16,64]{2,1,0:T(8,128)S(1)}, f32[32,16,64]{2,1,0:T(8,128)S(1)}, u32[]{:S(2)}, u32[]{:S(2)}) %collective-permute-start.46) | collective-permute-done | bytes 131104 | tf_op jit(solution)/shard_map/ppermute | solution.py:41
  172.4 2.6 %shard_map.335 = (f32[32,16,128]{2,1,0:T(8,128)}, f32[32,16,128]{2,1,0:T(8,128)}, f32[32,16,128]{2,1,0:T(8,128)}, f32[32,16,64]{2,1,0:T(8,128)}, f32[32,16,64]{2,1,0:T(8,128)}, /*index=5*/f32[32,16,64]{2,1,0:T(8,128)}) custom-call(s32[2]{0:T(128)S(1)} %pad_add_fusion.4.info, f32[32,1,320]{2,1,0:T(1,128)S(1)} %collective-permute-done.32.above, ...), custom_call_target="tpu_custom_call" | custom-call | bytes 4194304 | tf_op jit(solution)/shard_map/pallas_call | solution.py:432
  175.1 1.7 shard_map.336
  (144 shorter events, 32.4 us)
Async XLA Ops:
  0.6 31.0 %collective-permute-start = (f32[16,128,128]{2,1,0:T(8,128)}, f32[16,128,128]{2,1,0:T(8,128)S(1)}, u32[]{:S(2)}, u32[]{:S(2)}) collective-permute-start(f32[16,128,128]{2,1,0:T(8,128)} %target_a.1), channel_id=1, source_target_pairs={{0,2},{1,3},{2,0},{3,1},{4,6},{5,7},{6,4},{7,5},{8,10},{9,11},{10,... | collective-permute-start | bytes 3145736 | tf_op jit(solution)/shard_map/ppermute | solution.py:41
  2.3 6.8 %collective-permute-start.10 = (f32[128,256]{1,0:T(8,128)S(1)}, f32[128,256]{1,0:T(8,128)S(1)}, u32[]{:S(2)}, u32[]{:S(2)}) collective-permute-start(f32[128,256]{1,0:T(8,128)S(1)} %shard_map.315.refs_1_), channel_id=1, source_target_pairs={{0,4},{1,5},{2,6},{3,7},{4,12},{5,13},{6,14},{7,15},{8,0},{9,1},{1... | collective-permute-start | bytes 393224 | tf_op jit(solution)/shard_map/ppermute | solution.py:41
  4.8 7.4 %collective-permute-start.8 = (f32[128,256]{1,0:T(8,128)S(1)}, f32[128,256]{1,0:T(8,128)S(1)}, u32[]{:S(2)}, u32[]{:S(2)}) collective-permute-start(f32[128,256]{1,0:T(8,128)S(1)} %shard_map.315.refs_1_), channel_id=1, source_target_pairs={{0,8},{1,9},{2,10},{3,11},{4,0},{5,1},{6,2},{7,3},{8,16},{9,17},{1... | collective-permute-start | bytes 393224 | tf_op jit(solution)/shard_map/ppermute | solution.py:41
  9.0 5.3 %collective-permute-start.11 = (f32[128,256]{1,0:T(8,128)S(1)}, f32[128,256]{1,0:T(8,128)S(1)}, u32[]{:S(2)}, u32[]{:S(2)}) collective-permute-start(f32[128,256]{1,0:T(8,128)S(1)} %collective-permute-done.10.refs_1_), channel_id=1, source_target_pairs={{0,4},{1,5},{2,6},{3,7},{4,12},{5,13},{6,14},{7,15},{8,0},{9,1},{1... | collective-permute-start | bytes 393224 | tf_op jit(solution)/shard_map/ppermute | solution.py:41
  10.7 7.8 %collective-permute-start.3 = (f32[32,16,64]{2,1,0:T(8,128)}, f32[32,16,64]{2,1,0:T(8,128)S(1)}, u32[]{:S(2)}, u32[]{:S(2)}) collective-permute-start(f32[32,16,64]{2,1,0:T(8,128)} %refs_5_.1), channel_id=1, source_target_pairs={{0,1},{1,0},{2,3},{3,2},{4,5},{5,4},{6,7},{7,6},{8,9},{9,8},{10,11... | collective-permute-start | bytes 393224 | tf_op jit(solution)/shard_map/ppermute | solution.py:41
  12.2 6.3 %collective-permute-start.9 = (f32[128,256]{1,0:T(8,128)S(1)}, f32[128,256]{1,0:T(8,128)S(1)}, u32[]{:S(2)}, u32[]{:S(2)}) collective-permute-start(f32[128,256]{1,0:T(8,128)S(1)} %collective-permute-done.8.refs_1_), channel_id=1, source_target_pairs={{0,8},{1,9},{2,10},{3,11},{4,0},{5,1},{6,2},{7,3},{8,16},{9,17},{1... | collective-permute-start | bytes 393224 | tf_op jit(solution)/shard_map/ppermute | solution.py:41
  15.8 10.3 %collective-permute-start.2 = (f32[32,16,64]{2,1,0:T(8,128)}, f32[32,16,64]{2,1,0:T(8,128)S(1)}, u32[]{:S(2)}, u32[]{:S(2)}) collective-permute-start(f32[32,16,64]{2,1,0:T(8,128)} %refs_5_.1), channel_id=1, source_target_pairs={{0,2},{1,3},{2,0},{3,1},{4,6},{5,7},{6,4},{7,5},{8,10},{9,11},{10,... | collective-permute-start | bytes 393224 | tf_op jit(solution)/shard_map/ppermute | solution.py:41
  18.5 8.1 %collective-permute-start.1 = (f32[32,16,128]{2,1,0:T(8,128)}, f32[32,16,128]{2,1,0:T(8,128)S(1)}, u32[]{:S(2)}, u32[]{:S(2)}) collective-permute-start(f32[32,16,128]{2,1,0:T(8,128)} %refs_0_.3), channel_id=1, source_target_pairs={{0,2},{1,3},{2,0},{3,1},{4,6},{5,7},{6,4},{7,5},{8,10},{9,11},{10,... | collective-permute-start | bytes 786440 | tf_op jit(solution)/shard_map/ppermute | solution.py:41
  18.5 8.1 %collective-permute-start.4 = (f32[32,16,64]{2,1,0:T(8,128)S(1)}, f32[32,16,64]{2,1,0:T(8,128)S(1)}, u32[]{:S(2)}, u32[]{:S(2)}) collective-permute-start(f32[32,16,64]{2,1,0:T(8,128)S(1)} %collective-permute-done.3.refs_2_), channel_id=1, source_target_pairs={{0,2},{1,3},{2,0},{3,1},{4,6},{5,7},{6,4},{7,5},{8,10},{9,11},{10,... | collective-permute-start | bytes 393224 | tf_op jit(solution)/shard_map/ppermute | solution.py:41
  19.3 5.2 %collective-permute-start.12 = (f32[128,256]{1,0:T(8,128)S(1)}, f32[128,256]{1,0:T(8,128)S(1)}, u32[]{:S(2)}, u32[]{:S(2)}) collective-permute-start(f32[128,256]{1,0:T(8,128)S(1)} %collective-permute-done.9.refs_2_), channel_id=1, source_target_pairs={{0,8},{1,9},{2,10},{3,11},{4,0},{5,1},{6,2},{7,3},{8,16},{9,17},{1... | collective-permute-start | bytes 393224 | tf_op jit(solution)/shard_map/ppermute | solution.py:41
  24.5 7.1 %collective-permute-start.15 = (f32[64,256]{1,0:T(8,128)S(1)}, f32[64,256]{1,0:T(8,128)S(1)}, u32[]{:S(2)}, u32[]{:S(2)}) collective-permute-start(f32[64,256]{1,0:T(8,128)S(1)} %slice.33), channel_id=1, source_target_pairs={{0,4},{1,5},{2,6},{3,7},{4,12},{5,13},{6,14},{7,15},{8,0},{9,1},{1... | collective-permute-start | bytes 196616 | tf_op jit(solution)/shard_map/ppermute | solution.py:41
  26.1 5.5 %collective-permute-start.14 = (f32[64,256]{1,0:T(8,128)S(1)}, f32[64,256]{1,0:T(8,128)S(1)}, u32[]{:S(2)}, u32[]{:S(2)}) collective-permute-start(f32[64,256]{1,0:T(8,128)S(1)} %slice.32), channel_id=1, source_target_pairs={{0,8},{1,9},{2,10},{3,11},{4,0},{5,1},{6,2},{7,3},{8,16},{9,17},{1... | collective-permute-start | bytes 196616 | tf_op jit(solution)/shard_map/ppermute | solution.py:41
  50.2 21.8 %collective-permute-start.24 = (f32[64,256]{1,0:T(8,128)S(1)}, f32[64,256]{1,0:T(8,128)S(1)}, u32[]{:S(2)}, u32[]{:S(2)}) collective-permute-start(f32[64,256]{1,0:T(8,128)S(1)} %get-tuple-element.221), channel_id=1, source_target_pairs={{0,4},{1,5},{2,6},{3,7},{4,12},{5,13},{6,14},{7,15},{8,0},{9,1},{1... | collective-permute-start | bytes 196616 | tf_op jit(solution)/shard_map/ppermute | solution.py:41
  51.8 18.8 %collective-permute-start.20 = (f32[64,256]{1,0:T(8,128)S(1)}, f32[64,256]{1,0:T(8,128)S(1)}, u32[]{:S(2)}, u32[]{:S(2)}) collective-permute-start(f32[64,256]{1,0:T(8,128)S(1)} %get-tuple-element.222), channel_id=1, source_target_pairs={{0,8},{1,9},{2,10},{3,11},{4,0},{5,1},{6,2},{7,3},{8,16},{9,17},{1... | collective-permute-start | bytes 196616 | tf_op jit(solution)/shard_map/ppermute | solution.py:41
  70.1 21.2 %collective-permute-start.16 = (f32[32,16,128]{2,1,0:T(8,128)S(1)}, f32[32,16,128]{2,1,0:T(8,128)S(1)}, u32[]{:S(2)}, u32[]{:S(2)}) collective-permute-start(f32[32,16,128]{2,1,0:T(8,128)S(1)} %get-tuple-element.147), channel_id=1, source_target_pairs={{0,2},{1,3},{2,0},{3,1},{4,6},{5,7},{6,4},{7,5},{8,10},{9,11},{10,... | collective-permute-start | bytes 786440 | tf_op jit(solution)/shard_map/ppermute | solution.py:41
  70.1 8.4 %collective-permute-start.18 = (f32[32,16,64]{2,1,0:T(8,128)S(1)}, f32[32,16,64]{2,1,0:T(8,128)S(1)}, u32[]{:S(2)}, u32[]{:S(2)}) collective-permute-start(f32[32,16,64]{2,1,0:T(8,128)S(1)} %get-tuple-element.151), channel_id=1, source_target_pairs={{0,2},{1,3},{2,0},{3,1},{4,6},{5,7},{6,4},{7,5},{8,10},{9,11},{10,... | collective-permute-start | bytes 393224 | tf_op jit(solution)/shard_map/ppermute | solution.py:41
  70.6 12.3 %collective-permute-start.21 = (f32[128,256]{1,0:T(8,128)S(1)}, f32[128,256]{1,0:T(8,128)S(1)}, u32[]{:S(2)}, u32[]{:S(2)}) collective-permute-start(f32[128,256]{1,0:T(8,128)S(1)} %pad_add_fusion.3), channel_id=1, source_target_pairs={{0,8},{1,9},{2,10},{3,11},{4,0},{5,1},{6,2},{7,3},{8,16},{9,17},{1... | collective-permute-start | bytes 393224 | tf_op jit(solution)/shard_map/ppermute | solution.py:41
  72.0 12.5 %collective-permute-start.25 = (f32[128,256]{1,0:T(8,128)S(1)}, f32[128,256]{1,0:T(8,128)S(1)}, u32[]{:S(2)}, u32[]{:S(2)}) collective-permute-start(f32[128,256]{1,0:T(8,128)S(1)} %pad_add_fusion.2), channel_id=1, source_target_pairs={{0,4},{1,5},{2,6},{3,7},{4,12},{5,13},{6,14},{7,15},{8,0},{9,1},{1... | collective-permute-start | bytes 393224 | tf_op jit(solution)/shard_map/ppermute | solution.py:41
  78.6 8.3 %collective-permute-start.6 = (f32[32,1,320]{2,1,0:T(1,128)S(1)}, f32[32,1,320]{2,1,0:T(1,128)S(1)}, u32[]{:S(2)}, u32[]{:S(2)}) collective-permute-start(f32[32,1,320]{2,1,0:T(1,128)S(1)} %get-tuple-element.124), channel_id=1, source_target_pairs={{2,0},{4,2},{6,4},{8,6},{10,8},{12,10},{14,12},{16,14},{18,16},{20... | collective-permute-start | bytes 122888 | tf_op jit(solution)/shard_map/ppermute | solution.py:507
  79.9 7.0 %collective-permute-start.17 = (f32[32,16,64]{2,1,0:T(8,128)S(1)}, f32[32,16,64]{2,1,0:T(8,128)S(1)}, u32[]{:S(2)}, u32[]{:S(2)}) collective-permute-start(f32[32,16,64]{2,1,0:T(8,128)S(1)} %get-tuple-element.149), channel_id=1, source_target_pairs={{0,2},{1,3},{2,0},{3,1},{4,6},{5,7},{6,4},{7,5},{8,10},{9,11},{10,... | collective-permute-start | bytes 393224 | tf_op jit(solution)/shard_map/ppermute | solution.py:41
  82.9 8.3 %collective-permute-start.19 = (f32[32,16,64]{2,1,0:T(8,128)S(1)}, f32[32,16,64]{2,1,0:T(8,128)S(1)}, u32[]{:S(2)}, u32[]{:S(2)}) collective-permute-start(f32[32,16,64]{2,1,0:T(8,128)S(1)} %add.50), channel_id=1, source_target_pairs={{0,1},{1,0},{2,3},{3,2},{4,5},{5,4},{6,7},{7,6},{8,9},{9,8},{10,11... | collective-permute-start | bytes 393224 | tf_op jit(solution)/shard_map/ppermute | solution.py:41
  84.5 10.1 %collective-permute-start.22 = (f32[128,256]{1,0:T(8,128)S(1)}, f32[128,256]{1,0:T(8,128)S(1)}, u32[]{:S(2)}, u32[]{:S(2)}) collective-permute-start(f32[128,256]{1,0:T(8,128)S(1)} %add.52), channel_id=1, source_target_pairs={{0,8},{1,9},{2,10},{3,11},{4,0},{5,1},{6,2},{7,3},{8,16},{9,17},{1... | collective-permute-start | bytes 393224 | tf_op jit(solution)/shard_map/ppermute | solution.py:41
  86.9 10.4 %collective-permute-start.26 = (f32[128,256]{1,0:T(8,128)S(1)}, f32[128,256]{1,0:T(8,128)S(1)}, u32[]{:S(2)}, u32[]{:S(2)}) collective-permute-start(f32[128,256]{1,0:T(8,128)S(1)} %add.55), channel_id=1, source_target_pairs={{0,4},{1,5},{2,6},{3,7},{4,12},{5,13},{6,14},{7,15},{8,0},{9,1},{1... | collective-permute-start | bytes 393224 | tf_op jit(solution)/shard_map/ppermute | solution.py:41
  93.0 7.5 %collective-permute-start.30 = (f32[32,16,64]{2,1,0:T(8,128)S(1)}, f32[32,16,64]{2,1,0:T(8,128)S(1)}, u32[]{:S(2)}, u32[]{:S(2)}) collective-permute-start(f32[32,16,64]{2,1,0:T(8,128)S(1)} %get-tuple-element.153.refs_0_.xz.refs_5_), channel_id=1, source_target_pairs={{0,1},{1,0},{2,3},{3,2},{4,5},{5,4},{6,7},{7,6},{8,9},{9,8},{10,11... | collective-permute-start | bytes 393224 | tf_op jit(solution)/shard_map/ppermute | solution.py:41
  94.6 5.9 %collective-permute-start.23 = (f32[128,256]{1,0:T(8,128)S(1)}, f32[128,256]{1,0:T(8,128)S(1)}, u32[]{:S(2)}, u32[]{:S(2)}) collective-permute-start(f32[128,256]{1,0:T(8,128)S(1)} %add.53), channel_id=1, source_target_pairs={{0,8},{1,9},{2,10},{3,11},{4,0},{5,1},{6,2},{7,3},{8,16},{9,17},{1... | collective-permute-start | bytes 393224 | tf_op jit(solution)/shard_map/ppermute | solution.py:41
  97.4 8.1 %collective-permute-start.28 = (f32[32,16,128]{2,1,0:T(8,128)S(1)}, f32[32,16,128]{2,1,0:T(8,128)S(1)}, u32[]{:S(2)}, u32[]{:S(2)}) collective-permute-start(f32[32,16,128]{2,1,0:T(8,128)S(1)} %get-tuple-element.152.xy_a.xy.refs_0_), channel_id=1, source_target_pairs={{0,2},{1,3},{2,0},{3,1},{4,6},{5,7},{6,4},{7,5},{8,10},{9,11},{10,... | collective-permute-start | bytes 786440 | tf_op jit(solution)/shard_map/ppermute | solution.py:41
  97.5 8.0 %collective-permute-start.29 = (f32[32,16,64]{2,1,0:T(8,128)S(1)}, f32[32,16,64]{2,1,0:T(8,128)S(1)}, u32[]{:S(2)}, u32[]{:S(2)}) collective-permute-start(f32[32,16,64]{2,1,0:T(8,128)S(1)} %get-tuple-element.153.refs_0_.xz.refs_5_), channel_id=1, source_target_pairs={{0,2},{1,3},{2,0},{3,1},{4,6},{5,7},{6,4},{7,5},{8,10},{9,11},{10,... | collective-permute-start | bytes 393224 | tf_op jit(solution)/shard_map/ppermute | solution.py:41
  103.4 5.4 %collective-permute-start.37 = (f32[128,256]{1,0:T(8,128)S(1)}, f32[128,256]{1,0:T(8,128)S(1)}, u32[]{:S(2)}, u32[]{:S(2)}) collective-permute-start(f32[128,256]{1,0:T(8,128)S(1)} %get-tuple-element.165.refs_1_), channel_id=1, source_target_pairs={{0,4},{1,5},{2,6},{3,7},{4,12},{5,13},{6,14},{7,15},{8,0},{9,1},{1... | collective-permute-start | bytes 393224 | tf_op jit(solution)/shard_map/ppermute | solution.py:41
  104.0 5.9 %collective-permute-start.35 = (f32[128,256]{1,0:T(8,128)S(1)}, f32[128,256]{1,0:T(8,128)S(1)}, u32[]{:S(2)}, u32[]{:S(2)}) collective-permute-start(f32[128,256]{1,0:T(8,128)S(1)} %get-tuple-element.165.refs_1_), channel_id=1, source_target_pairs={{0,8},{1,9},{2,10},{3,11},{4,0},{5,1},{6,2},{7,3},{8,16},{9,17},{1... | collective-permute-start | bytes 393224 | tf_op jit(solution)/shard_map/ppermute | solution.py:41
  108.8 5.5 %collective-permute-start.38 = (f32[128,256]{1,0:T(8,128)S(1)}, f32[128,256]{1,0:T(8,128)S(1)}, u32[]{:S(2)}, u32[]{:S(2)}) collective-permute-start(f32[128,256]{1,0:T(8,128)S(1)} %collective-permute-done.37.refs_1_), channel_id=1, source_target_pairs={{0,4},{1,5},{2,6},{3,7},{4,12},{5,13},{6,14},{7,15},{8,0},{9,1},{1... | collective-permute-start | bytes 393224 | tf_op jit(solution)/shard_map/ppermute | solution.py:41
  109.9 5.6 %collective-permute-start.36 = (f32[128,256]{1,0:T(8,128)S(1)}, f32[128,256]{1,0:T(8,128)S(1)}, u32[]{:S(2)}, u32[]{:S(2)}) collective-permute-start(f32[128,256]{1,0:T(8,128)S(1)} %collective-permute-done.35.refs_1_), channel_id=1, source_target_pairs={{0,8},{1,9},{2,10},{3,11},{4,0},{5,1},{6,2},{7,3},{8,16},{9,17},{1... | collective-permute-start | bytes 393224 | tf_op jit(solution)/shard_map/ppermute | solution.py:41
  114.3 5.7 %collective-permute-start.40 = (f32[128,256]{1,0:T(8,128)S(1)}, f32[128,256]{1,0:T(8,128)S(1)}, u32[]{:S(2)}, u32[]{:S(2)}) collective-permute-start(f32[128,256]{1,0:T(8,128)S(1)} %collective-permute-done.38.refs_3_), channel_id=1, source_target_pairs={{0,4},{1,5},{2,6},{3,7},{4,12},{5,13},{6,14},{7,15},{8,0},{9,1},{1... | collective-permute-start | bytes 393224 | tf_op jit(solution)/shard_map/ppermute | solution.py:41
  115.5 5.7 %collective-permute-start.39 = (f32[128,256]{1,0:T(8,128)S(1)}, f32[128,256]{1,0:T(8,128)S(1)}, u32[]{:S(2)}, u32[]{:S(2)}) collective-permute-start(f32[128,256]{1,0:T(8,128)S(1)} %collective-permute-done.36.refs_2_), channel_id=1, source_target_pairs={{0,8},{1,9},{2,10},{3,11},{4,0},{5,1},{6,2},{7,3},{8,16},{9,17},{1... | collective-permute-start | bytes 393224 | tf_op jit(solution)/shard_map/ppermute | solution.py:41
  120.0 5.8 %collective-permute-start.42 = (f32[64,256]{1,0:T(8,128)S(1)}, f32[64,256]{1,0:T(8,128)S(1)}, u32[]{:S(2)}, u32[]{:S(2)}) collective-permute-start(f32[64,256]{1,0:T(8,128)S(1)} %slice.35), channel_id=1, source_target_pairs={{0,4},{1,5},{2,6},{3,7},{4,12},{5,13},{6,14},{7,15},{8,0},{9,1},{1... | collective-permute-start | bytes 196616 | tf_op jit(solution)/shard_map/ppermute | solution.py:41
  129.5 11.2 %collective-permute-start.51 = (f32[64,256]{1,0:T(8,128)S(1)}, f32[64,256]{1,0:T(8,128)S(1)}, u32[]{:S(2)}, u32[]{:S(2)}) collective-permute-start(f32[64,256]{1,0:T(8,128)S(1)} %get-tuple-element.219), channel_id=1, source_target_pairs={{0,4},{1,5},{2,6},{3,7},{4,12},{5,13},{6,14},{7,15},{8,0},{9,1},{1... | collective-permute-start | bytes 196616 | tf_op jit(solution)/shard_map/ppermute | solution.py:41
  130.9 8.0 %collective-permute-start.47 = (f32[64,256]{1,0:T(8,128)S(1)}, f32[64,256]{1,0:T(8,128)S(1)}, u32[]{:S(2)}, u32[]{:S(2)}) collective-permute-start(f32[64,256]{1,0:T(8,128)S(1)} %get-tuple-element.220), channel_id=1, source_target_pairs={{0,8},{1,9},{2,10},{3,11},{4,0},{5,1},{6,2},{7,3},{8,16},{9,17},{1... | collective-permute-start | bytes 196616 | tf_op jit(solution)/shard_map/ppermute | solution.py:41
  138.9 13.2 %collective-permute-start.48 = (f32[128,256]{1,0:T(8,128)S(1)}, f32[128,256]{1,0:T(8,128)S(1)}, u32[]{:S(2)}, u32[]{:S(2)}) collective-permute-start(f32[128,256]{1,0:T(8,128)S(1)} %pad_add_fusion.1), channel_id=1, source_target_pairs={{0,8},{1,9},{2,10},{3,11},{4,0},{5,1},{6,2},{7,3},{8,16},{9,17},{1... | collective-permute-start | bytes 393224 | tf_op jit(solution)/shard_map/ppermute | solution.py:41
  140.7 13.2 %collective-permute-start.52 = (f32[128,256]{1,0:T(8,128)S(1)}, f32[128,256]{1,0:T(8,128)S(1)}, u32[]{:S(2)}, u32[]{:S(2)}) collective-permute-start(f32[128,256]{1,0:T(8,128)S(1)} %pad_add_fusion), channel_id=1, source_target_pairs={{0,4},{1,5},{2,6},{3,7},{4,12},{5,13},{6,14},{7,15},{8,0},{9,1},{1... | collective-permute-start | bytes 393224 | tf_op jit(solution)/shard_map/ppermute | solution.py:41
  151.5 8.5 %collective-permute-start.45 = (f32[32,16,64]{2,1,0:T(8,128)S(1)}, f32[32,16,64]{2,1,0:T(8,128)S(1)}, u32[]{:S(2)}, u32[]{:S(2)}) collective-permute-start(f32[32,16,64]{2,1,0:T(8,128)S(1)} %get-tuple-element.199), channel_id=1, source_target_pairs={{0,2},{1,3},{2,0},{3,1},{4,6},{5,7},{6,4},{7,5},{8,10},{9,11},{10,... | collective-permute-start | bytes 393224 | tf_op jit(solution)/shard_map/ppermute | solution.py:41
  151.6 17.2 %collective-permute-start.43 = (f32[32,16,128]{2,1,0:T(8,128)S(1)}, f32[32,16,128]{2,1,0:T(8,128)S(1)}, u32[]{:S(2)}, u32[]{:S(2)}) collective-permute-start(f32[32,16,128]{2,1,0:T(8,128)S(1)} %get-tuple-element.193), channel_id=1, source_target_pairs={{0,2},{1,3},{2,0},{3,1},{4,6},{5,7},{6,4},{7,5},{8,10},{9,11},{10,... | collective-permute-start | bytes 786440 | tf_op jit(solution)/shard_map/ppermute | solution.py:41
  152.1 9.3 %collective-permute-start.49 = (f32[128,256]{1,0:T(8,128)S(1)}, f32[128,256]{1,0:T(8,128)S(1)}, u32[]{:S(2)}, u32[]{:S(2)}) collective-permute-start(f32[128,256]{1,0:T(8,128)S(1)} %add.59), channel_id=1, source_target_pairs={{0,8},{1,9},{2,10},{3,11},{4,0},{5,1},{6,2},{7,3},{8,16},{9,17},{1... | collective-permute-start | bytes 393224 | tf_op jit(solution)/shard_map/ppermute | solution.py:41
  153.9 10.2 %collective-permute-start.53 = (f32[128,256]{1,0:T(8,128)S(1)}, f32[128,256]{1,0:T(8,128)S(1)}, u32[]{:S(2)}, u32[]{:S(2)}) collective-permute-start(f32[128,256]{1,0:T(8,128)S(1)} %add.62), channel_id=1, source_target_pairs={{0,4},{1,5},{2,6},{3,7},{4,12},{5,13},{6,14},{7,15},{8,0},{9,1},{1... | collective-permute-start | bytes 393224 | tf_op jit(solution)/shard_map/ppermute | solution.py:41
  158.7 6.9 %collective-permute-start.32 = (f32[32,1,320]{2,1,0:T(1,128)S(1)}, f32[32,1,320]{2,1,0:T(1,128)S(1)}, u32[]{:S(2)}, u32[]{:S(2)}) collective-permute-start(f32[32,1,320]{2,1,0:T(1,128)S(1)} %get-tuple-element.167), channel_id=1, source_target_pairs={{0,2},{2,4},{4,6},{6,8},{8,10},{10,12},{12,14},{14,16},{16,18},{18... | collective-permute-start | bytes 122888 | tf_op jit(solution)/shard_map/ppermute | solution.py:506
  160.0 8.7 %collective-permute-start.33 = (f32[32,1,320]{2,1,0:T(1,128)S(1)}, f32[32,1,320]{2,1,0:T(1,128)S(1)}, u32[]{:S(2)}, u32[]{:S(2)}) collective-permute-start(f32[32,1,320]{2,1,0:T(1,128)S(1)} %get-tuple-element.168), channel_id=1, source_target_pairs={{2,0},{4,2},{6,4},{8,6},{10,8},{12,10},{14,12},{16,14},{18,16},{20... | collective-permute-start | bytes 122888 | tf_op jit(solution)/shard_map/ppermute | solution.py:507
  161.4 7.4 %collective-permute-start.44 = (f32[32,16,64]{2,1,0:T(8,128)S(1)}, f32[32,16,64]{2,1,0:T(8,128)S(1)}, u32[]{:S(2)}, u32[]{:S(2)}) collective-permute-start(f32[32,16,64]{2,1,0:T(8,128)S(1)} %get-tuple-element.197), channel_id=1, source_target_pairs={{0,2},{1,3},{2,0},{3,1},{4,6},{5,7},{6,4},{7,5},{8,10},{9,11},{10,... | collective-permute-start | bytes 393224 | tf_op jit(solution)/shard_map/ppermute | solution.py:41
  164.1 8.3 %collective-permute-start.46 = (f32[32,16,64]{2,1,0:T(8,128)S(1)}, f32[32,16,64]{2,1,0:T(8,128)S(1)}, u32[]{:S(2)}, u32[]{:S(2)}) collective-permute-start(f32[32,16,64]{2,1,0:T(8,128)S(1)} %add.57), channel_id=1, source_target_pairs={{0,1},{1,0},{2,3},{3,2},{4,5},{5,4},{6,7},{7,6},{8,9},{9,8},{10,11... | collective-permute-start | bytes 393224 | tf_op jit(solution)/shard_map/ppermute | solution.py:41
  165.7 9.4 %collective-permute-start.50 = (f32[128,256]{1,0:T(8,128)S(1)}, f32[128,256]{1,0:T(8,128)S(1)}, u32[]{:S(2)}, u32[]{:S(2)}) collective-permute-start(f32[128,256]{1,0:T(8,128)S(1)} %add.60), channel_id=1, source_target_pairs={{0,8},{1,9},{2,10},{3,11},{4,0},{5,1},{6,2},{7,3},{8,16},{9,17},{1... | collective-permute-start | bytes 393224 | tf_op jit(solution)/shard_map/ppermute | solution.py:41
  168.8 6.3 %collective-permute-start.54 = (f32[128,256]{1,0:T(8,128)S(1)}, f32[128,256]{1,0:T(8,128)S(1)}, u32[]{:S(2)}, u32[]{:S(2)}) collective-permute-start(f32[128,256]{1,0:T(8,128)S(1)} %add.63), channel_id=1, source_target_pairs={{0,4},{1,5},{2,6},{3,7},{4,12},{5,13},{6,14},{7,15},{8,0},{9,1},{1... | collective-permute-start | bytes 393224 | tf_op jit(solution)/shard_map/ppermute | solution.py:41
  (23 other events, 264.2 us)

commit v5 on v4

--- a/solution.py
+++ b/solution.py
@@ -93,7 +93,7 @@
 
 
 def fixed_kernel(
-    chips, zl, info, b_output, target_a, target_b, w, w_t, w_o, b, o, wanted, w_in, w_out, w_back, bias, scale
+    chips, zl, info, b_output, target_a, target_b, w, b, o, wanted, w_in, w_out, w_back, bias, scale
 ):
     gx = info[0]
     x_count = target_a.shape[0]
@@ -112,11 +112,12 @@
 
         lax.fori_loop(0, x_count, one, 0)
     times = w_in.shape[0] // w.shape[0]
-    w_in[...] = diagonal(0.5 * w[...].astype(f32), times).astype(bf16)
-    w_out[...] = diagonal(w_o[...], times).astype(bf16)
-    w_back[...] = diagonal(w_t[...], times).astype(bf16)
+    wide, line = w[...].astype(f32), o[...].astype(f32)
+    w_in[...] = diagonal(0.5 * wide, times).astype(bf16)
+    w_out[...] = diagonal(jnp.broadcast_to(line, wide.shape).T, times).astype(bf16)
+    w_back[...] = diagonal(wide.T, times).astype(bf16)
     bias[...] = jnp.concatenate([0.5 * b[...]] * times, axis=1)
-    scale[...] = jnp.concatenate([0.5 * o[...]] * times, axis=1)
+    scale[...] = jnp.concatenate([0.5 * line] * times, axis=1)
 
 
 def fixed_parts(info, target, target_b, zl, w_hidden, b_hidden, w_output, b_output):
@@ -128,7 +129,7 @@
     line = jax.ShapeDtypeStruct((1, width), f32)
     return pl.pallas_call(
         functools.partial(fixed_kernel, chips, zl),
-        in_specs=[SCALARS, SCALARS] + vmem(7),
+        in_specs=[SCALARS, SCALARS] + vmem(5),
         out_specs=vmem(6),
         out_shape=[
             jax.ShapeDtypeStruct((2 * x_count, y_count, z_count), bf16),
@@ -146,10 +147,8 @@
         target,
         target_b,
         w_hidden,
-        w_hidden.T,
-        jnp.broadcast_to(w_output[:, None], (hidden, hidden)),
         b_hidden[None],
-        w_output.astype(f32)[None],
+        w_output[None],
     )
 
 
@@ -215,11 +214,35 @@
     )(info, xy_a, xy_b, *xzs)
 
 
-def collect_kernel(chips, peers, zl, info, part_xy, xy_a, xy_b, *refs):
-    parts, outs, held = refs[:chips], refs[chips : chips + 2 + 2 * peers], refs[chips + 2 + 2 * peers]
+def collect_xy_kernel(part, xy_a, xy_b, *outs):
     c, x_count, _ = xy_a.shape
-    outs_xz = outs[2:]
-    zs = outs_xz[0].shape[2]
+
+    def some(i, carry):
+        for x in range(UNROLL):
+            x += i * UNROLL
+            for side, ref in enumerate((xy_a, xy_b)):
+                rows = part[side * x_count + x].T
+                total = sum(rows[j * c : (j + 1) * c] for j in range(LANES // c))
+                outs[side][:, x, :] = total / ref[:, x, :]
+        return carry
+
+    lax.fori_loop(0, x_count // UNROLL, some, 0)
+
+
+def collect_xy(part, xy_a, xy_b):
+    return pl.pallas_call(
+        collect_xy_kernel,
+        in_specs=vmem(3),
+        out_specs=vmem(2),
+        out_shape=[jax.ShapeDtypeStruct(xy_a.shape, f32)] * 2,
+        compiler_params=SMALL,
+        cost_estimate=cost(0, 4 * 2**20),
+    )(part, xy_a, xy_b)
+
+
+def collect_xz_kernel(chips, peers, zl, info, *refs):
+    parts, outs, held = refs[:chips], refs[chips : chips + 2 * peers], refs[chips + 2 * peers]
+    c, x_count, zs = outs[0].shape
     held[...] = jnp.zeros_like(held)
     for p in range(chips):
         at = z_places(info[0], info[1], p, chips, peers, zl, zs)
@@ -230,13 +253,9 @@
     def some(i, carry):
         for x in range(UNROLL):
             x += i * UNROLL
-            for side, ref in enumerate((xy_a, xy_b)):
-                rows = part_xy[side * x_count + x].T
-                total = sum(rows[j * c : (j + 1) * c] for j in range(LANES // c))
-                outs[side][:, x, :] = total / ref[:, x, :]
             for s in range(peers):
                 for side in range(2):
-                    outs_xz[2 * s + side][:, x, :] = held[
+                    outs[2 * s + side][:, x, :] = held[
                         s * zs : (s + 1) * zs, side * x_count + x, :
                     ].T
         return carry
@@ -244,20 +263,18 @@
     lax.fori_loop(0, x_count // UNROLL, some, 0)
 
 
-def collect(info, part_xy, xy_a, xy_b, parts_xz, shape_xz, zl):
+def collect_xz(info, parts, shape, zl):
     peers, chips = lax.axis_size("gy"), lax.axis_size("gx") // 2
-    c, x_count, _ = xy_a.shape
-    outs = pl.pallas_call(
-        functools.partial(collect_kernel, chips, peers, zl),
-        in_specs=[SCALARS] + vmem(3 + chips),
-        out_specs=vmem(2 + 2 * peers),
-        out_shape=[jax.ShapeDtypeStruct(xy_a.shape, f32)] * 2
-        + [jax.ShapeDtypeStruct(shape_xz, f32)] * (2 * peers),
-        scratch_shapes=[pltpu.VMEM((peers * shape_xz[2], 2 * x_count, c), f32)],
-        compiler_params=SMALL,
-        cost_estimate=cost(0, 8 * 2**20),
-    )(info, part_xy, xy_a, xy_b, *parts_xz)
-    return outs[0], outs[1], outs[2:]
+    c, x_count, zs = shape
+    return pl.pallas_call(
+        functools.partial(collect_xz_kernel, chips, peers, zl),
+        in_specs=[SCALARS] + vmem(chips),
+        out_specs=vmem(2 * peers),
+        out_shape=[jax.ShapeDtypeStruct(shape, f32)] * (2 * peers),
+        scratch_shapes=[pltpu.VMEM((peers * zs, 2 * x_count, c), f32)],
+        compiler_params=SMALL,
+        cost_estimate=cost(0, 4 * 2**20),
+    )(info, *parts)
 
 
 def grads_kernel(count, first, slot, w_in, w_out, w_back, bias, scale, wanted, xy, *refs):
@@ -570,7 +587,7 @@
             )
             for o, line, block in zip(group, lines, blocks):
                 parts_xz[slot[o]], parts_yz[o] = line, block
-            if group == (0,):
+            if group == (1,):
                 around = borders(info, (plane_xy, plane_xz, plane_yz), lines[0])
         block = parts_yz[half]
         send_ahead, send_back = to_ring(block[:middle], 1), to_ring(block[middle:], -1)
@@ -581,9 +598,8 @@
             send_ahead, send_back = parts_yz[d] + send_ahead, parts_yz[-d] + send_back
             send_ahead, send_back = to_ring(send_ahead, 1), to_ring(send_back, -1)
 
-        grad_xy, far_xy, pieces = collect(
-            info, part_xy, plane_xy, xy_b, [parts_xz[i] for i in range(chips)], plane_xz.shape, zl
-        )
+        pieces = collect_xz(info, [parts_xz[i] for i in range(chips)], plane_xz.shape, zl)
+        grad_xy, far_xy = collect_xy(part_xy, plane_xy, xy_b)
         sides = [pieces[2 * s] + to_core(pieces[2 * s + 1]) for s in range(1, peers)]
         grads_xz = [to_gy(side, -s) for s, side in enumerate(sides, 1)]
         near_xz, far_xz = pieces[0], to_core(pieces[1])

time: 177 us -> 175 us (0.989)
  waiting for transfers between devices: 27.3 us -> 24.5 us
    ppermute x49, waiting for transfers between devices: 23 us -> 20.2 us  [send(): return lax.ppermute(x, BOTH, pairs)]
    pallas_call x2 -> x4, Pallas kernels: 6.41 us -> 7.19 us  [the longest x2 5.26 us: collect_xz(): pl.pallas_call(functools.partial(collect_xz_kernel, chips, peers, zl), in...]
    unnamed x33 -> x32, local copies, waits for them, and re-layouts: 3.65 us -> 2.87 us
  transfers between devices with their start and end apart: 55 -> 55, of which waited for: 12 -> 13; matrix products, arithmetic and copies ran while one was open for 1% -> 0% of each run, Pallas kernels for 34% -> 35%
where the time goes in v5:
time: 175 us; the launch traced here: 174 us
  Pallas kernels  83.9 us (48%)
  starting transfers between devices  59.9 us (34%)
  waiting for transfers between devices  24.5 us (14%)
  local copies, waits for them, and re-layouts  2.92 us (2%)
  between operations  1.97 us (1%)
    pallas_call x12, Pallas kernels, block_grads(): pl.pallas_call(functools.partial(grads_kernel, count, before is None), gr...  57.8 us
    ppermute x49, starting transfers between devices, send(): return lax.ppermute(x, BOTH, pairs)  51.7 us
    ppermute x49, waiting for transfers between devices, send(): return lax.ppermute(x, BOTH, pairs)  20.2 us
    pallas_call x2, Pallas kernels, spread(): pl.pallas_call(functools.partial(spread_kernel, chips, peers, zl), in_spe...  6.07 us
    pallas_call x2, Pallas kernels, collect_xz(): pl.pallas_call(functools.partial(collect_xz_kernel, chips, peers, zl), in...  5.26 us
    pallas_call x2, Pallas kernels, update_two(): pl.pallas_call(functools.partial(update_two_kernel, ends, count), in_spec...  4.39 us
    ppermute x2, waiting for transfers between devices, borders(): left = right = lax.ppermute(outs[2], 'gy', [(0, 1), (1, 0)])  4.27 us
    pallas_call x1, Pallas kernels, fixed_parts(): pl.pallas_call(functools.partial(fixed_kernel, chips, zl), in_specs=[SCAL...  4.1 us
  transfers between devices with their start and end apart: 55, of which 13 were waited for; matrix products, arithmetic and copies ran while one was open for 0% of the time, Pallas kernels for 35%

profile of v5, /device:TPU:0, one launch (start us, length us, event | category | flops | bytes accessed | tf_op | source)
XLA Modules:
  0.0 173.5 jit_solution(4496449822112680928)
XLA Ops:
  2.3 2.6 %collective-permute-start.6 = (f32[128,256]{1,0:T(8,128)S(1)}, f32[128,256]{1,0:T(8,128)S(1)}, u32[]{:S(2)}, u32[]{:S(2)}) collective-permute-start(f32[128,256]{1,0:T(8,128)S(1)} %shard_map.315.refs_1_), channel_id=1, source_target_pairs={{0,8},{1,9},{2,10},{3,11},{4,0},{5,1},{6,2},{7,3},{8,16},{9,17},{1... | collective-permute-start | bytes 393224 | tf_op jit(solution)/shard_map/ppermute | solution.py:41
  4.9 4.1 %collective-permute-done.6.refs_1_ = f32[128,256]{1,0:T(8,128)S(1)} collective-permute-done((f32[128,256]{1,0:T(8,128)S(1)}, f32[128,256]{1,0:T(8,128)S(1)}, u32[]{:S(2)}, u32[]{:S(2)}) %collective-permute-start.6) | collective-permute-done | bytes 131104 | tf_op jit(solution)/shard_map/ppermute | solution.py:41
  9.0 1.8 %collective-permute-start.10 = (f32[128,256]{1,0:T(8,128)S(1)}, f32[128,256]{1,0:T(8,128)S(1)}, u32[]{:S(2)}, u32[]{:S(2)}) collective-permute-start(f32[128,256]{1,0:T(8,128)S(1)} %collective-permute-done.6.refs_1_), channel_id=1, source_target_pairs={{0,8},{1,9},{2,10},{3,11},{4,0},{5,1},{6,2},{7,3},{8,16},{9,17},{1... | collective-permute-start | bytes 393224 | tf_op jit(solution)/shard_map/ppermute | solution.py:41
  11.0 1.7 collective-permute-start.3
  12.7 1.6 collective-permute-done.10.refs_2_
  14.3 1.5 collective-permute-start.12
  16.3 2.5 %collective-permute-done.3.refs_2_ = f32[32,16,64]{2,1,0:T(8,128)S(1)} collective-permute-done((f32[32,16,64]{2,1,0:T(8,128)}, f32[32,16,64]{2,1,0:T(8,128)S(1)}, u32[]{:S(2)}, u32[]{:S(2)}) %collective-permute-start.3) | collective-permute-done | bytes 131104 | tf_op jit(solution)/shard_map/ppermute | solution.py:41
  20.8 1.6 collective-permute-start.14
  24.9 3.0 %shard_map.314 = (f32[32,128,128]{2,1,0:T(8,128)S(1)}, f32[32,256]{1,0:T(8,128)S(1)}, f32[32,256]{1,0:T(8,128)S(1)}, f32[32,256]{1,0:T(8,128)S(1)}, f32[32,256]{...) custom-call(s32[2]{0:T(128)S(1)} %pad_add_fusion.4.info, ...), custom_call_target="tpu_custom_call" | custom-call | bytes 4194304 | tf_op jit(solution)/shard_map/pallas_call | solution.py:205
  28.0 4.1 %shard_map.313 = (bf16[32,128,128]{2,1,0:T(8,128)(2,1)S(1)}, bf16[256,256]{1,0:T(8,128)(2,1)S(1)}, bf16[256,256]{1,0:T(8,128)(2,1)S(1)}, bf16[256,256]{1,0:T(8,1...) custom-call(s32[2]{0:T(128)S(1)} %pad_add_fusion.4.info, f32[1]{0:T(128)S(6)} %copy.35.b_output, ...), custom_call_target="tpu_custom_call" | custom-call | bytes 4194304 | tf_op jit(solution)/shard_map/pallas_call | solution.py:130
  32.1 3.5 %shard_map.316 = (f32[32,128,128]{2,1,0:T(8,128)S(1)}, f32[32,256]{1,0:T(8,128)S(1)}, f32[128,256]{1,0:T(8,128)S(1)}) custom-call(s32[1]{0:T(128)} %constant.23.clone.slot, bf16[256,256]{1,0:T(8,128)(2,1)S(1)} %get-tuple-element.114.w_in, bf16[256,256]{1,0:T(8,128)(2,1)S(1)} %get-tuple-element.115.w_out, bf16[256,256]{1,0:T(8,128)(2,1)S(1)} %get-tuple-element.116.w_back, ...), custom_call_target="tpu_custom_call" | custom-call | flops 1610612736 | bytes 10485760 | tf_op jit(solution)/shard_map/pallas_call | solution.py:366
  35.6 3.6 %shard_map.317 = (f32[32,128,128]{2,1,0:T(8,128)S(1)}, f32[32,256]{1,0:T(8,128)S(1)}, f32[128,256]{1,0:T(8,128)S(1)}) custom-call(s32[1]{0:T(128)} %constant.24.clone.slot, bf16[256,256]{1,0:T(8,128)(2,1)S(1)} %get-tuple-element.114.w_in, bf16[256,256]{1,0:T(8,128)(2,1)S(1)} %get-tuple-element.115.w_out, bf16[256,256]{1,0:T(8,128)(2,1)S(1)} %get-tuple-element.116.w_back, ...), custom_call_target="tpu_custom_call" | custom-call | flops 1610612736 | bytes 10485760 | tf_op jit(solution)/shard_map/pallas_call | solution.py:366
  39.2 3.5 %shard_map.318 = (f32[32,128,128]{2,1,0:T(8,128)S(1)}, f32[32,256]{1,0:T(8,128)S(1)}, f32[128,256]{1,0:T(8,128)S(1)}) custom-call(s32[1]{0:T(128)} %constant.25.clone.slot, bf16[256,256]{1,0:T(8,128)(2,1)S(1)} %get-tuple-element.114.w_in, bf16[256,256]{1,0:T(8,128)(2,1)S(1)} %get-tuple-element.115.w_out, bf16[256,256]{1,0:T(8,128)(2,1)S(1)} %get-tuple-element.116.w_back, ...), custom_call_target="tpu_custom_call" | custom-call | flops 1610612736 | bytes 10485760 | tf_op jit(solution)/shard_map/pallas_call | solution.py:366
  42.8 3.6 %shard_map.320 = (f32[32,128,128]{2,1,0:T(8,128)S(1)}, f32[32,256]{1,0:T(8,128)S(1)}, f32[128,256]{1,0:T(8,128)S(1)}) custom-call(s32[1]{0:T(128)} %constant.26.clone.slot, bf16[256,256]{1,0:T(8,128)(2,1)S(1)} %get-tuple-element.114.w_in, bf16[256,256]{1,0:T(8,128)(2,1)S(1)} %get-tuple-element.115.w_out, bf16[256,256]{1,0:T(8,128)(2,1)S(1)} %get-tuple-element.116.w_back, ...), custom_call_target="tpu_custom_call" | custom-call | flops 1610612736 | bytes 10485760 | tf_op jit(solution)/shard_map/pallas_call | solution.py:366
  48.5 7.3 %shard_map.321 = (f32[32,128,128]{2,1,0:T(8,128)S(1)}, f32[32,256]{1,0:T(8,128)S(1)}, f32[32,256]{1,0:T(8,128)S(1)}, f32[128,256]{1,0:T(8,128)S(1)}, f32[128,256]{1,0:T(8,128)S(1)}) custom-call(s32[1]{0:T(128)} %constant.27.clone.slot, bf16[256,256]{1,0:T(8,128)(2,1)S(1)} %get-tuple-element.114.w_in, bf16[256,256]{1,0:T(8,128)(2,1)S(1)} %get-tuple-element.115.w_out, ...), custom_call_target="tpu_custom_call" | custom-call | flops 3221225472 | bytes 20971520 | tf_op jit(solution)/shard_map/pallas_call | solution.py:366
  55.8 7.3 %shard_map.322 = (f32[32,128,128]{2,1,0:T(8,128)S(1)}, f32[32,256]{1,0:T(8,128)S(1)}, f32[32,256]{1,0:T(8,128)S(1)}, f32[128,256]{1,0:T(8,128)S(1)}, f32[128,256]{1,0:T(8,128)S(1)}) custom-call(s32[1]{0:T(128)} %constant.28.clone.slot, bf16[256,256]{1,0:T(8,128)(2,1)S(1)} %get-tuple-element.114.w_in, bf16[256,256]{1,0:T(8,128)(2,1)S(1)} %get-tuple-element.115.w_out, ...), custom_call_target="tpu_custom_call" | custom-call | flops 3221225472 | bytes 20971520 | tf_op jit(solution)/shard_map/pallas_call | solution.py:366
  64.3 2.6 %shard_map.324 = (f32[32,16,64]{2,1,0:T(8,128)S(1)}, f32[32,16,64]{2,1,0:T(8,128)S(1)}, f32[32,16,64]{2,1,0:T(8,128)S(1)}, f32[32,16,64]{2,1,0:T(8,128)S(1)}) custom-call(s32[2]{0:T(128)S(1)} %pad_add_fusion.4.info, f32[32,256]{1,0:T(8,128)S(1)} %get-tuple-element.141.refs_0_, f32[32,256]{1,0:T(8,128)S(1)} %get-tuple-element.142.refs_1_, ...), custom_call_target="tpu_custom_call" | custom-call | bytes 4194304 | tf_op jit(solution)/shard_map/pallas_call | solution.py:269
  67.5 1.6 collective-permute-start.21
  70.4 1.6 collective-permute-start.9
  71.9 2.1 %collective-permute-done.9.left.right = f32[1,1280]{1,0:T(1,128)S(1)} collective-permute-done((f32[1,1280]{1,0:T(1,128)S(1)}, f32[1,1280]{1,0:T(1,128)S(1)}, u32[]{:S(2)}, u32[]{:S(2)}) %collective-permute-start.9) | collective-permute-done | bytes 5152 | tf_op jit(solution)/shard_map/ppermute | solution.py:526
  76.7 2.1 %collective-permute-start.17 = (f32[32,16,64]{2,1,0:T(8,128)S(1)}, f32[32,16,64]{2,1,0:T(8,128)S(1)}, u32[]{:S(2)}, u32[]{:S(2)}) collective-permute-start(f32[32,16,64]{2,1,0:T(8,128)S(1)} %get-tuple-element.149), channel_id=1, source_target_pairs={{0,2},{1,3},{2,0},{3,1},{4,6},{5,7},{6,4},{7,5},{8,10},{9,11},{10,... | collective-permute-start | bytes 393224 | tf_op jit(solution)/shard_map/ppermute | solution.py:41
  80.4 3.5 %collective-permute-start.22 = (f32[128,256]{1,0:T(8,128)S(1)}, f32[128,256]{1,0:T(8,128)S(1)}, u32[]{:S(2)}, u32[]{:S(2)}) collective-permute-start(f32[128,256]{1,0:T(8,128)S(1)} %add.52), channel_id=1, source_target_pairs={{0,8},{1,9},{2,10},{3,11},{4,0},{5,1},{6,2},{7,3},{8,16},{9,17},{1... | collective-permute-start | bytes 393224 | tf_op jit(solution)/shard_map/ppermute | solution.py:41
  84.0 3.1 %collective-permute-done.19.refs_10_ = f32[32,16,64]{2,1,0:T(8,128)S(1)} collective-permute-done((f32[32,16,64]{2,1,0:T(8,128)S(1)}, f32[32,16,64]{2,1,0:T(8,128)S(1)}, u32[]{:S(2)}, u32[]{:S(2)}) %collective-permute-start.19) | collective-permute-done | bytes 131104 | tf_op jit(solution)/shard_map/ppermute | solution.py:41
  87.2 1.8 %shard_map.325 = (f32[32,16,128]{2,1,0:T(8,128)S(1)}, f32[32,16,128]{2,1,0:T(8,128)S(1)}, f32[32,16,128]{2,1,0:T(8,128)S(1)}, f32[32,16,64]{2,1,0:T(8,128)S(1)},...) custom-call(s32[2]{0:T(128)S(1)} %pad_add_fusion.4.info, f32[32,1,320]{2,1,0:T(1,128)S(1)} %collective-permute-done.7.above, ...), custom_call_target="tpu_custom_call" | custom-call | bytes 4194304 | tf_op jit(solution)/shard_map/pallas_call | solution.py:449
  88.9 1.6 collective-permute-start.30
  90.5 3.9 %collective-permute-start.23 = (f32[128,256]{1,0:T(8,128)S(1)}, f32[128,256]{1,0:T(8,128)S(1)}, u32[]{:S(2)}, u32[]{:S(2)}) collective-permute-start(f32[128,256]{1,0:T(8,128)S(1)} %add.53), channel_id=1, source_target_pairs={{0,8},{1,9},{2,10},{3,11},{4,0},{5,1},{6,2},{7,3},{8,16},{9,17},{1... | collective-permute-start | bytes 393224 | tf_op jit(solution)/shard_map/ppermute | solution.py:41
  96.9 2.5 %collective-permute-done.27.d = f32[128,256]{1,0:T(8,128)S(1)} collective-permute-done((f32[128,256]{1,0:T(8,128)S(1)}, f32[128,256]{1,0:T(8,128)S(1)}, u32[]{:S(2)}, u32[]{:S(2)}) %collective-permute-start.27) | collective-permute-done | bytes 131104 | tf_op jit(solution)/shard_map/ppermute | solution.py:41
  100.5 1.6 collective-permute-start.33
  102.6 3.1 %shard_map.327 = (f32[32,128,128]{2,1,0:T(8,128)S(1)}, f32[32,256]{1,0:T(8,128)S(1)}, f32[32,256]{1,0:T(8,128)S(1)}, f32[32,256]{1,0:T(8,128)S(1)}, f32[32,256]{...) custom-call(s32[2]{0:T(128)S(1)} %pad_add_fusion.4.info, ...), custom_call_target="tpu_custom_call" | custom-call | bytes 4194304 | tf_op jit(solution)/shard_map/pallas_call | solution.py:205
  105.6 2.0 %collective-permute-start.37 = (f32[128,256]{1,0:T(8,128)S(1)}, f32[128,256]{1,0:T(8,128)S(1)}, u32[]{:S(2)}, u32[]{:S(2)}) collective-permute-start(f32[128,256]{1,0:T(8,128)S(1)} %collective-permute-done.33.refs_1_), channel_id=1, source_target_pairs={{0,8},{1,9},{2,10},{3,11},{4,0},{5,1},{6,2},{7,3},{8,16},{9,17},{1... | collective-permute-start | bytes 393224 | tf_op jit(solution)/shard_map/ppermute | solution.py:41
  107.7 3.5 %shard_map.328 = (f32[32,128,128]{2,1,0:T(8,128)S(1)}, f32[32,256]{1,0:T(8,128)S(1)}, f32[128,256]{1,0:T(8,128)S(1)}) custom-call(s32[1]{0:T(128)} %constant.23.clone.slot, bf16[256,256]{1,0:T(8,128)(2,1)S(1)} %get-tuple-element.114.w_in, bf16[256,256]{1,0:T(8,128)(2,1)S(1)} %get-tuple-element.115.w_out, bf16[256,256]{1,0:T(8,128)(2,1)S(1)} %get-tuple-element.116.w_back, ...), custom_call_target="tpu_custom_call" | custom-call | flops 1610612736 | bytes 10485760 | tf_op jit(solution)/shard_map/pallas_call | solution.py:366
  111.2 2.0 %collective-permute-start.39 = (f32[128,256]{1,0:T(8,128)S(1)}, f32[128,256]{1,0:T(8,128)S(1)}, u32[]{:S(2)}, u32[]{:S(2)}) collective-permute-start(f32[128,256]{1,0:T(8,128)S(1)} %collective-permute-done.37.refs_2_), channel_id=1, source_target_pairs={{0,8},{1,9},{2,10},{3,11},{4,0},{5,1},{6,2},{7,3},{8,16},{9,17},{1... | collective-permute-start | bytes 393224 | tf_op jit(solution)/shard_map/ppermute | solution.py:41
  113.3 3.6 %shard_map.329 = (f32[32,128,128]{2,1,0:T(8,128)S(1)}, f32[32,256]{1,0:T(8,128)S(1)}, f32[128,256]{1,0:T(8,128)S(1)}) custom-call(s32[1]{0:T(128)} %constant.24.clone.slot, bf16[256,256]{1,0:T(8,128)(2,1)S(1)} %get-tuple-element.114.w_in, bf16[256,256]{1,0:T(8,128)(2,1)S(1)} %get-tuple-element.115.w_out, bf16[256,256]{1,0:T(8,128)(2,1)S(1)} %get-tuple-element.116.w_back, ...), custom_call_target="tpu_custom_call" | custom-call | flops 1610612736 | bytes 10485760 | tf_op jit(solution)/shard_map/pallas_call | solution.py:366
  116.9 2.0 %collective-permute-start.41 = (f32[64,256]{1,0:T(8,128)S(1)}, f32[64,256]{1,0:T(8,128)S(1)}, u32[]{:S(2)}, u32[]{:S(2)}) collective-permute-start(f32[64,256]{1,0:T(8,128)S(1)} %slice.34), channel_id=1, source_target_pairs={{0,8},{1,9},{2,10},{3,11},{4,0},{5,1},{6,2},{7,3},{8,16},{9,17},{1... | collective-permute-start | bytes 196616 | tf_op jit(solution)/shard_map/ppermute | solution.py:41
  119.1 3.6 %shard_map.330 = (f32[32,128,128]{2,1,0:T(8,128)S(1)}, f32[32,256]{1,0:T(8,128)S(1)}, f32[128,256]{1,0:T(8,128)S(1)}) custom-call(s32[1]{0:T(128)} %constant.25.clone.slot, bf16[256,256]{1,0:T(8,128)(2,1)S(1)} %get-tuple-element.114.w_in, bf16[256,256]{1,0:T(8,128)(2,1)S(1)} %get-tuple-element.115.w_out, bf16[256,256]{1,0:T(8,128)(2,1)S(1)} %get-tuple-element.116.w_back, ...), custom_call_target="tpu_custom_call" | custom-call | flops 1610612736 | bytes 10485760 | tf_op jit(solution)/shard_map/pallas_call | solution.py:366
  123.3 3.6 %shard_map.332 = (f32[32,128,128]{2,1,0:T(8,128)S(1)}, f32[32,256]{1,0:T(8,128)S(1)}, f32[128,256]{1,0:T(8,128)S(1)}) custom-call(s32[1]{0:T(128)} %constant.26.clone.slot, bf16[256,256]{1,0:T(8,128)(2,1)S(1)} %get-tuple-element.114.w_in, bf16[256,256]{1,0:T(8,128)(2,1)S(1)} %get-tuple-element.115.w_out, bf16[256,256]{1,0:T(8,128)(2,1)S(1)} %get-tuple-element.116.w_back, ...), custom_call_target="tpu_custom_call" | custom-call | flops 1610612736 | bytes 10485760 | tf_op jit(solution)/shard_map/pallas_call | solution.py:366
  127.1 1.9 %collective-permute-start.47 = (f32[64,256]{1,0:T(8,128)S(1)}, f32[64,256]{1,0:T(8,128)S(1)}, u32[]{:S(2)}, u32[]{:S(2)}) collective-permute-start(f32[64,256]{1,0:T(8,128)S(1)} %get-tuple-element.220), channel_id=1, source_target_pairs={{0,8},{1,9},{2,10},{3,11},{4,0},{5,1},{6,2},{7,3},{8,16},{9,17},{1... | collective-permute-start | bytes 196616 | tf_op jit(solution)/shard_map/ppermute | solution.py:41
  129.0 7.3 %shard_map.333 = (f32[32,128,128]{2,1,0:T(8,128)S(1)}, f32[32,256]{1,0:T(8,128)S(1)}, f32[32,256]{1,0:T(8,128)S(1)}, f32[128,256]{1,0:T(8,128)S(1)}, f32[128,256]{1,0:T(8,128)S(1)}) custom-call(s32[1]{0:T(128)} %constant.27.clone.slot, bf16[256,256]{1,0:T(8,128)(2,1)S(1)} %get-tuple-element.114.w_in, bf16[256,256]{1,0:T(8,128)(2,1)S(1)} %get-tuple-element.115.w_out, ...), custom_call_target="tpu_custom_call" | custom-call | flops 3221225472 | bytes 20971520 | tf_op jit(solution)/shard_map/pallas_call | solution.py:366
  136.3 1.6 collective-permute-start.48
  138.5 7.3 %shard_map.334 = (f32[32,128,128]{2,1,0:T(8,128)S(1)}, f32[32,256]{1,0:T(8,128)S(1)}, f32[32,256]{1,0:T(8,128)S(1)}, f32[128,256]{1,0:T(8,128)S(1)}, f32[128,256]{1,0:T(8,128)S(1)}) custom-call(s32[1]{0:T(128)} %constant.28.clone.slot, bf16[256,256]{1,0:T(8,128)(2,1)S(1)} %get-tuple-element.114.w_in, bf16[256,256]{1,0:T(8,128)(2,1)S(1)} %get-tuple-element.115.w_out, ...), custom_call_target="tpu_custom_call" | custom-call | flops 3221225472 | bytes 20971520 | tf_op jit(solution)/shard_map/pallas_call | solution.py:366
  145.8 2.7 %shard_map.336 = (f32[32,16,64]{2,1,0:T(8,128)S(1)}, f32[32,16,64]{2,1,0:T(8,128)S(1)}, f32[32,16,64]{2,1,0:T(8,128)S(1)}, f32[32,16,64]{2,1,0:T(8,128)S(1)}) custom-call(s32[2]{0:T(128)S(1)} %pad_add_fusion.4.info, f32[32,256]{1,0:T(8,128)S(1)} %get-tuple-element.189.refs_0_, f32[32,256]{1,0:T(8,128)S(1)} %get-tuple-element.190.refs_1_, ...), custom_call_target="tpu_custom_call" | custom-call | bytes 4194304 | tf_op jit(solution)/shard_map/pallas_call | solution.py:269
  150.1 1.6 collective-permute-start.49
  153.0 1.6 collective-permute-start.36
  154.5 2.1 %collective-permute-done.36.left.right = f32[1,1280]{1,0:T(1,128)S(1)} collective-permute-done((f32[1,1280]{1,0:T(1,128)S(1)}, f32[1,1280]{1,0:T(1,128)S(1)}, u32[]{:S(2)}, u32[]{:S(2)}) %collective-permute-start.36) | collective-permute-done | bytes 5152 | tf_op jit(solution)/shard_map/ppermute | solution.py:526
  162.4 4.2 %collective-permute-start.50 = (f32[128,256]{1,0:T(8,128)S(1)}, f32[128,256]{1,0:T(8,128)S(1)}, u32[]{:S(2)}, u32[]{:S(2)}) collective-permute-start(f32[128,256]{1,0:T(8,128)S(1)} %add.60), channel_id=1, source_target_pairs={{0,8},{1,9},{2,10},{3,11},{4,0},{5,1},{6,2},{7,3},{8,16},{9,17},{1... | collective-permute-start | bytes 393224 | tf_op jit(solution)/shard_map/ppermute | solution.py:41
  166.6 2.6 %collective-permute-done.46.refs_10_ = f32[32,16,64]{2,1,0:T(8,128)S(1)} collective-permute-done((f32[32,16,64]{2,1,0:T(8,128)S(1)}, f32[32,16,64]{2,1,0:T(8,128)S(1)}, u32[]{:S(2)}, u32[]{:S(2)}) %collective-permute-start.46) | collective-permute-done | bytes 131104 | tf_op jit(solution)/shard_map/ppermute | solution.py:41
  169.1 2.6 %shard_map.337 = (f32[32,16,128]{2,1,0:T(8,128)}, f32[32,16,128]{2,1,0:T(8,128)}, f32[32,16,128]{2,1,0:T(8,128)}, f32[32,16,64]{2,1,0:T(8,128)}, f32[32,16,64]{2,1,0:T(8,128)}, /*index=5*/f32[32,16,64]{2,1,0:T(8,128)}) custom-call(s32[2]{0:T(128)S(1)} %pad_add_fusion.4.info, f32[32,1,320]{2,1,0:T(1,128)S(1)} %collective-permute-done.34.above, ...), custom_call_target="tpu_custom_call" | custom-call | bytes 4194304 | tf_op jit(solution)/shard_map/pallas_call | solution.py:449
  171.8 1.7 %shard_map.338 = (f32[32,8,128]{2,1,0:T(8,128)}, f32[32,8,128]{2,1,0:T(8,128)}, f32[32,8,128]{2,1,0:T(8,128)}, f32[128,256]{1,0:T(8,128)}) custom-call(s32[2]{0:T(128)S(1)} %pad_add_fusion.4.info, f32[32,1,320]{2,1,0:T(1,128)S(1)} %collective-permute-done.34.above, f32[32,1,320]{2,1,0:T(1,128)S(1)} %collective-permute-done.35.below, ...), custom_call_target="tpu_custom_call" | custom-call | bytes 2097152 | tf_op jit(solution)/shard_map/pallas_call | solution.py:477
  (143 shorter events, 29.6 us)
Async XLA Ops:
  0.6 27.3 %collective-permute-start = (f32[16,128,128]{2,1,0:T(8,128)}, f32[16,128,128]{2,1,0:T(8,128)S(1)}, u32[]{:S(2)}, u32[]{:S(2)}) collective-permute-start(f32[16,128,128]{2,1,0:T(8,128)} %target_a.1), channel_id=1, source_target_pairs={{0,2},{1,3},{2,0},{3,1},{4,6},{5,7},{6,4},{7,5},{8,10},{9,11},{10,... | collective-permute-start | bytes 3145736 | tf_op jit(solution)/shard_map/ppermute | solution.py:41
  2.3 6.7 %collective-permute-start.6 = (f32[128,256]{1,0:T(8,128)S(1)}, f32[128,256]{1,0:T(8,128)S(1)}, u32[]{:S(2)}, u32[]{:S(2)}) collective-permute-start(f32[128,256]{1,0:T(8,128)S(1)} %shard_map.315.refs_1_), channel_id=1, source_target_pairs={{0,8},{1,9},{2,10},{3,11},{4,0},{5,1},{6,2},{7,3},{8,16},{9,17},{1... | collective-permute-start | bytes 393224 | tf_op jit(solution)/shard_map/ppermute | solution.py:41
  4.9 5.9 %collective-permute-start.5 = (f32[128,256]{1,0:T(8,128)S(1)}, f32[128,256]{1,0:T(8,128)S(1)}, u32[]{:S(2)}, u32[]{:S(2)}) collective-permute-start(f32[128,256]{1,0:T(8,128)S(1)} %shard_map.315.refs_1_), channel_id=1, source_target_pairs={{0,4},{1,5},{2,6},{3,7},{4,12},{5,13},{6,14},{7,15},{8,0},{9,1},{1... | collective-permute-start | bytes 393224 | tf_op jit(solution)/shard_map/ppermute | solution.py:41
  9.0 5.3 %collective-permute-start.10 = (f32[128,256]{1,0:T(8,128)S(1)}, f32[128,256]{1,0:T(8,128)S(1)}, u32[]{:S(2)}, u32[]{:S(2)}) collective-permute-start(f32[128,256]{1,0:T(8,128)S(1)} %collective-permute-done.6.refs_1_), channel_id=1, source_target_pairs={{0,8},{1,9},{2,10},{3,11},{4,0},{5,1},{6,2},{7,3},{8,16},{9,17},{1... | collective-permute-start | bytes 393224 | tf_op jit(solution)/shard_map/ppermute | solution.py:41
  10.8 5.0 %collective-permute-start.11 = (f32[128,256]{1,0:T(8,128)S(1)}, f32[128,256]{1,0:T(8,128)S(1)}, u32[]{:S(2)}, u32[]{:S(2)}) collective-permute-start(f32[128,256]{1,0:T(8,128)S(1)} %collective-permute-done.5.refs_1_), channel_id=1, source_target_pairs={{0,4},{1,5},{2,6},{3,7},{4,12},{5,13},{6,14},{7,15},{8,0},{9,1},{1... | collective-permute-start | bytes 393224 | tf_op jit(solution)/shard_map/ppermute | solution.py:41
  11.0 7.8 %collective-permute-start.3 = (f32[32,16,64]{2,1,0:T(8,128)}, f32[32,16,64]{2,1,0:T(8,128)S(1)}, u32[]{:S(2)}, u32[]{:S(2)}) collective-permute-start(f32[32,16,64]{2,1,0:T(8,128)} %refs_5_.1), channel_id=1, source_target_pairs={{0,1},{1,0},{2,3},{3,2},{4,5},{5,4},{6,7},{7,6},{8,9},{9,8},{10,11... | collective-permute-start | bytes 393224 | tf_op jit(solution)/shard_map/ppermute | solution.py:41
  12.7 10.2 %collective-permute-start.1 = (f32[32,16,128]{2,1,0:T(8,128)}, f32[32,16,128]{2,1,0:T(8,128)S(1)}, u32[]{:S(2)}, u32[]{:S(2)}) collective-permute-start(f32[32,16,128]{2,1,0:T(8,128)} %refs_0_.3), channel_id=1, source_target_pairs={{0,2},{1,3},{2,0},{3,1},{4,6},{5,7},{6,4},{7,5},{8,10},{9,11},{10,... | collective-permute-start | bytes 786440 | tf_op jit(solution)/shard_map/ppermute | solution.py:41
  15.8 5.0 %collective-permute-start.13 = (f32[128,256]{1,0:T(8,128)S(1)}, f32[128,256]{1,0:T(8,128)S(1)}, u32[]{:S(2)}, u32[]{:S(2)}) collective-permute-start(f32[128,256]{1,0:T(8,128)S(1)} %collective-permute-done.11.refs_3_), channel_id=1, source_target_pairs={{0,4},{1,5},{2,6},{3,7},{4,12},{5,13},{6,14},{7,15},{8,0},{9,1},{1... | collective-permute-start | bytes 393224 | tf_op jit(solution)/shard_map/ppermute | solution.py:41
  20.8 7.1 %collective-permute-start.14 = (f32[64,256]{1,0:T(8,128)S(1)}, f32[64,256]{1,0:T(8,128)S(1)}, u32[]{:S(2)}, u32[]{:S(2)}) collective-permute-start(f32[64,256]{1,0:T(8,128)S(1)} %slice.32), channel_id=1, source_target_pairs={{0,8},{1,9},{2,10},{3,11},{4,0},{5,1},{6,2},{7,3},{8,16},{9,17},{1... | collective-permute-start | bytes 196616 | tf_op jit(solution)/shard_map/ppermute | solution.py:41
  22.4 5.5 %collective-permute-start.15 = (f32[64,256]{1,0:T(8,128)S(1)}, f32[64,256]{1,0:T(8,128)S(1)}, u32[]{:S(2)}, u32[]{:S(2)}) collective-permute-start(f32[64,256]{1,0:T(8,128)S(1)} %slice.33), channel_id=1, source_target_pairs={{0,4},{1,5},{2,6},{3,7},{4,12},{5,13},{6,14},{7,15},{8,0},{9,1},{1... | collective-permute-start | bytes 196616 | tf_op jit(solution)/shard_map/ppermute | solution.py:41
  46.4 22.7 %collective-permute-start.24 = (f32[64,256]{1,0:T(8,128)S(1)}, f32[64,256]{1,0:T(8,128)S(1)}, u32[]{:S(2)}, u32[]{:S(2)}) collective-permute-start(f32[64,256]{1,0:T(8,128)S(1)} %get-tuple-element.221), channel_id=1, source_target_pairs={{0,4},{1,5},{2,6},{3,7},{4,12},{5,13},{6,14},{7,15},{8,0},{9,1},{1... | collective-permute-start | bytes 196616 | tf_op jit(solution)/shard_map/ppermute | solution.py:41
  47.2 20.3 %collective-permute-start.20 = (f32[64,256]{1,0:T(8,128)S(1)}, f32[64,256]{1,0:T(8,128)S(1)}, u32[]{:S(2)}, u32[]{:S(2)}) collective-permute-start(f32[64,256]{1,0:T(8,128)S(1)} %get-tuple-element.222), channel_id=1, source_target_pairs={{0,8},{1,9},{2,10},{3,11},{4,0},{5,1},{6,2},{7,3},{8,16},{9,17},{1... | collective-permute-start | bytes 196616 | tf_op jit(solution)/shard_map/ppermute | solution.py:41
  64.2 23.0 %collective-permute-start.16 = (f32[32,16,128]{2,1,0:T(8,128)S(1)}, f32[32,16,128]{2,1,0:T(8,128)S(1)}, u32[]{:S(2)}, u32[]{:S(2)}) collective-permute-start(f32[32,16,128]{2,1,0:T(8,128)S(1)} %get-tuple-element.140), channel_id=1, source_target_pairs={{0,2},{1,3},{2,0},{3,1},{4,6},{5,7},{6,4},{7,5},{8,10},{9,11},{10,... | collective-permute-start | bytes 786440 | tf_op jit(solution)/shard_map/ppermute | solution.py:41
  66.9 8.5 %collective-permute-start.18 = (f32[32,16,64]{2,1,0:T(8,128)S(1)}, f32[32,16,64]{2,1,0:T(8,128)S(1)}, u32[]{:S(2)}, u32[]{:S(2)}) collective-permute-start(f32[32,16,64]{2,1,0:T(8,128)S(1)} %get-tuple-element.151), channel_id=1, source_target_pairs={{0,2},{1,3},{2,0},{3,1},{4,6},{5,7},{6,4},{7,5},{8,10},{9,11},{10,... | collective-permute-start | bytes 393224 | tf_op jit(solution)/shard_map/ppermute | solution.py:41
  67.5 11.4 %collective-permute-start.21 = (f32[128,256]{1,0:T(8,128)S(1)}, f32[128,256]{1,0:T(8,128)S(1)}, u32[]{:S(2)}, u32[]{:S(2)}) collective-permute-start(f32[128,256]{1,0:T(8,128)S(1)} %pad_add_fusion.3), channel_id=1, source_target_pairs={{0,8},{1,9},{2,10},{3,11},{4,0},{5,1},{6,2},{7,3},{8,16},{9,17},{1... | collective-permute-start | bytes 393224 | tf_op jit(solution)/shard_map/ppermute | solution.py:41
  69.1 11.3 %collective-permute-start.25 = (f32[128,256]{1,0:T(8,128)S(1)}, f32[128,256]{1,0:T(8,128)S(1)}, u32[]{:S(2)}, u32[]{:S(2)}) collective-permute-start(f32[128,256]{1,0:T(8,128)S(1)} %pad_add_fusion.2), channel_id=1, source_target_pairs={{0,4},{1,5},{2,6},{3,7},{4,12},{5,13},{6,14},{7,15},{8,0},{9,1},{1... | collective-permute-start | bytes 393224 | tf_op jit(solution)/shard_map/ppermute | solution.py:41
  75.4 8.6 %collective-permute-start.8 = (f32[32,1,320]{2,1,0:T(1,128)S(1)}, f32[32,1,320]{2,1,0:T(1,128)S(1)}, u32[]{:S(2)}, u32[]{:S(2)}) collective-permute-start(f32[32,1,320]{2,1,0:T(1,128)S(1)} %get-tuple-element.128), channel_id=1, source_target_pairs={{2,0},{4,2},{6,4},{8,6},{10,8},{12,10},{14,12},{16,14},{18,16},{20... | collective-permute-start | bytes 122888 | tf_op jit(solution)/shard_map/ppermute | solution.py:524
  76.7 7.3 %collective-permute-start.17 = (f32[32,16,64]{2,1,0:T(8,128)S(1)}, f32[32,16,64]{2,1,0:T(8,128)S(1)}, u32[]{:S(2)}, u32[]{:S(2)}) collective-permute-start(f32[32,16,64]{2,1,0:T(8,128)S(1)} %get-tuple-element.149), channel_id=1, source_target_pairs={{0,2},{1,3},{2,0},{3,1},{4,6},{5,7},{6,4},{7,5},{8,10},{9,11},{10,... | collective-permute-start | bytes 393224 | tf_op jit(solution)/shard_map/ppermute | solution.py:41
  78.8 8.3 %collective-permute-start.19 = (f32[32,16,64]{2,1,0:T(8,128)S(1)}, f32[32,16,64]{2,1,0:T(8,128)S(1)}, u32[]{:S(2)}, u32[]{:S(2)}) collective-permute-start(f32[32,16,64]{2,1,0:T(8,128)S(1)} %add.50), channel_id=1, source_target_pairs={{0,1},{1,0},{2,3},{3,2},{4,5},{5,4},{6,7},{7,6},{8,9},{9,8},{10,11... | collective-permute-start | bytes 393224 | tf_op jit(solution)/shard_map/ppermute | solution.py:41
  80.4 10.1 %collective-permute-start.22 = (f32[128,256]{1,0:T(8,128)S(1)}, f32[128,256]{1,0:T(8,128)S(1)}, u32[]{:S(2)}, u32[]{:S(2)}) collective-permute-start(f32[128,256]{1,0:T(8,128)S(1)} %add.52), channel_id=1, source_target_pairs={{0,8},{1,9},{2,10},{3,11},{4,0},{5,1},{6,2},{7,3},{8,16},{9,17},{1... | collective-permute-start | bytes 393224 | tf_op jit(solution)/shard_map/ppermute | solution.py:41
  84.0 10.4 %collective-permute-start.26 = (f32[128,256]{1,0:T(8,128)S(1)}, f32[128,256]{1,0:T(8,128)S(1)}, u32[]{:S(2)}, u32[]{:S(2)}) collective-permute-start(f32[128,256]{1,0:T(8,128)S(1)} %add.55), channel_id=1, source_target_pairs={{0,4},{1,5},{2,6},{3,7},{4,12},{5,13},{6,14},{7,15},{8,0},{9,1},{1... | collective-permute-start | bytes 393224 | tf_op jit(solution)/shard_map/ppermute | solution.py:41
  88.9 7.5 %collective-permute-start.30 = (f32[32,16,64]{2,1,0:T(8,128)S(1)}, f32[32,16,64]{2,1,0:T(8,128)S(1)}, u32[]{:S(2)}, u32[]{:S(2)}) collective-permute-start(f32[32,16,64]{2,1,0:T(8,128)S(1)} %get-tuple-element.153.refs_0_.xz.refs_5_), channel_id=1, source_target_pairs={{0,1},{1,0},{2,3},{3,2},{4,5},{5,4},{6,7},{7,6},{8,9},{9,8},{10,11... | collective-permute-start | bytes 393224 | tf_op jit(solution)/shard_map/ppermute | solution.py:41
  90.5 6.4 %collective-permute-start.23 = (f32[128,256]{1,0:T(8,128)S(1)}, f32[128,256]{1,0:T(8,128)S(1)}, u32[]{:S(2)}, u32[]{:S(2)}) collective-permute-start(f32[128,256]{1,0:T(8,128)S(1)} %add.53), channel_id=1, source_target_pairs={{0,8},{1,9},{2,10},{3,11},{4,0},{5,1},{6,2},{7,3},{8,16},{9,17},{1... | collective-permute-start | bytes 393224 | tf_op jit(solution)/shard_map/ppermute | solution.py:41
  94.4 5.0 %collective-permute-start.27 = (f32[128,256]{1,0:T(8,128)S(1)}, f32[128,256]{1,0:T(8,128)S(1)}, u32[]{:S(2)}, u32[]{:S(2)}) collective-permute-start(f32[128,256]{1,0:T(8,128)S(1)} %add.56), channel_id=1, source_target_pairs={{0,4},{1,5},{2,6},{3,7},{4,12},{5,13},{6,14},{7,15},{8,0},{9,1},{1... | collective-permute-start | bytes 393224 | tf_op jit(solution)/shard_map/ppermute | solution.py:41
  94.5 8.1 %collective-permute-start.28 = (f32[32,16,128]{2,1,0:T(8,128)S(1)}, f32[32,16,128]{2,1,0:T(8,128)S(1)}, u32[]{:S(2)}, u32[]{:S(2)}) collective-permute-start(f32[32,16,128]{2,1,0:T(8,128)S(1)} %get-tuple-element.152.xy_a.xy.refs_0_), channel_id=1, source_target_pairs={{0,2},{1,3},{2,0},{3,1},{4,6},{5,7},{6,4},{7,5},{8,10},{9,11},{10,... | collective-permute-start | bytes 786440 | tf_op jit(solution)/shard_map/ppermute | solution.py:41
  94.6 8.0 %collective-permute-start.29 = (f32[32,16,64]{2,1,0:T(8,128)S(1)}, f32[32,16,64]{2,1,0:T(8,128)S(1)}, u32[]{:S(2)}, u32[]{:S(2)}) collective-permute-start(f32[32,16,64]{2,1,0:T(8,128)S(1)} %get-tuple-element.153.refs_0_.xz.refs_5_), channel_id=1, source_target_pairs={{0,2},{1,3},{2,0},{3,1},{4,6},{5,7},{6,4},{7,5},{8,10},{9,11},{10,... | collective-permute-start | bytes 393224 | tf_op jit(solution)/shard_map/ppermute | solution.py:41
  96.4 6.1 %collective-permute-start.31 = (f32[32,16,64]{2,1,0:T(8,128)S(1)}, f32[32,16,64]{2,1,0:T(8,128)S(1)}, u32[]{:S(2)}, u32[]{:S(2)}) collective-permute-start(f32[32,16,64]{2,1,0:T(8,128)S(1)} %collective-permute-done.30.refs_2_), channel_id=1, source_target_pairs={{0,2},{1,3},{2,0},{3,1},{4,6},{5,7},{6,4},{7,5},{8,10},{9,11},{10,... | collective-permute-start | bytes 393224 | tf_op jit(solution)/shard_map/ppermute | solution.py:41
  100.5 5.1 %collective-permute-start.33 = (f32[128,256]{1,0:T(8,128)S(1)}, f32[128,256]{1,0:T(8,128)S(1)}, u32[]{:S(2)}, u32[]{:S(2)}) collective-permute-start(f32[128,256]{1,0:T(8,128)S(1)} %get-tuple-element.165.refs_1_), channel_id=1, source_target_pairs={{0,8},{1,9},{2,10},{3,11},{4,0},{5,1},{6,2},{7,3},{8,16},{9,17},{1... | collective-permute-start | bytes 393224 | tf_op jit(solution)/shard_map/ppermute | solution.py:41
  102.1 5.5 %collective-permute-start.32 = (f32[128,256]{1,0:T(8,128)S(1)}, f32[128,256]{1,0:T(8,128)S(1)}, u32[]{:S(2)}, u32[]{:S(2)}) collective-permute-start(f32[128,256]{1,0:T(8,128)S(1)} %get-tuple-element.165.refs_1_), channel_id=1, source_target_pairs={{0,4},{1,5},{2,6},{3,7},{4,12},{5,13},{6,14},{7,15},{8,0},{9,1},{1... | collective-permute-start | bytes 393224 | tf_op jit(solution)/shard_map/ppermute | solution.py:41
  105.6 5.6 %collective-permute-start.37 = (f32[128,256]{1,0:T(8,128)S(1)}, f32[128,256]{1,0:T(8,128)S(1)}, u32[]{:S(2)}, u32[]{:S(2)}) collective-permute-start(f32[128,256]{1,0:T(8,128)S(1)} %collective-permute-done.33.refs_1_), channel_id=1, source_target_pairs={{0,8},{1,9},{2,10},{3,11},{4,0},{5,1},{6,2},{7,3},{8,16},{9,17},{1... | collective-permute-start | bytes 393224 | tf_op jit(solution)/shard_map/ppermute | solution.py:41
  107.6 5.6 %collective-permute-start.38 = (f32[128,256]{1,0:T(8,128)S(1)}, f32[128,256]{1,0:T(8,128)S(1)}, u32[]{:S(2)}, u32[]{:S(2)}) collective-permute-start(f32[128,256]{1,0:T(8,128)S(1)} %collective-permute-done.32.refs_1_), channel_id=1, source_target_pairs={{0,4},{1,5},{2,6},{3,7},{4,12},{5,13},{6,14},{7,15},{8,0},{9,1},{1... | collective-permute-start | bytes 393224 | tf_op jit(solution)/shard_map/ppermute | solution.py:41
  111.2 5.7 %collective-permute-start.39 = (f32[128,256]{1,0:T(8,128)S(1)}, f32[128,256]{1,0:T(8,128)S(1)}, u32[]{:S(2)}, u32[]{:S(2)}) collective-permute-start(f32[128,256]{1,0:T(8,128)S(1)} %collective-permute-done.37.refs_2_), channel_id=1, source_target_pairs={{0,8},{1,9},{2,10},{3,11},{4,0},{5,1},{6,2},{7,3},{8,16},{9,17},{1... | collective-permute-start | bytes 393224 | tf_op jit(solution)/shard_map/ppermute | solution.py:41
  113.2 5.7 %collective-permute-start.40 = (f32[128,256]{1,0:T(8,128)S(1)}, f32[128,256]{1,0:T(8,128)S(1)}, u32[]{:S(2)}, u32[]{:S(2)}) collective-permute-start(f32[128,256]{1,0:T(8,128)S(1)} %collective-permute-done.38.refs_3_), channel_id=1, source_target_pairs={{0,4},{1,5},{2,6},{3,7},{4,12},{5,13},{6,14},{7,15},{8,0},{9,1},{1... | collective-permute-start | bytes 393224 | tf_op jit(solution)/shard_map/ppermute | solution.py:41
  116.9 5.8 %collective-permute-start.41 = (f32[64,256]{1,0:T(8,128)S(1)}, f32[64,256]{1,0:T(8,128)S(1)}, u32[]{:S(2)}, u32[]{:S(2)}) collective-permute-start(f32[64,256]{1,0:T(8,128)S(1)} %slice.34), channel_id=1, source_target_pairs={{0,8},{1,9},{2,10},{3,11},{4,0},{5,1},{6,2},{7,3},{8,16},{9,17},{1... | collective-permute-start | bytes 196616 | tf_op jit(solution)/shard_map/ppermute | solution.py:41
  126.9 11.0 %collective-permute-start.51 = (f32[64,256]{1,0:T(8,128)S(1)}, f32[64,256]{1,0:T(8,128)S(1)}, u32[]{:S(2)}, u32[]{:S(2)}) collective-permute-start(f32[64,256]{1,0:T(8,128)S(1)} %get-tuple-element.219), channel_id=1, source_target_pairs={{0,4},{1,5},{2,6},{3,7},{4,12},{5,13},{6,14},{7,15},{8,0},{9,1},{1... | collective-permute-start | bytes 196616 | tf_op jit(solution)/shard_map/ppermute | solution.py:41
  127.1 9.2 %collective-permute-start.47 = (f32[64,256]{1,0:T(8,128)S(1)}, f32[64,256]{1,0:T(8,128)S(1)}, u32[]{:S(2)}, u32[]{:S(2)}) collective-permute-start(f32[64,256]{1,0:T(8,128)S(1)} %get-tuple-element.220), channel_id=1, source_target_pairs={{0,8},{1,9},{2,10},{3,11},{4,0},{5,1},{6,2},{7,3},{8,16},{9,17},{1... | collective-permute-start | bytes 196616 | tf_op jit(solution)/shard_map/ppermute | solution.py:41
  136.3 13.7 %collective-permute-start.48 = (f32[128,256]{1,0:T(8,128)S(1)}, f32[128,256]{1,0:T(8,128)S(1)}, u32[]{:S(2)}, u32[]{:S(2)}) collective-permute-start(f32[128,256]{1,0:T(8,128)S(1)} %pad_add_fusion.1), channel_id=1, source_target_pairs={{0,8},{1,9},{2,10},{3,11},{4,0},{5,1},{6,2},{7,3},{8,16},{9,17},{1... | collective-permute-start | bytes 393224 | tf_op jit(solution)/shard_map/ppermute | solution.py:41
  138.0 13.7 %collective-permute-start.52 = (f32[128,256]{1,0:T(8,128)S(1)}, f32[128,256]{1,0:T(8,128)S(1)}, u32[]{:S(2)}, u32[]{:S(2)}) collective-permute-start(f32[128,256]{1,0:T(8,128)S(1)} %pad_add_fusion), channel_id=1, source_target_pairs={{0,4},{1,5},{2,6},{3,7},{4,12},{5,13},{6,14},{7,15},{8,0},{9,1},{1... | collective-permute-start | bytes 393224 | tf_op jit(solution)/shard_map/ppermute | solution.py:41
  148.4 9.5 %collective-permute-start.45 = (f32[32,16,64]{2,1,0:T(8,128)S(1)}, f32[32,16,64]{2,1,0:T(8,128)S(1)}, u32[]{:S(2)}, u32[]{:S(2)}) collective-permute-start(f32[32,16,64]{2,1,0:T(8,128)S(1)} %get-tuple-element.199), channel_id=1, source_target_pairs={{0,2},{1,3},{2,0},{3,1},{4,6},{5,7},{6,4},{7,5},{8,10},{9,11},{10,... | collective-permute-start | bytes 393224 | tf_op jit(solution)/shard_map/ppermute | solution.py:41
  149.5 17.1 %collective-permute-start.43 = (f32[32,16,128]{2,1,0:T(8,128)S(1)}, f32[32,16,128]{2,1,0:T(8,128)S(1)}, u32[]{:S(2)}, u32[]{:S(2)}) collective-permute-start(f32[32,16,128]{2,1,0:T(8,128)S(1)} %get-tuple-element.186), channel_id=1, source_target_pairs={{0,2},{1,3},{2,0},{3,1},{4,6},{5,7},{6,4},{7,5},{8,10},{9,11},{10,... | collective-permute-start | bytes 786440 | tf_op jit(solution)/shard_map/ppermute | solution.py:41
  150.1 9.3 %collective-permute-start.49 = (f32[128,256]{1,0:T(8,128)S(1)}, f32[128,256]{1,0:T(8,128)S(1)}, u32[]{:S(2)}, u32[]{:S(2)}) collective-permute-start(f32[128,256]{1,0:T(8,128)S(1)} %add.59), channel_id=1, source_target_pairs={{0,8},{1,9},{2,10},{3,11},{4,0},{5,1},{6,2},{7,3},{8,16},{9,17},{1... | collective-permute-start | bytes 393224 | tf_op jit(solution)/shard_map/ppermute | solution.py:41
  151.7 9.1 %collective-permute-start.53 = (f32[128,256]{1,0:T(8,128)S(1)}, f32[128,256]{1,0:T(8,128)S(1)}, u32[]{:S(2)}, u32[]{:S(2)}) collective-permute-start(f32[128,256]{1,0:T(8,128)S(1)} %add.62), channel_id=1, source_target_pairs={{0,4},{1,5},{2,6},{3,7},{4,12},{5,13},{6,14},{7,15},{8,0},{9,1},{1... | collective-permute-start | bytes 393224 | tf_op jit(solution)/shard_map/ppermute | solution.py:41
  156.7 5.7 %collective-permute-start.34 = (f32[32,1,320]{2,1,0:T(1,128)S(1)}, f32[32,1,320]{2,1,0:T(1,128)S(1)}, u32[]{:S(2)}, u32[]{:S(2)}) collective-permute-start(f32[32,1,320]{2,1,0:T(1,128)S(1)} %get-tuple-element.171), channel_id=1, source_target_pairs={{0,2},{2,4},{4,6},{6,8},{8,10},{10,12},{12,14},{14,16},{16,18},{18... | collective-permute-start | bytes 122888 | tf_op jit(solution)/shard_map/ppermute | solution.py:523
  158.0 8.6 %collective-permute-start.35 = (f32[32,1,320]{2,1,0:T(1,128)S(1)}, f32[32,1,320]{2,1,0:T(1,128)S(1)}, u32[]{:S(2)}, u32[]{:S(2)}) collective-permute-start(f32[32,1,320]{2,1,0:T(1,128)S(1)} %get-tuple-element.172), channel_id=1, source_target_pairs={{2,0},{4,2},{6,4},{8,6},{10,8},{12,10},{14,12},{16,14},{18,16},{20... | collective-permute-start | bytes 122888 | tf_op jit(solution)/shard_map/ppermute | solution.py:524
  159.3 7.2 %collective-permute-start.44 = (f32[32,16,64]{2,1,0:T(8,128)S(1)}, f32[32,16,64]{2,1,0:T(8,128)S(1)}, u32[]{:S(2)}, u32[]{:S(2)}) collective-permute-start(f32[32,16,64]{2,1,0:T(8,128)S(1)} %get-tuple-element.197), channel_id=1, source_target_pairs={{0,2},{1,3},{2,0},{3,1},{4,6},{5,7},{6,4},{7,5},{8,10},{9,11},{10,... | collective-permute-start | bytes 393224 | tf_op jit(solution)/shard_map/ppermute | solution.py:41
  160.8 8.3 %collective-permute-start.46 = (f32[32,16,64]{2,1,0:T(8,128)S(1)}, f32[32,16,64]{2,1,0:T(8,128)S(1)}, u32[]{:S(2)}, u32[]{:S(2)}) collective-permute-start(f32[32,16,64]{2,1,0:T(8,128)S(1)} %add.57), channel_id=1, source_target_pairs={{0,1},{1,0},{2,3},{3,2},{4,5},{5,4},{6,7},{7,6},{8,9},{9,8},{10,11... | collective-permute-start | bytes 393224 | tf_op jit(solution)/shard_map/ppermute | solution.py:41
  162.4 9.4 %collective-permute-start.50 = (f32[128,256]{1,0:T(8,128)S(1)}, f32[128,256]{1,0:T(8,128)S(1)}, u32[]{:S(2)}, u32[]{:S(2)}) collective-permute-start(f32[128,256]{1,0:T(8,128)S(1)} %add.60), channel_id=1, source_target_pairs={{0,8},{1,9},{2,10},{3,11},{4,0},{5,1},{6,2},{7,3},{8,16},{9,17},{1... | collective-permute-start | bytes 393224 | tf_op jit(solution)/shard_map/ppermute | solution.py:41
  166.5 5.3 %collective-permute-start.54 = (f32[128,256]{1,0:T(8,128)S(1)}, f32[128,256]{1,0:T(8,128)S(1)}, u32[]{:S(2)}, u32[]{:S(2)}) collective-permute-start(f32[128,256]{1,0:T(8,128)S(1)} %add.63), channel_id=1, source_target_pairs={{0,4},{1,5},{2,6},{3,7},{4,12},{5,13},{6,14},{7,15},{8,0},{9,1},{1... | collective-permute-start | bytes 393224 | tf_op jit(solution)/shard_map/ppermute | solution.py:41
  (23 other events, 260.5 us)

commit v6 on v5

--- a/solution.py
+++ b/solution.py
@@ -177,41 +177,61 @@
     return (gy - z // zs + peers) % peers * zs + z % zs
 
 
-def spread_kernel(chips, peers, zl, info, xy_a, xy_b, *refs):
-    xzs, xy, xz, held = refs[: 2 * peers], refs[2 * peers], refs[2 * peers + 1 : -1], refs[-1]
+def spread_xy_kernel(xy_a, xy_b, xy):
     c, x_count, _ = xy_a.shape
-    zs = xzs[0].shape[2]
 
     def some(i, carry):
         for x in range(UNROLL):
             x += i * UNROLL
             for side, ref in enumerate((xy_a, xy_b)):
                 xy[side * x_count + x] = jnp.concatenate([ref[:, x, :]] * (LANES // c), axis=0).T
+        return carry
+
+    lax.fori_loop(0, x_count // UNROLL, some, 0)
+
+
+def spread_xy(xy_a, xy_b):
+    _, x_count, y_count = xy_a.shape
+    return pl.pallas_call(
+        spread_xy_kernel,
+        in_specs=vmem(2),
+        out_specs=vmem(1)[0],
+        out_shape=jax.ShapeDtypeStruct((2 * x_count, y_count, LANES), f32),
+        compiler_params=SMALL,
+        cost_estimate=cost(0, 3 * 2**20),
+    )(xy_a, xy_b)
+
+
+def spread_xz_kernel(chips, peers, zl, info, *refs):
+    xzs, xz, held = refs[: 2 * peers], refs[2 * peers : -1], refs[-1]
+    _, x_count, zs = xzs[0].shape
+
+    def some(i, carry):
+        for x in range(UNROLL):
+            x += i * UNROLL
             for s in range(peers):
                 for side in range(2):
                     held[s * zs : (s + 1) * zs, side * x_count + x, :] = xzs[2 * s + side][:, x, :].T
         return carry
 
     lax.fori_loop(0, x_count // UNROLL, some, 0)
-
     for p in range(chips):
         at = z_places(info[0], info[1], p, chips, peers, zl, zs)
         xz[p][...] = jnp.concatenate([held[at + j] for j in range(zl)], axis=1)
 
 
-def spread(info, xy_a, xy_b, xzs, zl):
+def spread_xz(info, xzs, zl):
     peers, chips = lax.axis_size("gy"), lax.axis_size("gx") // 2
-    c, x_count, y_count = xy_a.shape
+    c, x_count, zs = xzs[0].shape
     return pl.pallas_call(
-        functools.partial(spread_kernel, chips, peers, zl),
-        in_specs=[SCALARS] + vmem(2 + len(xzs)),
-        out_specs=vmem(1 + chips),
-        out_shape=[jax.ShapeDtypeStruct((2 * x_count, y_count, LANES), f32)]
-        + [jax.ShapeDtypeStruct((2 * x_count, zl * c), f32)] * chips,
-        scratch_shapes=[pltpu.VMEM((peers * xzs[0].shape[2], 2 * x_count, c), f32)],
-        compiler_params=SMALL,
-        cost_estimate=cost(0, 4 * 2**20),
-    )(info, xy_a, xy_b, *xzs)
+        functools.partial(spread_xz_kernel, chips, peers, zl),
+        in_specs=[SCALARS] + vmem(len(xzs)),
+        out_specs=vmem(chips),
+        out_shape=[jax.ShapeDtypeStruct((2 * x_count, zl * c), f32)] * chips,
+        scratch_shapes=[pltpu.VMEM((peers * zs, 2 * x_count, c), f32)],
+        compiler_params=SMALL,
+        cost_estimate=cost(0, 3 * 2**20),
+    )(info, *xzs)
 
 
 def collect_xy_kernel(part, xy_a, xy_b, *outs):
@@ -434,27 +454,23 @@
     outs[0][...] = p - LEARN_RATE * (m / corr_one) / (jnp.sqrt(v / corr_two) + EPSILON)
 
 
-def update_two_kernel(ends, count, info, above, below, left, right, *refs):
+def update_one_kernel(ends, count, at_row, at_col, info, above, below, left, right, *refs):
+    state, grads, outs = refs[:3], refs[3:-3], refs[-3:]
+    grad = sum(g[...] for g in grads)
     borders = (above, below, left, right)
-    xy, xz, outs = refs[:5], refs[5:11], refs[11:]
-    width_y = xy[0].shape[2]
-    rows = xy[0].shape[1]
-    update(info, ends, count, *xy[:3], xy[3][...] + xy[4][...], borders, 0, 0, outs[:3])
-    update(info, ends, count, *xz[:3], xz[3][...] + xz[4][...] + xz[5][...], borders, 2 * width_y, xy[0].shape[0] * rows, outs[3:])
-
-
-def update_two(info, count, borders, xy, xz):
+    update(info, ends, count, *state, grad, borders, at_row, at_col, outs)
+
+
+def update_one(info, count, borders, state, grads, at_row, at_col):
     ends = (lax.axis_size("gx") - 1, lax.axis_size("gy") - 1)
-    shapes = [jax.ShapeDtypeStruct(a.shape, f32) for a in (*xy[:3], *xz[:3])]
-    outs = pl.pallas_call(
-        functools.partial(update_two_kernel, ends, count),
-        in_specs=[SCALARS] + vmem(15),
-        out_specs=vmem(6),
-        out_shape=shapes,
-        compiler_params=SMALL,
-        cost_estimate=cost(0, 4 * 2**20),
-    )(info, *borders, *xy, *xz)
-    return outs[:3], outs[3:]
+    return pl.pallas_call(
+        functools.partial(update_one_kernel, ends, count, at_row, at_col),
+        in_specs=[SCALARS] + vmem(7 + len(grads)),
+        out_specs=vmem(3),
+        out_shape=[jax.ShapeDtypeStruct(a.shape, f32) for a in state],
+        compiler_params=SMALL,
+        cost_estimate=cost(0, 2 * 2**20),
+    )(info, *borders, *state, *grads)
 
 
 def update_yz_kernel(ends, count, info, above, below, left, right, plane, first, second, a, b, d, *refs):
@@ -486,7 +502,7 @@
     return outs[:3], outs[3]
 
 
-def edges_kernel(peers, info, xy, xz, yz, gate, *outs):
+def edges_kernel(peers, info, xy, xz, yz, *outs):
     width = xy.shape[2]
     for ref, at in ((xy, 0), (yz, width), (xz, 2 * width)):
         rows, cols = ref.shape[1:]
@@ -506,19 +522,19 @@
         at += c * rows
 
 
-def borders(info, planes, gate):
+def borders(info, planes):
     n, peers = lax.axis_size("gx"), lax.axis_size("gy")
     c = planes[0].shape[0]
     row = jax.ShapeDtypeStruct((c, 1, sum(p.shape[2] for p in planes)), f32)
     col = jax.ShapeDtypeStruct((1, sum(c * p.shape[1] for p in planes)), f32)
     outs = pl.pallas_call(
         functools.partial(edges_kernel, peers),
-        in_specs=[SCALARS] + vmem(3) + [pl.BlockSpec(memory_space=pl.ANY)],
+        in_specs=[SCALARS] + vmem(3),
         out_specs=vmem(3 if peers == 2 else 4),
         out_shape=[row, row] + [col] * (1 if peers == 2 else 2),
         compiler_params=SMALL,
         cost_estimate=cost(0, 2**20),
-    )(info, *planes, gate)
+    )(info, *planes)
     up = [(i, i + 1) for i in range(n - 1)]
     above = lax.ppermute(outs[0], "gx", up)
     below = lax.ppermute(outs[1], "gx", [(j, i) for i, j in up])
@@ -573,10 +589,12 @@
         for s in range(1, peers):
             xz_y = to_gy(plane_xz, s)
             xzs += [xz_y, to_core(xz_y)]
+        around = borders(info, (plane_xy, plane_xz, plane_yz))
         if fixed is None:
             fixed = fixed_parts(info, target, target_b, zl, w_hidden, b_hidden, w_output, b_output)
         wanted, weights = fixed[0], fixed[1:]
-        xy, *xz = spread(info, plane_xy, xy_b, xzs, zl)
+        xy = spread_xy(plane_xy, xy_b)
+        xz = spread_xz(info, xzs, zl)
 
         order = [(0,), (-1,), (1,), (half,)] + [(-d, d) for d in range(half - 1, 1, -1)]
         part_xy, parts_xz, parts_yz = None, {}, {}
@@ -587,8 +605,6 @@
             )
             for o, line, block in zip(group, lines, blocks):
                 parts_xz[slot[o]], parts_yz[o] = line, block
-            if group == (1,):
-                around = borders(info, (plane_xy, plane_xz, plane_yz), lines[0])
         block = parts_yz[half]
         send_ahead, send_back = to_ring(block[:middle], 1), to_ring(block[middle:], -1)
         for d in range(half - 1, 0, -1):
@@ -606,12 +622,15 @@
         for extra in grads_xz[1:]:
             near_xz = near_xz + extra
         count = START + iteration + 1
-        (plane_xy, first_xy, second_xy), (plane_xz, first_xz, second_xz) = update_two(
-            info,
-            count,
-            around,
-            (plane_xy, first_xy, second_xy, grad_xy, to_core(far_xy)),
-            (plane_xz, first_xz, second_xz, near_xz, far_xz, grads_xz[0]),
+        channels, rows, width = plane_xy.shape
+        state = (plane_xz, first_xz, second_xz)
+        plane_xz, first_xz, second_xz = update_one(
+            info, count, around, state, (near_xz, far_xz, grads_xz[0]), 2 * width, channels * rows
+        )
+        state = (plane_xy, first_xy, second_xy)
+        far_xy = to_core(far_xy)
+        plane_xy, first_xy, second_xy = update_one(
+            info, count, around, state, (grad_xy, far_xy), 0, 0
         )
         (plane_yz, first_yz, second_yz), lanes = update_yz(
             info, count, around, (plane_yz, first_yz, second_yz), (parts_yz[0], send_ahead, send_back)

time: 175 us -> 176 us (level)
  Pallas kernels: 83.9 us -> 87.4 us
    pallas_call x4 -> x8, Pallas kernels: 10.5 us -> 13.5 us  [the longest x4 6.43 us: update_one(): pl.pallas_call(functools.partial(update_one_kernel, ends, count, at_row,...]
  transfers between devices with their start and end apart: 55 -> 55, of which waited for: 13 -> 12; matrix products, arithmetic and copies ran while one was open for 0% -> 0% of each run, Pallas kernels for 35% -> 36%
where the time goes in v6:
time: 176 us; the launch traced here: 174 us
  Pallas kernels  87.4 us (50%)
  starting transfers between devices  59.9 us (34%)
  waiting for transfers between devices  22.8 us (13%)
  between operations  1.99 us (1%)
  local copies, waits for them, and re-layouts  1.97 us (1%)
    pallas_call x12, Pallas kernels, block_grads(): pl.pallas_call(functools.partial(grads_kernel, count, before is None), gr...  58.1 us
    ppermute x49, starting transfers between devices, send(): return lax.ppermute(x, BOTH, pairs)  50.8 us
    ppermute x49, waiting for transfers between devices, send(): return lax.ppermute(x, BOTH, pairs)  18.8 us
    pallas_call x4, Pallas kernels, update_one(): pl.pallas_call(functools.partial(update_one_kernel, ends, count, at_row,...  6.43 us
    pallas_call x2, Pallas kernels, spread_xz(): pl.pallas_call(functools.partial(spread_xz_kernel, chips, peers, zl), in_...  5.33 us
    pallas_call x2, Pallas kernels, collect_xz(): pl.pallas_call(functools.partial(collect_xz_kernel, chips, peers, zl), in...  5.28 us
    pallas_call x1, Pallas kernels, fixed_parts(): pl.pallas_call(functools.partial(fixed_kernel, chips, zl), in_specs=[SCAL...  4.1 us
    ppermute x2, waiting for transfers between devices, borders(): left = right = lax.ppermute(outs[2], 'gy', [(0, 1), (1, 0)])  3.97 us
  transfers between devices with their start and end apart: 55, of which 12 were waited for; matrix products, arithmetic and copies ran while one was open for 0% of the time, Pallas kernels for 36%

profile of v6, /device:TPU:0, one launch (start us, length us, event | category | flops | bytes accessed | tf_op | source)
XLA Modules:
  0.0 174.4 jit_solution(13155047181689787032)
XLA Ops:
  2.3 2.6 %collective-permute-start.8 = (f32[128,256]{1,0:T(8,128)S(1)}, f32[128,256]{1,0:T(8,128)S(1)}, u32[]{:S(2)}, u32[]{:S(2)}) collective-permute-start(f32[128,256]{1,0:T(8,128)S(1)} %shard_map.317.refs_1_), channel_id=1, source_target_pairs={{0,8},{1,9},{2,10},{3,11},{4,0},{5,1},{6,2},{7,3},{8,16},{9,17},{1... | collective-permute-start | bytes 393224 | tf_op jit(solution)/shard_map/ppermute | solution.py:41
  4.9 4.1 %collective-permute-done.8.refs_1_ = f32[128,256]{1,0:T(8,128)S(1)} collective-permute-done((f32[128,256]{1,0:T(8,128)S(1)}, f32[128,256]{1,0:T(8,128)S(1)}, u32[]{:S(2)}, u32[]{:S(2)}) %collective-permute-start.8) | collective-permute-done | bytes 131104 | tf_op jit(solution)/shard_map/ppermute | solution.py:41
  9.0 1.8 %collective-permute-start.9 = (f32[128,256]{1,0:T(8,128)S(1)}, f32[128,256]{1,0:T(8,128)S(1)}, u32[]{:S(2)}, u32[]{:S(2)}) collective-permute-start(f32[128,256]{1,0:T(8,128)S(1)} %collective-permute-done.8.refs_1_), channel_id=1, source_target_pairs={{0,8},{1,9},{2,10},{3,11},{4,0},{5,1},{6,2},{7,3},{8,16},{9,17},{1... | collective-permute-start | bytes 393224 | tf_op jit(solution)/shard_map/ppermute | solution.py:41
  11.0 1.7 collective-permute-start.6
  12.7 1.6 collective-permute-done.9.refs_2_
  16.3 3.6 %collective-permute-done.6.refs_2_ = f32[32,16,64]{2,1,0:T(8,128)S(1)} collective-permute-done((f32[32,16,64]{2,1,0:T(8,128)}, f32[32,16,64]{2,1,0:T(8,128)S(1)}, u32[]{:S(2)}, u32[]{:S(2)}) %collective-permute-start.6) | collective-permute-done | bytes 131104 | tf_op jit(solution)/shard_map/ppermute | solution.py:41
  21.2 1.8 %collective-permute-start.14 = (f32[64,256]{1,0:T(8,128)S(1)}, f32[64,256]{1,0:T(8,128)S(1)}, u32[]{:S(2)}, u32[]{:S(2)}) collective-permute-start(f32[64,256]{1,0:T(8,128)S(1)} %slice.32), channel_id=1, source_target_pairs={{0,8},{1,9},{2,10},{3,11},{4,0},{5,1},{6,2},{7,3},{8,16},{9,17},{1... | collective-permute-start | bytes 196616 | tf_op jit(solution)/shard_map/ppermute | solution.py:41
  25.2 2.7 %shard_map.316 = (f32[32,256]{1,0:T(8,128)S(1)}, f32[32,256]{1,0:T(8,128)S(1)}, f32[32,256]{1,0:T(8,128)S(1)}, f32[32,256]{1,0:T(8,128)S(1)}, f32[32,256]{1,0:T(...) custom-call(s32[2]{0:T(128)S(1)} %pad_add_fusion.4.info, ...), custom_call_target="tpu_custom_call" | custom-call | bytes 3145728 | tf_op jit(solution)/shard_map/pallas_call | solution.py:226
  28.0 4.1 %shard_map.314 = (bf16[32,128,128]{2,1,0:T(8,128)(2,1)S(1)}, bf16[256,256]{1,0:T(8,128)(2,1)S(1)}, bf16[256,256]{1,0:T(8,128)(2,1)S(1)}, bf16[256,256]{1,0:T(8,1...) custom-call(s32[2]{0:T(128)S(1)} %pad_add_fusion.4.info, f32[1]{0:T(128)S(6)} %copy.35.b_output, ...), custom_call_target="tpu_custom_call" | custom-call | bytes 4194304 | tf_op jit(solution)/shard_map/pallas_call | solution.py:130
  32.1 3.5 %shard_map.318 = (f32[32,128,128]{2,1,0:T(8,128)S(1)}, f32[32,256]{1,0:T(8,128)S(1)}, f32[128,256]{1,0:T(8,128)S(1)}) custom-call(s32[1]{0:T(128)} %constant.23.clone.slot, bf16[256,256]{1,0:T(8,128)(2,1)S(1)} %get-tuple-element.115.w_in, bf16[256,256]{1,0:T(8,128)(2,1)S(1)} %get-tuple-element.116.w_out, bf16[256,256]{1,0:T(8,128)(2,1)S(1)} %get-tuple-element.117.w_back, ...), custom_call_target="tpu_custom_call" | custom-call | flops 1610612736 | bytes 10485760 | tf_op jit(solution)/shard_map/pallas_call | solution.py:386
  35.6 3.6 %shard_map.319 = (f32[32,128,128]{2,1,0:T(8,128)S(1)}, f32[32,256]{1,0:T(8,128)S(1)}, f32[128,256]{1,0:T(8,128)S(1)}) custom-call(s32[1]{0:T(128)} %constant.24.clone.slot, bf16[256,256]{1,0:T(8,128)(2,1)S(1)} %get-tuple-element.115.w_in, bf16[256,256]{1,0:T(8,128)(2,1)S(1)} %get-tuple-element.116.w_out, bf16[256,256]{1,0:T(8,128)(2,1)S(1)} %get-tuple-element.117.w_back, ...), custom_call_target="tpu_custom_call" | custom-call | flops 1610612736 | bytes 10485760 | tf_op jit(solution)/shard_map/pallas_call | solution.py:386
  39.3 3.6 %shard_map.320 = (f32[32,128,128]{2,1,0:T(8,128)S(1)}, f32[32,256]{1,0:T(8,128)S(1)}, f32[128,256]{1,0:T(8,128)S(1)}) custom-call(s32[1]{0:T(128)} %constant.25.clone.slot, bf16[256,256]{1,0:T(8,128)(2,1)S(1)} %get-tuple-element.115.w_in, bf16[256,256]{1,0:T(8,128)(2,1)S(1)} %get-tuple-element.116.w_out, bf16[256,256]{1,0:T(8,128)(2,1)S(1)} %get-tuple-element.117.w_back, ...), custom_call_target="tpu_custom_call" | custom-call | flops 1610612736 | bytes 10485760 | tf_op jit(solution)/shard_map/pallas_call | solution.py:386
  43.0 3.7 %shard_map.321 = (f32[32,128,128]{2,1,0:T(8,128)S(1)}, f32[32,256]{1,0:T(8,128)S(1)}, f32[128,256]{1,0:T(8,128)S(1)}) custom-call(s32[1]{0:T(128)} %constant.26.clone.slot, bf16[256,256]{1,0:T(8,128)(2,1)S(1)} %get-tuple-element.115.w_in, bf16[256,256]{1,0:T(8,128)(2,1)S(1)} %get-tuple-element.116.w_out, bf16[256,256]{1,0:T(8,128)(2,1)S(1)} %get-tuple-element.117.w_back, ...), custom_call_target="tpu_custom_call" | custom-call | flops 1610612736 | bytes 10485760 | tf_op jit(solution)/shard_map/pallas_call | solution.py:386
  46.6 2.0 %collective-permute-start.24 = (f32[64,256]{1,0:T(8,128)S(1)}, f32[64,256]{1,0:T(8,128)S(1)}, u32[]{:S(2)}, u32[]{:S(2)}) collective-permute-start(f32[64,256]{1,0:T(8,128)S(1)} %get-tuple-element.217), channel_id=1, source_target_pairs={{0,4},{1,5},{2,6},{3,7},{4,12},{5,13},{6,14},{7,15},{8,0},{9,1},{1... | collective-permute-start | bytes 196616 | tf_op jit(solution)/shard_map/ppermute | solution.py:41
  48.6 7.3 %shard_map.322 = (f32[32,128,128]{2,1,0:T(8,128)S(1)}, f32[32,256]{1,0:T(8,128)S(1)}, f32[32,256]{1,0:T(8,128)S(1)}, f32[128,256]{1,0:T(8,128)S(1)}, f32[128,256]{1,0:T(8,128)S(1)}) custom-call(s32[1]{0:T(128)} %constant.27.clone.slot, bf16[256,256]{1,0:T(8,128)(2,1)S(1)} %get-tuple-element.115.w_in, bf16[256,256]{1,0:T(8,128)(2,1)S(1)} %get-tuple-element.116.w_out, ...), custom_call_target="tpu_custom_call" | custom-call | flops 3221225472 | bytes 20971520 | tf_op jit(solution)/shard_map/pallas_call | solution.py:386
  55.9 7.3 %shard_map.323 = (f32[32,128,128]{2,1,0:T(8,128)S(1)}, f32[32,256]{1,0:T(8,128)S(1)}, f32[32,256]{1,0:T(8,128)S(1)}, f32[128,256]{1,0:T(8,128)S(1)}, f32[128,256]{1,0:T(8,128)S(1)}) custom-call(s32[1]{0:T(128)} %constant.28.clone.slot, bf16[256,256]{1,0:T(8,128)(2,1)S(1)} %get-tuple-element.115.w_in, bf16[256,256]{1,0:T(8,128)(2,1)S(1)} %get-tuple-element.116.w_out, ...), custom_call_target="tpu_custom_call" | custom-call | flops 3221225472 | bytes 20971520 | tf_op jit(solution)/shard_map/pallas_call | solution.py:386
  63.3 2.6 %shard_map.326 = (f32[32,16,64]{2,1,0:T(8,128)S(1)}, f32[32,16,64]{2,1,0:T(8,128)S(1)}, f32[32,16,64]{2,1,0:T(8,128)S(1)}, f32[32,16,64]{2,1,0:T(8,128)S(1)}) custom-call(s32[2]{0:T(128)S(1)} %pad_add_fusion.4.info, f32[32,256]{1,0:T(8,128)S(1)} %get-tuple-element.138.refs_0_, f32[32,256]{1,0:T(8,128)S(1)} %get-tuple-element.139.refs_1_, ...), custom_call_target="tpu_custom_call" | custom-call | bytes 4194304 | tf_op jit(solution)/shard_map/pallas_call | solution.py:289
  66.4 1.8 %collective-permute-start.25 = (f32[128,256]{1,0:T(8,128)S(1)}, f32[128,256]{1,0:T(8,128)S(1)}, u32[]{:S(2)}, u32[]{:S(2)}) collective-permute-start(f32[128,256]{1,0:T(8,128)S(1)} %pad_add_fusion.2), channel_id=1, source_target_pairs={{0,4},{1,5},{2,6},{3,7},{4,12},{5,13},{6,14},{7,15},{8,0},{9,1},{1... | collective-permute-start | bytes 393224 | tf_op jit(solution)/shard_map/ppermute | solution.py:41
  68.2 2.3 %collective-permute-done.20 = f32[64,256]{1,0:T(8,128)S(1)} collective-permute-done((f32[64,256]{1,0:T(8,128)S(1)}, f32[64,256]{1,0:T(8,128)S(1)}, u32[]{:S(2)}, u32[]{:S(2)}) %collective-permute-start.20) | collective-permute-done | bytes 65568 | tf_op jit(solution)/shard_map/ppermute | solution.py:41
  72.7 1.8 %collective-permute-start.2 = (f32[1,1280]{1,0:T(1,128)S(1)}, f32[1,1280]{1,0:T(1,128)S(1)}, u32[]{:S(2)}, u32[]{:S(2)}) collective-permute-start(f32[1,1280]{1,0:T(1,128)S(1)} %get-tuple-element.114), channel_id=1, source_target_pairs={{0,1},{1,0},{2,3},{3,2},{4,5},{5,4},{6,7},{7,6},{8,9},{9,8},{10,11... | collective-permute-start | bytes 15368 | tf_op jit(solution)/shard_map/ppermute | solution.py:542
  74.5 1.9 %collective-permute-done.2.left.right = f32[1,1280]{1,0:T(1,128)S(1)} collective-permute-done((f32[1,1280]{1,0:T(1,128)S(1)}, f32[1,1280]{1,0:T(1,128)S(1)}, u32[]{:S(2)}, u32[]{:S(2)}) %collective-permute-start.2) | collective-permute-done | bytes 5152 | tf_op jit(solution)/shard_map/ppermute | solution.py:542
  79.1 3.2 %collective-permute-start.17 = (f32[32,16,64]{2,1,0:T(8,128)S(1)}, f32[32,16,64]{2,1,0:T(8,128)S(1)}, u32[]{:S(2)}, u32[]{:S(2)}) collective-permute-start(f32[32,16,64]{2,1,0:T(8,128)S(1)} %get-tuple-element.147), channel_id=1, source_target_pairs={{0,2},{1,3},{2,0},{3,1},{4,6},{5,7},{6,4},{7,5},{8,10},{9,11},{10,... | collective-permute-start | bytes 393224 | tf_op jit(solution)/shard_map/ppermute | solution.py:41
  83.8 1.8 %collective-permute-start.26 = (f32[128,256]{1,0:T(8,128)S(1)}, f32[128,256]{1,0:T(8,128)S(1)}, u32[]{:S(2)}, u32[]{:S(2)}) collective-permute-start(f32[128,256]{1,0:T(8,128)S(1)} %add.55), channel_id=1, source_target_pairs={{0,4},{1,5},{2,6},{3,7},{4,12},{5,13},{6,14},{7,15},{8,0},{9,1},{1... | collective-permute-start | bytes 393224 | tf_op jit(solution)/shard_map/ppermute | solution.py:41
  86.6 3.9 %collective-permute-done.19.refs_5_ = f32[32,16,64]{2,1,0:T(8,128)S(1)} collective-permute-done((f32[32,16,64]{2,1,0:T(8,128)S(1)}, f32[32,16,64]{2,1,0:T(8,128)S(1)}, u32[]{:S(2)}, u32[]{:S(2)}) %collective-permute-start.19) | collective-permute-done | bytes 131104 | tf_op jit(solution)/shard_map/ppermute | solution.py:41
  91.8 1.6 collective-permute-start.33
  93.3 2.1 %collective-permute-start.27 = (f32[128,256]{1,0:T(8,128)S(1)}, f32[128,256]{1,0:T(8,128)S(1)}, u32[]{:S(2)}, u32[]{:S(2)}) collective-permute-start(f32[128,256]{1,0:T(8,128)S(1)} %add.56), channel_id=1, source_target_pairs={{0,4},{1,5},{2,6},{3,7},{4,12},{5,13},{6,14},{7,15},{8,0},{9,1},{1... | collective-permute-start | bytes 393224 | tf_op jit(solution)/shard_map/ppermute | solution.py:41
  101.5 2.2 %collective-permute-start.35 = (f32[128,256]{1,0:T(8,128)S(1)}, f32[128,256]{1,0:T(8,128)S(1)}, u32[]{:S(2)}, u32[]{:S(2)}) collective-permute-start(f32[128,256]{1,0:T(8,128)S(1)} %get-tuple-element.167.refs_1_), channel_id=1, source_target_pairs={{0,8},{1,9},{2,10},{3,11},{4,0},{5,1},{6,2},{7,3},{8,16},{9,17},{1... | collective-permute-start | bytes 393224 | tf_op jit(solution)/shard_map/ppermute | solution.py:41
  103.8 2.7 %shard_map.331 = (f32[32,256]{1,0:T(8,128)S(1)}, f32[32,256]{1,0:T(8,128)S(1)}, f32[32,256]{1,0:T(8,128)S(1)}, f32[32,256]{1,0:T(8,128)S(1)}, f32[32,256]{1,0:T(...) custom-call(s32[2]{0:T(128)S(1)} %pad_add_fusion.4.info, ...), custom_call_target="tpu_custom_call" | custom-call | bytes 3145728 | tf_op jit(solution)/shard_map/pallas_call | solution.py:226
  107.3 2.3 %collective-permute-start.36 = (f32[128,256]{1,0:T(8,128)S(1)}, f32[128,256]{1,0:T(8,128)S(1)}, u32[]{:S(2)}, u32[]{:S(2)}) collective-permute-start(f32[128,256]{1,0:T(8,128)S(1)} %collective-permute-done.35.refs_1_), channel_id=1, source_target_pairs={{0,8},{1,9},{2,10},{3,11},{4,0},{5,1},{6,2},{7,3},{8,16},{9,17},{1... | collective-permute-start | bytes 393224 | tf_op jit(solution)/shard_map/ppermute | solution.py:41
  109.7 3.5 %shard_map.332 = (f32[32,128,128]{2,1,0:T(8,128)S(1)}, f32[32,256]{1,0:T(8,128)S(1)}, f32[128,256]{1,0:T(8,128)S(1)}) custom-call(s32[1]{0:T(128)} %constant.23.clone.slot, bf16[256,256]{1,0:T(8,128)(2,1)S(1)} %get-tuple-element.115.w_in, bf16[256,256]{1,0:T(8,128)(2,1)S(1)} %get-tuple-element.116.w_out, bf16[256,256]{1,0:T(8,128)(2,1)S(1)} %get-tuple-element.117.w_back, ...), custom_call_target="tpu_custom_call" | custom-call | flops 1610612736 | bytes 10485760 | tf_op jit(solution)/shard_map/pallas_call | solution.py:386
  113.2 2.1 %collective-permute-start.39 = (f32[128,256]{1,0:T(8,128)S(1)}, f32[128,256]{1,0:T(8,128)S(1)}, u32[]{:S(2)}, u32[]{:S(2)}) collective-permute-start(f32[128,256]{1,0:T(8,128)S(1)} %collective-permute-done.36.refs_2_), channel_id=1, source_target_pairs={{0,8},{1,9},{2,10},{3,11},{4,0},{5,1},{6,2},{7,3},{8,16},{9,17},{1... | collective-permute-start | bytes 393224 | tf_op jit(solution)/shard_map/ppermute | solution.py:41
  115.3 3.6 %shard_map.333 = (f32[32,128,128]{2,1,0:T(8,128)S(1)}, f32[32,256]{1,0:T(8,128)S(1)}, f32[128,256]{1,0:T(8,128)S(1)}) custom-call(s32[1]{0:T(128)} %constant.24.clone.slot, bf16[256,256]{1,0:T(8,128)(2,1)S(1)} %get-tuple-element.115.w_in, bf16[256,256]{1,0:T(8,128)(2,1)S(1)} %get-tuple-element.116.w_out, bf16[256,256]{1,0:T(8,128)(2,1)S(1)} %get-tuple-element.117.w_back, ...), custom_call_target="tpu_custom_call" | custom-call | flops 1610612736 | bytes 10485760 | tf_op jit(solution)/shard_map/pallas_call | solution.py:386
  118.9 2.1 %collective-permute-start.41 = (f32[64,256]{1,0:T(8,128)S(1)}, f32[64,256]{1,0:T(8,128)S(1)}, u32[]{:S(2)}, u32[]{:S(2)}) collective-permute-start(f32[64,256]{1,0:T(8,128)S(1)} %slice.34), channel_id=1, source_target_pairs={{0,8},{1,9},{2,10},{3,11},{4,0},{5,1},{6,2},{7,3},{8,16},{9,17},{1... | collective-permute-start | bytes 196616 | tf_op jit(solution)/shard_map/ppermute | solution.py:41
  121.1 3.6 %shard_map.334 = (f32[32,128,128]{2,1,0:T(8,128)S(1)}, f32[32,256]{1,0:T(8,128)S(1)}, f32[128,256]{1,0:T(8,128)S(1)}) custom-call(s32[1]{0:T(128)} %constant.25.clone.slot, bf16[256,256]{1,0:T(8,128)(2,1)S(1)} %get-tuple-element.115.w_in, bf16[256,256]{1,0:T(8,128)(2,1)S(1)} %get-tuple-element.116.w_out, bf16[256,256]{1,0:T(8,128)(2,1)S(1)} %get-tuple-element.117.w_back, ...), custom_call_target="tpu_custom_call" | custom-call | flops 1610612736 | bytes 10485760 | tf_op jit(solution)/shard_map/pallas_call | solution.py:386
  125.3 3.6 %shard_map.335 = (f32[32,128,128]{2,1,0:T(8,128)S(1)}, f32[32,256]{1,0:T(8,128)S(1)}, f32[128,256]{1,0:T(8,128)S(1)}) custom-call(s32[1]{0:T(128)} %constant.26.clone.slot, bf16[256,256]{1,0:T(8,128)(2,1)S(1)} %get-tuple-element.115.w_in, bf16[256,256]{1,0:T(8,128)(2,1)S(1)} %get-tuple-element.116.w_out, bf16[256,256]{1,0:T(8,128)(2,1)S(1)} %get-tuple-element.117.w_back, ...), custom_call_target="tpu_custom_call" | custom-call | flops 1610612736 | bytes 10485760 | tf_op jit(solution)/shard_map/pallas_call | solution.py:386
  131.1 7.3 %shard_map.336 = (f32[32,128,128]{2,1,0:T(8,128)S(1)}, f32[32,256]{1,0:T(8,128)S(1)}, f32[32,256]{1,0:T(8,128)S(1)}, f32[128,256]{1,0:T(8,128)S(1)}, f32[128,256]{1,0:T(8,128)S(1)}) custom-call(s32[1]{0:T(128)} %constant.27.clone.slot, bf16[256,256]{1,0:T(8,128)(2,1)S(1)} %get-tuple-element.115.w_in, bf16[256,256]{1,0:T(8,128)(2,1)S(1)} %get-tuple-element.116.w_out, ...), custom_call_target="tpu_custom_call" | custom-call | flops 3221225472 | bytes 20971520 | tf_op jit(solution)/shard_map/pallas_call | solution.py:386
  139.0 1.6 collective-permute-start.48
  140.6 7.3 %shard_map.337 = (f32[32,128,128]{2,1,0:T(8,128)S(1)}, f32[32,256]{1,0:T(8,128)S(1)}, f32[32,256]{1,0:T(8,128)S(1)}, f32[128,256]{1,0:T(8,128)S(1)}, f32[128,256]{1,0:T(8,128)S(1)}) custom-call(s32[1]{0:T(128)} %constant.28.clone.slot, bf16[256,256]{1,0:T(8,128)(2,1)S(1)} %get-tuple-element.115.w_in, bf16[256,256]{1,0:T(8,128)(2,1)S(1)} %get-tuple-element.116.w_out, ...), custom_call_target="tpu_custom_call" | custom-call | flops 3221225472 | bytes 20971520 | tf_op jit(solution)/shard_map/pallas_call | solution.py:386
  147.9 2.6 %shard_map.340 = (f32[32,16,64]{2,1,0:T(8,128)S(1)}, f32[32,16,64]{2,1,0:T(8,128)S(1)}, f32[32,16,64]{2,1,0:T(8,128)S(1)}, f32[32,16,64]{2,1,0:T(8,128)S(1)}) custom-call(s32[2]{0:T(128)S(1)} %pad_add_fusion.4.info, f32[32,256]{1,0:T(8,128)S(1)} %get-tuple-element.185.refs_0_, f32[32,256]{1,0:T(8,128)S(1)} %get-tuple-element.186.refs_1_, ...), custom_call_target="tpu_custom_call" | custom-call | bytes 4194304 | tf_op jit(solution)/shard_map/pallas_call | solution.py:289
  152.5 1.6 collective-permute-start.49
  154.8 1.9 %collective-permute-start.28 = (f32[32,1,320]{2,1,0:T(1,128)S(1)}, f32[32,1,320]{2,1,0:T(1,128)S(1)}, u32[]{:S(2)}, u32[]{:S(2)}) collective-permute-start(f32[32,1,320]{2,1,0:T(1,128)S(1)} %get-tuple-element.160), channel_id=1, source_target_pairs={{0,2},{2,4},{4,6},{6,8},{8,10},{10,12},{12,14},{14,16},{16,18},{18... | collective-permute-start | bytes 122888 | tf_op jit(solution)/shard_map/ppermute | solution.py:539
  158.1 1.6 collective-permute-start.30
  159.7 2.1 %collective-permute-done.30.left.right = f32[1,1280]{1,0:T(1,128)S(1)} collective-permute-done((f32[1,1280]{1,0:T(1,128)S(1)}, f32[1,1280]{1,0:T(1,128)S(1)}, u32[]{:S(2)}, u32[]{:S(2)}) %collective-permute-start.30) | collective-permute-done | bytes 5152 | tf_op jit(solution)/shard_map/ppermute | solution.py:542
  163.4 2.8 %collective-permute-start.54 = (f32[128,256]{1,0:T(8,128)S(1)}, f32[128,256]{1,0:T(8,128)S(1)}, u32[]{:S(2)}, u32[]{:S(2)}) collective-permute-start(f32[128,256]{1,0:T(8,128)S(1)} %add.63), channel_id=1, source_target_pairs={{0,4},{1,5},{2,6},{3,7},{4,12},{5,13},{6,14},{7,15},{8,0},{9,1},{1... | collective-permute-start | bytes 393224 | tf_op jit(solution)/shard_map/ppermute | solution.py:41
  166.2 2.1 %collective-permute-start.50 = (f32[128,256]{1,0:T(8,128)S(1)}, f32[128,256]{1,0:T(8,128)S(1)}, u32[]{:S(2)}, u32[]{:S(2)}) collective-permute-start(f32[128,256]{1,0:T(8,128)S(1)} %add.60), channel_id=1, source_target_pairs={{0,8},{1,9},{2,10},{3,11},{4,0},{5,1},{6,2},{7,3},{8,16},{9,17},{1... | collective-permute-start | bytes 393224 | tf_op jit(solution)/shard_map/ppermute | solution.py:41
  168.3 2.0 %shard_map.339 = (f32[32,16,128]{2,1,0:T(8,128)}, f32[32,16,128]{2,1,0:T(8,128)}, f32[32,16,128]{2,1,0:T(8,128)}) custom-call(s32[2]{0:T(128)S(1)} %pad_add_fusion.4.info, f32[32,1,320]{2,1,0:T(1,128)S(1)} %collective-permute-done.28.above, f32[32,1,320]{2,1,0:T(1,128)S(1)} %collective-permute-done.29.below, ...), custom_call_target="tpu_custom_call" | custom-call | bytes 2097152 | tf_op jit(solution)/shard_map/pallas_call | solution.py:466
  170.5 2.1 %shard_map.341 = (f32[32,16,64]{2,1,0:T(8,128)}, f32[32,16,64]{2,1,0:T(8,128)}, f32[32,16,64]{2,1,0:T(8,128)}) custom-call(s32[2]{0:T(128)S(1)} %pad_add_fusion.4.info, f32[32,1,320]{2,1,0:T(1,128)S(1)} %collective-permute-done.28.above, f32[32,1,320]{2,1,0:T(1,128)S(1)} %collective-permute-done.29.below, f32[1,1280]{1,0:T(1,128)S(1)} %collective-permute-done.30.left.right, ...), custom_call_target="tpu_custom_call" | custom-call | bytes 2097152 | tf_op jit(solution)/shard_map/pallas_call | solution.py:466
  172.6 1.8 %shard_map.342 = (f32[32,8,128]{2,1,0:T(8,128)}, f32[32,8,128]{2,1,0:T(8,128)}, f32[32,8,128]{2,1,0:T(8,128)}, f32[128,256]{1,0:T(8,128)}) custom-call(s32[2]{0:T(128)S(1)} %pad_add_fusion.4.info, f32[32,1,320]{2,1,0:T(1,128)S(1)} %collective-permute-done.28.above, f32[32,1,320]{2,1,0:T(1,128)S(1)} %collective-permute-done.29.below, ...), custom_call_target="tpu_custom_call" | custom-call | bytes 2097152 | tf_op jit(solution)/shard_map/pallas_call | solution.py:493
  (145 shorter events, 31.9 us)
Async XLA Ops:
  0.7 27.3 %collective-permute-start.3 = (f32[16,128,128]{2,1,0:T(8,128)}, f32[16,128,128]{2,1,0:T(8,128)S(1)}, u32[]{:S(2)}, u32[]{:S(2)}) collective-permute-start(f32[16,128,128]{2,1,0:T(8,128)} %target_a.1), channel_id=1, source_target_pairs={{0,2},{1,3},{2,0},{3,1},{4,6},{5,7},{6,4},{7,5},{8,10},{9,11},{10,... | collective-permute-start | bytes 3145736 | tf_op jit(solution)/shard_map/ppermute | solution.py:41
  2.3 6.7 %collective-permute-start.8 = (f32[128,256]{1,0:T(8,128)S(1)}, f32[128,256]{1,0:T(8,128)S(1)}, u32[]{:S(2)}, u32[]{:S(2)}) collective-permute-start(f32[128,256]{1,0:T(8,128)S(1)} %shard_map.317.refs_1_), channel_id=1, source_target_pairs={{0,8},{1,9},{2,10},{3,11},{4,0},{5,1},{6,2},{7,3},{8,16},{9,17},{1... | collective-permute-start | bytes 393224 | tf_op jit(solution)/shard_map/ppermute | solution.py:41
  4.9 5.9 %collective-permute-start.10 = (f32[128,256]{1,0:T(8,128)S(1)}, f32[128,256]{1,0:T(8,128)S(1)}, u32[]{:S(2)}, u32[]{:S(2)}) collective-permute-start(f32[128,256]{1,0:T(8,128)S(1)} %shard_map.317.refs_1_), channel_id=1, source_target_pairs={{0,4},{1,5},{2,6},{3,7},{4,12},{5,13},{6,14},{7,15},{8,0},{9,1},{1... | collective-permute-start | bytes 393224 | tf_op jit(solution)/shard_map/ppermute | solution.py:41
  9.0 5.3 %collective-permute-start.9 = (f32[128,256]{1,0:T(8,128)S(1)}, f32[128,256]{1,0:T(8,128)S(1)}, u32[]{:S(2)}, u32[]{:S(2)}) collective-permute-start(f32[128,256]{1,0:T(8,128)S(1)} %collective-permute-done.8.refs_1_), channel_id=1, source_target_pairs={{0,8},{1,9},{2,10},{3,11},{4,0},{5,1},{6,2},{7,3},{8,16},{9,17},{1... | collective-permute-start | bytes 393224 | tf_op jit(solution)/shard_map/ppermute | solution.py:41
  10.8 5.0 %collective-permute-start.11 = (f32[128,256]{1,0:T(8,128)S(1)}, f32[128,256]{1,0:T(8,128)S(1)}, u32[]{:S(2)}, u32[]{:S(2)}) collective-permute-start(f32[128,256]{1,0:T(8,128)S(1)} %collective-permute-done.10.refs_1_), channel_id=1, source_target_pairs={{0,4},{1,5},{2,6},{3,7},{4,12},{5,13},{6,14},{7,15},{8,0},{9,1},{1... | collective-permute-start | bytes 393224 | tf_op jit(solution)/shard_map/ppermute | solution.py:41
  11.0 12.0 %collective-permute-start.4 = (f32[32,16,128]{2,1,0:T(8,128)}, f32[32,16,128]{2,1,0:T(8,128)S(1)}, u32[]{:S(2)}, u32[]{:S(2)}) collective-permute-start(f32[32,16,128]{2,1,0:T(8,128)} %refs_0_.4), channel_id=1, source_target_pairs={{0,2},{1,3},{2,0},{3,1},{4,6},{5,7},{6,4},{7,5},{8,10},{9,11},{10,... | collective-permute-start | bytes 786440 | tf_op jit(solution)/shard_map/ppermute | solution.py:41
  11.0 8.9 %collective-permute-start.6 = (f32[32,16,64]{2,1,0:T(8,128)}, f32[32,16,64]{2,1,0:T(8,128)S(1)}, u32[]{:S(2)}, u32[]{:S(2)}) collective-permute-start(f32[32,16,64]{2,1,0:T(8,128)} %refs_0_.5), channel_id=1, source_target_pairs={{0,1},{1,0},{2,3},{3,2},{4,5},{5,4},{6,7},{7,6},{8,9},{9,8},{10,11... | collective-permute-start | bytes 393224 | tf_op jit(solution)/shard_map/ppermute | solution.py:41
  14.3 5.7 %collective-permute-start.12 = (f32[128,256]{1,0:T(8,128)S(1)}, f32[128,256]{1,0:T(8,128)S(1)}, u32[]{:S(2)}, u32[]{:S(2)}) collective-permute-start(f32[128,256]{1,0:T(8,128)S(1)} %collective-permute-done.9.refs_2_), channel_id=1, source_target_pairs={{0,8},{1,9},{2,10},{3,11},{4,0},{5,1},{6,2},{7,3},{8,16},{9,17},{1... | collective-permute-start | bytes 393224 | tf_op jit(solution)/shard_map/ppermute | solution.py:41
  15.8 5.3 %collective-permute-start.13 = (f32[128,256]{1,0:T(8,128)S(1)}, f32[128,256]{1,0:T(8,128)S(1)}, u32[]{:S(2)}, u32[]{:S(2)}) collective-permute-start(f32[128,256]{1,0:T(8,128)S(1)} %collective-permute-done.11.refs_3_), channel_id=1, source_target_pairs={{0,4},{1,5},{2,6},{3,7},{4,12},{5,13},{6,14},{7,15},{8,0},{9,1},{1... | collective-permute-start | bytes 393224 | tf_op jit(solution)/shard_map/ppermute | solution.py:41
  19.9 5.3 %collective-permute-start.5 = (f32[32,16,64]{2,1,0:T(8,128)}, f32[32,16,64]{2,1,0:T(8,128)S(1)}, u32[]{:S(2)}, u32[]{:S(2)}) collective-permute-start(f32[32,16,64]{2,1,0:T(8,128)} %refs_0_.5), channel_id=1, source_target_pairs={{0,2},{1,3},{2,0},{3,1},{4,6},{5,7},{6,4},{7,5},{8,10},{9,11},{10,... | collective-permute-start | bytes 393224 | tf_op jit(solution)/shard_map/ppermute | solution.py:41
  20.0 5.3 %collective-permute-start.7 = (f32[32,16,64]{2,1,0:T(8,128)S(1)}, f32[32,16,64]{2,1,0:T(8,128)S(1)}, u32[]{:S(2)}, u32[]{:S(2)}) collective-permute-start(f32[32,16,64]{2,1,0:T(8,128)S(1)} %collective-permute-done.6.refs_2_), channel_id=1, source_target_pairs={{0,2},{1,3},{2,0},{3,1},{4,6},{5,7},{6,4},{7,5},{8,10},{9,11},{10,... | collective-permute-start | bytes 393224 | tf_op jit(solution)/shard_map/ppermute | solution.py:41
  21.2 6.7 %collective-permute-start.14 = (f32[64,256]{1,0:T(8,128)S(1)}, f32[64,256]{1,0:T(8,128)S(1)}, u32[]{:S(2)}, u32[]{:S(2)}) collective-permute-start(f32[64,256]{1,0:T(8,128)S(1)} %slice.32), channel_id=1, source_target_pairs={{0,8},{1,9},{2,10},{3,11},{4,0},{5,1},{6,2},{7,3},{8,16},{9,17},{1... | collective-permute-start | bytes 196616 | tf_op jit(solution)/shard_map/ppermute | solution.py:41
  46.6 19.7 %collective-permute-start.24 = (f32[64,256]{1,0:T(8,128)S(1)}, f32[64,256]{1,0:T(8,128)S(1)}, u32[]{:S(2)}, u32[]{:S(2)}) collective-permute-start(f32[64,256]{1,0:T(8,128)S(1)} %get-tuple-element.217), channel_id=1, source_target_pairs={{0,4},{1,5},{2,6},{3,7},{4,12},{5,13},{6,14},{7,15},{8,0},{9,1},{1... | collective-permute-start | bytes 196616 | tf_op jit(solution)/shard_map/ppermute | solution.py:41
  65.9 11.8 %collective-permute-start.18 = (f32[32,16,64]{2,1,0:T(8,128)S(1)}, f32[32,16,64]{2,1,0:T(8,128)S(1)}, u32[]{:S(2)}, u32[]{:S(2)}) collective-permute-start(f32[32,16,64]{2,1,0:T(8,128)S(1)} %get-tuple-element.149), channel_id=1, source_target_pairs={{0,2},{1,3},{2,0},{3,1},{4,6},{5,7},{6,4},{7,5},{8,10},{9,11},{10,... | collective-permute-start | bytes 393224 | tf_op jit(solution)/shard_map/ppermute | solution.py:41
  66.4 15.9 %collective-permute-start.25 = (f32[128,256]{1,0:T(8,128)S(1)}, f32[128,256]{1,0:T(8,128)S(1)}, u32[]{:S(2)}, u32[]{:S(2)}) collective-permute-start(f32[128,256]{1,0:T(8,128)S(1)} %pad_add_fusion.2), channel_id=1, source_target_pairs={{0,4},{1,5},{2,6},{3,7},{4,12},{5,13},{6,14},{7,15},{8,0},{9,1},{1... | collective-permute-start | bytes 393224 | tf_op jit(solution)/shard_map/ppermute | solution.py:41
  70.5 13.2 %collective-permute-start.21 = (f32[128,256]{1,0:T(8,128)S(1)}, f32[128,256]{1,0:T(8,128)S(1)}, u32[]{:S(2)}, u32[]{:S(2)}) collective-permute-start(f32[128,256]{1,0:T(8,128)S(1)} %pad_add_fusion.3), channel_id=1, source_target_pairs={{0,8},{1,9},{2,10},{3,11},{4,0},{5,1},{6,2},{7,3},{8,16},{9,17},{1... | collective-permute-start | bytes 393224 | tf_op jit(solution)/shard_map/ppermute | solution.py:41
  71.9 24.6 %collective-permute-start.16 = (f32[32,16,128]{2,1,0:T(8,128)S(1)}, f32[32,16,128]{2,1,0:T(8,128)S(1)}, u32[]{:S(2)}, u32[]{:S(2)}) collective-permute-start(f32[32,16,128]{2,1,0:T(8,128)S(1)} %get-tuple-element.136), channel_id=1, source_target_pairs={{0,2},{1,3},{2,0},{3,1},{4,6},{5,7},{6,4},{7,5},{8,10},{9,11},{10,... | collective-permute-start | bytes 786440 | tf_op jit(solution)/shard_map/ppermute | solution.py:41
  77.7 7.8 %collective-permute-start.1 = (f32[32,1,320]{2,1,0:T(1,128)S(1)}, f32[32,1,320]{2,1,0:T(1,128)S(1)}, u32[]{:S(2)}, u32[]{:S(2)}) collective-permute-start(f32[32,1,320]{2,1,0:T(1,128)S(1)} %get-tuple-element.113), channel_id=1, source_target_pairs={{2,0},{4,2},{6,4},{8,6},{10,8},{12,10},{14,12},{16,14},{18,16},{20... | collective-permute-start | bytes 122888 | tf_op jit(solution)/shard_map/ppermute | solution.py:540
  79.1 7.5 %collective-permute-start.17 = (f32[32,16,64]{2,1,0:T(8,128)S(1)}, f32[32,16,64]{2,1,0:T(8,128)S(1)}, u32[]{:S(2)}, u32[]{:S(2)}) collective-permute-start(f32[32,16,64]{2,1,0:T(8,128)S(1)} %get-tuple-element.147), channel_id=1, source_target_pairs={{0,2},{1,3},{2,0},{3,1},{4,6},{5,7},{6,4},{7,5},{8,10},{9,11},{10,... | collective-permute-start | bytes 393224 | tf_op jit(solution)/shard_map/ppermute | solution.py:41
  82.3 8.3 %collective-permute-start.19 = (f32[32,16,64]{2,1,0:T(8,128)S(1)}, f32[32,16,64]{2,1,0:T(8,128)S(1)}, u32[]{:S(2)}, u32[]{:S(2)}) collective-permute-start(f32[32,16,64]{2,1,0:T(8,128)S(1)} %add.50), channel_id=1, source_target_pairs={{0,1},{1,0},{2,3},{3,2},{4,5},{5,4},{6,7},{7,6},{8,9},{9,8},{10,11... | collective-permute-start | bytes 393224 | tf_op jit(solution)/shard_map/ppermute | solution.py:41
  83.8 9.5 %collective-permute-start.26 = (f32[128,256]{1,0:T(8,128)S(1)}, f32[128,256]{1,0:T(8,128)S(1)}, u32[]{:S(2)}, u32[]{:S(2)}) collective-permute-start(f32[128,256]{1,0:T(8,128)S(1)} %add.55), channel_id=1, source_target_pairs={{0,4},{1,5},{2,6},{3,7},{4,12},{5,13},{6,14},{7,15},{8,0},{9,1},{1... | collective-permute-start | bytes 393224 | tf_op jit(solution)/shard_map/ppermute | solution.py:41
  85.6 9.9 %collective-permute-start.22 = (f32[128,256]{1,0:T(8,128)S(1)}, f32[128,256]{1,0:T(8,128)S(1)}, u32[]{:S(2)}, u32[]{:S(2)}) collective-permute-start(f32[128,256]{1,0:T(8,128)S(1)} %add.52), channel_id=1, source_target_pairs={{0,8},{1,9},{2,10},{3,11},{4,0},{5,1},{6,2},{7,3},{8,16},{9,17},{1... | collective-permute-start | bytes 393224 | tf_op jit(solution)/shard_map/ppermute | solution.py:41
  91.8 7.5 %collective-permute-start.33 = (f32[32,16,64]{2,1,0:T(8,128)S(1)}, f32[32,16,64]{2,1,0:T(8,128)S(1)}, u32[]{:S(2)}, u32[]{:S(2)}) collective-permute-start(f32[32,16,64]{2,1,0:T(8,128)S(1)} %get-tuple-element.150.xz.refs_0_), channel_id=1, source_target_pairs={{0,1},{1,0},{2,3},{3,2},{4,5},{5,4},{6,7},{7,6},{8,9},{9,8},{10,11... | collective-permute-start | bytes 393224 | tf_op jit(solution)/shard_map/ppermute | solution.py:41
  93.3 6.0 %collective-permute-start.27 = (f32[128,256]{1,0:T(8,128)S(1)}, f32[128,256]{1,0:T(8,128)S(1)}, u32[]{:S(2)}, u32[]{:S(2)}) collective-permute-start(f32[128,256]{1,0:T(8,128)S(1)} %add.56), channel_id=1, source_target_pairs={{0,4},{1,5},{2,6},{3,7},{4,12},{5,13},{6,14},{7,15},{8,0},{9,1},{1... | collective-permute-start | bytes 393224 | tf_op jit(solution)/shard_map/ppermute | solution.py:41
  95.5 5.0 %collective-permute-start.23 = (f32[128,256]{1,0:T(8,128)S(1)}, f32[128,256]{1,0:T(8,128)S(1)}, u32[]{:S(2)}, u32[]{:S(2)}) collective-permute-start(f32[128,256]{1,0:T(8,128)S(1)} %add.53), channel_id=1, source_target_pairs={{0,8},{1,9},{2,10},{3,11},{4,0},{5,1},{6,2},{7,3},{8,16},{9,17},{1... | collective-permute-start | bytes 393224 | tf_op jit(solution)/shard_map/ppermute | solution.py:41
  97.7 8.8 %collective-permute-start.31 = (f32[32,16,128]{2,1,0:T(8,128)S(1)}, f32[32,16,128]{2,1,0:T(8,128)S(1)}, u32[]{:S(2)}, u32[]{:S(2)}) collective-permute-start(f32[32,16,128]{2,1,0:T(8,128)S(1)} %get-tuple-element.137.xy.xy_a.refs_0_), channel_id=1, source_target_pairs={{0,2},{1,3},{2,0},{3,1},{4,6},{5,7},{6,4},{7,5},{8,10},{9,11},{10,... | collective-permute-start | bytes 786440 | tf_op jit(solution)/shard_map/ppermute | solution.py:41
  97.7 6.0 %collective-permute-start.32 = (f32[32,16,64]{2,1,0:T(8,128)S(1)}, f32[32,16,64]{2,1,0:T(8,128)S(1)}, u32[]{:S(2)}, u32[]{:S(2)}) collective-permute-start(f32[32,16,64]{2,1,0:T(8,128)S(1)} %get-tuple-element.150.xz.refs_0_), channel_id=1, source_target_pairs={{0,2},{1,3},{2,0},{3,1},{4,6},{5,7},{6,4},{7,5},{8,10},{9,11},{10,... | collective-permute-start | bytes 393224 | tf_op jit(solution)/shard_map/ppermute | solution.py:41
  101.5 5.8 %collective-permute-start.35 = (f32[128,256]{1,0:T(8,128)S(1)}, f32[128,256]{1,0:T(8,128)S(1)}, u32[]{:S(2)}, u32[]{:S(2)}) collective-permute-start(f32[128,256]{1,0:T(8,128)S(1)} %get-tuple-element.167.refs_1_), channel_id=1, source_target_pairs={{0,8},{1,9},{2,10},{3,11},{4,0},{5,1},{6,2},{7,3},{8,16},{9,17},{1... | collective-permute-start | bytes 393224 | tf_op jit(solution)/shard_map/ppermute | solution.py:41
  103.7 5.9 %collective-permute-start.37 = (f32[128,256]{1,0:T(8,128)S(1)}, f32[128,256]{1,0:T(8,128)S(1)}, u32[]{:S(2)}, u32[]{:S(2)}) collective-permute-start(f32[128,256]{1,0:T(8,128)S(1)} %get-tuple-element.167.refs_1_), channel_id=1, source_target_pairs={{0,4},{1,5},{2,6},{3,7},{4,12},{5,13},{6,14},{7,15},{8,0},{9,1},{1... | collective-permute-start | bytes 393224 | tf_op jit(solution)/shard_map/ppermute | solution.py:41
  107.3 5.9 %collective-permute-start.36 = (f32[128,256]{1,0:T(8,128)S(1)}, f32[128,256]{1,0:T(8,128)S(1)}, u32[]{:S(2)}, u32[]{:S(2)}) collective-permute-start(f32[128,256]{1,0:T(8,128)S(1)} %collective-permute-done.35.refs_1_), channel_id=1, source_target_pairs={{0,8},{1,9},{2,10},{3,11},{4,0},{5,1},{6,2},{7,3},{8,16},{9,17},{1... | collective-permute-start | bytes 393224 | tf_op jit(solution)/shard_map/ppermute | solution.py:41
  109.7 5.6 %collective-permute-start.38 = (f32[128,256]{1,0:T(8,128)S(1)}, f32[128,256]{1,0:T(8,128)S(1)}, u32[]{:S(2)}, u32[]{:S(2)}) collective-permute-start(f32[128,256]{1,0:T(8,128)S(1)} %collective-permute-done.37.refs_1_), channel_id=1, source_target_pairs={{0,4},{1,5},{2,6},{3,7},{4,12},{5,13},{6,14},{7,15},{8,0},{9,1},{1... | collective-permute-start | bytes 393224 | tf_op jit(solution)/shard_map/ppermute | solution.py:41
  113.2 5.7 %collective-permute-start.39 = (f32[128,256]{1,0:T(8,128)S(1)}, f32[128,256]{1,0:T(8,128)S(1)}, u32[]{:S(2)}, u32[]{:S(2)}) collective-permute-start(f32[128,256]{1,0:T(8,128)S(1)} %collective-permute-done.36.refs_2_), channel_id=1, source_target_pairs={{0,8},{1,9},{2,10},{3,11},{4,0},{5,1},{6,2},{7,3},{8,16},{9,17},{1... | collective-permute-start | bytes 393224 | tf_op jit(solution)/shard_map/ppermute | solution.py:41
  115.3 5.7 %collective-permute-start.40 = (f32[128,256]{1,0:T(8,128)S(1)}, f32[128,256]{1,0:T(8,128)S(1)}, u32[]{:S(2)}, u32[]{:S(2)}) collective-permute-start(f32[128,256]{1,0:T(8,128)S(1)} %collective-permute-done.38.refs_3_), channel_id=1, source_target_pairs={{0,4},{1,5},{2,6},{3,7},{4,12},{5,13},{6,14},{7,15},{8,0},{9,1},{1... | collective-permute-start | bytes 393224 | tf_op jit(solution)/shard_map/ppermute | solution.py:41
  118.9 5.7 %collective-permute-start.41 = (f32[64,256]{1,0:T(8,128)S(1)}, f32[64,256]{1,0:T(8,128)S(1)}, u32[]{:S(2)}, u32[]{:S(2)}) collective-permute-start(f32[64,256]{1,0:T(8,128)S(1)} %slice.34), channel_id=1, source_target_pairs={{0,8},{1,9},{2,10},{3,11},{4,0},{5,1},{6,2},{7,3},{8,16},{9,17},{1... | collective-permute-start | bytes 196616 | tf_op jit(solution)/shard_map/ppermute | solution.py:41
  129.0 9.4 %collective-permute-start.51 = (f32[64,256]{1,0:T(8,128)S(1)}, f32[64,256]{1,0:T(8,128)S(1)}, u32[]{:S(2)}, u32[]{:S(2)}) collective-permute-start(f32[64,256]{1,0:T(8,128)S(1)} %get-tuple-element.215), channel_id=1, source_target_pairs={{0,4},{1,5},{2,6},{3,7},{4,12},{5,13},{6,14},{7,15},{8,0},{9,1},{1... | collective-permute-start | bytes 196616 | tf_op jit(solution)/shard_map/ppermute | solution.py:41
  129.6 9.4 %collective-permute-start.47 = (f32[64,256]{1,0:T(8,128)S(1)}, f32[64,256]{1,0:T(8,128)S(1)}, u32[]{:S(2)}, u32[]{:S(2)}) collective-permute-start(f32[64,256]{1,0:T(8,128)S(1)} %get-tuple-element.216), channel_id=1, source_target_pairs={{0,8},{1,9},{2,10},{3,11},{4,0},{5,1},{6,2},{7,3},{8,16},{9,17},{1... | collective-permute-start | bytes 196616 | tf_op jit(solution)/shard_map/ppermute | solution.py:41
  138.5 12.2 %collective-permute-start.52 = (f32[128,256]{1,0:T(8,128)S(1)}, f32[128,256]{1,0:T(8,128)S(1)}, u32[]{:S(2)}, u32[]{:S(2)}) collective-permute-start(f32[128,256]{1,0:T(8,128)S(1)} %pad_add_fusion), channel_id=1, source_target_pairs={{0,4},{1,5},{2,6},{3,7},{4,12},{5,13},{6,14},{7,15},{8,0},{9,1},{1... | collective-permute-start | bytes 393224 | tf_op jit(solution)/shard_map/ppermute | solution.py:41
  139.0 13.5 %collective-permute-start.48 = (f32[128,256]{1,0:T(8,128)S(1)}, f32[128,256]{1,0:T(8,128)S(1)}, u32[]{:S(2)}, u32[]{:S(2)}) collective-permute-start(f32[128,256]{1,0:T(8,128)S(1)} %pad_add_fusion.1), channel_id=1, source_target_pairs={{0,8},{1,9},{2,10},{3,11},{4,0},{5,1},{6,2},{7,3},{8,16},{9,17},{1... | collective-permute-start | bytes 393224 | tf_op jit(solution)/shard_map/ppermute | solution.py:41
  150.6 6.2 %collective-permute-start.45 = (f32[32,16,64]{2,1,0:T(8,128)S(1)}, f32[32,16,64]{2,1,0:T(8,128)S(1)}, u32[]{:S(2)}, u32[]{:S(2)}) collective-permute-start(f32[32,16,64]{2,1,0:T(8,128)S(1)} %get-tuple-element.196), channel_id=1, source_target_pairs={{0,2},{1,3},{2,0},{3,1},{4,6},{5,7},{6,4},{7,5},{8,10},{9,11},{10,... | collective-permute-start | bytes 393224 | tf_op jit(solution)/shard_map/ppermute | solution.py:41
  150.7 7.4 %collective-permute-start.53 = (f32[128,256]{1,0:T(8,128)S(1)}, f32[128,256]{1,0:T(8,128)S(1)}, u32[]{:S(2)}, u32[]{:S(2)}) collective-permute-start(f32[128,256]{1,0:T(8,128)S(1)} %add.62), channel_id=1, source_target_pairs={{0,4},{1,5},{2,6},{3,7},{4,12},{5,13},{6,14},{7,15},{8,0},{9,1},{1... | collective-permute-start | bytes 393224 | tf_op jit(solution)/shard_map/ppermute | solution.py:41
  152.2 16.1 %collective-permute-start.43 = (f32[32,16,128]{2,1,0:T(8,128)S(1)}, f32[32,16,128]{2,1,0:T(8,128)S(1)}, u32[]{:S(2)}, u32[]{:S(2)}) collective-permute-start(f32[32,16,128]{2,1,0:T(8,128)S(1)} %get-tuple-element.181), channel_id=1, source_target_pairs={{0,2},{1,3},{2,0},{3,1},{4,6},{5,7},{6,4},{7,5},{8,10},{9,11},{10,... | collective-permute-start | bytes 786440 | tf_op jit(solution)/shard_map/ppermute | solution.py:41
  152.5 9.4 %collective-permute-start.49 = (f32[128,256]{1,0:T(8,128)S(1)}, f32[128,256]{1,0:T(8,128)S(1)}, u32[]{:S(2)}, u32[]{:S(2)}) collective-permute-start(f32[128,256]{1,0:T(8,128)S(1)} %add.59), channel_id=1, source_target_pairs={{0,8},{1,9},{2,10},{3,11},{4,0},{5,1},{6,2},{7,3},{8,16},{9,17},{1... | collective-permute-start | bytes 393224 | tf_op jit(solution)/shard_map/ppermute | solution.py:41
  154.8 8.6 %collective-permute-start.28 = (f32[32,1,320]{2,1,0:T(1,128)S(1)}, f32[32,1,320]{2,1,0:T(1,128)S(1)}, u32[]{:S(2)}, u32[]{:S(2)}) collective-permute-start(f32[32,1,320]{2,1,0:T(1,128)S(1)} %get-tuple-element.160), channel_id=1, source_target_pairs={{0,2},{2,4},{4,6},{6,8},{8,10},{10,12},{12,14},{14,16},{16,18},{18... | collective-permute-start | bytes 122888 | tf_op jit(solution)/shard_map/ppermute | solution.py:539
  156.8 9.4 %collective-permute-start.29 = (f32[32,1,320]{2,1,0:T(1,128)S(1)}, f32[32,1,320]{2,1,0:T(1,128)S(1)}, u32[]{:S(2)}, u32[]{:S(2)}) collective-permute-start(f32[32,1,320]{2,1,0:T(1,128)S(1)} %get-tuple-element.161), channel_id=1, source_target_pairs={{2,0},{4,2},{6,4},{8,6},{10,8},{12,10},{14,12},{16,14},{18,16},{20... | collective-permute-start | bytes 122888 | tf_op jit(solution)/shard_map/ppermute | solution.py:540
  161.8 8.5 %collective-permute-start.44 = (f32[32,16,64]{2,1,0:T(8,128)S(1)}, f32[32,16,64]{2,1,0:T(8,128)S(1)}, u32[]{:S(2)}, u32[]{:S(2)}) collective-permute-start(f32[32,16,64]{2,1,0:T(8,128)S(1)} %get-tuple-element.194), channel_id=1, source_target_pairs={{0,2},{1,3},{2,0},{3,1},{4,6},{5,7},{6,4},{7,5},{8,10},{9,11},{10,... | collective-permute-start | bytes 393224 | tf_op jit(solution)/shard_map/ppermute | solution.py:41
  161.9 8.6 %collective-permute-start.46 = (f32[32,16,64]{2,1,0:T(8,128)S(1)}, f32[32,16,64]{2,1,0:T(8,128)S(1)}, u32[]{:S(2)}, u32[]{:S(2)}) collective-permute-start(f32[32,16,64]{2,1,0:T(8,128)S(1)} %add.57), channel_id=1, source_target_pairs={{0,1},{1,0},{2,3},{3,2},{4,5},{5,4},{6,7},{7,6},{8,9},{9,8},{10,11... | collective-permute-start | bytes 393224 | tf_op jit(solution)/shard_map/ppermute | solution.py:41
  163.4 9.2 %collective-permute-start.54 = (f32[128,256]{1,0:T(8,128)S(1)}, f32[128,256]{1,0:T(8,128)S(1)}, u32[]{:S(2)}, u32[]{:S(2)}) collective-permute-start(f32[128,256]{1,0:T(8,128)S(1)} %add.63), channel_id=1, source_target_pairs={{0,4},{1,5},{2,6},{3,7},{4,12},{5,13},{6,14},{7,15},{8,0},{9,1},{1... | collective-permute-start | bytes 393224 | tf_op jit(solution)/shard_map/ppermute | solution.py:41
  166.2 6.4 %collective-permute-start.50 = (f32[128,256]{1,0:T(8,128)S(1)}, f32[128,256]{1,0:T(8,128)S(1)}, u32[]{:S(2)}, u32[]{:S(2)}) collective-permute-start(f32[128,256]{1,0:T(8,128)S(1)} %add.60), channel_id=1, source_target_pairs={{0,8},{1,9},{2,10},{3,11},{4,0},{5,1},{6,2},{7,3},{8,16},{9,17},{1... | collective-permute-start | bytes 393224 | tf_op jit(solution)/shard_map/ppermute | solution.py:41
  (22 other events, 219.2 us)

commit v7 on v6

--- a/solution.py
+++ b/solution.py
@@ -436,7 +436,9 @@
 
 
 def update(info, ends, count, plane, first, second, grad, borders, at_row, at_col, outs):
-    above, below, left, right = borders
+    chip, core, left, right = borders
+    odd = info[0] % 2 == 1
+    above, below = jnp.where(odd, core[...], chip[...]), jnp.where(odd, chip[...], core[...])
     p = plane[...]
     rows, cols = p.shape[1:]
     above = jnp.where(info[0] == 0, p[:, :1, :], above[:, :, at_row : at_row + cols])
@@ -502,12 +504,14 @@
     return outs[:3], outs[3]
 
 
-def edges_kernel(peers, info, xy, xz, yz, *outs):
+def edges_kernel(peers, info, xy, xz, yz, gate, *outs):
     width = xy.shape[2]
     for ref, at in ((xy, 0), (yz, width), (xz, 2 * width)):
         rows, cols = ref.shape[1:]
-        outs[0][:, :, at : at + cols] = ref[:, rows - 1 :, :]
-        outs[1][:, :, at : at + cols] = ref[:, :1, :]
+        last, first = ref[:, rows - 1 :, :], ref[:, :1, :]
+        odd = info[0] % 2 == 1
+        outs[0][:, :, at : at + cols] = jnp.where(odd, last, first)
+        outs[1][:, :, at : at + cols] = jnp.where(odd, first, last)
     at = 0
     for ref in (xy, xz, yz):
         c, rows, cols = ref.shape
@@ -522,29 +526,32 @@
         at += c * rows
 
 
-def borders(info, planes):
+def borders(info, planes, gate):
     n, peers = lax.axis_size("gx"), lax.axis_size("gy")
     c = planes[0].shape[0]
     row = jax.ShapeDtypeStruct((c, 1, sum(p.shape[2] for p in planes)), f32)
     col = jax.ShapeDtypeStruct((1, sum(c * p.shape[1] for p in planes)), f32)
     outs = pl.pallas_call(
         functools.partial(edges_kernel, peers),
-        in_specs=[SCALARS] + vmem(3),
+        in_specs=[SCALARS] + vmem(3) + [pl.BlockSpec(memory_space=pl.ANY)],
         out_specs=vmem(3 if peers == 2 else 4),
         out_shape=[row, row] + [col] * (1 if peers == 2 else 2),
         compiler_params=SMALL,
         cost_estimate=cost(0, 2**20),
-    )(info, *planes)
-    up = [(i, i + 1) for i in range(n - 1)]
-    above = lax.ppermute(outs[0], "gx", up)
-    below = lax.ppermute(outs[1], "gx", [(j, i) for i, j in up])
+    )(info, *planes, gate)
+
+    def next_chip(k, c, y):
+        to = k + 1 if c == 1 else k - 1
+        return (to, 1 - c, y) if 0 <= to < n // 2 else None
+
+    chip, core = send(outs[0], next_chip), to_core(outs[1])
     if peers == 2:
         left = right = lax.ppermute(outs[2], "gy", [(0, 1), (1, 0)])
     else:
         up = [(i, i + 1) for i in range(peers - 1)]
         left = lax.ppermute(outs[2], "gy", up)
         right = lax.ppermute(outs[3], "gy", [(j, i) for i, j in up])
-    return above, below, left, right
+    return chip, core, left, right
 
 
 def per_device(
@@ -589,7 +596,6 @@
         for s in range(1, peers):
             xz_y = to_gy(plane_xz, s)
             xzs += [xz_y, to_core(xz_y)]
-        around = borders(info, (plane_xy, plane_xz, plane_yz))
         if fixed is None:
             fixed = fixed_parts(info, target, target_b, zl, w_hidden, b_hidden, w_output, b_output)
         wanted, weights = fixed[0], fixed[1:]
@@ -605,6 +611,8 @@
             )
             for o, line, block in zip(group, lines, blocks):
                 parts_xz[slot[o]], parts_yz[o] = line, block
+            if group == (1,):
+                around = borders(info, (plane_xy, plane_xz, plane_yz), lines[0])
         block = parts_yz[half]
         send_ahead, send_back = to_ring(block[:middle], 1), to_ring(block[middle:], -1)
         for d in range(half - 1, 0, -1):

time: 176 us -> 172 us (0.977)
  starting transfers between devices: 59.9 us -> 55.9 us
    ppermute x4 -> x0, starting transfers between devices: 5.8 us -> none  [the longest x2 3.22 us: borders(): above = lax.ppermute(outs[0], 'gx', up)]
    ppermute x49 -> x53, starting transfers between devices: 50.8 us -> 52.7 us  [send(): return lax.ppermute(x, BOTH, pairs)]
    ppermute x49 -> x53, waiting for transfers between devices: 18.8 us -> 19.8 us  [send(): return lax.ppermute(x, BOTH, pairs)]
  transfers between devices with their start and end apart: 55 -> 55, of which waited for: 12 -> 10; matrix products, arithmetic and copies ran while one was open for 0% -> 0% of each run, Pallas kernels for 36% -> 37%
where the time goes in v7:
time: 172 us; the launch traced here: 171 us
  Pallas kernels  87.4 us (51%)
  starting transfers between devices  55.9 us (32%)
  waiting for transfers between devices  23.7 us (14%)
  between operations  2 us (1%)
  local copies, waits for them, and re-layouts  1.97 us (1%)
    pallas_call x12, Pallas kernels, block_grads(): pl.pallas_call(functools.partial(grads_kernel, count, before is None), gr...  58.1 us
    ppermute x53, starting transfers between devices, send(): return lax.ppermute(x, BOTH, pairs)  52.7 us
    ppermute x53, waiting for transfers between devices, send(): return lax.ppermute(x, BOTH, pairs)  19.8 us
    pallas_call x4, Pallas kernels, update_one(): pl.pallas_call(functools.partial(update_one_kernel, ends, count, at_row,...  6.37 us
    pallas_call x2, Pallas kernels, spread_xz(): pl.pallas_call(functools.partial(spread_xz_kernel, chips, peers, zl), in_...  5.33 us
    pallas_call x2, Pallas kernels, collect_xz(): pl.pallas_call(functools.partial(collect_xz_kernel, chips, peers, zl), in...  5.3 us
    pallas_call x1, Pallas kernels, fixed_parts(): pl.pallas_call(functools.partial(fixed_kernel, chips, zl), in_specs=[SCAL...  4.1 us
    ppermute x2, waiting for transfers between devices, borders(): left = right = lax.ppermute(outs[2], 'gy', [(0, 1), (1, 0)])  3.98 us
  transfers between devices with their start and end apart: 55, of which 10 were waited for; matrix products, arithmetic and copies ran while one was open for 0% of the time, Pallas kernels for 37%

profile of v7, /device:TPU:0, one launch (start us, length us, event | category | flops | bytes accessed | tf_op | source)
XLA Modules:
  0.0 171.4 jit_solution(5312529612709439591)
XLA Ops:
  2.3 2.6 %collective-permute-start.6 = (f32[128,256]{1,0:T(8,128)S(1)}, f32[128,256]{1,0:T(8,128)S(1)}, u32[]{:S(2)}, u32[]{:S(2)}) collective-permute-start(f32[128,256]{1,0:T(8,128)S(1)} %shard_map.316.refs_1_), channel_id=1, source_target_pairs={{0,8},{1,9},{2,10},{3,11},{4,0},{5,1},{6,2},{7,3},{8,16},{9,17},{1... | collective-permute-start | bytes 393224 | tf_op jit(solution)/shard_map/ppermute | solution.py:41
  4.9 4.1 %collective-permute-done.6.refs_1_ = f32[128,256]{1,0:T(8,128)S(1)} collective-permute-done((f32[128,256]{1,0:T(8,128)S(1)}, f32[128,256]{1,0:T(8,128)S(1)}, u32[]{:S(2)}, u32[]{:S(2)}) %collective-permute-start.6) | collective-permute-done | bytes 131104 | tf_op jit(solution)/shard_map/ppermute | solution.py:41
  9.0 1.8 %collective-permute-start.10 = (f32[128,256]{1,0:T(8,128)S(1)}, f32[128,256]{1,0:T(8,128)S(1)}, u32[]{:S(2)}, u32[]{:S(2)}) collective-permute-start(f32[128,256]{1,0:T(8,128)S(1)} %collective-permute-done.6.refs_1_), channel_id=1, source_target_pairs={{0,8},{1,9},{2,10},{3,11},{4,0},{5,1},{6,2},{7,3},{8,16},{9,17},{1... | collective-permute-start | bytes 393224 | tf_op jit(solution)/shard_map/ppermute | solution.py:41
  11.0 1.7 collective-permute-start.3
  12.7 1.6 collective-permute-done.10.refs_2_
  16.3 3.6 %collective-permute-done.3.refs_2_ = f32[32,16,64]{2,1,0:T(8,128)S(1)} collective-permute-done((f32[32,16,64]{2,1,0:T(8,128)}, f32[32,16,64]{2,1,0:T(8,128)S(1)}, u32[]{:S(2)}, u32[]{:S(2)}) %collective-permute-start.3) | collective-permute-done | bytes 131104 | tf_op jit(solution)/shard_map/ppermute | solution.py:41
  21.2 1.8 %collective-permute-start.14 = (f32[64,256]{1,0:T(8,128)S(1)}, f32[64,256]{1,0:T(8,128)S(1)}, u32[]{:S(2)}, u32[]{:S(2)}) collective-permute-start(f32[64,256]{1,0:T(8,128)S(1)} %slice.32), channel_id=1, source_target_pairs={{0,8},{1,9},{2,10},{3,11},{4,0},{5,1},{6,2},{7,3},{8,16},{9,17},{1... | collective-permute-start | bytes 196616 | tf_op jit(solution)/shard_map/ppermute | solution.py:41
  25.2 2.7 %shard_map.315 = (f32[32,256]{1,0:T(8,128)S(1)}, f32[32,256]{1,0:T(8,128)S(1)}, f32[32,256]{1,0:T(8,128)S(1)}, f32[32,256]{1,0:T(8,128)S(1)}, f32[32,256]{1,0:T(...) custom-call(s32[2]{0:T(128)S(1)} %pad_add_fusion.4.info, ...), custom_call_target="tpu_custom_call" | custom-call | bytes 3145728 | tf_op jit(solution)/shard_map/pallas_call | solution.py:226
  28.0 4.1 %shard_map.313 = (bf16[32,128,128]{2,1,0:T(8,128)(2,1)S(1)}, bf16[256,256]{1,0:T(8,128)(2,1)S(1)}, bf16[256,256]{1,0:T(8,128)(2,1)S(1)}, bf16[256,256]{1,0:T(8,1...) custom-call(s32[2]{0:T(128)S(1)} %pad_add_fusion.4.info, f32[1]{0:T(128)S(6)} %copy.35.b_output, ...), custom_call_target="tpu_custom_call" | custom-call | bytes 4194304 | tf_op jit(solution)/shard_map/pallas_call | solution.py:130
  32.1 3.5 %shard_map.317 = (f32[32,128,128]{2,1,0:T(8,128)S(1)}, f32[32,256]{1,0:T(8,128)S(1)}, f32[128,256]{1,0:T(8,128)S(1)}) custom-call(s32[1]{0:T(128)} %constant.23.clone.slot, bf16[256,256]{1,0:T(8,128)(2,1)S(1)} %get-tuple-element.112.w_in, bf16[256,256]{1,0:T(8,128)(2,1)S(1)} %get-tuple-element.113.w_out, bf16[256,256]{1,0:T(8,128)(2,1)S(1)} %get-tuple-element.114.w_back, ...), custom_call_target="tpu_custom_call" | custom-call | flops 1610612736 | bytes 10485760 | tf_op jit(solution)/shard_map/pallas_call | solution.py:386
  35.6 3.6 %shard_map.318 = (f32[32,128,128]{2,1,0:T(8,128)S(1)}, f32[32,256]{1,0:T(8,128)S(1)}, f32[128,256]{1,0:T(8,128)S(1)}) custom-call(s32[1]{0:T(128)} %constant.24.clone.slot, bf16[256,256]{1,0:T(8,128)(2,1)S(1)} %get-tuple-element.112.w_in, bf16[256,256]{1,0:T(8,128)(2,1)S(1)} %get-tuple-element.113.w_out, bf16[256,256]{1,0:T(8,128)(2,1)S(1)} %get-tuple-element.114.w_back, ...), custom_call_target="tpu_custom_call" | custom-call | flops 1610612736 | bytes 10485760 | tf_op jit(solution)/shard_map/pallas_call | solution.py:386
  39.3 3.6 %shard_map.319 = (f32[32,128,128]{2,1,0:T(8,128)S(1)}, f32[32,256]{1,0:T(8,128)S(1)}, f32[128,256]{1,0:T(8,128)S(1)}) custom-call(s32[1]{0:T(128)} %constant.25.clone.slot, bf16[256,256]{1,0:T(8,128)(2,1)S(1)} %get-tuple-element.112.w_in, bf16[256,256]{1,0:T(8,128)(2,1)S(1)} %get-tuple-element.113.w_out, bf16[256,256]{1,0:T(8,128)(2,1)S(1)} %get-tuple-element.114.w_back, ...), custom_call_target="tpu_custom_call" | custom-call | flops 1610612736 | bytes 10485760 | tf_op jit(solution)/shard_map/pallas_call | solution.py:386
  43.0 3.6 %shard_map.321 = (f32[32,128,128]{2,1,0:T(8,128)S(1)}, f32[32,256]{1,0:T(8,128)S(1)}, f32[128,256]{1,0:T(8,128)S(1)}) custom-call(s32[1]{0:T(128)} %constant.26.clone.slot, bf16[256,256]{1,0:T(8,128)(2,1)S(1)} %get-tuple-element.112.w_in, bf16[256,256]{1,0:T(8,128)(2,1)S(1)} %get-tuple-element.113.w_out, bf16[256,256]{1,0:T(8,128)(2,1)S(1)} %get-tuple-element.114.w_back, ...), custom_call_target="tpu_custom_call" | custom-call | flops 1610612736 | bytes 10485760 | tf_op jit(solution)/shard_map/pallas_call | solution.py:386
  46.6 1.8 %collective-permute-start.24 = (f32[64,256]{1,0:T(8,128)S(1)}, f32[64,256]{1,0:T(8,128)S(1)}, u32[]{:S(2)}, u32[]{:S(2)}) collective-permute-start(f32[64,256]{1,0:T(8,128)S(1)} %get-tuple-element.217), channel_id=1, source_target_pairs={{0,4},{1,5},{2,6},{3,7},{4,12},{5,13},{6,14},{7,15},{8,0},{9,1},{1... | collective-permute-start | bytes 196616 | tf_op jit(solution)/shard_map/ppermute | solution.py:41
  48.7 7.3 %shard_map.322 = (f32[32,128,128]{2,1,0:T(8,128)S(1)}, f32[32,256]{1,0:T(8,128)S(1)}, f32[32,256]{1,0:T(8,128)S(1)}, f32[128,256]{1,0:T(8,128)S(1)}, f32[128,256]{1,0:T(8,128)S(1)}) custom-call(s32[1]{0:T(128)} %constant.27.clone.slot, bf16[256,256]{1,0:T(8,128)(2,1)S(1)} %get-tuple-element.112.w_in, bf16[256,256]{1,0:T(8,128)(2,1)S(1)} %get-tuple-element.113.w_out, ...), custom_call_target="tpu_custom_call" | custom-call | flops 3221225472 | bytes 20971520 | tf_op jit(solution)/shard_map/pallas_call | solution.py:386
  56.1 7.3 %shard_map.323 = (f32[32,128,128]{2,1,0:T(8,128)S(1)}, f32[32,256]{1,0:T(8,128)S(1)}, f32[32,256]{1,0:T(8,128)S(1)}, f32[128,256]{1,0:T(8,128)S(1)}, f32[128,256]{1,0:T(8,128)S(1)}) custom-call(s32[1]{0:T(128)} %constant.28.clone.slot, bf16[256,256]{1,0:T(8,128)(2,1)S(1)} %get-tuple-element.112.w_in, bf16[256,256]{1,0:T(8,128)(2,1)S(1)} %get-tuple-element.113.w_out, ...), custom_call_target="tpu_custom_call" | custom-call | flops 3221225472 | bytes 20971520 | tf_op jit(solution)/shard_map/pallas_call | solution.py:386
  63.4 2.7 %shard_map.326 = (f32[32,16,64]{2,1,0:T(8,128)S(1)}, f32[32,16,64]{2,1,0:T(8,128)S(1)}, f32[32,16,64]{2,1,0:T(8,128)S(1)}, f32[32,16,64]{2,1,0:T(8,128)S(1)}) custom-call(s32[2]{0:T(128)S(1)} %pad_add_fusion.4.info, f32[32,256]{1,0:T(8,128)S(1)} %get-tuple-element.139.refs_0_, f32[32,256]{1,0:T(8,128)S(1)} %get-tuple-element.140.refs_1_, ...), custom_call_target="tpu_custom_call" | custom-call | bytes 4194304 | tf_op jit(solution)/shard_map/pallas_call | solution.py:289
  66.2 1.8 %collective-permute-start.21 = (f32[128,256]{1,0:T(8,128)S(1)}, f32[128,256]{1,0:T(8,128)S(1)}, u32[]{:S(2)}, u32[]{:S(2)}) collective-permute-start(f32[128,256]{1,0:T(8,128)S(1)} %pad_add_fusion.3), channel_id=1, source_target_pairs={{0,8},{1,9},{2,10},{3,11},{4,0},{5,1},{6,2},{7,3},{8,16},{9,17},{1... | collective-permute-start | bytes 393224 | tf_op jit(solution)/shard_map/ppermute | solution.py:41
  70.3 1.8 %collective-permute-start.9 = (f32[1,1280]{1,0:T(1,128)S(1)}, f32[1,1280]{1,0:T(1,128)S(1)}, u32[]{:S(2)}, u32[]{:S(2)}) collective-permute-start(f32[1,1280]{1,0:T(1,128)S(1)} %get-tuple-element.126), channel_id=1, source_target_pairs={{0,1},{1,0},{2,3},{3,2},{4,5},{5,4},{6,7},{7,6},{8,9},{9,8},{10,11... | collective-permute-start | bytes 15368 | tf_op jit(solution)/shard_map/ppermute | solution.py:549
  72.0 1.9 %collective-permute-done.9.left.right = f32[1,1280]{1,0:T(1,128)S(1)} collective-permute-done((f32[1,1280]{1,0:T(1,128)S(1)}, f32[1,1280]{1,0:T(1,128)S(1)}, u32[]{:S(2)}, u32[]{:S(2)}) %collective-permute-start.9) | collective-permute-done | bytes 5152 | tf_op jit(solution)/shard_map/ppermute | solution.py:549
  74.6 3.1 %collective-permute-start.8 = (f32[32,1,320]{2,1,0:T(1,128)S(1)}, f32[32,1,320]{2,1,0:T(1,128)S(1)}, u32[]{:S(2)}, u32[]{:S(2)}) collective-permute-start(f32[32,1,320]{2,1,0:T(1,128)S(1)} %get-tuple-element.125), channel_id=1, source_target_pairs={{0,2},{1,3},{2,0},{3,1},{4,6},{5,7},{6,4},{7,5},{8,10},{9,11},{10,... | collective-permute-start | bytes 122888 | tf_op jit(solution)/shard_map/ppermute | solution.py:41
  77.8 1.6 collective-permute-start.17
  81.0 2.6 %collective-permute-start.22 = (f32[128,256]{1,0:T(8,128)S(1)}, f32[128,256]{1,0:T(8,128)S(1)}, u32[]{:S(2)}, u32[]{:S(2)}) collective-permute-start(f32[128,256]{1,0:T(8,128)S(1)} %add.52), channel_id=1, source_target_pairs={{0,8},{1,9},{2,10},{3,11},{4,0},{5,1},{6,2},{7,3},{8,16},{9,17},{1... | collective-permute-start | bytes 393224 | tf_op jit(solution)/shard_map/ppermute | solution.py:41
  83.7 4.0 %collective-permute-done.19.refs_5_ = f32[32,16,64]{2,1,0:T(8,128)S(1)} collective-permute-done((f32[32,16,64]{2,1,0:T(8,128)S(1)}, f32[32,16,64]{2,1,0:T(8,128)S(1)}, u32[]{:S(2)}, u32[]{:S(2)}) %collective-permute-start.19) | collective-permute-done | bytes 131104 | tf_op jit(solution)/shard_map/ppermute | solution.py:41
  88.9 1.6 collective-permute-start.30
  90.5 3.1 %collective-permute-start.23 = (f32[128,256]{1,0:T(8,128)S(1)}, f32[128,256]{1,0:T(8,128)S(1)}, u32[]{:S(2)}, u32[]{:S(2)}) collective-permute-start(f32[128,256]{1,0:T(8,128)S(1)} %add.53), channel_id=1, source_target_pairs={{0,8},{1,9},{2,10},{3,11},{4,0},{5,1},{6,2},{7,3},{8,16},{9,17},{1... | collective-permute-start | bytes 393224 | tf_op jit(solution)/shard_map/ppermute | solution.py:41
  96.3 2.3 %collective-permute-done.27.d = f32[128,256]{1,0:T(8,128)S(1)} collective-permute-done((f32[128,256]{1,0:T(8,128)S(1)}, f32[128,256]{1,0:T(8,128)S(1)}, u32[]{:S(2)}, u32[]{:S(2)}) %collective-permute-start.27) | collective-permute-done | bytes 131104 | tf_op jit(solution)/shard_map/ppermute | solution.py:41
  99.7 1.6 collective-permute-start.33
  101.8 2.7 %shard_map.330 = (f32[32,256]{1,0:T(8,128)S(1)}, f32[32,256]{1,0:T(8,128)S(1)}, f32[32,256]{1,0:T(8,128)S(1)}, f32[32,256]{1,0:T(8,128)S(1)}, f32[32,256]{1,0:T(...) custom-call(s32[2]{0:T(128)S(1)} %pad_add_fusion.4.info, ...), custom_call_target="tpu_custom_call" | custom-call | bytes 3145728 | tf_op jit(solution)/shard_map/pallas_call | solution.py:226
  105.3 1.6 collective-permute-start.37
  107.4 3.5 %shard_map.331 = (f32[32,128,128]{2,1,0:T(8,128)S(1)}, f32[32,256]{1,0:T(8,128)S(1)}, f32[128,256]{1,0:T(8,128)S(1)}) custom-call(s32[1]{0:T(128)} %constant.23.clone.slot, bf16[256,256]{1,0:T(8,128)(2,1)S(1)} %get-tuple-element.112.w_in, bf16[256,256]{1,0:T(8,128)(2,1)S(1)} %get-tuple-element.113.w_out, bf16[256,256]{1,0:T(8,128)(2,1)S(1)} %get-tuple-element.114.w_back, ...), custom_call_target="tpu_custom_call" | custom-call | flops 1610612736 | bytes 10485760 | tf_op jit(solution)/shard_map/pallas_call | solution.py:386
  110.9 1.6 collective-permute-start.39
  113.0 3.6 %shard_map.332 = (f32[32,128,128]{2,1,0:T(8,128)S(1)}, f32[32,256]{1,0:T(8,128)S(1)}, f32[128,256]{1,0:T(8,128)S(1)}) custom-call(s32[1]{0:T(128)} %constant.24.clone.slot, bf16[256,256]{1,0:T(8,128)(2,1)S(1)} %get-tuple-element.112.w_in, bf16[256,256]{1,0:T(8,128)(2,1)S(1)} %get-tuple-element.113.w_out, bf16[256,256]{1,0:T(8,128)(2,1)S(1)} %get-tuple-element.114.w_back, ...), custom_call_target="tpu_custom_call" | custom-call | flops 1610612736 | bytes 10485760 | tf_op jit(solution)/shard_map/pallas_call | solution.py:386
  116.7 1.6 collective-permute-start.41
  118.8 3.5 %shard_map.333 = (f32[32,128,128]{2,1,0:T(8,128)S(1)}, f32[32,256]{1,0:T(8,128)S(1)}, f32[128,256]{1,0:T(8,128)S(1)}) custom-call(s32[1]{0:T(128)} %constant.25.clone.slot, bf16[256,256]{1,0:T(8,128)(2,1)S(1)} %get-tuple-element.112.w_in, bf16[256,256]{1,0:T(8,128)(2,1)S(1)} %get-tuple-element.113.w_out, bf16[256,256]{1,0:T(8,128)(2,1)S(1)} %get-tuple-element.114.w_back, ...), custom_call_target="tpu_custom_call" | custom-call | flops 1610612736 | bytes 10485760 | tf_op jit(solution)/shard_map/pallas_call | solution.py:386
  122.7 3.6 %shard_map.335 = (f32[32,128,128]{2,1,0:T(8,128)S(1)}, f32[32,256]{1,0:T(8,128)S(1)}, f32[128,256]{1,0:T(8,128)S(1)}) custom-call(s32[1]{0:T(128)} %constant.26.clone.slot, bf16[256,256]{1,0:T(8,128)(2,1)S(1)} %get-tuple-element.112.w_in, bf16[256,256]{1,0:T(8,128)(2,1)S(1)} %get-tuple-element.113.w_out, bf16[256,256]{1,0:T(8,128)(2,1)S(1)} %get-tuple-element.114.w_back, ...), custom_call_target="tpu_custom_call" | custom-call | flops 1610612736 | bytes 10485760 | tf_op jit(solution)/shard_map/pallas_call | solution.py:386
  128.4 7.3 %shard_map.336 = (f32[32,128,128]{2,1,0:T(8,128)S(1)}, f32[32,256]{1,0:T(8,128)S(1)}, f32[32,256]{1,0:T(8,128)S(1)}, f32[128,256]{1,0:T(8,128)S(1)}, f32[128,256]{1,0:T(8,128)S(1)}) custom-call(s32[1]{0:T(128)} %constant.27.clone.slot, bf16[256,256]{1,0:T(8,128)(2,1)S(1)} %get-tuple-element.112.w_in, bf16[256,256]{1,0:T(8,128)(2,1)S(1)} %get-tuple-element.113.w_out, ...), custom_call_target="tpu_custom_call" | custom-call | flops 3221225472 | bytes 20971520 | tf_op jit(solution)/shard_map/pallas_call | solution.py:386
  135.8 1.6 collective-permute-start.48
  137.9 7.3 %shard_map.337 = (f32[32,128,128]{2,1,0:T(8,128)S(1)}, f32[32,256]{1,0:T(8,128)S(1)}, f32[32,256]{1,0:T(8,128)S(1)}, f32[128,256]{1,0:T(8,128)S(1)}, f32[128,256]{1,0:T(8,128)S(1)}) custom-call(s32[1]{0:T(128)} %constant.28.clone.slot, bf16[256,256]{1,0:T(8,128)(2,1)S(1)} %get-tuple-element.112.w_in, bf16[256,256]{1,0:T(8,128)(2,1)S(1)} %get-tuple-element.113.w_out, ...), custom_call_target="tpu_custom_call" | custom-call | flops 3221225472 | bytes 20971520 | tf_op jit(solution)/shard_map/pallas_call | solution.py:386
  145.2 2.6 %shard_map.340 = (f32[32,16,64]{2,1,0:T(8,128)S(1)}, f32[32,16,64]{2,1,0:T(8,128)S(1)}, f32[32,16,64]{2,1,0:T(8,128)S(1)}, f32[32,16,64]{2,1,0:T(8,128)S(1)}) custom-call(s32[2]{0:T(128)S(1)} %pad_add_fusion.4.info, f32[32,256]{1,0:T(8,128)S(1)} %get-tuple-element.186.refs_0_, f32[32,256]{1,0:T(8,128)S(1)} %get-tuple-element.187.refs_1_, ...), custom_call_target="tpu_custom_call" | custom-call | bytes 4194304 | tf_op jit(solution)/shard_map/pallas_call | solution.py:289
  148.0 1.6 collective-permute-start.49
  152.9 2.3 %collective-permute-start.35 = (f32[32,1,320]{2,1,0:T(1,128)S(1)}, f32[32,1,320]{2,1,0:T(1,128)S(1)}, u32[]{:S(2)}, u32[]{:S(2)}) collective-permute-start(f32[32,1,320]{2,1,0:T(1,128)S(1)} %get-tuple-element.168), channel_id=1, source_target_pairs={{0,2},{1,3},{2,0},{3,1},{4,6},{5,7},{6,4},{7,5},{8,10},{9,11},{10,... | collective-permute-start | bytes 122888 | tf_op jit(solution)/shard_map/ppermute | solution.py:41
  156.8 2.1 %collective-permute-done.36.left.right = f32[1,1280]{1,0:T(1,128)S(1)} collective-permute-done((f32[1,1280]{1,0:T(1,128)S(1)}, f32[1,1280]{1,0:T(1,128)S(1)}, u32[]{:S(2)}, u32[]{:S(2)}) %collective-permute-start.36) | collective-permute-done | bytes 5152 | tf_op jit(solution)/shard_map/ppermute | solution.py:549
  160.3 1.6 collective-permute-start.50
  162.6 2.0 %shard_map.339 = (f32[32,16,128]{2,1,0:T(8,128)}, f32[32,16,128]{2,1,0:T(8,128)}, f32[32,16,128]{2,1,0:T(8,128)}) custom-call(s32[2]{0:T(128)S(1)} %pad_add_fusion.4.info, f32[32,1,320]{2,1,0:T(1,128)S(1)} %collective-permute-done.34.above, f32[32,1,320]{2,1,0:T(1,128)S(1)} %collective-permute-done.35.below, ...), custom_call_target="tpu_custom_call" | custom-call | bytes 2097152 | tf_op jit(solution)/shard_map/pallas_call | solution.py:468
  164.6 3.0 %collective-permute-done.46.refs_5_ = f32[32,16,64]{2,1,0:T(8,128)S(1)} collective-permute-done((f32[32,16,64]{2,1,0:T(8,128)S(1)}, f32[32,16,64]{2,1,0:T(8,128)S(1)}, u32[]{:S(2)}, u32[]{:S(2)}) %collective-permute-start.46) | collective-permute-done | bytes 131104 | tf_op jit(solution)/shard_map/ppermute | solution.py:41
  167.5 2.1 %shard_map.341 = (f32[32,16,64]{2,1,0:T(8,128)}, f32[32,16,64]{2,1,0:T(8,128)}, f32[32,16,64]{2,1,0:T(8,128)}) custom-call(s32[2]{0:T(128)S(1)} %pad_add_fusion.4.info, f32[32,1,320]{2,1,0:T(1,128)S(1)} %collective-permute-done.34.above, f32[32,1,320]{2,1,0:T(1,128)S(1)} %collective-permute-done.35.below, f32[1,1280]{1,0:T(1,128)S(1)} %collective-permute-done.36.left.right, ...), custom_call_target="tpu_custom_call" | custom-call | bytes 2097152 | tf_op jit(solution)/shard_map/pallas_call | solution.py:468
  169.6 1.8 %shard_map.342 = (f32[32,8,128]{2,1,0:T(8,128)}, f32[32,8,128]{2,1,0:T(8,128)}, f32[32,8,128]{2,1,0:T(8,128)}, f32[128,256]{1,0:T(8,128)}) custom-call(s32[2]{0:T(128)S(1)} %pad_add_fusion.4.info, f32[32,1,320]{2,1,0:T(1,128)S(1)} %collective-permute-done.34.above, f32[32,1,320]{2,1,0:T(1,128)S(1)} %collective-permute-done.35.below, ...), custom_call_target="tpu_custom_call" | custom-call | bytes 2097152 | tf_op jit(solution)/shard_map/pallas_call | solution.py:495
  (145 shorter events, 29.1 us)
Async XLA Ops:
  0.7 27.3 %collective-permute-start = (f32[16,128,128]{2,1,0:T(8,128)}, f32[16,128,128]{2,1,0:T(8,128)S(1)}, u32[]{:S(2)}, u32[]{:S(2)}) collective-permute-start(f32[16,128,128]{2,1,0:T(8,128)} %target_a.1), channel_id=1, source_target_pairs={{0,2},{1,3},{2,0},{3,1},{4,6},{5,7},{6,4},{7,5},{8,10},{9,11},{10,... | collective-permute-start | bytes 3145736 | tf_op jit(solution)/shard_map/ppermute | solution.py:41
  2.3 6.7 %collective-permute-start.6 = (f32[128,256]{1,0:T(8,128)S(1)}, f32[128,256]{1,0:T(8,128)S(1)}, u32[]{:S(2)}, u32[]{:S(2)}) collective-permute-start(f32[128,256]{1,0:T(8,128)S(1)} %shard_map.316.refs_1_), channel_id=1, source_target_pairs={{0,8},{1,9},{2,10},{3,11},{4,0},{5,1},{6,2},{7,3},{8,16},{9,17},{1... | collective-permute-start | bytes 393224 | tf_op jit(solution)/shard_map/ppermute | solution.py:41
  4.9 5.9 %collective-permute-start.5 = (f32[128,256]{1,0:T(8,128)S(1)}, f32[128,256]{1,0:T(8,128)S(1)}, u32[]{:S(2)}, u32[]{:S(2)}) collective-permute-start(f32[128,256]{1,0:T(8,128)S(1)} %shard_map.316.refs_1_), channel_id=1, source_target_pairs={{0,4},{1,5},{2,6},{3,7},{4,12},{5,13},{6,14},{7,15},{8,0},{9,1},{1... | collective-permute-start | bytes 393224 | tf_op jit(solution)/shard_map/ppermute | solution.py:41
  9.0 5.3 %collective-permute-start.10 = (f32[128,256]{1,0:T(8,128)S(1)}, f32[128,256]{1,0:T(8,128)S(1)}, u32[]{:S(2)}, u32[]{:S(2)}) collective-permute-start(f32[128,256]{1,0:T(8,128)S(1)} %collective-permute-done.6.refs_1_), channel_id=1, source_target_pairs={{0,8},{1,9},{2,10},{3,11},{4,0},{5,1},{6,2},{7,3},{8,16},{9,17},{1... | collective-permute-start | bytes 393224 | tf_op jit(solution)/shard_map/ppermute | solution.py:41
  10.8 5.0 %collective-permute-start.11 = (f32[128,256]{1,0:T(8,128)S(1)}, f32[128,256]{1,0:T(8,128)S(1)}, u32[]{:S(2)}, u32[]{:S(2)}) collective-permute-start(f32[128,256]{1,0:T(8,128)S(1)} %collective-permute-done.5.refs_1_), channel_id=1, source_target_pairs={{0,4},{1,5},{2,6},{3,7},{4,12},{5,13},{6,14},{7,15},{8,0},{9,1},{1... | collective-permute-start | bytes 393224 | tf_op jit(solution)/shard_map/ppermute | solution.py:41
  11.0 12.0 %collective-permute-start.1 = (f32[32,16,128]{2,1,0:T(8,128)}, f32[32,16,128]{2,1,0:T(8,128)S(1)}, u32[]{:S(2)}, u32[]{:S(2)}) collective-permute-start(f32[32,16,128]{2,1,0:T(8,128)} %refs_0_.4), channel_id=1, source_target_pairs={{0,2},{1,3},{2,0},{3,1},{4,6},{5,7},{6,4},{7,5},{8,10},{9,11},{10,... | collective-permute-start | bytes 786440 | tf_op jit(solution)/shard_map/ppermute | solution.py:41
  11.0 8.9 %collective-permute-start.3 = (f32[32,16,64]{2,1,0:T(8,128)}, f32[32,16,64]{2,1,0:T(8,128)S(1)}, u32[]{:S(2)}, u32[]{:S(2)}) collective-permute-start(f32[32,16,64]{2,1,0:T(8,128)} %refs_0_.5), channel_id=1, source_target_pairs={{0,1},{1,0},{2,3},{3,2},{4,5},{5,4},{6,7},{7,6},{8,9},{9,8},{10,11... | collective-permute-start | bytes 393224 | tf_op jit(solution)/shard_map/ppermute | solution.py:41
  14.3 5.7 %collective-permute-start.12 = (f32[128,256]{1,0:T(8,128)S(1)}, f32[128,256]{1,0:T(8,128)S(1)}, u32[]{:S(2)}, u32[]{:S(2)}) collective-permute-start(f32[128,256]{1,0:T(8,128)S(1)} %collective-permute-done.10.refs_2_), channel_id=1, source_target_pairs={{0,8},{1,9},{2,10},{3,11},{4,0},{5,1},{6,2},{7,3},{8,16},{9,17},{1... | collective-permute-start | bytes 393224 | tf_op jit(solution)/shard_map/ppermute | solution.py:41
  15.8 5.3 %collective-permute-start.13 = (f32[128,256]{1,0:T(8,128)S(1)}, f32[128,256]{1,0:T(8,128)S(1)}, u32[]{:S(2)}, u32[]{:S(2)}) collective-permute-start(f32[128,256]{1,0:T(8,128)S(1)} %collective-permute-done.11.refs_3_), channel_id=1, source_target_pairs={{0,4},{1,5},{2,6},{3,7},{4,12},{5,13},{6,14},{7,15},{8,0},{9,1},{1... | collective-permute-start | bytes 393224 | tf_op jit(solution)/shard_map/ppermute | solution.py:41
  19.9 5.3 %collective-permute-start.2 = (f32[32,16,64]{2,1,0:T(8,128)}, f32[32,16,64]{2,1,0:T(8,128)S(1)}, u32[]{:S(2)}, u32[]{:S(2)}) collective-permute-start(f32[32,16,64]{2,1,0:T(8,128)} %refs_0_.5), channel_id=1, source_target_pairs={{0,2},{1,3},{2,0},{3,1},{4,6},{5,7},{6,4},{7,5},{8,10},{9,11},{10,... | collective-permute-start | bytes 393224 | tf_op jit(solution)/shard_map/ppermute | solution.py:41
  20.0 5.3 %collective-permute-start.4 = (f32[32,16,64]{2,1,0:T(8,128)S(1)}, f32[32,16,64]{2,1,0:T(8,128)S(1)}, u32[]{:S(2)}, u32[]{:S(2)}) collective-permute-start(f32[32,16,64]{2,1,0:T(8,128)S(1)} %collective-permute-done.3.refs_2_), channel_id=1, source_target_pairs={{0,2},{1,3},{2,0},{3,1},{4,6},{5,7},{6,4},{7,5},{8,10},{9,11},{10,... | collective-permute-start | bytes 393224 | tf_op jit(solution)/shard_map/ppermute | solution.py:41
  21.2 6.7 %collective-permute-start.14 = (f32[64,256]{1,0:T(8,128)S(1)}, f32[64,256]{1,0:T(8,128)S(1)}, u32[]{:S(2)}, u32[]{:S(2)}) collective-permute-start(f32[64,256]{1,0:T(8,128)S(1)} %slice.32), channel_id=1, source_target_pairs={{0,8},{1,9},{2,10},{3,11},{4,0},{5,1},{6,2},{7,3},{8,16},{9,17},{1... | collective-permute-start | bytes 196616 | tf_op jit(solution)/shard_map/ppermute | solution.py:41
  46.6 21.4 %collective-permute-start.24 = (f32[64,256]{1,0:T(8,128)S(1)}, f32[64,256]{1,0:T(8,128)S(1)}, u32[]{:S(2)}, u32[]{:S(2)}) collective-permute-start(f32[64,256]{1,0:T(8,128)S(1)} %get-tuple-element.217), channel_id=1, source_target_pairs={{0,4},{1,5},{2,6},{3,7},{4,12},{5,13},{6,14},{7,15},{8,0},{9,1},{1... | collective-permute-start | bytes 196616 | tf_op jit(solution)/shard_map/ppermute | solution.py:41
  48.4 17.7 %collective-permute-start.20 = (f32[64,256]{1,0:T(8,128)S(1)}, f32[64,256]{1,0:T(8,128)S(1)}, u32[]{:S(2)}, u32[]{:S(2)}) collective-permute-start(f32[64,256]{1,0:T(8,128)S(1)} %get-tuple-element.218), channel_id=1, source_target_pairs={{0,8},{1,9},{2,10},{3,11},{4,0},{5,1},{6,2},{7,3},{8,16},{9,17},{1... | collective-permute-start | bytes 196616 | tf_op jit(solution)/shard_map/ppermute | solution.py:41
  66.1 8.5 %collective-permute-start.18 = (f32[32,16,64]{2,1,0:T(8,128)S(1)}, f32[32,16,64]{2,1,0:T(8,128)S(1)}, u32[]{:S(2)}, u32[]{:S(2)}) collective-permute-start(f32[32,16,64]{2,1,0:T(8,128)S(1)} %get-tuple-element.149), channel_id=1, source_target_pairs={{0,2},{1,3},{2,0},{3,1},{4,6},{5,7},{6,4},{7,5},{8,10},{9,11},{10,... | collective-permute-start | bytes 393224 | tf_op jit(solution)/shard_map/ppermute | solution.py:41
  66.2 13.3 %collective-permute-start.21 = (f32[128,256]{1,0:T(8,128)S(1)}, f32[128,256]{1,0:T(8,128)S(1)}, u32[]{:S(2)}, u32[]{:S(2)}) collective-permute-start(f32[128,256]{1,0:T(8,128)S(1)} %pad_add_fusion.3), channel_id=1, source_target_pairs={{0,8},{1,9},{2,10},{3,11},{4,0},{5,1},{6,2},{7,3},{8,16},{9,17},{1... | collective-permute-start | bytes 393224 | tf_op jit(solution)/shard_map/ppermute | solution.py:41
  68.0 12.9 %collective-permute-start.25 = (f32[128,256]{1,0:T(8,128)S(1)}, f32[128,256]{1,0:T(8,128)S(1)}, u32[]{:S(2)}, u32[]{:S(2)}) collective-permute-start(f32[128,256]{1,0:T(8,128)S(1)} %pad_add_fusion.2), channel_id=1, source_target_pairs={{0,4},{1,5},{2,6},{3,7},{4,12},{5,13},{6,14},{7,15},{8,0},{9,1},{1... | collective-permute-start | bytes 393224 | tf_op jit(solution)/shard_map/ppermute | solution.py:41
  69.3 24.4 %collective-permute-start.16 = (f32[32,16,128]{2,1,0:T(8,128)S(1)}, f32[32,16,128]{2,1,0:T(8,128)S(1)}, u32[]{:S(2)}, u32[]{:S(2)}) collective-permute-start(f32[32,16,128]{2,1,0:T(8,128)S(1)} %get-tuple-element.137), channel_id=1, source_target_pairs={{0,2},{1,3},{2,0},{3,1},{4,6},{5,7},{6,4},{7,5},{8,10},{9,11},{10,... | collective-permute-start | bytes 786440 | tf_op jit(solution)/shard_map/ppermute | solution.py:41
  74.6 9.0 %collective-permute-start.8 = (f32[32,1,320]{2,1,0:T(1,128)S(1)}, f32[32,1,320]{2,1,0:T(1,128)S(1)}, u32[]{:S(2)}, u32[]{:S(2)}) collective-permute-start(f32[32,1,320]{2,1,0:T(1,128)S(1)} %get-tuple-element.125), channel_id=1, source_target_pairs={{0,2},{1,3},{2,0},{3,1},{4,6},{5,7},{6,4},{7,5},{8,10},{9,11},{10,... | collective-permute-start | bytes 122888 | tf_op jit(solution)/shard_map/ppermute | solution.py:41
  77.8 5.9 %collective-permute-start.17 = (f32[32,16,64]{2,1,0:T(8,128)S(1)}, f32[32,16,64]{2,1,0:T(8,128)S(1)}, u32[]{:S(2)}, u32[]{:S(2)}) collective-permute-start(f32[32,16,64]{2,1,0:T(8,128)S(1)} %get-tuple-element.147), channel_id=1, source_target_pairs={{0,2},{1,3},{2,0},{3,1},{4,6},{5,7},{6,4},{7,5},{8,10},{9,11},{10,... | collective-permute-start | bytes 393224 | tf_op jit(solution)/shard_map/ppermute | solution.py:41
  79.4 8.2 %collective-permute-start.19 = (f32[32,16,64]{2,1,0:T(8,128)S(1)}, f32[32,16,64]{2,1,0:T(8,128)S(1)}, u32[]{:S(2)}, u32[]{:S(2)}) collective-permute-start(f32[32,16,64]{2,1,0:T(8,128)S(1)} %add.50), channel_id=1, source_target_pairs={{0,1},{1,0},{2,3},{3,2},{4,5},{5,4},{6,7},{7,6},{8,9},{9,8},{10,11... | collective-permute-start | bytes 393224 | tf_op jit(solution)/shard_map/ppermute | solution.py:41
  81.0 9.5 %collective-permute-start.22 = (f32[128,256]{1,0:T(8,128)S(1)}, f32[128,256]{1,0:T(8,128)S(1)}, u32[]{:S(2)}, u32[]{:S(2)}) collective-permute-start(f32[128,256]{1,0:T(8,128)S(1)} %add.52), channel_id=1, source_target_pairs={{0,8},{1,9},{2,10},{3,11},{4,0},{5,1},{6,2},{7,3},{8,16},{9,17},{1... | collective-permute-start | bytes 393224 | tf_op jit(solution)/shard_map/ppermute | solution.py:41
  83.6 10.0 %collective-permute-start.26 = (f32[128,256]{1,0:T(8,128)S(1)}, f32[128,256]{1,0:T(8,128)S(1)}, u32[]{:S(2)}, u32[]{:S(2)}) collective-permute-start(f32[128,256]{1,0:T(8,128)S(1)} %add.55), channel_id=1, source_target_pairs={{0,4},{1,5},{2,6},{3,7},{4,12},{5,13},{6,14},{7,15},{8,0},{9,1},{1... | collective-permute-start | bytes 393224 | tf_op jit(solution)/shard_map/ppermute | solution.py:41
  88.9 7.4 %collective-permute-start.30 = (f32[32,16,64]{2,1,0:T(8,128)S(1)}, f32[32,16,64]{2,1,0:T(8,128)S(1)}, u32[]{:S(2)}, u32[]{:S(2)}) collective-permute-start(f32[32,16,64]{2,1,0:T(8,128)S(1)} %get-tuple-element.150.refs_0_.xz), channel_id=1, source_target_pairs={{0,1},{1,0},{2,3},{3,2},{4,5},{5,4},{6,7},{7,6},{8,9},{9,8},{10,11... | collective-permute-start | bytes 393224 | tf_op jit(solution)/shard_map/ppermute | solution.py:41
  90.5 5.8 %collective-permute-start.23 = (f32[128,256]{1,0:T(8,128)S(1)}, f32[128,256]{1,0:T(8,128)S(1)}, u32[]{:S(2)}, u32[]{:S(2)}) collective-permute-start(f32[128,256]{1,0:T(8,128)S(1)} %add.53), channel_id=1, source_target_pairs={{0,8},{1,9},{2,10},{3,11},{4,0},{5,1},{6,2},{7,3},{8,16},{9,17},{1... | collective-permute-start | bytes 393224 | tf_op jit(solution)/shard_map/ppermute | solution.py:41
  94.8 9.6 %collective-permute-start.28 = (f32[32,16,128]{2,1,0:T(8,128)S(1)}, f32[32,16,128]{2,1,0:T(8,128)S(1)}, u32[]{:S(2)}, u32[]{:S(2)}) collective-permute-start(f32[32,16,128]{2,1,0:T(8,128)S(1)} %get-tuple-element.138.xy_a.xy.refs_0_), channel_id=1, source_target_pairs={{0,2},{1,3},{2,0},{3,1},{4,6},{5,7},{6,4},{7,5},{8,10},{9,11},{10,... | collective-permute-start | bytes 786440 | tf_op jit(solution)/shard_map/ppermute | solution.py:41
  94.9 6.9 %collective-permute-start.29 = (f32[32,16,64]{2,1,0:T(8,128)S(1)}, f32[32,16,64]{2,1,0:T(8,128)S(1)}, u32[]{:S(2)}, u32[]{:S(2)}) collective-permute-start(f32[32,16,64]{2,1,0:T(8,128)S(1)} %get-tuple-element.150.refs_0_.xz), channel_id=1, source_target_pairs={{0,2},{1,3},{2,0},{3,1},{4,6},{5,7},{6,4},{7,5},{8,10},{9,11},{10,... | collective-permute-start | bytes 393224 | tf_op jit(solution)/shard_map/ppermute | solution.py:41
  96.3 5.5 %collective-permute-start.31 = (f32[32,16,64]{2,1,0:T(8,128)S(1)}, f32[32,16,64]{2,1,0:T(8,128)S(1)}, u32[]{:S(2)}, u32[]{:S(2)}) collective-permute-start(f32[32,16,64]{2,1,0:T(8,128)S(1)} %collective-permute-done.30.refs_2_), channel_id=1, source_target_pairs={{0,2},{1,3},{2,0},{3,1},{4,6},{5,7},{6,4},{7,5},{8,10},{9,11},{10,... | collective-permute-start | bytes 393224 | tf_op jit(solution)/shard_map/ppermute | solution.py:41
  99.7 5.6 %collective-permute-start.33 = (f32[128,256]{1,0:T(8,128)S(1)}, f32[128,256]{1,0:T(8,128)S(1)}, u32[]{:S(2)}, u32[]{:S(2)}) collective-permute-start(f32[128,256]{1,0:T(8,128)S(1)} %get-tuple-element.161.refs_1_), channel_id=1, source_target_pairs={{0,8},{1,9},{2,10},{3,11},{4,0},{5,1},{6,2},{7,3},{8,16},{9,17},{1... | collective-permute-start | bytes 393224 | tf_op jit(solution)/shard_map/ppermute | solution.py:41
  101.3 5.6 %collective-permute-start.32 = (f32[128,256]{1,0:T(8,128)S(1)}, f32[128,256]{1,0:T(8,128)S(1)}, u32[]{:S(2)}, u32[]{:S(2)}) collective-permute-start(f32[128,256]{1,0:T(8,128)S(1)} %get-tuple-element.161.refs_1_), channel_id=1, source_target_pairs={{0,4},{1,5},{2,6},{3,7},{4,12},{5,13},{6,14},{7,15},{8,0},{9,1},{1... | collective-permute-start | bytes 393224 | tf_op jit(solution)/shard_map/ppermute | solution.py:41
  105.3 5.6 %collective-permute-start.37 = (f32[128,256]{1,0:T(8,128)S(1)}, f32[128,256]{1,0:T(8,128)S(1)}, u32[]{:S(2)}, u32[]{:S(2)}) collective-permute-start(f32[128,256]{1,0:T(8,128)S(1)} %collective-permute-done.33.refs_1_), channel_id=1, source_target_pairs={{0,8},{1,9},{2,10},{3,11},{4,0},{5,1},{6,2},{7,3},{8,16},{9,17},{1... | collective-permute-start | bytes 393224 | tf_op jit(solution)/shard_map/ppermute | solution.py:41
  107.0 5.6 %collective-permute-start.38 = (f32[128,256]{1,0:T(8,128)S(1)}, f32[128,256]{1,0:T(8,128)S(1)}, u32[]{:S(2)}, u32[]{:S(2)}) collective-permute-start(f32[128,256]{1,0:T(8,128)S(1)} %collective-permute-done.32.refs_1_), channel_id=1, source_target_pairs={{0,4},{1,5},{2,6},{3,7},{4,12},{5,13},{6,14},{7,15},{8,0},{9,1},{1... | collective-permute-start | bytes 393224 | tf_op jit(solution)/shard_map/ppermute | solution.py:41
  110.9 5.7 %collective-permute-start.39 = (f32[128,256]{1,0:T(8,128)S(1)}, f32[128,256]{1,0:T(8,128)S(1)}, u32[]{:S(2)}, u32[]{:S(2)}) collective-permute-start(f32[128,256]{1,0:T(8,128)S(1)} %collective-permute-done.37.refs_2_), channel_id=1, source_target_pairs={{0,8},{1,9},{2,10},{3,11},{4,0},{5,1},{6,2},{7,3},{8,16},{9,17},{1... | collective-permute-start | bytes 393224 | tf_op jit(solution)/shard_map/ppermute | solution.py:41
  112.6 5.7 %collective-permute-start.40 = (f32[128,256]{1,0:T(8,128)S(1)}, f32[128,256]{1,0:T(8,128)S(1)}, u32[]{:S(2)}, u32[]{:S(2)}) collective-permute-start(f32[128,256]{1,0:T(8,128)S(1)} %collective-permute-done.38.refs_3_), channel_id=1, source_target_pairs={{0,4},{1,5},{2,6},{3,7},{4,12},{5,13},{6,14},{7,15},{8,0},{9,1},{1... | collective-permute-start | bytes 393224 | tf_op jit(solution)/shard_map/ppermute | solution.py:41
  116.7 5.7 %collective-permute-start.41 = (f32[64,256]{1,0:T(8,128)S(1)}, f32[64,256]{1,0:T(8,128)S(1)}, u32[]{:S(2)}, u32[]{:S(2)}) collective-permute-start(f32[64,256]{1,0:T(8,128)S(1)} %slice.34), channel_id=1, source_target_pairs={{0,8},{1,9},{2,10},{3,11},{4,0},{5,1},{6,2},{7,3},{8,16},{9,17},{1... | collective-permute-start | bytes 196616 | tf_op jit(solution)/shard_map/ppermute | solution.py:41
  126.3 11.1 %collective-permute-start.51 = (f32[64,256]{1,0:T(8,128)S(1)}, f32[64,256]{1,0:T(8,128)S(1)}, u32[]{:S(2)}, u32[]{:S(2)}) collective-permute-start(f32[64,256]{1,0:T(8,128)S(1)} %get-tuple-element.215), channel_id=1, source_target_pairs={{0,4},{1,5},{2,6},{3,7},{4,12},{5,13},{6,14},{7,15},{8,0},{9,1},{1... | collective-permute-start | bytes 196616 | tf_op jit(solution)/shard_map/ppermute | solution.py:41
  127.3 8.5 %collective-permute-start.47 = (f32[64,256]{1,0:T(8,128)S(1)}, f32[64,256]{1,0:T(8,128)S(1)}, u32[]{:S(2)}, u32[]{:S(2)}) collective-permute-start(f32[64,256]{1,0:T(8,128)S(1)} %get-tuple-element.216), channel_id=1, source_target_pairs={{0,8},{1,9},{2,10},{3,11},{4,0},{5,1},{6,2},{7,3},{8,16},{9,17},{1... | collective-permute-start | bytes 196616 | tf_op jit(solution)/shard_map/ppermute | solution.py:41
  135.8 12.2 %collective-permute-start.48 = (f32[128,256]{1,0:T(8,128)S(1)}, f32[128,256]{1,0:T(8,128)S(1)}, u32[]{:S(2)}, u32[]{:S(2)}) collective-permute-start(f32[128,256]{1,0:T(8,128)S(1)} %pad_add_fusion.1), channel_id=1, source_target_pairs={{0,8},{1,9},{2,10},{3,11},{4,0},{5,1},{6,2},{7,3},{8,16},{9,17},{1... | collective-permute-start | bytes 393224 | tf_op jit(solution)/shard_map/ppermute | solution.py:41
  137.4 13.5 %collective-permute-start.52 = (f32[128,256]{1,0:T(8,128)S(1)}, f32[128,256]{1,0:T(8,128)S(1)}, u32[]{:S(2)}, u32[]{:S(2)}) collective-permute-start(f32[128,256]{1,0:T(8,128)S(1)} %pad_add_fusion), channel_id=1, source_target_pairs={{0,4},{1,5},{2,6},{3,7},{4,12},{5,13},{6,14},{7,15},{8,0},{9,1},{1... | collective-permute-start | bytes 393224 | tf_op jit(solution)/shard_map/ppermute | solution.py:41
  148.0 7.2 %collective-permute-start.49 = (f32[128,256]{1,0:T(8,128)S(1)}, f32[128,256]{1,0:T(8,128)S(1)}, u32[]{:S(2)}, u32[]{:S(2)}) collective-permute-start(f32[128,256]{1,0:T(8,128)S(1)} %add.59), channel_id=1, source_target_pairs={{0,8},{1,9},{2,10},{3,11},{4,0},{5,1},{6,2},{7,3},{8,16},{9,17},{1... | collective-permute-start | bytes 393224 | tf_op jit(solution)/shard_map/ppermute | solution.py:41
  150.6 12.0 %collective-permute-start.43 = (f32[32,16,128]{2,1,0:T(8,128)S(1)}, f32[32,16,128]{2,1,0:T(8,128)S(1)}, u32[]{:S(2)}, u32[]{:S(2)}) collective-permute-start(f32[32,16,128]{2,1,0:T(8,128)S(1)} %get-tuple-element.182), channel_id=1, source_target_pairs={{0,2},{1,3},{2,0},{3,1},{4,6},{5,7},{6,4},{7,5},{8,10},{9,11},{10,... | collective-permute-start | bytes 786440 | tf_op jit(solution)/shard_map/ppermute | solution.py:41
  150.9 7.9 %collective-permute-start.53 = (f32[128,256]{1,0:T(8,128)S(1)}, f32[128,256]{1,0:T(8,128)S(1)}, u32[]{:S(2)}, u32[]{:S(2)}) collective-permute-start(f32[128,256]{1,0:T(8,128)S(1)} %add.62), channel_id=1, source_target_pairs={{0,4},{1,5},{2,6},{3,7},{4,12},{5,13},{6,14},{7,15},{8,0},{9,1},{1... | collective-permute-start | bytes 393224 | tf_op jit(solution)/shard_map/ppermute | solution.py:41
  152.2 8.1 %collective-permute-start.34 = (f32[32,1,320]{2,1,0:T(1,128)S(1)}, f32[32,1,320]{2,1,0:T(1,128)S(1)}, u32[]{:S(2)}, u32[]{:S(2)}) collective-permute-start(f32[32,1,320]{2,1,0:T(1,128)S(1)} %get-tuple-element.167), channel_id=1, source_target_pairs={{2,4},{3,5},{4,2},{5,3},{6,8},{7,9},{8,6},{9,7},{10,12},{11,13},{1... | collective-permute-start | bytes 122888 | tf_op jit(solution)/shard_map/ppermute | solution.py:41
  152.9 9.1 %collective-permute-start.35 = (f32[32,1,320]{2,1,0:T(1,128)S(1)}, f32[32,1,320]{2,1,0:T(1,128)S(1)}, u32[]{:S(2)}, u32[]{:S(2)}) collective-permute-start(f32[32,1,320]{2,1,0:T(1,128)S(1)} %get-tuple-element.168), channel_id=1, source_target_pairs={{0,2},{1,3},{2,0},{3,1},{4,6},{5,7},{6,4},{7,5},{8,10},{9,11},{10,... | collective-permute-start | bytes 122888 | tf_op jit(solution)/shard_map/ppermute | solution.py:41
  158.8 5.8 %collective-permute-start.44 = (f32[32,16,64]{2,1,0:T(8,128)S(1)}, f32[32,16,64]{2,1,0:T(8,128)S(1)}, u32[]{:S(2)}, u32[]{:S(2)}) collective-permute-start(f32[32,16,64]{2,1,0:T(8,128)S(1)} %get-tuple-element.194), channel_id=1, source_target_pairs={{0,2},{1,3},{2,0},{3,1},{4,6},{5,7},{6,4},{7,5},{8,10},{9,11},{10,... | collective-permute-start | bytes 393224 | tf_op jit(solution)/shard_map/ppermute | solution.py:41
  158.8 8.7 %collective-permute-start.46 = (f32[32,16,64]{2,1,0:T(8,128)S(1)}, f32[32,16,64]{2,1,0:T(8,128)S(1)}, u32[]{:S(2)}, u32[]{:S(2)}) collective-permute-start(f32[32,16,64]{2,1,0:T(8,128)S(1)} %add.57), channel_id=1, source_target_pairs={{0,1},{1,0},{2,3},{3,2},{4,5},{5,4},{6,7},{7,6},{8,9},{9,8},{10,11... | collective-permute-start | bytes 393224 | tf_op jit(solution)/shard_map/ppermute | solution.py:41
  160.3 9.3 %collective-permute-start.50 = (f32[128,256]{1,0:T(8,128)S(1)}, f32[128,256]{1,0:T(8,128)S(1)}, u32[]{:S(2)}, u32[]{:S(2)}) collective-permute-start(f32[128,256]{1,0:T(8,128)S(1)} %add.60), channel_id=1, source_target_pairs={{0,8},{1,9},{2,10},{3,11},{4,0},{5,1},{6,2},{7,3},{8,16},{9,17},{1... | collective-permute-start | bytes 393224 | tf_op jit(solution)/shard_map/ppermute | solution.py:41
  162.0 7.6 %collective-permute-start.54 = (f32[128,256]{1,0:T(8,128)S(1)}, f32[128,256]{1,0:T(8,128)S(1)}, u32[]{:S(2)}, u32[]{:S(2)}) collective-permute-start(f32[128,256]{1,0:T(8,128)S(1)} %add.63), channel_id=1, source_target_pairs={{0,4},{1,5},{2,6},{3,7},{4,12},{5,13},{6,14},{7,15},{8,0},{9,1},{1... | collective-permute-start | bytes 393224 | tf_op jit(solution)/shard_map/ppermute | solution.py:41
  (22 other events, 214.9 us)

commit v8 on v7

--- a/solution.py
+++ b/solution.py
@@ -263,6 +263,7 @@
 def collect_xz_kernel(chips, peers, zl, info, *refs):
     parts, outs, held = refs[:chips], refs[chips : chips + 2 * peers], refs[chips + 2 * peers]
     c, x_count, zs = outs[0].shape
+    half = x_count // 2
     held[...] = jnp.zeros_like(held)
     for p in range(chips):
         at = z_places(info[0], info[1], p, chips, peers, zl, zs)
@@ -270,17 +271,21 @@
         for j in range(zl):
             held[at + j] = rows[:, j * c : (j + 1) * c]
 
+    def turned(s, side, x):
+        return held[s * zs : (s + 1) * zs, side * x_count + x, :].T
+
     def some(i, carry):
-        for x in range(UNROLL):
-            x += i * UNROLL
-            for s in range(peers):
-                for side in range(2):
-                    outs[2 * s + side][:, x, :] = held[
-                        s * zs : (s + 1) * zs, side * x_count + x, :
-                    ].T
+        for x in range(UNROLL // 2):
+            x += i * (UNROLL // 2)
+            for side in range(2):
+                for far in (0, half):
+                    outs[side][:, x + far, :] = turned(0, side, x + far)
+                for s in range(1, peers):
+                    pair = turned(s, side, x), turned(s, side, x + half)
+                    outs[2 * s + side][:, x, :] = jnp.concatenate(pair, axis=1)
         return carry
 
-    lax.fori_loop(0, x_count // UNROLL, some, 0)
+    lax.fori_loop(0, half // (UNROLL // 2), some, 0)
 
 
 def collect_xz(info, parts, shape, zl):
@@ -290,7 +295,8 @@
         functools.partial(collect_xz_kernel, chips, peers, zl),
         in_specs=[SCALARS] + vmem(chips),
         out_specs=vmem(2 * peers),
-        out_shape=[jax.ShapeDtypeStruct(shape, f32)] * (2 * peers),
+        out_shape=[jax.ShapeDtypeStruct(shape, f32)] * 2
+        + [jax.ShapeDtypeStruct((c, x_count // 2, 2 * zs), f32)] * (2 * peers - 2),
         scratch_shapes=[pltpu.VMEM((peers * zs, 2 * x_count, c), f32)],
         compiler_params=SMALL,
         cost_estimate=cost(0, 4 * 2**20),
@@ -458,7 +464,13 @@
 
 def update_one_kernel(ends, count, at_row, at_col, info, above, below, left, right, *refs):
     state, grads, outs = refs[:3], refs[3:-3], refs[-3:]
-    grad = sum(g[...] for g in grads)
+    grad = 0.0
+    for ref in grads:
+        g = ref[...]
+        if g.shape != state[0].shape:
+            wide = g.shape[2] // 2
+            g = jnp.concatenate([g[:, :, :wide], g[:, :, wide:]], axis=1)
+        grad = grad + g
     borders = (above, below, left, right)
     update(info, ends, count, *state, grad, borders, at_row, at_col, outs)
 
@@ -626,14 +638,14 @@
         grad_xy, far_xy = collect_xy(part_xy, plane_xy, xy_b)
         sides = [pieces[2 * s] + to_core(pieces[2 * s + 1]) for s in range(1, peers)]
         grads_xz = [to_gy(side, -s) for s, side in enumerate(sides, 1)]
-        near_xz, far_xz = pieces[0], to_core(pieces[1])
+        far_xz, across_xz = to_core(pieces[1]), grads_xz[0]
         for extra in grads_xz[1:]:
-            near_xz = near_xz + extra
+            across_xz = across_xz + extra
         count = START + iteration + 1
         channels, rows, width = plane_xy.shape
         state = (plane_xz, first_xz, second_xz)
         plane_xz, first_xz, second_xz = update_one(
-            info, count, around, state, (near_xz, far_xz, grads_xz[0]), 2 * width, channels * rows
+            info, count, around, state, (pieces[0], far_xz, across_xz), 2 * width, channels * rows
         )
         state = (plane_xy, first_xy, second_xy)
         far_xy = to_core(far_xy)

time: 172 us -> 167 us (0.971)
  waiting for transfers between devices: 23.7 us -> 18.6 us
    ppermute x53, waiting for transfers between devices: 19.8 us -> 14.6 us  [send(): return lax.ppermute(x, BOTH, pairs)]
  transfers between devices with their start and end apart: 55 -> 55, of which waited for: 10 -> 11; matrix products, arithmetic and copies ran while one was open for 0% -> 0% of each run, Pallas kernels for 37% -> 38%
where the time goes in v8:
time: 167 us
  Pallas kernels  87.9 us (53%)
  starting transfers between devices  55.9 us (33%)
  waiting for transfers between devices  18.6 us (11%)
  between operations  2.01 us (1%)
  local copies, waits for them, and re-layouts  1.97 us (1%)
    pallas_call x12, Pallas kernels, block_grads(): pl.pallas_call(functools.partial(grads_kernel, count, before is None), gr...  58 us
    ppermute x53, starting transfers between devices, send(): return lax.ppermute(x, BOTH, pairs)  52.7 us
    ppermute x53, waiting for transfers between devices, send(): return lax.ppermute(x, BOTH, pairs)  14.6 us
    pallas_call x4, Pallas kernels, update_one(): pl.pallas_call(functools.partial(update_one_kernel, ends, count, at_row,...  6.46 us
    pallas_call x2, Pallas kernels, collect_xz(): pl.pallas_call(functools.partial(collect_xz_kernel, chips, peers, zl), in...  5.9 us
    pallas_call x2, Pallas kernels, spread_xz(): pl.pallas_call(functools.partial(spread_xz_kernel, chips, peers, zl), in_...  5.33 us
    pallas_call x1, Pallas kernels, fixed_parts(): pl.pallas_call(functools.partial(fixed_kernel, chips, zl), in_specs=[SCAL...  4.1 us
    ppermute x2, waiting for transfers between devices, borders(): left = right = lax.ppermute(outs[2], 'gy', [(0, 1), (1, 0)])  4 us
  transfers between devices with their start and end apart: 55, of which 11 were waited for; matrix products, arithmetic and copies ran while one was open for 0% of the time, Pallas kernels for 38%

profile of v8, /device:TPU:0, one launch (start us, length us, event | category | flops | bytes accessed | tf_op | source)
XLA Modules:
  0.0 166.7 jit_solution(13855136518866014792)
XLA Ops:
  2.3 2.6 %collective-permute-start.6 = (f32[128,256]{1,0:T(8,128)S(1)}, f32[128,256]{1,0:T(8,128)S(1)}, u32[]{:S(2)}, u32[]{:S(2)}) collective-permute-start(f32[128,256]{1,0:T(8,128)S(1)} %shard_map.316.refs_1_), channel_id=1, source_target_pairs={{0,8},{1,9},{2,10},{3,11},{4,0},{5,1},{6,2},{7,3},{8,16},{9,17},{1... | collective-permute-start | bytes 393224 | tf_op jit(solution)/shard_map/ppermute | solution.py:41
  4.9 4.1 %collective-permute-done.6.refs_1_ = f32[128,256]{1,0:T(8,128)S(1)} collective-permute-done((f32[128,256]{1,0:T(8,128)S(1)}, f32[128,256]{1,0:T(8,128)S(1)}, u32[]{:S(2)}, u32[]{:S(2)}) %collective-permute-start.6) | collective-permute-done | bytes 131104 | tf_op jit(solution)/shard_map/ppermute | solution.py:41
  9.0 1.8 %collective-permute-start.10 = (f32[128,256]{1,0:T(8,128)S(1)}, f32[128,256]{1,0:T(8,128)S(1)}, u32[]{:S(2)}, u32[]{:S(2)}) collective-permute-start(f32[128,256]{1,0:T(8,128)S(1)} %collective-permute-done.6.refs_1_), channel_id=1, source_target_pairs={{0,8},{1,9},{2,10},{3,11},{4,0},{5,1},{6,2},{7,3},{8,16},{9,17},{1... | collective-permute-start | bytes 393224 | tf_op jit(solution)/shard_map/ppermute | solution.py:41
  11.0 1.7 %collective-permute-start.3 = (f32[32,16,64]{2,1,0:T(8,128)}, f32[32,16,64]{2,1,0:T(8,128)S(1)}, u32[]{:S(2)}, u32[]{:S(2)}) collective-permute-start(f32[32,16,64]{2,1,0:T(8,128)} %refs_0_.5), channel_id=1, source_target_pairs={{0,1},{1,0},{2,3},{3,2},{4,5},{5,4},{6,7},{7,6},{8,9},{9,8},{10,11... | collective-permute-start | bytes 393224 | tf_op jit(solution)/shard_map/ppermute | solution.py:41
  12.7 1.6 collective-permute-done.10.refs_2_
  14.3 1.5 collective-permute-start.12
  16.3 3.6 %collective-permute-done.3.refs_2_ = f32[32,16,64]{2,1,0:T(8,128)S(1)} collective-permute-done((f32[32,16,64]{2,1,0:T(8,128)}, f32[32,16,64]{2,1,0:T(8,128)S(1)}, u32[]{:S(2)}, u32[]{:S(2)}) %collective-permute-start.3) | collective-permute-done | bytes 131104 | tf_op jit(solution)/shard_map/ppermute | solution.py:41
  21.2 1.8 %collective-permute-start.14 = (f32[64,256]{1,0:T(8,128)S(1)}, f32[64,256]{1,0:T(8,128)S(1)}, u32[]{:S(2)}, u32[]{:S(2)}) collective-permute-start(f32[64,256]{1,0:T(8,128)S(1)} %slice.32), channel_id=1, source_target_pairs={{0,8},{1,9},{2,10},{3,11},{4,0},{5,1},{6,2},{7,3},{8,16},{9,17},{1... | collective-permute-start | bytes 196616 | tf_op jit(solution)/shard_map/ppermute | solution.py:41
  25.2 2.7 %shard_map.315 = (f32[32,256]{1,0:T(8,128)S(1)}, f32[32,256]{1,0:T(8,128)S(1)}, f32[32,256]{1,0:T(8,128)S(1)}, f32[32,256]{1,0:T(8,128)S(1)}, f32[32,256]{1,0:T(...) custom-call(s32[2]{0:T(128)S(1)} %pad_add_fusion.4.info, ...), custom_call_target="tpu_custom_call" | custom-call | bytes 3145728 | tf_op jit(solution)/shard_map/pallas_call | solution.py:226
  28.0 4.1 %shard_map.313 = (bf16[32,128,128]{2,1,0:T(8,128)(2,1)S(1)}, bf16[256,256]{1,0:T(8,128)(2,1)S(1)}, bf16[256,256]{1,0:T(8,128)(2,1)S(1)}, bf16[256,256]{1,0:T(8,1...) custom-call(s32[2]{0:T(128)S(1)} %pad_add_fusion.4.info, f32[1]{0:T(128)S(6)} %copy.35.b_output, ...), custom_call_target="tpu_custom_call" | custom-call | bytes 4194304 | tf_op jit(solution)/shard_map/pallas_call | solution.py:130
  32.1 3.5 %shard_map.317 = (f32[32,128,128]{2,1,0:T(8,128)S(1)}, f32[32,256]{1,0:T(8,128)S(1)}, f32[128,256]{1,0:T(8,128)S(1)}) custom-call(s32[1]{0:T(128)} %constant.23.clone.slot, bf16[256,256]{1,0:T(8,128)(2,1)S(1)} %get-tuple-element.112.w_in, bf16[256,256]{1,0:T(8,128)(2,1)S(1)} %get-tuple-element.113.w_out, bf16[256,256]{1,0:T(8,128)(2,1)S(1)} %get-tuple-element.114.w_back, ...), custom_call_target="tpu_custom_call" | custom-call | flops 1610612736 | bytes 10485760 | tf_op jit(solution)/shard_map/pallas_call | solution.py:392
  35.6 3.6 %shard_map.318 = (f32[32,128,128]{2,1,0:T(8,128)S(1)}, f32[32,256]{1,0:T(8,128)S(1)}, f32[128,256]{1,0:T(8,128)S(1)}) custom-call(s32[1]{0:T(128)} %constant.24.clone.slot, bf16[256,256]{1,0:T(8,128)(2,1)S(1)} %get-tuple-element.112.w_in, bf16[256,256]{1,0:T(8,128)(2,1)S(1)} %get-tuple-element.113.w_out, bf16[256,256]{1,0:T(8,128)(2,1)S(1)} %get-tuple-element.114.w_back, ...), custom_call_target="tpu_custom_call" | custom-call | flops 1610612736 | bytes 10485760 | tf_op jit(solution)/shard_map/pallas_call | solution.py:392
  39.3 3.6 %shard_map.319 = (f32[32,128,128]{2,1,0:T(8,128)S(1)}, f32[32,256]{1,0:T(8,128)S(1)}, f32[128,256]{1,0:T(8,128)S(1)}) custom-call(s32[1]{0:T(128)} %constant.25.clone.slot, bf16[256,256]{1,0:T(8,128)(2,1)S(1)} %get-tuple-element.112.w_in, bf16[256,256]{1,0:T(8,128)(2,1)S(1)} %get-tuple-element.113.w_out, bf16[256,256]{1,0:T(8,128)(2,1)S(1)} %get-tuple-element.114.w_back, ...), custom_call_target="tpu_custom_call" | custom-call | flops 1610612736 | bytes 10485760 | tf_op jit(solution)/shard_map/pallas_call | solution.py:392
  43.0 3.7 %shard_map.321 = (f32[32,128,128]{2,1,0:T(8,128)S(1)}, f32[32,256]{1,0:T(8,128)S(1)}, f32[128,256]{1,0:T(8,128)S(1)}) custom-call(s32[1]{0:T(128)} %constant.26.clone.slot, bf16[256,256]{1,0:T(8,128)(2,1)S(1)} %get-tuple-element.112.w_in, bf16[256,256]{1,0:T(8,128)(2,1)S(1)} %get-tuple-element.113.w_out, bf16[256,256]{1,0:T(8,128)(2,1)S(1)} %get-tuple-element.114.w_back, ...), custom_call_target="tpu_custom_call" | custom-call | flops 1610612736 | bytes 10485760 | tf_op jit(solution)/shard_map/pallas_call | solution.py:392
  46.6 1.8 %collective-permute-start.24 = (f32[64,256]{1,0:T(8,128)S(1)}, f32[64,256]{1,0:T(8,128)S(1)}, u32[]{:S(2)}, u32[]{:S(2)}) collective-permute-start(f32[64,256]{1,0:T(8,128)S(1)} %get-tuple-element.217), channel_id=1, source_target_pairs={{0,4},{1,5},{2,6},{3,7},{4,12},{5,13},{6,14},{7,15},{8,0},{9,1},{1... | collective-permute-start | bytes 196616 | tf_op jit(solution)/shard_map/ppermute | solution.py:41
  48.7 7.2 %shard_map.322 = (f32[32,128,128]{2,1,0:T(8,128)S(1)}, f32[32,256]{1,0:T(8,128)S(1)}, f32[32,256]{1,0:T(8,128)S(1)}, f32[128,256]{1,0:T(8,128)S(1)}, f32[128,256]{1,0:T(8,128)S(1)}) custom-call(s32[1]{0:T(128)} %constant.27.clone.slot, bf16[256,256]{1,0:T(8,128)(2,1)S(1)} %get-tuple-element.112.w_in, bf16[256,256]{1,0:T(8,128)(2,1)S(1)} %get-tuple-element.113.w_out, ...), custom_call_target="tpu_custom_call" | custom-call | flops 3221225472 | bytes 20971520 | tf_op jit(solution)/shard_map/pallas_call | solution.py:392
  55.9 7.3 %shard_map.323 = (f32[32,128,128]{2,1,0:T(8,128)S(1)}, f32[32,256]{1,0:T(8,128)S(1)}, f32[32,256]{1,0:T(8,128)S(1)}, f32[128,256]{1,0:T(8,128)S(1)}, f32[128,256]{1,0:T(8,128)S(1)}) custom-call(s32[1]{0:T(128)} %constant.28.clone.slot, bf16[256,256]{1,0:T(8,128)(2,1)S(1)} %get-tuple-element.112.w_in, bf16[256,256]{1,0:T(8,128)(2,1)S(1)} %get-tuple-element.113.w_out, ...), custom_call_target="tpu_custom_call" | custom-call | flops 3221225472 | bytes 20971520 | tf_op jit(solution)/shard_map/pallas_call | solution.py:392
  63.3 2.9 %shard_map.326 = (f32[32,16,64]{2,1,0:T(8,128)S(1)}, f32[32,16,64]{2,1,0:T(8,128)S(1)}, f32[32,8,128]{2,1,0:T(8,128)S(1)}, f32[32,8,128]{2,1,0:T(8,128)S(1)}) custom-call(s32[2]{0:T(128)S(1)} %pad_add_fusion.4.info, f32[32,256]{1,0:T(8,128)S(1)} %get-tuple-element.139.refs_0_, f32[32,256]{1,0:T(8,128)S(1)} %get-tuple-element.140.refs_1_, ...), custom_call_target="tpu_custom_call" | custom-call | bytes 4194304 | tf_op jit(solution)/shard_map/pallas_call | solution.py:294
  66.3 1.8 %collective-permute-start.21 = (f32[128,256]{1,0:T(8,128)S(1)}, f32[128,256]{1,0:T(8,128)S(1)}, u32[]{:S(2)}, u32[]{:S(2)}) collective-permute-start(f32[128,256]{1,0:T(8,128)S(1)} %pad_add_fusion.3), channel_id=1, source_target_pairs={{0,8},{1,9},{2,10},{3,11},{4,0},{5,1},{6,2},{7,3},{8,16},{9,17},{1... | collective-permute-start | bytes 393224 | tf_op jit(solution)/shard_map/ppermute | solution.py:41
  70.4 1.8 %collective-permute-start.9 = (f32[1,1280]{1,0:T(1,128)S(1)}, f32[1,1280]{1,0:T(1,128)S(1)}, u32[]{:S(2)}, u32[]{:S(2)}) collective-permute-start(f32[1,1280]{1,0:T(1,128)S(1)} %get-tuple-element.126), channel_id=1, source_target_pairs={{0,1},{1,0},{2,3},{3,2},{4,5},{5,4},{6,7},{7,6},{8,9},{9,8},{10,11... | collective-permute-start | bytes 15368 | tf_op jit(solution)/shard_map/ppermute | solution.py:561
  72.2 1.9 %collective-permute-done.9.left.right = f32[1,1280]{1,0:T(1,128)S(1)} collective-permute-done((f32[1,1280]{1,0:T(1,128)S(1)}, f32[1,1280]{1,0:T(1,128)S(1)}, u32[]{:S(2)}, u32[]{:S(2)}) %collective-permute-start.9) | collective-permute-done | bytes 5152 | tf_op jit(solution)/shard_map/ppermute | solution.py:561
  74.8 3.2 %collective-permute-start.8 = (f32[32,1,320]{2,1,0:T(1,128)S(1)}, f32[32,1,320]{2,1,0:T(1,128)S(1)}, u32[]{:S(2)}, u32[]{:S(2)}) collective-permute-start(f32[32,1,320]{2,1,0:T(1,128)S(1)} %get-tuple-element.125), channel_id=1, source_target_pairs={{0,2},{1,3},{2,0},{3,1},{4,6},{5,7},{6,4},{7,5},{8,10},{9,11},{10,... | collective-permute-start | bytes 122888 | tf_op jit(solution)/shard_map/ppermute | solution.py:41
  77.9 1.7 collective-permute-start.17
  81.1 2.6 %collective-permute-start.22 = (f32[128,256]{1,0:T(8,128)S(1)}, f32[128,256]{1,0:T(8,128)S(1)}, u32[]{:S(2)}, u32[]{:S(2)}) collective-permute-start(f32[128,256]{1,0:T(8,128)S(1)} %add.52), channel_id=1, source_target_pairs={{0,8},{1,9},{2,10},{3,11},{4,0},{5,1},{6,2},{7,3},{8,16},{9,17},{1... | collective-permute-start | bytes 393224 | tf_op jit(solution)/shard_map/ppermute | solution.py:41
  86.3 1.6 collective-permute-start.30
  87.8 3.1 %collective-permute-start.23 = (f32[128,256]{1,0:T(8,128)S(1)}, f32[128,256]{1,0:T(8,128)S(1)}, u32[]{:S(2)}, u32[]{:S(2)}) collective-permute-start(f32[128,256]{1,0:T(8,128)S(1)} %add.53), channel_id=1, source_target_pairs={{0,8},{1,9},{2,10},{3,11},{4,0},{5,1},{6,2},{7,3},{8,16},{9,17},{1... | collective-permute-start | bytes 393224 | tf_op jit(solution)/shard_map/ppermute | solution.py:41
  93.7 2.3 %collective-permute-done.27.d = f32[128,256]{1,0:T(8,128)S(1)} collective-permute-done((f32[128,256]{1,0:T(8,128)S(1)}, f32[128,256]{1,0:T(8,128)S(1)}, u32[]{:S(2)}, u32[]{:S(2)}) %collective-permute-start.27) | collective-permute-done | bytes 131104 | tf_op jit(solution)/shard_map/ppermute | solution.py:41
  97.1 1.6 collective-permute-start.33
  99.1 2.7 %shard_map.330 = (f32[32,256]{1,0:T(8,128)S(1)}, f32[32,256]{1,0:T(8,128)S(1)}, f32[32,256]{1,0:T(8,128)S(1)}, f32[32,256]{1,0:T(8,128)S(1)}, f32[32,256]{1,0:T(...) custom-call(s32[2]{0:T(128)S(1)} %pad_add_fusion.4.info, ...), custom_call_target="tpu_custom_call" | custom-call | bytes 3145728 | tf_op jit(solution)/shard_map/pallas_call | solution.py:226
  102.7 1.6 collective-permute-start.37
  104.8 3.5 %shard_map.331 = (f32[32,128,128]{2,1,0:T(8,128)S(1)}, f32[32,256]{1,0:T(8,128)S(1)}, f32[128,256]{1,0:T(8,128)S(1)}) custom-call(s32[1]{0:T(128)} %constant.23.clone.slot, bf16[256,256]{1,0:T(8,128)(2,1)S(1)} %get-tuple-element.112.w_in, bf16[256,256]{1,0:T(8,128)(2,1)S(1)} %get-tuple-element.113.w_out, bf16[256,256]{1,0:T(8,128)(2,1)S(1)} %get-tuple-element.114.w_back, ...), custom_call_target="tpu_custom_call" | custom-call | flops 1610612736 | bytes 10485760 | tf_op jit(solution)/shard_map/pallas_call | solution.py:392
  108.3 1.6 collective-permute-start.39
  110.4 3.6 %shard_map.332 = (f32[32,128,128]{2,1,0:T(8,128)S(1)}, f32[32,256]{1,0:T(8,128)S(1)}, f32[128,256]{1,0:T(8,128)S(1)}) custom-call(s32[1]{0:T(128)} %constant.24.clone.slot, bf16[256,256]{1,0:T(8,128)(2,1)S(1)} %get-tuple-element.112.w_in, bf16[256,256]{1,0:T(8,128)(2,1)S(1)} %get-tuple-element.113.w_out, bf16[256,256]{1,0:T(8,128)(2,1)S(1)} %get-tuple-element.114.w_back, ...), custom_call_target="tpu_custom_call" | custom-call | flops 1610612736 | bytes 10485760 | tf_op jit(solution)/shard_map/pallas_call | solution.py:392
  114.0 1.6 collective-permute-start.41
  116.2 3.5 %shard_map.333 = (f32[32,128,128]{2,1,0:T(8,128)S(1)}, f32[32,256]{1,0:T(8,128)S(1)}, f32[128,256]{1,0:T(8,128)S(1)}) custom-call(s32[1]{0:T(128)} %constant.25.clone.slot, bf16[256,256]{1,0:T(8,128)(2,1)S(1)} %get-tuple-element.112.w_in, bf16[256,256]{1,0:T(8,128)(2,1)S(1)} %get-tuple-element.113.w_out, bf16[256,256]{1,0:T(8,128)(2,1)S(1)} %get-tuple-element.114.w_back, ...), custom_call_target="tpu_custom_call" | custom-call | flops 1610612736 | bytes 10485760 | tf_op jit(solution)/shard_map/pallas_call | solution.py:392
  120.0 3.6 %shard_map.335 = (f32[32,128,128]{2,1,0:T(8,128)S(1)}, f32[32,256]{1,0:T(8,128)S(1)}, f32[128,256]{1,0:T(8,128)S(1)}) custom-call(s32[1]{0:T(128)} %constant.26.clone.slot, bf16[256,256]{1,0:T(8,128)(2,1)S(1)} %get-tuple-element.112.w_in, bf16[256,256]{1,0:T(8,128)(2,1)S(1)} %get-tuple-element.113.w_out, bf16[256,256]{1,0:T(8,128)(2,1)S(1)} %get-tuple-element.114.w_back, ...), custom_call_target="tpu_custom_call" | custom-call | flops 1610612736 | bytes 10485760 | tf_op jit(solution)/shard_map/pallas_call | solution.py:392
  125.8 7.3 %shard_map.336 = (f32[32,128,128]{2,1,0:T(8,128)S(1)}, f32[32,256]{1,0:T(8,128)S(1)}, f32[32,256]{1,0:T(8,128)S(1)}, f32[128,256]{1,0:T(8,128)S(1)}, f32[128,256]{1,0:T(8,128)S(1)}) custom-call(s32[1]{0:T(128)} %constant.27.clone.slot, bf16[256,256]{1,0:T(8,128)(2,1)S(1)} %get-tuple-element.112.w_in, bf16[256,256]{1,0:T(8,128)(2,1)S(1)} %get-tuple-element.113.w_out, ...), custom_call_target="tpu_custom_call" | custom-call | flops 3221225472 | bytes 20971520 | tf_op jit(solution)/shard_map/pallas_call | solution.py:392
  133.1 1.6 collective-permute-start.48
  135.3 7.3 %shard_map.337 = (f32[32,128,128]{2,1,0:T(8,128)S(1)}, f32[32,256]{1,0:T(8,128)S(1)}, f32[32,256]{1,0:T(8,128)S(1)}, f32[128,256]{1,0:T(8,128)S(1)}, f32[128,256]{1,0:T(8,128)S(1)}) custom-call(s32[1]{0:T(128)} %constant.28.clone.slot, bf16[256,256]{1,0:T(8,128)(2,1)S(1)} %get-tuple-element.112.w_in, bf16[256,256]{1,0:T(8,128)(2,1)S(1)} %get-tuple-element.113.w_out, ...), custom_call_target="tpu_custom_call" | custom-call | flops 3221225472 | bytes 20971520 | tf_op jit(solution)/shard_map/pallas_call | solution.py:392
  142.6 3.0 %shard_map.340 = (f32[32,16,64]{2,1,0:T(8,128)S(1)}, f32[32,16,64]{2,1,0:T(8,128)S(1)}, f32[32,8,128]{2,1,0:T(8,128)S(1)}, f32[32,8,128]{2,1,0:T(8,128)S(1)}) custom-call(s32[2]{0:T(128)S(1)} %pad_add_fusion.4.info, f32[32,256]{1,0:T(8,128)S(1)} %get-tuple-element.186.refs_0_, f32[32,256]{1,0:T(8,128)S(1)} %get-tuple-element.187.refs_1_, ...), custom_call_target="tpu_custom_call" | custom-call | bytes 4194304 | tf_op jit(solution)/shard_map/pallas_call | solution.py:294
  145.7 1.6 collective-permute-start.49
  150.5 2.3 %collective-permute-start.35 = (f32[32,1,320]{2,1,0:T(1,128)S(1)}, f32[32,1,320]{2,1,0:T(1,128)S(1)}, u32[]{:S(2)}, u32[]{:S(2)}) collective-permute-start(f32[32,1,320]{2,1,0:T(1,128)S(1)} %get-tuple-element.168), channel_id=1, source_target_pairs={{0,2},{1,3},{2,0},{3,1},{4,6},{5,7},{6,4},{7,5},{8,10},{9,11},{10,... | collective-permute-start | bytes 122888 | tf_op jit(solution)/shard_map/ppermute | solution.py:41
  154.4 2.1 %collective-permute-done.36.left.right = f32[1,1280]{1,0:T(1,128)S(1)} collective-permute-done((f32[1,1280]{1,0:T(1,128)S(1)}, f32[1,1280]{1,0:T(1,128)S(1)}, u32[]{:S(2)}, u32[]{:S(2)}) %collective-permute-start.36) | collective-permute-done | bytes 5152 | tf_op jit(solution)/shard_map/ppermute | solution.py:561
  156.5 1.5 collective-permute-start.46
  158.0 1.6 collective-permute-start.50
  160.3 2.0 %shard_map.339 = (f32[32,16,128]{2,1,0:T(8,128)}, f32[32,16,128]{2,1,0:T(8,128)}, f32[32,16,128]{2,1,0:T(8,128)}) custom-call(s32[2]{0:T(128)S(1)} %pad_add_fusion.4.info, f32[32,1,320]{2,1,0:T(1,128)S(1)} %collective-permute-done.34.above, f32[32,1,320]{2,1,0:T(1,128)S(1)} %collective-permute-done.35.below, ...), custom_call_target="tpu_custom_call" | custom-call | bytes 2097152 | tf_op jit(solution)/shard_map/pallas_call | solution.py:480
  162.4 2.1 %shard_map.341 = (f32[32,16,64]{2,1,0:T(8,128)}, f32[32,16,64]{2,1,0:T(8,128)}, f32[32,16,64]{2,1,0:T(8,128)}) custom-call(s32[2]{0:T(128)S(1)} %pad_add_fusion.4.info, f32[32,1,320]{2,1,0:T(1,128)S(1)} %collective-permute-done.34.above, f32[32,1,320]{2,1,0:T(1,128)S(1)} %collective-permute-done.35.below, f32[1,1280]{1,0:T(1,128)S(1)} %collective-permute-done.36.left.right, ...), custom_call_target="tpu_custom_call" | custom-call | bytes 2097152 | tf_op jit(solution)/shard_map/pallas_call | solution.py:480
  165.0 1.8 %shard_map.342 = (f32[32,8,128]{2,1,0:T(8,128)}, f32[32,8,128]{2,1,0:T(8,128)}, f32[32,8,128]{2,1,0:T(8,128)}, f32[128,256]{1,0:T(8,128)}) custom-call(s32[2]{0:T(128)S(1)} %pad_add_fusion.4.info, f32[32,1,320]{2,1,0:T(1,128)S(1)} %collective-permute-done.34.above, f32[32,1,320]{2,1,0:T(1,128)S(1)} %collective-permute-done.35.below, ...), custom_call_target="tpu_custom_call" | custom-call | bytes 2097152 | tf_op jit(solution)/shard_map/pallas_call | solution.py:507
  (145 shorter events, 27.8 us)
Async XLA Ops:
  0.7 27.3 %collective-permute-start = (f32[16,128,128]{2,1,0:T(8,128)}, f32[16,128,128]{2,1,0:T(8,128)S(1)}, u32[]{:S(2)}, u32[]{:S(2)}) collective-permute-start(f32[16,128,128]{2,1,0:T(8,128)} %target_a.1), channel_id=1, source_target_pairs={{0,2},{1,3},{2,0},{3,1},{4,6},{5,7},{6,4},{7,5},{8,10},{9,11},{10,... | collective-permute-start | bytes 3145736 | tf_op jit(solution)/shard_map/ppermute | solution.py:41
  2.3 6.7 %collective-permute-start.6 = (f32[128,256]{1,0:T(8,128)S(1)}, f32[128,256]{1,0:T(8,128)S(1)}, u32[]{:S(2)}, u32[]{:S(2)}) collective-permute-start(f32[128,256]{1,0:T(8,128)S(1)} %shard_map.316.refs_1_), channel_id=1, source_target_pairs={{0,8},{1,9},{2,10},{3,11},{4,0},{5,1},{6,2},{7,3},{8,16},{9,17},{1... | collective-permute-start | bytes 393224 | tf_op jit(solution)/shard_map/ppermute | solution.py:41
  4.9 5.9 %collective-permute-start.5 = (f32[128,256]{1,0:T(8,128)S(1)}, f32[128,256]{1,0:T(8,128)S(1)}, u32[]{:S(2)}, u32[]{:S(2)}) collective-permute-start(f32[128,256]{1,0:T(8,128)S(1)} %shard_map.316.refs_1_), channel_id=1, source_target_pairs={{0,4},{1,5},{2,6},{3,7},{4,12},{5,13},{6,14},{7,15},{8,0},{9,1},{1... | collective-permute-start | bytes 393224 | tf_op jit(solution)/shard_map/ppermute | solution.py:41
  9.0 5.3 %collective-permute-start.10 = (f32[128,256]{1,0:T(8,128)S(1)}, f32[128,256]{1,0:T(8,128)S(1)}, u32[]{:S(2)}, u32[]{:S(2)}) collective-permute-start(f32[128,256]{1,0:T(8,128)S(1)} %collective-permute-done.6.refs_1_), channel_id=1, source_target_pairs={{0,8},{1,9},{2,10},{3,11},{4,0},{5,1},{6,2},{7,3},{8,16},{9,17},{1... | collective-permute-start | bytes 393224 | tf_op jit(solution)/shard_map/ppermute | solution.py:41
  10.8 5.0 %collective-permute-start.11 = (f32[128,256]{1,0:T(8,128)S(1)}, f32[128,256]{1,0:T(8,128)S(1)}, u32[]{:S(2)}, u32[]{:S(2)}) collective-permute-start(f32[128,256]{1,0:T(8,128)S(1)} %collective-permute-done.5.refs_1_), channel_id=1, source_target_pairs={{0,4},{1,5},{2,6},{3,7},{4,12},{5,13},{6,14},{7,15},{8,0},{9,1},{1... | collective-permute-start | bytes 393224 | tf_op jit(solution)/shard_map/ppermute | solution.py:41
  11.0 12.0 %collective-permute-start.1 = (f32[32,16,128]{2,1,0:T(8,128)}, f32[32,16,128]{2,1,0:T(8,128)S(1)}, u32[]{:S(2)}, u32[]{:S(2)}) collective-permute-start(f32[32,16,128]{2,1,0:T(8,128)} %refs_0_.4), channel_id=1, source_target_pairs={{0,2},{1,3},{2,0},{3,1},{4,6},{5,7},{6,4},{7,5},{8,10},{9,11},{10,... | collective-permute-start | bytes 786440 | tf_op jit(solution)/shard_map/ppermute | solution.py:41
  11.0 8.9 %collective-permute-start.3 = (f32[32,16,64]{2,1,0:T(8,128)}, f32[32,16,64]{2,1,0:T(8,128)S(1)}, u32[]{:S(2)}, u32[]{:S(2)}) collective-permute-start(f32[32,16,64]{2,1,0:T(8,128)} %refs_0_.5), channel_id=1, source_target_pairs={{0,1},{1,0},{2,3},{3,2},{4,5},{5,4},{6,7},{7,6},{8,9},{9,8},{10,11... | collective-permute-start | bytes 393224 | tf_op jit(solution)/shard_map/ppermute | solution.py:41
  14.3 5.7 %collective-permute-start.12 = (f32[128,256]{1,0:T(8,128)S(1)}, f32[128,256]{1,0:T(8,128)S(1)}, u32[]{:S(2)}, u32[]{:S(2)}) collective-permute-start(f32[128,256]{1,0:T(8,128)S(1)} %collective-permute-done.10.refs_2_), channel_id=1, source_target_pairs={{0,8},{1,9},{2,10},{3,11},{4,0},{5,1},{6,2},{7,3},{8,16},{9,17},{1... | collective-permute-start | bytes 393224 | tf_op jit(solution)/shard_map/ppermute | solution.py:41
  15.8 5.3 %collective-permute-start.13 = (f32[128,256]{1,0:T(8,128)S(1)}, f32[128,256]{1,0:T(8,128)S(1)}, u32[]{:S(2)}, u32[]{:S(2)}) collective-permute-start(f32[128,256]{1,0:T(8,128)S(1)} %collective-permute-done.11.refs_3_), channel_id=1, source_target_pairs={{0,4},{1,5},{2,6},{3,7},{4,12},{5,13},{6,14},{7,15},{8,0},{9,1},{1... | collective-permute-start | bytes 393224 | tf_op jit(solution)/shard_map/ppermute | solution.py:41
  19.9 5.3 %collective-permute-start.2 = (f32[32,16,64]{2,1,0:T(8,128)}, f32[32,16,64]{2,1,0:T(8,128)S(1)}, u32[]{:S(2)}, u32[]{:S(2)}) collective-permute-start(f32[32,16,64]{2,1,0:T(8,128)} %refs_0_.5), channel_id=1, source_target_pairs={{0,2},{1,3},{2,0},{3,1},{4,6},{5,7},{6,4},{7,5},{8,10},{9,11},{10,... | collective-permute-start | bytes 393224 | tf_op jit(solution)/shard_map/ppermute | solution.py:41
  20.0 5.3 %collective-permute-start.4 = (f32[32,16,64]{2,1,0:T(8,128)S(1)}, f32[32,16,64]{2,1,0:T(8,128)S(1)}, u32[]{:S(2)}, u32[]{:S(2)}) collective-permute-start(f32[32,16,64]{2,1,0:T(8,128)S(1)} %collective-permute-done.3.refs_2_), channel_id=1, source_target_pairs={{0,2},{1,3},{2,0},{3,1},{4,6},{5,7},{6,4},{7,5},{8,10},{9,11},{10,... | collective-permute-start | bytes 393224 | tf_op jit(solution)/shard_map/ppermute | solution.py:41
  21.2 6.7 %collective-permute-start.14 = (f32[64,256]{1,0:T(8,128)S(1)}, f32[64,256]{1,0:T(8,128)S(1)}, u32[]{:S(2)}, u32[]{:S(2)}) collective-permute-start(f32[64,256]{1,0:T(8,128)S(1)} %slice.32), channel_id=1, source_target_pairs={{0,8},{1,9},{2,10},{3,11},{4,0},{5,1},{6,2},{7,3},{8,16},{9,17},{1... | collective-permute-start | bytes 196616 | tf_op jit(solution)/shard_map/ppermute | solution.py:41
  46.6 21.5 %collective-permute-start.24 = (f32[64,256]{1,0:T(8,128)S(1)}, f32[64,256]{1,0:T(8,128)S(1)}, u32[]{:S(2)}, u32[]{:S(2)}) collective-permute-start(f32[64,256]{1,0:T(8,128)S(1)} %get-tuple-element.217), channel_id=1, source_target_pairs={{0,4},{1,5},{2,6},{3,7},{4,12},{5,13},{6,14},{7,15},{8,0},{9,1},{1... | collective-permute-start | bytes 196616 | tf_op jit(solution)/shard_map/ppermute | solution.py:41
  48.4 17.9 %collective-permute-start.20 = (f32[64,256]{1,0:T(8,128)S(1)}, f32[64,256]{1,0:T(8,128)S(1)}, u32[]{:S(2)}, u32[]{:S(2)}) collective-permute-start(f32[64,256]{1,0:T(8,128)S(1)} %get-tuple-element.218), channel_id=1, source_target_pairs={{0,8},{1,9},{2,10},{3,11},{4,0},{5,1},{6,2},{7,3},{8,16},{9,17},{1... | collective-permute-start | bytes 196616 | tf_op jit(solution)/shard_map/ppermute | solution.py:41
  66.2 8.5 %collective-permute-start.18 = (f32[32,8,128]{2,1,0:T(8,128)S(1)}, f32[32,8,128]{2,1,0:T(8,128)S(1)}, u32[]{:S(2)}, u32[]{:S(2)}) collective-permute-start(f32[32,8,128]{2,1,0:T(8,128)S(1)} %get-tuple-element.149), channel_id=1, source_target_pairs={{0,2},{1,3},{2,0},{3,1},{4,6},{5,7},{6,4},{7,5},{8,10},{9,11},{10,... | collective-permute-start | bytes 393224 | tf_op jit(solution)/shard_map/ppermute | solution.py:41
  66.3 13.3 %collective-permute-start.21 = (f32[128,256]{1,0:T(8,128)S(1)}, f32[128,256]{1,0:T(8,128)S(1)}, u32[]{:S(2)}, u32[]{:S(2)}) collective-permute-start(f32[128,256]{1,0:T(8,128)S(1)} %pad_add_fusion.3), channel_id=1, source_target_pairs={{0,8},{1,9},{2,10},{3,11},{4,0},{5,1},{6,2},{7,3},{8,16},{9,17},{1... | collective-permute-start | bytes 393224 | tf_op jit(solution)/shard_map/ppermute | solution.py:41
  68.2 12.9 %collective-permute-start.25 = (f32[128,256]{1,0:T(8,128)S(1)}, f32[128,256]{1,0:T(8,128)S(1)}, u32[]{:S(2)}, u32[]{:S(2)}) collective-permute-start(f32[128,256]{1,0:T(8,128)S(1)} %pad_add_fusion.2), channel_id=1, source_target_pairs={{0,4},{1,5},{2,6},{3,7},{4,12},{5,13},{6,14},{7,15},{8,0},{9,1},{1... | collective-permute-start | bytes 393224 | tf_op jit(solution)/shard_map/ppermute | solution.py:41
  69.5 21.6 %collective-permute-start.16 = (f32[32,16,128]{2,1,0:T(8,128)S(1)}, f32[32,16,128]{2,1,0:T(8,128)S(1)}, u32[]{:S(2)}, u32[]{:S(2)}) collective-permute-start(f32[32,16,128]{2,1,0:T(8,128)S(1)} %get-tuple-element.137), channel_id=1, source_target_pairs={{0,2},{1,3},{2,0},{3,1},{4,6},{5,7},{6,4},{7,5},{8,10},{9,11},{10,... | collective-permute-start | bytes 786440 | tf_op jit(solution)/shard_map/ppermute | solution.py:41
  74.8 9.0 %collective-permute-start.8 = (f32[32,1,320]{2,1,0:T(1,128)S(1)}, f32[32,1,320]{2,1,0:T(1,128)S(1)}, u32[]{:S(2)}, u32[]{:S(2)}) collective-permute-start(f32[32,1,320]{2,1,0:T(1,128)S(1)} %get-tuple-element.125), channel_id=1, source_target_pairs={{0,2},{1,3},{2,0},{3,1},{4,6},{5,7},{6,4},{7,5},{8,10},{9,11},{10,... | collective-permute-start | bytes 122888 | tf_op jit(solution)/shard_map/ppermute | solution.py:41
  77.9 5.9 %collective-permute-start.17 = (f32[32,16,64]{2,1,0:T(8,128)S(1)}, f32[32,16,64]{2,1,0:T(8,128)S(1)}, u32[]{:S(2)}, u32[]{:S(2)}) collective-permute-start(f32[32,16,64]{2,1,0:T(8,128)S(1)} %get-tuple-element.147), channel_id=1, source_target_pairs={{0,2},{1,3},{2,0},{3,1},{4,6},{5,7},{6,4},{7,5},{8,10},{9,11},{10,... | collective-permute-start | bytes 393224 | tf_op jit(solution)/shard_map/ppermute | solution.py:41
  79.6 5.4 %collective-permute-start.19 = (f32[32,8,128]{2,1,0:T(8,128)S(1)}, f32[32,8,128]{2,1,0:T(8,128)S(1)}, u32[]{:S(2)}, u32[]{:S(2)}) collective-permute-start(f32[32,8,128]{2,1,0:T(8,128)S(1)} %add.50), channel_id=1, source_target_pairs={{0,1},{1,0},{2,3},{3,2},{4,5},{5,4},{6,7},{7,6},{8,9},{9,8},{10,11... | collective-permute-start | bytes 393224 | tf_op jit(solution)/shard_map/ppermute | solution.py:41
  81.1 6.7 %collective-permute-start.22 = (f32[128,256]{1,0:T(8,128)S(1)}, f32[128,256]{1,0:T(8,128)S(1)}, u32[]{:S(2)}, u32[]{:S(2)}) collective-permute-start(f32[128,256]{1,0:T(8,128)S(1)} %add.52), channel_id=1, source_target_pairs={{0,8},{1,9},{2,10},{3,11},{4,0},{5,1},{6,2},{7,3},{8,16},{9,17},{1... | collective-permute-start | bytes 393224 | tf_op jit(solution)/shard_map/ppermute | solution.py:41
  83.8 7.2 %collective-permute-start.26 = (f32[128,256]{1,0:T(8,128)S(1)}, f32[128,256]{1,0:T(8,128)S(1)}, u32[]{:S(2)}, u32[]{:S(2)}) collective-permute-start(f32[128,256]{1,0:T(8,128)S(1)} %add.55), channel_id=1, source_target_pairs={{0,4},{1,5},{2,6},{3,7},{4,12},{5,13},{6,14},{7,15},{8,0},{9,1},{1... | collective-permute-start | bytes 393224 | tf_op jit(solution)/shard_map/ppermute | solution.py:41
  86.3 7.4 %collective-permute-start.30 = (f32[32,16,64]{2,1,0:T(8,128)S(1)}, f32[32,16,64]{2,1,0:T(8,128)S(1)}, u32[]{:S(2)}, u32[]{:S(2)}) collective-permute-start(f32[32,16,64]{2,1,0:T(8,128)S(1)} %get-tuple-element.150.refs_0_.xz), channel_id=1, source_target_pairs={{0,1},{1,0},{2,3},{3,2},{4,5},{5,4},{6,7},{7,6},{8,9},{9,8},{10,11... | collective-permute-start | bytes 393224 | tf_op jit(solution)/shard_map/ppermute | solution.py:41
  87.8 5.8 %collective-permute-start.23 = (f32[128,256]{1,0:T(8,128)S(1)}, f32[128,256]{1,0:T(8,128)S(1)}, u32[]{:S(2)}, u32[]{:S(2)}) collective-permute-start(f32[128,256]{1,0:T(8,128)S(1)} %add.53), channel_id=1, source_target_pairs={{0,8},{1,9},{2,10},{3,11},{4,0},{5,1},{6,2},{7,3},{8,16},{9,17},{1... | collective-permute-start | bytes 393224 | tf_op jit(solution)/shard_map/ppermute | solution.py:41
  92.2 9.6 %collective-permute-start.28 = (f32[32,16,128]{2,1,0:T(8,128)S(1)}, f32[32,16,128]{2,1,0:T(8,128)S(1)}, u32[]{:S(2)}, u32[]{:S(2)}) collective-permute-start(f32[32,16,128]{2,1,0:T(8,128)S(1)} %get-tuple-element.138.xy_a.xy.refs_0_), channel_id=1, source_target_pairs={{0,2},{1,3},{2,0},{3,1},{4,6},{5,7},{6,4},{7,5},{8,10},{9,11},{10,... | collective-permute-start | bytes 786440 | tf_op jit(solution)/shard_map/ppermute | solution.py:41
  92.3 6.8 %collective-permute-start.29 = (f32[32,16,64]{2,1,0:T(8,128)S(1)}, f32[32,16,64]{2,1,0:T(8,128)S(1)}, u32[]{:S(2)}, u32[]{:S(2)}) collective-permute-start(f32[32,16,64]{2,1,0:T(8,128)S(1)} %get-tuple-element.150.refs_0_.xz), channel_id=1, source_target_pairs={{0,2},{1,3},{2,0},{3,1},{4,6},{5,7},{6,4},{7,5},{8,10},{9,11},{10,... | collective-permute-start | bytes 393224 | tf_op jit(solution)/shard_map/ppermute | solution.py:41
  93.7 5.5 %collective-permute-start.31 = (f32[32,16,64]{2,1,0:T(8,128)S(1)}, f32[32,16,64]{2,1,0:T(8,128)S(1)}, u32[]{:S(2)}, u32[]{:S(2)}) collective-permute-start(f32[32,16,64]{2,1,0:T(8,128)S(1)} %collective-permute-done.30.refs_2_), channel_id=1, source_target_pairs={{0,2},{1,3},{2,0},{3,1},{4,6},{5,7},{6,4},{7,5},{8,10},{9,11},{10,... | collective-permute-start | bytes 393224 | tf_op jit(solution)/shard_map/ppermute | solution.py:41
  97.1 5.6 %collective-permute-start.33 = (f32[128,256]{1,0:T(8,128)S(1)}, f32[128,256]{1,0:T(8,128)S(1)}, u32[]{:S(2)}, u32[]{:S(2)}) collective-permute-start(f32[128,256]{1,0:T(8,128)S(1)} %get-tuple-element.161.refs_1_), channel_id=1, source_target_pairs={{0,8},{1,9},{2,10},{3,11},{4,0},{5,1},{6,2},{7,3},{8,16},{9,17},{1... | collective-permute-start | bytes 393224 | tf_op jit(solution)/shard_map/ppermute | solution.py:41
  98.7 5.6 %collective-permute-start.32 = (f32[128,256]{1,0:T(8,128)S(1)}, f32[128,256]{1,0:T(8,128)S(1)}, u32[]{:S(2)}, u32[]{:S(2)}) collective-permute-start(f32[128,256]{1,0:T(8,128)S(1)} %get-tuple-element.161.refs_1_), channel_id=1, source_target_pairs={{0,4},{1,5},{2,6},{3,7},{4,12},{5,13},{6,14},{7,15},{8,0},{9,1},{1... | collective-permute-start | bytes 393224 | tf_op jit(solution)/shard_map/ppermute | solution.py:41
  102.7 5.6 %collective-permute-start.37 = (f32[128,256]{1,0:T(8,128)S(1)}, f32[128,256]{1,0:T(8,128)S(1)}, u32[]{:S(2)}, u32[]{:S(2)}) collective-permute-start(f32[128,256]{1,0:T(8,128)S(1)} %collective-permute-done.33.refs_1_), channel_id=1, source_target_pairs={{0,8},{1,9},{2,10},{3,11},{4,0},{5,1},{6,2},{7,3},{8,16},{9,17},{1... | collective-permute-start | bytes 393224 | tf_op jit(solution)/shard_map/ppermute | solution.py:41
  104.3 5.6 %collective-permute-start.38 = (f32[128,256]{1,0:T(8,128)S(1)}, f32[128,256]{1,0:T(8,128)S(1)}, u32[]{:S(2)}, u32[]{:S(2)}) collective-permute-start(f32[128,256]{1,0:T(8,128)S(1)} %collective-permute-done.32.refs_1_), channel_id=1, source_target_pairs={{0,4},{1,5},{2,6},{3,7},{4,12},{5,13},{6,14},{7,15},{8,0},{9,1},{1... | collective-permute-start | bytes 393224 | tf_op jit(solution)/shard_map/ppermute | solution.py:41
  108.3 5.7 %collective-permute-start.39 = (f32[128,256]{1,0:T(8,128)S(1)}, f32[128,256]{1,0:T(8,128)S(1)}, u32[]{:S(2)}, u32[]{:S(2)}) collective-permute-start(f32[128,256]{1,0:T(8,128)S(1)} %collective-permute-done.37.refs_2_), channel_id=1, source_target_pairs={{0,8},{1,9},{2,10},{3,11},{4,0},{5,1},{6,2},{7,3},{8,16},{9,17},{1... | collective-permute-start | bytes 393224 | tf_op jit(solution)/shard_map/ppermute | solution.py:41
  109.9 5.7 %collective-permute-start.40 = (f32[128,256]{1,0:T(8,128)S(1)}, f32[128,256]{1,0:T(8,128)S(1)}, u32[]{:S(2)}, u32[]{:S(2)}) collective-permute-start(f32[128,256]{1,0:T(8,128)S(1)} %collective-permute-done.38.refs_3_), channel_id=1, source_target_pairs={{0,4},{1,5},{2,6},{3,7},{4,12},{5,13},{6,14},{7,15},{8,0},{9,1},{1... | collective-permute-start | bytes 393224 | tf_op jit(solution)/shard_map/ppermute | solution.py:41
  114.0 5.7 %collective-permute-start.41 = (f32[64,256]{1,0:T(8,128)S(1)}, f32[64,256]{1,0:T(8,128)S(1)}, u32[]{:S(2)}, u32[]{:S(2)}) collective-permute-start(f32[64,256]{1,0:T(8,128)S(1)} %slice.34), channel_id=1, source_target_pairs={{0,8},{1,9},{2,10},{3,11},{4,0},{5,1},{6,2},{7,3},{8,16},{9,17},{1... | collective-permute-start | bytes 196616 | tf_op jit(solution)/shard_map/ppermute | solution.py:41
  123.7 11.1 %collective-permute-start.51 = (f32[64,256]{1,0:T(8,128)S(1)}, f32[64,256]{1,0:T(8,128)S(1)}, u32[]{:S(2)}, u32[]{:S(2)}) collective-permute-start(f32[64,256]{1,0:T(8,128)S(1)} %get-tuple-element.215), channel_id=1, source_target_pairs={{0,4},{1,5},{2,6},{3,7},{4,12},{5,13},{6,14},{7,15},{8,0},{9,1},{1... | collective-permute-start | bytes 196616 | tf_op jit(solution)/shard_map/ppermute | solution.py:41
  124.6 8.5 %collective-permute-start.47 = (f32[64,256]{1,0:T(8,128)S(1)}, f32[64,256]{1,0:T(8,128)S(1)}, u32[]{:S(2)}, u32[]{:S(2)}) collective-permute-start(f32[64,256]{1,0:T(8,128)S(1)} %get-tuple-element.216), channel_id=1, source_target_pairs={{0,8},{1,9},{2,10},{3,11},{4,0},{5,1},{6,2},{7,3},{8,16},{9,17},{1... | collective-permute-start | bytes 196616 | tf_op jit(solution)/shard_map/ppermute | solution.py:41
  133.1 12.5 %collective-permute-start.48 = (f32[128,256]{1,0:T(8,128)S(1)}, f32[128,256]{1,0:T(8,128)S(1)}, u32[]{:S(2)}, u32[]{:S(2)}) collective-permute-start(f32[128,256]{1,0:T(8,128)S(1)} %pad_add_fusion.1), channel_id=1, source_target_pairs={{0,8},{1,9},{2,10},{3,11},{4,0},{5,1},{6,2},{7,3},{8,16},{9,17},{1... | collective-permute-start | bytes 393224 | tf_op jit(solution)/shard_map/ppermute | solution.py:41
  134.8 13.7 %collective-permute-start.52 = (f32[128,256]{1,0:T(8,128)S(1)}, f32[128,256]{1,0:T(8,128)S(1)}, u32[]{:S(2)}, u32[]{:S(2)}) collective-permute-start(f32[128,256]{1,0:T(8,128)S(1)} %pad_add_fusion), channel_id=1, source_target_pairs={{0,4},{1,5},{2,6},{3,7},{4,12},{5,13},{6,14},{7,15},{8,0},{9,1},{1... | collective-permute-start | bytes 393224 | tf_op jit(solution)/shard_map/ppermute | solution.py:41
  145.7 7.2 %collective-permute-start.49 = (f32[128,256]{1,0:T(8,128)S(1)}, f32[128,256]{1,0:T(8,128)S(1)}, u32[]{:S(2)}, u32[]{:S(2)}) collective-permute-start(f32[128,256]{1,0:T(8,128)S(1)} %add.59), channel_id=1, source_target_pairs={{0,8},{1,9},{2,10},{3,11},{4,0},{5,1},{6,2},{7,3},{8,16},{9,17},{1... | collective-permute-start | bytes 393224 | tf_op jit(solution)/shard_map/ppermute | solution.py:41
  148.3 12.0 %collective-permute-start.43 = (f32[32,16,128]{2,1,0:T(8,128)S(1)}, f32[32,16,128]{2,1,0:T(8,128)S(1)}, u32[]{:S(2)}, u32[]{:S(2)}) collective-permute-start(f32[32,16,128]{2,1,0:T(8,128)S(1)} %get-tuple-element.182), channel_id=1, source_target_pairs={{0,2},{1,3},{2,0},{3,1},{4,6},{5,7},{6,4},{7,5},{8,10},{9,11},{10,... | collective-permute-start | bytes 786440 | tf_op jit(solution)/shard_map/ppermute | solution.py:41
  148.5 7.9 %collective-permute-start.53 = (f32[128,256]{1,0:T(8,128)S(1)}, f32[128,256]{1,0:T(8,128)S(1)}, u32[]{:S(2)}, u32[]{:S(2)}) collective-permute-start(f32[128,256]{1,0:T(8,128)S(1)} %add.62), channel_id=1, source_target_pairs={{0,4},{1,5},{2,6},{3,7},{4,12},{5,13},{6,14},{7,15},{8,0},{9,1},{1... | collective-permute-start | bytes 393224 | tf_op jit(solution)/shard_map/ppermute | solution.py:41
  149.9 8.1 %collective-permute-start.34 = (f32[32,1,320]{2,1,0:T(1,128)S(1)}, f32[32,1,320]{2,1,0:T(1,128)S(1)}, u32[]{:S(2)}, u32[]{:S(2)}) collective-permute-start(f32[32,1,320]{2,1,0:T(1,128)S(1)} %get-tuple-element.167), channel_id=1, source_target_pairs={{2,4},{3,5},{4,2},{5,3},{6,8},{7,9},{8,6},{9,7},{10,12},{11,13},{1... | collective-permute-start | bytes 122888 | tf_op jit(solution)/shard_map/ppermute | solution.py:41
  150.5 9.1 %collective-permute-start.35 = (f32[32,1,320]{2,1,0:T(1,128)S(1)}, f32[32,1,320]{2,1,0:T(1,128)S(1)}, u32[]{:S(2)}, u32[]{:S(2)}) collective-permute-start(f32[32,1,320]{2,1,0:T(1,128)S(1)} %get-tuple-element.168), channel_id=1, source_target_pairs={{0,2},{1,3},{2,0},{3,1},{4,6},{5,7},{6,4},{7,5},{8,10},{9,11},{10,... | collective-permute-start | bytes 122888 | tf_op jit(solution)/shard_map/ppermute | solution.py:41
  156.5 5.8 %collective-permute-start.44 = (f32[32,16,64]{2,1,0:T(8,128)S(1)}, f32[32,16,64]{2,1,0:T(8,128)S(1)}, u32[]{:S(2)}, u32[]{:S(2)}) collective-permute-start(f32[32,16,64]{2,1,0:T(8,128)S(1)} %get-tuple-element.194), channel_id=1, source_target_pairs={{0,2},{1,3},{2,0},{3,1},{4,6},{5,7},{6,4},{7,5},{8,10},{9,11},{10,... | collective-permute-start | bytes 393224 | tf_op jit(solution)/shard_map/ppermute | solution.py:41
  156.5 5.9 %collective-permute-start.46 = (f32[32,8,128]{2,1,0:T(8,128)S(1)}, f32[32,8,128]{2,1,0:T(8,128)S(1)}, u32[]{:S(2)}, u32[]{:S(2)}) collective-permute-start(f32[32,8,128]{2,1,0:T(8,128)S(1)} %add.57), channel_id=1, source_target_pairs={{0,1},{1,0},{2,3},{3,2},{4,5},{5,4},{6,7},{7,6},{8,9},{9,8},{10,11... | collective-permute-start | bytes 393224 | tf_op jit(solution)/shard_map/ppermute | solution.py:41
  158.0 6.5 %collective-permute-start.50 = (f32[128,256]{1,0:T(8,128)S(1)}, f32[128,256]{1,0:T(8,128)S(1)}, u32[]{:S(2)}, u32[]{:S(2)}) collective-permute-start(f32[128,256]{1,0:T(8,128)S(1)} %add.60), channel_id=1, source_target_pairs={{0,8},{1,9},{2,10},{3,11},{4,0},{5,1},{6,2},{7,3},{8,16},{9,17},{1... | collective-permute-start | bytes 393224 | tf_op jit(solution)/shard_map/ppermute | solution.py:41
  159.6 5.3 %collective-permute-start.54 = (f32[128,256]{1,0:T(8,128)S(1)}, f32[128,256]{1,0:T(8,128)S(1)}, u32[]{:S(2)}, u32[]{:S(2)}) collective-permute-start(f32[128,256]{1,0:T(8,128)S(1)} %add.63), channel_id=1, source_target_pairs={{0,4},{1,5},{2,6},{3,7},{4,12},{5,13},{6,14},{7,15},{8,0},{9,1},{1... | collective-permute-start | bytes 393224 | tf_op jit(solution)/shard_map/ppermute | solution.py:41
  (22 other events, 205.9 us)
